TPU v7x, 128 devices: a whole 4x4x4 slice. The times are simulated.
128 devices in a mesh: row: 8 (over y, core), col: 16 (over x, z).
Axes of the slice: x: 4, y: 4, z: 4, core: 2. Of those that a mesh axis runs over, the one named last changes fastest.
Arguments:
- theta: float32 [64, 256, 256], P('row', None, 'col'), may hold values from -6 to 6
- left_env: float32 [32, 32, 256, 256], P('row', 'col'), as said below
- right_env: float32 [8, 32, 256, 256], P(None, 'col'), as said below
- left_sector: int32 [64], replicated, may hold values from 0 to 31, as said below
- right_sector: int32 [64], P('row'), may hold values from 0 to 7
- term_on: int32 [64, 32], P('row', 'col'), may hold values 0 or 1
- left_size: int32 [32], replicated, may hold values from 1 to 256, 5120 in all
- right_size: int32 [8], replicated, may hold values from 1 to 256, 1280 in all
Outputs:
- new_theta: float32 [64, 256, 256], P('row', None, 'col')
- energy: float32 [], replicated
Inputs may be any that keep to these rules, and one draw needn't show every extreme that they name: `left_sector`: left sector s belongs to row s // 4. Block k belongs to row k // 8. The 8 blocks of one row name distinct left sectors; they name either none or exactly 2 sectors belonging to any one row, and the blocks of every row name 2 sectors belonging to one common row. `left_env`: each tile is symmetric in its last two dimensions. `right_env`: each tile is symmetric in its last two dimensions.
All inputs are finite; a program needn't handle non-finite values. No bound on the sum of `term_on` on one device may be relied on, other than what follows from the above.
Results may differ from a plain program's by a relative error of at most 0.0001.
Values sent between devices are 32-bit elements; how exact they have to be, the bound alone decides.
No kernel may reach another device: no remote copies, remote signals or barrier semaphores. Data moves between devices by JAX's collectives and lax.ppermute only.
A program may use at most 128 MiB of HBM per device.

v0:
```python
import jax
import jax.numpy as jnp
from jax import lax
from jax.sharding import PartitionSpec as P

ITERS = 2


highest = lax.Precision.HIGHEST


def lookup(small_table, index_list):
    slot_hits = index_list[:, None] == jnp.arange(small_table.shape[0], dtype=jnp.int32)[None, :]
    return jnp.sum(jnp.where(slot_hits, small_table[None, :], 0), axis=1)


def tile_masks(left_ids, right_ids, left_size, right_size, tile_size, offset, span_cols):
    rows_live = lookup(left_size, left_ids)
    cols_live = lookup(right_size, right_ids)
    row_mask = (jnp.arange(tile_size, dtype=jnp.int32)[None, :] < rows_live[:, None]).astype(
        jnp.float32
    )
    col_mask = (
        (offset + jnp.arange(span_cols, dtype=jnp.int32))[None, :] < cols_live[:, None]
    ).astype(jnp.float32)
    return row_mask[:, :, None] * col_mask[:, None, :]


def local(theta, left_env, right_env, left_sector, right_sector, term_on, left_size, right_size):
    row_count = lax.axis_size("row")
    blocks, tile_size, thin_cols = theta.shape
    local_sectors = left_env.shape[0]
    capacity = max(2, 2 * blocks // row_count)
    row_index = lax.axis_index("row")
    col_index = lax.axis_index("col")
    own_left = lax.dynamic_slice_in_dim(left_sector, row_index * blocks, blocks)
    offset = col_index * thin_cols
    span_cols = theta.shape[2]
    start_mask = tile_masks(
        own_left, right_sector, left_size, right_size, tile_size, offset, span_cols
    )
    start_vec = theta * start_mask
    senders = row_index * local_sectors + jnp.arange(local_sectors, dtype=jnp.int32)
    wanted = left_sector.reshape(row_count, blocks)
    used_flag = jnp.any(wanted[:, :, None] == senders[None, None, :], axis=1)
    used_count = used_flag.astype(jnp.int32)
    before = jnp.cumsum(used_count, axis=1) - used_count
    pick_flag = used_flag[:, None, :] & (
        before[:, None, :] == jnp.arange(capacity, dtype=jnp.int32)[None, :, None]
    )
    filled = jnp.any(pick_flag, axis=2).reshape(-1)
    local_index = jnp.sum(
        jnp.where(pick_flag, jnp.arange(local_sectors, dtype=jnp.int32)[None, None, :], 0), axis=2
    ).reshape(-1)
    outgoing = (
        jnp.take(left_env, local_index, axis=0) * filled.astype(jnp.float32)[:, None, None, None]
    )
    arrived = lax.all_to_all(outgoing, "row", split_axis=0, concat_axis=0, tiled=True)
    every_sector = jnp.arange(row_count * local_sectors, dtype=jnp.int32)
    needed = (
        jnp.any(own_left[:, None] == every_sector[None, :], axis=0)
        .astype(jnp.int32)
        .reshape(row_count, local_sectors)
    )
    order_rank = (jnp.cumsum(needed, axis=1) - needed).reshape(-1)
    position = own_left // local_sectors * capacity + lookup(order_rank, own_left)
    left_pick = jnp.take(arrived, position, axis=0)
    right_pick = jnp.take(right_env, right_sector, axis=0)
    weights = term_on.astype(jnp.float32)

    def contract(full_vector):
        middle = (
            jnp.einsum("swia,sab->swib", left_pick, full_vector, precision=highest)
            * weights[:, :, None, None]
        )
        return jnp.einsum("swib,swjb->sij", middle, right_pick, precision=highest)

    def operate(vector):
        full_vector = lax.all_gather(vector, "col", axis=2, tiled=True)
        total_sum = lax.psum_scatter(contract(full_vector), "col", scatter_dimension=2, tiled=True)
        return total_sum * start_mask

    def combine(values):
        reduced = lax.psum(values, ("row", "col"))
        return reduced

    image_vec = operate(start_vec)
    norm_sq, correlation = combine((jnp.sum(start_vec * start_vec), jnp.sum(start_vec * image_vec)))
    inv_norm = 1.0 / jnp.sqrt(norm_sq)
    basis_vec = start_vec * inv_norm
    applied = image_vec * inv_norm
    ritz_value = correlation / norm_sq
    for turn_index in range(ITERS):
        residual = applied - ritz_value * basis_vec
        (res_sq,) = combine((jnp.sum(residual * residual),))
        length = jnp.sqrt(res_sq)
        fresh_vec = residual / length
        fresh_applied = operate(fresh_vec)
        (curvature,) = combine((jnp.sum(fresh_vec * fresh_applied),))
        half_gap = 0.5 * (ritz_value - curvature)
        root_term = jnp.sqrt(half_gap * half_gap + res_sq)
        lowest = 0.5 * (ritz_value + curvature) - root_term
        first_coef = curvature - lowest
        pair_norm = jnp.sqrt(first_coef * first_coef + res_sq)
        basis_vec = (first_coef * basis_vec - length * fresh_vec) / pair_norm
        applied = (first_coef * applied - length * fresh_applied) / pair_norm
        ritz_value = lowest
    total_entries = blocks * row_count * tile_size * tile_size
    output = basis_vec * jnp.sqrt(jnp.float32(total_entries))
    return (output, ritz_value)


def solution(mesh):
    placed = (
        P("row", None, "col"),
        P("row", "col", None, None),
        P(None, "col", None, None),
        P(),
        P("row"),
        P("row", "col"),
        P(),
        P(),
    )
    return jax.shard_map(
        local, mesh=mesh, in_specs=placed, out_specs=(P("row", None, "col"), P()), check_vma=False
    )
```

profile of v0, /device:TPU:1, one launch (start us, length us, event | category | flops | bytes accessed | tf_op | source)
XLA Modules:
  0.0 820.7 jit_solution(7117098073512323360)
XLA Ops:
  7.2 0.9 eq.29
  8.9 4.3 gather_fusion
  13.2 7.9 select_multiply_fusion
  21.1 6.4 all-to-all-start
  28.6 0.7 multiply_multiply_fusion.3
  29.5 4.9 gather_fusion.2
  34.5 86.8 %all-to-all-done = f32[16,2,256,256]{3,2,1,0:T(8,128)} async-done(((f32[16,2,256,256]{3,2,1,0:T(8,128)}), f32[16,2,256,256]{3,2,1,0:T(8,128)}, u32[]{:S(2)}, u32[]{:S(2)}) %all-to-all-start) | async-done | bytes 8388640 | tf_op jit(solution)/shard_map/all_to_all | solution.py:58
  121.4 6.2 gather_fusion.1
  127.6 6.8 fusion.13
  134.4 5.9 fusion.33
  140.3 73.6 %reduce-scatter.4.cloned.1.call-done = f32[8,256,16]{1,2,0:T(8,128)} async-done(((f32[8,256,256]{1,2,0:T(8,128)}), f32[8,256,16]{1,2,0:T(8,128)}) %reduce-scatter.4.cloned.1.call-update) | async-done | bytes 131088 | tf_op jit(solution)/shard_map/reduce_scatter | solution.py:80
  213.9 1.6 multiply_reduce_fusion.4
  215.6 65.9 %all-reduce = (f32[]{:T(128)}, f32[]{:T(128)}) all-reduce(f32[]{:T(128)} %get-tuple-element.3, f32[]{:T(128)} %get-tuple-element.2), channel_id=1, replica_groups=mesh['row'=8,'col'=16] {'row','col'}, use_global_device_ids=true, to_apply=%region_13.14 | all-reduce | flops 2 | bytes 16 | tf_op jit(solution)/shard_map/psum | solution.py:84
  283.5 1.6 multiply_reduce_fusion.2
  285.1 62.7 %psum.44 = f32[]{:T(128)} all-reduce(f32[]{:T(128)} %multiply_reduce_fusion.2), channel_id=1, replica_groups=mesh['row'=8,'col'=16] {'row','col'}, use_global_device_ids=true, to_apply=%region_15.16 | all-reduce | flops 1 | bytes 8 | tf_op jit(solution)/shard_map/psum | solution.py:84
  348.5 1.7 broadcast_divide_fusion.1
  350.2 41.4 %all-gather.6.cloned.1.call-done = f32[8,256,256]{1,2,0:T(8,128)} async-done(((f32[8,256,16]{1,2,0:T(8,128)}), f32[8,256,256]{1,2,0:T(8,128)}) %all-gather.6.cloned.1.call-update) | async-done | bytes 2097168 | tf_op jit(solution)/shard_map/all_gather | solution.py:79
  391.6 6.8 fusion.11
  398.5 5.9 fusion.38
  404.4 73.2 %reduce-scatter.6.cloned.1.call-done = f32[8,256,16]{1,2,0:T(8,128)} async-done(((f32[8,256,256]{1,2,0:T(8,128)}), f32[8,256,16]{1,2,0:T(8,128)}) %reduce-scatter.6.cloned.1.call-update) | async-done | bytes 131088 | tf_op jit(solution)/shard_map/reduce_scatter | solution.py:80
  477.6 1.6 multiply_reduce_fusion.1
  479.2 65.8 %psum.45 = f32[]{:T(128)} all-reduce(f32[]{:T(128)} %multiply_reduce_fusion.1), channel_id=1, replica_groups=mesh['row'=8,'col'=16] {'row','col'}, use_global_device_ids=true, to_apply=%region_18.19 | all-reduce | flops 1 | bytes 8 | tf_op jit(solution)/shard_map/psum | solution.py:84
  548.3 1.7 multiply_reduce_fusion
  550.0 62.5 %psum.46 = f32[]{:T(128)} all-reduce(f32[]{:T(128)} %get-tuple-element.8), channel_id=1, replica_groups=mesh['row'=8,'col'=16] {'row','col'}, use_global_device_ids=true, to_apply=%region_20.21 | all-reduce | flops 1 | bytes 8 | tf_op jit(solution)/shard_map/psum | solution.py:84
  613.2 0.7 broadcast_divide_fusion
  614.2 41.2 %all-gather.8.cloned.1.call-done = f32[8,256,256]{1,2,0:T(8,128)} async-done(((f32[8,256,16]{1,2,0:T(8,128)}), f32[8,256,256]{1,2,0:T(8,128)}) %all-gather.8.cloned.1.call-update) | async-done | bytes 2097168 | tf_op jit(solution)/shard_map/all_gather | solution.py:79
  655.3 6.8 fusion.9
  662.1 5.9 fusion.43
  668.0 73.2 %reduce-scatter.8.cloned.1.call-done = f32[8,256,16]{1,2,0:T(8,128)} async-done(((f32[8,256,256]{1,2,0:T(8,128)}), f32[8,256,16]{1,2,0:T(8,128)}) %reduce-scatter.8.cloned.1.call-update) | async-done | bytes 131088 | tf_op jit(solution)/shard_map/reduce_scatter | solution.py:80
  741.3 1.6 fusion.49
  742.9 65.8 %psum.47 = f32[]{:T(128)} all-reduce(f32[]{:T(128)} %fusion.49), channel_id=1, replica_groups=mesh['row'=8,'col'=16] {'row','col'}, use_global_device_ids=true, to_apply=%region_23.24 | all-reduce | flops 1 | bytes 8 | tf_op jit(solution)/shard_map/psum | solution.py:84
  812.0 0.8 divide_multiply_fusion
  (72 shorter events, 2.5 us)
Async XLA Ops:
  7.2 1.7 copy-start
  21.1 6.4 copy-start.7
  21.1 6.9 copy-start.10
  21.1 7.0 copy-start.11
  21.1 7.1 copy-start.9
  21.1 7.5 copy-start.4
  21.1 8.3 %copy-start.8 = (s32[8,2]{0,1:T(2,128)S(1)}, s32[8,2]{0,1:T(2,128)}, u32[]{:S(2)}) copy-start(s32[8,2]{0,1:T(2,128)} %param.13) | copy-start | bytes 196
  21.1 100.3 %all-to-all-start = ((f32[16,2,256,256]{3,2,1,0:T(8,128)}), f32[16,2,256,256]{3,2,1,0:T(8,128)}, u32[]{:S(2)}, u32[]{:S(2)}) async-start(f32[16,2,256,256]{3,2,1,0:T(8,128)} %select_multiply_fusion), calls=%async_computation | async-start | bytes 16777216 | tf_op jit(solution)/shard_map/all_to_all | solution.py:58
  27.5 100.0 %all-gather.4.cloned.1.call-start = ((), (), s32[]{:S(2)}) async-start(), calls=%async_computation.4 | async-start | bytes 2228224 | tf_op jit(solution)/shard_map/all_gather | solution.py:79
  29.3 184.6 %reduce-scatter.4.cloned.1.call-start = ((), (), s32[]{:S(2)}) async-start(), calls=%async_computation.5 | async-start | bytes 2228224 | tf_op jit(solution)/shard_map/reduce_scatter | solution.py:80
  127.6 6.8 copy-start.1
  140.3 251.4 %all-gather.6.cloned.1.call-start = ((), (), s32[]{:S(2)}) async-start(), calls=%async_computation.6 | async-start | bytes 2228224 | tf_op jit(solution)/shard_map/all_gather | solution.py:79
  350.2 127.4 %reduce-scatter.6.cloned.1.call-start = ((), (), s32[]{:S(2)}) async-start(), calls=%async_computation.7 | async-start | bytes 2228224 | tf_op jit(solution)/shard_map/reduce_scatter | solution.py:80
  391.6 6.8 copy-start.2
  398.4 79.2 %copy-start.5 = (f32[8,256,16]{1,2,0:T(8,128)S(1)}, f32[8,256,16]{1,2,0:T(8,128)}, u32[]{:S(2)}) copy-start(f32[8,256,16]{1,2,0:T(8,128)} %broadcast_divide_fusion.1) | copy-start | bytes 393220
  398.4 149.9 %copy-start.6 = (f32[8,256,16]{1,2,0:T(8,128)S(1)}, f32[8,256,16]{1,2,0:T(8,128)}, u32[]{:S(2)}) copy-start(f32[8,256,16]{1,2,0:T(8,128)} %reduce-scatter.4.cloned.1.call-done) | copy-start | bytes 393220
  404.4 251.0 %all-gather.8.cloned.1.call-start = ((), (), s32[]{:S(2)}) async-start(), calls=%async_computation.8 | async-start | bytes 2228224 | tf_op jit(solution)/shard_map/all_gather | solution.py:79
  613.9 127.4 %reduce-scatter.8.cloned.1.call-start = ((), (), s32[]{:S(2)}) async-start(), calls=%async_computation.9 | async-start | bytes 2228224 | tf_op jit(solution)/shard_map/reduce_scatter | solution.py:80
  655.3 6.8 copy-start.3
Sparse Core Ops, SparseCore 0:
  31.1 46.3 all-gather.3
  140.4 73.5 reduce-scatter.3
  350.3 41.2 all-gather.5
  404.5 73.0 reduce-scatter.5
  614.0 41.2 all-gather.7
  668.2 73.0 reduce-scatter.7
where the time goes:
time: 822 us; the launch traced here: 821 us
  waiting for transfers between devices  390 us (47%)
  blocking collectives  323 us (39%)
  matrix products  38 us (5%)
  between operations  25.5 us (3%)
  other arithmetic  21.1 us (3%)
  local copies, waits for them, and re-layouts  17.1 us (2%)
    psum x5, blocking collectives, combine(): reduced = lax.psum(values, ('row', 'col'))  323 us
    reduce_scatter x3, waiting for transfers between devices, operate(): lax.psum_scatter(contract(full_vector), 'col', scatter_dimension=2, tiled...  220 us
    all_to_all x1, waiting for transfers between devices, local(): lax.all_to_all(outgoing, 'row', split_axis=0, concat_axis=0, tiled=True)  86.8 us
    all_gather x3, waiting for transfers between devices, operate(): full_vector = lax.all_gather(vector, 'col', axis=2, tiled=True)  82.6 us
    dot_general x3, matrix products, contract(): jnp.einsum('swia,sab->swib', left_pick, full_vector, precision=highest)  20.3 us
    dot_general x3, matrix products, contract(): return jnp.einsum('swib,swjb->sij', middle, right_pick, precision=highest)  17.6 us
  transfers between devices with their start and end apart: 7, of which 6 were waited for; matrix products, arithmetic and copies ran while one was open for 2% of the time, Pallas kernels for 0%

commit v1 on v0

v1 whole, which is shorter than its diff:
```python
import jax
import jax.numpy as jnp
from jax import lax
from jax.sharding import Mesh, PartitionSpec as P

ITERS = 2
HALF = 128
COL = ("x", "z")
ALL = ("y", "c", "x", "z")
SWAP = [(0, 1), (1, 0)]
high = lax.Precision.HIGH


def grids():
    i = lax.broadcasted_iota(jnp.int32, (HALF, HALF), 0)
    j = lax.broadcasted_iota(jnp.int32, (HALF, HALF), 1)
    return i, j


def pack(tiles):
    i, j = grids()
    a00 = tiles[:, :HALF, :HALF]
    a01 = tiles[:, :HALF, HALF:]
    a11 = tiles[:, HALF:, HALF:]
    fold = jnp.where(i >= j, a00, a11)
    diag = jnp.sum(jnp.where(i == j, a11, 0.0), axis=1, keepdims=True)
    extra = jnp.pad(diag, ((0, 0), (0, 7), (0, HALF)))
    return jnp.concatenate([jnp.concatenate([fold, a01], axis=2), extra], axis=1)


def unpack(packed):
    i, j = grids()
    fold = packed[:, :HALF, :HALF]
    a01 = packed[:, :HALF, HALF:]
    diag = packed[:, HALF : HALF + 1, :HALF]
    flip = jnp.swapaxes(fold, 1, 2)
    a00 = jnp.where(i >= j, fold, flip)
    a11 = jnp.where(i == j, diag, jnp.where(i < j, fold, flip))
    top = jnp.concatenate([a00, a01], axis=2)
    low = jnp.concatenate([jnp.swapaxes(a01, 1, 2), a11], axis=2)
    return jnp.concatenate([top, low], axis=1)


def safe_div(value, norm):
    return jnp.where(norm > 0.0, value / jnp.where(norm > 0.0, norm, 1.0), 0.0)


def in_order(core, own, other):
    return jnp.where(
        core == 0, jnp.concatenate([own, other]), jnp.concatenate([other, own])
    )


def ritz_pair(stats):
    norm, a1, b1, a2, b2, a3 = [stats[:, m] for m in range(6)]

    def apply(x):
        return jnp.stack(
            [
                a1 * x[0] + b1 * x[1],
                b1 * x[0] + a2 * x[1] + b2 * x[2],
                b2 * x[1] + a3 * x[2],
            ]
        )

    zero = jnp.zeros_like(norm)
    start = jnp.stack([norm, zero, zero])
    image = apply(start)
    norm_sq = jnp.sum(start * start)
    correlation = jnp.sum(start * image)
    inv_norm = 1.0 / jnp.sqrt(norm_sq)
    basis = start * inv_norm
    applied = image * inv_norm
    ritz = correlation / norm_sq
    for _ in range(ITERS):
        residual = applied - ritz * basis
        res_sq = jnp.sum(residual * residual)
        length = jnp.sqrt(res_sq)
        fresh = residual / length
        fresh_applied = apply(fresh)
        curvature = jnp.sum(fresh * fresh_applied)
        half_gap = 0.5 * (ritz - curvature)
        root = jnp.sqrt(half_gap * half_gap + res_sq)
        lowest = 0.5 * (ritz + curvature) - root
        first = curvature - lowest
        pair = jnp.sqrt(first * first + res_sq)
        basis = (first * basis - length * fresh) / pair
        applied = (first * applied - length * fresh_applied) / pair
        ritz = lowest
    return basis, ritz


def local(theta, left_env, right_env, left_sector, right_sector, term_on, left_size, right_size):
    plane = lax.axis_index("y")
    core = lax.axis_index("c")
    place = lax.axis_index(COL)
    tile = theta.shape[1]
    blocks = theta.shape[0]
    thin = jnp.swapaxes(theta, 1, 2)

    about = jnp.concatenate([right_sector[:, None], term_on], axis=1)
    about16 = in_order(core, about, lax.ppermute(about, "c", SWAP))
    thin16 = in_order(core, thin, lax.ppermute(thin, "c", SWAP))
    right16 = about16[:, 0]
    on16 = jnp.where(core == 0, about16[:, 1], about16[:, 2]).astype(jnp.float32)
    left16 = lax.dynamic_slice_in_dim(left_sector, plane * 16, 16)

    mine = pack(lax.dynamic_index_in_dim(left_env, core, 1, keepdims=False))
    theirs = pack(lax.dynamic_index_in_dim(left_env, 1 - core, 1, keepdims=False))
    eight = in_order(core, mine, lax.ppermute(theirs, "c", SWAP))
    every = lax.all_gather(eight, "y", axis=0, tiled=True)

    right_term = lax.dynamic_index_in_dim(right_env, core, 1, keepdims=False)
    right_slots = pack(jnp.take(right_term, right16, axis=0) * on16[:, None, None])
    slots = jnp.concatenate([right_slots, thin16], axis=1)
    arrived = lax.all_to_all(slots, COL, 0, 0, tiled=True)
    right = unpack(arrived[:, :136])
    block = arrived[:, 136:].reshape(tile, tile)

    left = unpack(lax.all_to_all(jnp.take(every, left16, axis=0), COL, 0, 0, tiled=True))

    live_left = left_size[left16[place]]
    live_right = right_size[right16[place]]
    at = lax.broadcasted_iota(jnp.int32, (tile, tile), 0)
    along = lax.broadcasted_iota(jnp.int32, (tile, tile), 1)
    mask = ((at < live_right) & (along < live_left)).astype(jnp.float32)

    def half_image(u):
        middle = jnp.einsum("wjb,bi->wji", right, u, precision=high)
        return jnp.einsum("wja,wai->ji", middle, left, precision=high)

    def operate(u):
        part = half_image(u)
        return (part + lax.ppermute(part, "c", SWAP)) * mask

    start = block * mask
    norm = jnp.sqrt(jnp.sum(start * start))
    q1 = safe_div(start, norm)
    h1 = operate(q1)
    a1 = jnp.sum(q1 * h1)
    w1 = h1 - a1 * q1
    w1 = w1 - jnp.sum(q1 * w1) * q1
    b1 = jnp.sqrt(jnp.sum(w1 * w1))
    q2 = safe_div(w1, b1)
    h2 = operate(q2)
    a2 = jnp.sum(q2 * h2)
    w2 = h2 - a2 * q2 - b1 * q1
    w2 = w2 - jnp.sum(q2 * w2) * q2 - jnp.sum(q1 * w2) * q1
    b2 = jnp.sqrt(jnp.sum(w2 * w2))
    q3 = safe_div(w2, b2)
    a3 = jnp.sum(q3 * half_image(q3))

    sent = jnp.where(core == 0, q2, q3).reshape(16, theta.shape[2], tile)
    got = lax.all_to_all(sent, COL, 0, 0, tiled=True)
    keep = lax.dynamic_slice_in_dim(got, core * blocks, blocks)
    give = lax.dynamic_slice_in_dim(got, (1 - core) * blocks, blocks)
    back = lax.ppermute(give, "c", SWAP)
    thin2 = jnp.where(core == 0, keep, back)
    thin3 = jnp.where(core == 0, back, keep)

    zero = jnp.float32(0.0)
    mine_stats = jnp.stack([norm, a1, b1, a2, b2, a3, zero, zero])
    stats = lax.all_to_all(jnp.broadcast_to(mine_stats, (128, 8)), ALL, 0, 0, tiled=True)
    stats = stats.reshape(4, 2, 16, 8)
    both = jnp.concatenate([stats[:, 0, :, :5], stats[:, 0, :, 5:] + stats[:, 1, :, 5:]], axis=2)
    both = both.reshape(64, 8)
    basis, ritz = ritz_pair(both)

    scale = jnp.sqrt(jnp.float32(64 * tile * tile))
    row = plane * 2 + core
    first = safe_div(basis[0], both[:, 0])
    coef = jnp.stack([first, basis[1], basis[2]]) * scale
    coef = lax.dynamic_slice_in_dim(coef, row * blocks, blocks, axis=1)
    own_left = lax.dynamic_slice_in_dim(left16, core * blocks, blocks)
    rows_live = left_size[own_left]
    cols_live = right_size[right_sector]
    cols = place * theta.shape[2] + lax.broadcasted_iota(jnp.int32, thin.shape, 1)
    rows = lax.broadcasted_iota(jnp.int32, thin.shape, 2)
    live = (cols < cols_live[:, None, None]) & (rows < rows_live[:, None, None])
    out = (
        coef[0][:, None, None] * jnp.where(live, thin, 0.0)
        + coef[1][:, None, None] * thin2
        + coef[2][:, None, None] * thin3
    )
    return jnp.swapaxes(out, 1, 2), ritz


def solution(mesh):
    fine = Mesh(mesh.devices.reshape(4, 2, 4, 4), ALL)
    row = ("y", "c")
    placed = (
        P(row, None, COL),
        P(row, COL, None, None),
        P(None, COL, None, None),
        P(),
        P(row),
        P(row, COL),
        P(),
        P(),
    )
    return jax.shard_map(
        local, mesh=fine, in_specs=placed, out_specs=(P(row, None, COL), P()), check_vma=False
    )
```

time: 822 us -> 209 us (0.25)
  waiting for transfers between devices: 390 us -> 63.4 us
  blocking collectives: 323 us -> 0 us
  starting transfers between devices: 6.83 us -> 30 us
  matrix products: 38 us -> 18 us
  local copies, waits for them, and re-layouts: 17.1 us -> 31.4 us
  other arithmetic: 21.1 us -> 33 us
    psum x5 -> x0, blocking collectives: 323 us -> none  [combine(): reduced = lax.psum(values, ('row', 'col'))]
    reduce_scatter x3 -> x0, waiting for transfers between devices: 220 us -> none  [operate(): lax.psum_scatter(contract(full_vector), 'col', scatter_dimension=2, tiled...]
    all_to_all x1 -> x4, waiting for transfers between devices: 86.8 us -> 24.9 us  [the longest x1 16.2 us: local(): lax.all_to_all(jnp.take(every, left16, axis=0), COL, 0, 0, tiled=True)]
    all_gather x3 -> x1, waiting for transfers between devices: 82.6 us -> 34.8 us  [local(): every = lax.all_gather(eight, 'y', axis=0, tiled=True)]
    dot_general x6, matrix products: 38 us -> 18 us  [the longest x3 10.8 us: half_image(): middle = jnp.einsum('wjb,bi->wji', right, u, precision=high)]
    all_to_all x1 -> x4, starting transfers between devices: 6.4 us -> 22.7 us  [the longest x1 7.68 us: local(): arrived = lax.all_to_all(slots, COL, 0, 0, tiled=True)]
    select_n x2 -> x13, other arithmetic: 0.01 us -> 12.6 us  [the longest x1 5.35 us: unpack(): a00 = jnp.where(i >= j, fold, flip)]
  transfers between devices with their start and end apart: 7 -> 11, of which waited for: 6 -> 6; matrix products, arithmetic and copies ran while one was open for 2% -> 16% of each run, Pallas kernels for 0% -> 0%
where the time goes in v1:
time: 209 us; the launch traced here: 208 us
  waiting for transfers between devices  63.4 us (30%)
  other arithmetic  33 us (16%)
  between operations  31.8 us (15%)
  local copies, waits for them, and re-layouts  31.4 us (15%)
  starting transfers between devices  30 us (14%)
  matrix products  18 us (9%)
    all_gather x1, waiting for transfers between devices, local(): every = lax.all_gather(eight, 'y', axis=0, tiled=True)  34.8 us
    all_to_all x1, waiting for transfers between devices, local(): lax.all_to_all(jnp.take(every, left16, axis=0), COL, 0, 0, tiled=True)  16.2 us
    dot_general x3, matrix products, half_image(): middle = jnp.einsum('wjb,bi->wji', right, u, precision=high)  10.8 us
    all_to_all x1, waiting for transfers between devices, local(): lax.all_to_all(jnp.broadcast_to(mine_stats, (128, 8)), ALL, 0, 0, tiled=T...  8.72 us
    all_to_all x1, starting transfers between devices, local(): arrived = lax.all_to_all(slots, COL, 0, 0, tiled=True)  7.68 us
    dot_general x3, matrix products, half_image(): return jnp.einsum('wja,wai->ji', middle, left, precision=high)  7.13 us
    all_to_all x1, starting transfers between devices, local(): lax.all_to_all(jnp.take(every, left16, axis=0), COL, 0, 0, tiled=True)  6.71 us
    slice x3, local copies, waits for them, and re-layouts, unpack(): fold = packed[:, :HALF, :HALF]  5.98 us
  transfers between devices with their start and end apart: 11, of which 6 were waited for; matrix products, arithmetic and copies ran while one was open for 16% of the time, Pallas kernels for 0%

profile of v1, /device:TPU:1, one launch (start us, length us, event | category | flops | bytes accessed | tf_op | source)
XLA Modules:
  0.0 207.7 jit_solution(6810230765719790135)
XLA Ops:
  7.2 1.7 dynamic-slice_bitcast_fusion.1
  9.2 1.5 collective-permute-start.2
  10.7 1.6 collective-permute-done.2
  14.1 1.8 dynamic-slice_bitcast_fusion
  16.0 2.8 %gather_fusion = f32[16,256,256]{2,1,0:T(8,128)} fusion(f32[8,256,256]{2,1,0:T(8,128)S(1)} %dynamic-slice_bitcast_fusion, s32[1024]{0:T(1024)S(1)} %pad_clamp_fusion.3), kind=kCustom, calls=%fused_computation | custom fusion | bytes 8388672 | tf_op jit(solution)/shard_map/jit(_take)/gather | solution.py:114
  18.8 2.8 %select_multiply_fusion = f32[16,256,256]{2,1,0:T(8,128)S(1)} fusion(f32[16,256,256]{2,1,0:T(8,128)} %gather_fusion, f32[16]{0:T(128)S(1)} %get-tuple-element.64, pred[16]{0:T(512)(128)(4,1)S(1)} %and_bitcast_fusion), kind=kLoop, calls=%fused_computation.6 | loop fusion | flops 2097152 | bytes 8388688 | tf_op jit(solution)/shard_map/mul | solution.py:114
  21.9 1.7 fusion
  23.6 7.7 %all-to-all-start = ((f32[16,152,256]{2,1,0:T(8,128)}), f32[16,152,256]{2,1,0:T(8,128)S(1)}, u32[]{:S(2)}, u32[]{:S(2)}) async-start(f32[16,152,256]{2,1,0:T(8,128)} %fusion), calls=%async_computation | async-start | bytes 4980736 | tf_op jit(solution)/shard_map/all_to_all | solution.py:116
  31.4 34.8 %all-gather.2.cloned.1.call-done = f32[32,136,256]{2,1,0:T(8,128)} async-done(((f32[8,136,256]{2,1,0:T(8,128)}), f32[32,136,256]{2,1,0:T(8,128)}) %all-gather.2.cloned.1.call-update) | async-done | bytes 4456464 | tf_op jit(solution)/shard_map/all_gather | solution.py:111
  66.2 4.4 %gather_fusion.1 = f32[16,136,256]{2,1,0:T(8,128)} fusion(f32[32,136,256]{2,1,0:T(8,128)} %all-gather.2.cloned.1.call-done, s32[1024]{0:T(1024)S(1)} %pad_clamp_fusion.2), kind=kCustom, calls=%fused_computation.1 | custom fusion | bytes 4456512 | tf_op jit(solution)/shard_map/jit(_take)/gather | solution.py:120
  70.6 3.3 %broadcast_select_fusion = f32[16,136,256]{2,1,0:T(8,128)} fusion(f32[16,136,256]{2,1,0:T(8,128)} %gather_fusion.1, pred[16]{0:T(512)(128)(4,1)S(1)} %get-tuple-element.20), kind=kLoop, calls=%fused_computation.18 | loop fusion | flops 557056 | bytes 4456464 | tf_op jit(solution)/shard_map/jit(_take)/select_n | solution.py:120
  74.0 6.7 %all-to-all-start.1 = ((f32[16,136,256]{2,1,0:T(8,128)}), f32[16,136,256]{2,1,0:T(8,128)}, u32[]{:S(2)}, u32[]{:S(2)}) async-start(f32[16,136,256]{2,1,0:T(8,128)} %broadcast_select_fusion), calls=%async_computation.1 | async-start | bytes 4456448 | tf_op jit(solution)/shard_map/all_to_all | solution.py:120
  91.5 2.5 %copy.54 = f32[16,128,128]{1,2,0:T(8,128)} copy(f32[16,128,128]{2,1,0:T(8,128)} %slice.189) | data formatting | bytes 2097152 | tf_op jit(solution)/shard_map/slice | solution.py:33
  94.1 16.2 %all-to-all-done.1 = f32[16,136,256]{2,1,0:T(8,128)} async-done(((f32[16,136,256]{2,1,0:T(8,128)}), f32[16,136,256]{2,1,0:T(8,128)}, u32[]{:S(2)}, u32[]{:S(2)}) %all-to-all-start.1) | async-done | bytes 2228256 | tf_op jit(solution)/shard_map/all_to_all | solution.py:120
  110.3 2.3 %slice.198 = f32[16,128,128]{2,1,0:T(8,128)} slice(f32[16,136,256]{2,1,0:T(8,128)} %all-to-all-done.1), slice={[0:16], [0:128], [0:128]} | slice | bytes 2097152 | tf_op jit(solution)/shard_map/slice | solution.py:33
  112.7 2.6 %copy.66 = f32[16,128,128]{1,2,0:T(8,128)} copy(f32[16,128,128]{2,1,0:T(8,128)} %slice.198) | data formatting | bytes 2097152
  116.1 5.4 %bitcast_select_fusion.1 = (f32[16,128,128]{2,1,0:T(8,128)}, f32[16,128,128]{2,1,0:T(8,128)}, f32[16,128,128]{2,1,0:T(8,128)}, f32[16,128,128]{2,1,0:T(8,128)}, ...) fusion(f32[16,128,128]{1,2,0:T(8,128)} %copy.66, ...), kind=kLoop, calls=%fused_computation.21 | loop fusion | flops 1572864 | bytes 13697024 | tf_op jit(solution)/shard_map/jit(_where)/select_n | solution.py:37
  121.5 1.6 copy.56
  123.1 2.5 %copy.67 = f32[16,128,128]{1,2,0:T(8,128)} copy(f32[16,128,128]{2,1,0:T(8,128)} %get-tuple-element.33) | data formatting | bytes 2097152
  125.7 3.6 %fusion.7 = f32[16,256,256]{2,1,0:T(8,128)S(1)} fusion(f32[16,128,128]{2,1,0:T(8,128)} %get-tuple-element.46, f32[16,128,128]{2,1,0:T(8,128)S(1)} %copy.56, f32[16,128,128]{2,1,0:T(8,128)S(1)} %copy-done.2, f32[16,128,128]{2,1,0:T(8,128)} %get-tuple-element.47, f32[256,256]{1,0:T(8,128)S(1)} %fusion.10), kind=kOutput, calls=%fused_computation.31 | convolution fusion | flops 1613758464 | bytes 8650752 | tf_op jit(solution)/shard_map/wjb,bi->wji/dot_general | solution.py:129
  129.4 2.2 %convolution_bitcast_fusion.2 = f32[256,256]{1,0:T(8,128)S(1)} fusion(f32[16,256,256]{2,1,0:T(8,128)S(1)} %fusion.7, f32[16,128,128]{2,1,0:T(8,128)S(1)} %copy-done.12, f32[16,128,128]{2,1,0:T(8,128)S(1)} %bitcast.176, f32[16,128,128]{2,1,0:T(8,128)S(1)} %copy-done.3, f32[16,128,128]{2,1,0:T(8,128)S(1)} %copy-done.9), kind=kOutput, calls=%fused_computation.15 | convolution fusion | flops 1613758464 | bytes 8650752 | tf_op jit(solution)/shard_map/wja,wai->ji/dot_general | solution.py:130
  131.5 3.6 %collective-permute-start.3 = (f32[256,256]{1,0:T(8,128)S(1)}, f32[256,256]{1,0:T(8,128)S(1)}, u32[]{:S(2)}, u32[]{:S(2)}) collective-permute-start(f32[256,256]{1,0:T(8,128)S(1)} %convolution_bitcast_fusion.2), channel_id=1, source_target_pairs={{0,16},{16,0},{1,17},{17,1},{2,18},{18,2},{3,19},{19,3},{4,20},{20... | collective-permute-start | bytes 786440 | tf_op jit(solution)/shard_map/ppermute | solution.py:134
  138.5 2.0 multiply_reduce_fusion.4
  142.7 3.6 %fusion.6 = f32[16,256,256]{2,1,0:T(8,128)S(1)} fusion(f32[16,128,128]{2,1,0:T(8,128)} %get-tuple-element.46, f32[16,128,128]{2,1,0:T(8,128)S(1)} %copy.56, f32[16,128,128]{2,1,0:T(8,128)S(1)} %copy-done.2, f32[16,128,128]{2,1,0:T(8,128)} %get-tuple-element.47, f32[256,256]{1,0:T(8,128)S(1)} %divide_select_fusion.1), kind=kOutput, calls=%fused_computation.30 | convolution fusion | flops 1613758464 | bytes 8650752 | tf_op jit(solution)/shard_map/wjb,bi->wji/dot_general | solution.py:129
  146.4 2.2 %convolution_bitcast_fusion.1 = f32[256,256]{1,0:T(8,128)S(1)} fusion(f32[16,256,256]{2,1,0:T(8,128)S(1)} %fusion.6, f32[16,128,128]{2,1,0:T(8,128)S(1)} %copy-done.13, f32[16,128,128]{2,1,0:T(8,128)S(1)} %bitcast.177, f32[16,128,128]{2,1,0:T(8,128)S(1)} %copy-done.4, f32[16,128,128]{2,1,0:T(8,128)S(1)} %copy-done.10), kind=kOutput, calls=%fused_computation.14 | convolution fusion | flops 1613758464 | bytes 8650752 | tf_op jit(solution)/shard_map/wja,wai->ji/dot_general | solution.py:130
  152.5 2.7 %multiply_reduce_fusion = (f32[]{:T(128)}, f32[256,256]{1,0:T(8,128)S(1)}) fusion(f32[]{:T(128)} %get-tuple-element.7, f32[256,256]{1,0:T(8,128)S(1)} %divide_select_fusion.1, f32[]{:T(128)} %get-tuple-element.6, f32[]{:T(128)} %sqrt.31, f32[256,256]{1,0:T(8,128)S(1)} %get-tuple-element.17, f32[]{:T(128)} %get-tuple-element.16, f32[]{:T(128)S(6)} %select_n.228, ...), kind=kLoop, calls=%fused_computation.47 | loop fusion | flops 917503 | bytes 1049113 | tf_op jit(solution)/shard_map/reduce_sum | solution.py:149
  155.8 3.6 %fusion.5 = f32[16,256,256]{2,1,0:T(8,128)S(1)} fusion(f32[16,128,128]{2,1,0:T(8,128)} %get-tuple-element.46, f32[16,128,128]{2,1,0:T(8,128)S(1)} %copy.56, f32[16,128,128]{2,1,0:T(8,128)S(1)} %copy-done.2, f32[16,128,128]{2,1,0:T(8,128)} %get-tuple-element.47, f32[256,256]{1,0:T(8,128)S(1)} %get-tuple-element.15, f32[]{:T(128)S(6)} %select_n.249, pred[]{:T(512)S(6)} %gt.28), kind=kOutput, calls=%fused_computation.29 | convolution fusion | flops 1613889536 | bytes 8650757 | tf_op jit(solution)/shard_map/wjb,bi->wji/dot_general | solution.py:129
  159.5 2.8 %fusion.8 = f32[]{:T(128)} fusion(f32[16,256,256]{2,1,0:T(8,128)S(1)} %fusion.5, f32[16,128,128]{2,1,0:T(8,128)S(1)} %copy-done.14, f32[16,128,128]{2,1,0:T(8,128)S(1)} %bitcast.178, f32[16,128,128]{2,1,0:T(8,128)S(1)} %copy-done.5, f32[16,128,128]{2,1,0:T(8,128)S(1)} %copy-done.11, f32[256,256]{1,0:T(8,128)S(1)} %get-tuple-element.15, f32[]{:T(128)S(6)} %select_n.249, ...), kind=kOutput, calls=%fused_computation.32 | convolution fusion | flops 1614020608 | bytes 8650761 | tf_op jit(solution)/shard_map/wja,wai->ji/dot_general | solution.py:130
  162.2 1.8 stack.54
  164.7 4.8 %all-to-all-start.2 = ((f32[128,1,8]{2,1,0:T(1,128)}), f32[128,1,8]{2,1,0:T(1,128)S(1)}, u32[]{:S(2)}, u32[]{:S(2)}) async-start(f32[128,1,8]{2,1,0:T(1,128)} %broadcast_in_dim.146), calls=%async_computation.2 | async-start | bytes 131072 | tf_op jit(solution)/shard_map/all_to_all | solution.py:163
  170.3 8.7 %all-to-all-done.2 = f32[128,1,8]{2,1,0:T(1,128)S(1)} async-done(((f32[128,1,8]{2,1,0:T(1,128)}), f32[128,1,8]{2,1,0:T(1,128)S(1)}, u32[]{:S(2)}, u32[]{:S(2)}) %all-to-all-start.2) | async-done | bytes 4128 | tf_op jit(solution)/shard_map/all_to_all | solution.py:163
  179.0 3.5 %all-to-all-start.3 = ((f32[16,16,256]{2,1,0:T(8,128)}), f32[16,16,256]{2,1,0:T(8,128)S(1)}, u32[]{:S(2)}, u32[]{:S(2)}) async-start(f32[16,16,256]{2,1,0:T(8,128)} %bitcast.44), calls=%async_computation.3 | async-start | bytes 524288 | tf_op jit(solution)/shard_map/all_to_all | solution.py:154
  (122 shorter events, 26.7 us)
Async XLA Ops:
  7.2 59.1 %all-gather.2.cloned.1.call-start = ((), (), s32[]{:S(2)}) async-start(), calls=%async_computation.4 | async-start | bytes 5570560 | tf_op jit(solution)/shard_map/all_gather | solution.py:111
  8.9 4.5 %copy-start.16 = (s32[8,2]{0,1:T(2,128)S(1)}, s32[8,2]{0,1:T(2,128)}, u32[]{:S(2)}) copy-start(s32[8,2]{0,1:T(2,128)} %param.13) | copy-start | bytes 196
  9.0 4.5 %copy-start.17 = (s32[8]{0:T(128)S(1)}, s32[8]{0:T(128)}, u32[]{:S(2)}) copy-start(s32[8]{0:T(128)} %param.12) | copy-start | bytes 100
  9.0 5.0 %copy-start.15 = (f32[8,256,16]{1,2,0:T(8,128)S(1)}, f32[8,256,16]{1,2,0:T(8,128)}, u32[]{:S(2)}) copy-start(f32[8,256,16]{1,2,0:T(8,128)} %param.8) | copy-start | bytes 393220
  9.2 3.1 %collective-permute-start.2 = (f32[4,136,256]{2,1,0:T(8,128)S(1)}, f32[4,136,256]{2,1,0:T(8,128)S(1)}, u32[]{:S(2)}, u32[]{:S(2)}) collective-permute-start(f32[4,136,256]{2,1,0:T(8,128)S(1)} %select_maximum_fusion.1), channel_id=1, source_target_pairs={{0,16},{16,0},{1,17},{17,1},{2,18},{18,2},{3,19},{19,3},{4,20},{20... | collective-permute-start | bytes 1671176 | tf_op jit(solution)/shard_map/ppermute | solution.py:110
  13.5 2.4 %collective-permute-start = (s32[8,3]{0,1:T(4,128)S(1)}, s32[8,3]{0,1:T(4,128)S(1)}, u32[]{:S(2)}, u32[]{:S(2)}) collective-permute-start(s32[8,3]{0,1:T(4,128)S(1)} %pad_add_fusion), channel_id=1, source_target_pairs={{0,16},{16,0},{1,17},{17,1},{2,18},{18,2},{3,19},{19,3},{4,20},{20... | collective-permute-start | bytes 296 | tf_op jit(solution)/shard_map/ppermute | solution.py:102
  13.9 7.9 %collective-permute-start.1 = (f32[8,16,256]{2,1,0:T(8,128)S(1)}, f32[8,16,256]{2,1,0:T(8,128)S(1)}, u32[]{:S(2)}, u32[]{:S(2)}) collective-permute-start(f32[8,16,256]{2,1,0:T(8,128)S(1)} %bitcast.179), channel_id=1, source_target_pairs={{0,16},{16,0},{1,17},{17,1},{2,18},{18,2},{3,19},{19,3},{4,20},{20... | collective-permute-start | bytes 393224 | tf_op jit(solution)/shard_map/ppermute | solution.py:103
  21.9 9.4 %copy-start.18 = (s32[64]{0:T(128)S(1)}, s32[64]{0:T(128)}, u32[]{:S(2)}) copy-start(s32[64]{0:T(128)} %param.11) | copy-start | bytes 772
  23.6 50.4 %all-to-all-start = ((f32[16,152,256]{2,1,0:T(8,128)}), f32[16,152,256]{2,1,0:T(8,128)S(1)}, u32[]{:S(2)}, u32[]{:S(2)}) async-start(f32[16,152,256]{2,1,0:T(8,128)} %fusion), calls=%async_computation | async-start | bytes 4980736 | tf_op jit(solution)/shard_map/all_to_all | solution.py:116
  70.6 12.6 %copy-start = (s32[32]{0:T(128)S(1)}, s32[32]{0:T(128)}, u32[]{:S(2)}) copy-start(s32[32]{0:T(128)} %param.14) | copy-start | bytes 388
  70.6 15.8 %copy-start.1 = (s32[8]{0:T(128)S(1)}, s32[8]{0:T(128)}, u32[]{:S(2)}) copy-start(s32[8]{0:T(128)} %param.15) | copy-start | bytes 100
  74.0 36.4 %all-to-all-start.1 = ((f32[16,136,256]{2,1,0:T(8,128)}), f32[16,136,256]{2,1,0:T(8,128)}, u32[]{:S(2)}, u32[]{:S(2)}) async-start(f32[16,136,256]{2,1,0:T(8,128)} %broadcast_select_fusion), calls=%async_computation.1 | async-start | bytes 4456448 | tf_op jit(solution)/shard_map/all_to_all | solution.py:120
  121.5 4.2 %copy-start.2 = (f32[16,128,128]{2,1,0:T(8,128)S(1)}, f32[16,128,128]{2,1,0:T(8,128)}, u32[]{:S(2)}) copy-start(f32[16,128,128]{2,1,0:T(8,128)} %get-tuple-element.44) | copy-start | bytes 3145732
  125.7 3.7 %copy-start.3 = (f32[16,128,128]{2,1,0:T(8,128)S(1)}, f32[16,128,128]{2,1,0:T(8,128)}, u32[]{:S(2)}) copy-start(f32[16,128,128]{2,1,0:T(8,128)} %get-tuple-element.33) | copy-start | bytes 3145732
  125.7 3.7 %copy-start.6 = (f32[16,128,128]{1,2,0:T(8,128)S(1)}, f32[16,128,128]{1,2,0:T(8,128)}, u32[]{:S(2)}) copy-start(f32[16,128,128]{1,2,0:T(8,128)} %copy.67) | copy-start | bytes 3145732
  125.7 3.7 %copy-start.9 = (f32[16,128,128]{2,1,0:T(8,128)S(1)}, f32[16,128,128]{2,1,0:T(8,128)}, u32[]{:S(2)}) copy-start(f32[16,128,128]{2,1,0:T(8,128)} %get-tuple-element.27) | copy-start | bytes 3145732
  125.7 3.7 %copy-start.12 = (f32[16,128,128]{2,1,0:T(8,128)S(1)}, f32[16,128,128]{2,1,0:T(8,128)}, u32[]{:S(2)}) copy-start(f32[16,128,128]{2,1,0:T(8,128)} %get-tuple-element.28) | copy-start | bytes 3145732
  131.5 4.8 %collective-permute-start.3 = (f32[256,256]{1,0:T(8,128)S(1)}, f32[256,256]{1,0:T(8,128)S(1)}, u32[]{:S(2)}, u32[]{:S(2)}) collective-permute-start(f32[256,256]{1,0:T(8,128)S(1)} %convolution_bitcast_fusion.2), channel_id=1, source_target_pairs={{0,16},{16,0},{1,17},{17,1},{2,18},{18,2},{3,19},{19,3},{4,20},{20... | collective-permute-start | bytes 786440 | tf_op jit(solution)/shard_map/ppermute | solution.py:134
  142.7 3.7 %copy-start.4 = (f32[16,128,128]{2,1,0:T(8,128)S(1)}, f32[16,128,128]{2,1,0:T(8,128)}, u32[]{:S(2)}) copy-start(f32[16,128,128]{2,1,0:T(8,128)} %get-tuple-element.33) | copy-start | bytes 3145732
  142.7 3.7 %copy-start.7 = (f32[16,128,128]{1,2,0:T(8,128)S(1)}, f32[16,128,128]{1,2,0:T(8,128)}, u32[]{:S(2)}) copy-start(f32[16,128,128]{1,2,0:T(8,128)} %copy.67) | copy-start | bytes 3145732
  142.7 3.7 %copy-start.10 = (f32[16,128,128]{2,1,0:T(8,128)S(1)}, f32[16,128,128]{2,1,0:T(8,128)}, u32[]{:S(2)}) copy-start(f32[16,128,128]{2,1,0:T(8,128)} %get-tuple-element.27) | copy-start | bytes 3145732
  142.7 3.7 %copy-start.13 = (f32[16,128,128]{2,1,0:T(8,128)S(1)}, f32[16,128,128]{2,1,0:T(8,128)}, u32[]{:S(2)}) copy-start(f32[16,128,128]{2,1,0:T(8,128)} %get-tuple-element.28) | copy-start | bytes 3145732
  148.6 1.8 collective-permute-start.4
  155.8 3.6 %copy-start.5 = (f32[16,128,128]{2,1,0:T(8,128)S(1)}, f32[16,128,128]{2,1,0:T(8,128)}, u32[]{:S(2)}) copy-start(f32[16,128,128]{2,1,0:T(8,128)} %get-tuple-element.33) | copy-start | bytes 3145732
  155.8 3.6 %copy-start.8 = (f32[16,128,128]{1,2,0:T(8,128)S(1)}, f32[16,128,128]{1,2,0:T(8,128)}, u32[]{:S(2)}) copy-start(f32[16,128,128]{1,2,0:T(8,128)} %copy.67) | copy-start | bytes 3145732
  155.8 3.6 %copy-start.11 = (f32[16,128,128]{2,1,0:T(8,128)S(1)}, f32[16,128,128]{2,1,0:T(8,128)}, u32[]{:S(2)}) copy-start(f32[16,128,128]{2,1,0:T(8,128)} %get-tuple-element.27) | copy-start | bytes 3145732
  155.8 3.6 %copy-start.14 = (f32[16,128,128]{2,1,0:T(8,128)S(1)}, f32[16,128,128]{2,1,0:T(8,128)}, u32[]{:S(2)}) copy-start(f32[16,128,128]{2,1,0:T(8,128)} %get-tuple-element.28) | copy-start | bytes 3145732
  164.7 14.3 %all-to-all-start.2 = ((f32[128,1,8]{2,1,0:T(1,128)}), f32[128,1,8]{2,1,0:T(1,128)S(1)}, u32[]{:S(2)}, u32[]{:S(2)}) async-start(f32[128,1,8]{2,1,0:T(1,128)} %broadcast_in_dim.146), calls=%async_computation.2 | async-start | bytes 131072 | tf_op jit(solution)/shard_map/all_to_all | solution.py:163
  179.0 17.8 %all-to-all-start.3 = ((f32[16,16,256]{2,1,0:T(8,128)}), f32[16,16,256]{2,1,0:T(8,128)S(1)}, u32[]{:S(2)}, u32[]{:S(2)}) async-start(f32[16,16,256]{2,1,0:T(8,128)} %bitcast.44), calls=%async_computation.3 | async-start | bytes 524288 | tf_op jit(solution)/shard_map/all_to_all | solution.py:154
  196.8 2.1 %collective-permute-start.5 = (f32[8,16,256]{2,1,0:T(8,128)S(1)}, f32[8,16,256]{2,1,0:T(8,128)S(1)}, u32[]{:S(2)}, u32[]{:S(2)}) collective-permute-start(f32[8,16,256]{2,1,0:T(8,128)S(1)} %constant_dynamic-slice_fusion), channel_id=1, source_target_pairs={{0,16},{16,0},{1,17},{17,1},{2,18},{18,2},{3,19},{19,3},{4,20},{20... | collective-permute-start | bytes 393224 | tf_op jit(solution)/shard_map/ppermute | solution.py:157
Sparse Core Ops, SparseCore 0:
  13.6 52.6 all-gather.1

commit v2 on v1

v2 whole, which is shorter than its diff:
```python
import jax
import jax.numpy as jnp
from jax import lax
from jax.experimental import pallas as pl
from jax.experimental.pallas import tpu as pltpu
from jax.sharding import Mesh, PartitionSpec as P

ITERS = 2
TILE = 256
HALF = 128
TERMS = 16
LEFT_ROWS = 136
SLOT_ROWS = 152
STEP = 2
COL = ("x", "z")
ALL = ("y", "c", "x", "z")
SWAP = [(0, 1), (1, 0)]
UP = [(i, (i + 1) % 4) for i in range(4)]
DOWN = [(i, (i - 1) % 4) for i in range(4)]
f32 = jnp.float32
bf16 = jnp.bfloat16
PARAMS = pltpu.CompilerParams(vmem_limit_bytes=48 * 1024 * 1024)


def vmem():
    return pl.BlockSpec(memory_space=pltpu.VMEM)


def grids(rows, cols):
    i = lax.broadcasted_iota(jnp.int32, (rows, cols), 0)
    j = lax.broadcasted_iota(jnp.int32, (rows, cols), 1)
    return i, j


def fold_tile(tile):
    i, j = grids(HALF, HALF)
    a00 = tile[:HALF, :HALF]
    a11 = tile[HALF:, HALF:]
    fold = jnp.where(i >= j, a00, a11)
    diag = jnp.sum(jnp.where(i == j, a11, 0.0), axis=0, keepdims=True)
    return fold, tile[:HALF, HALF:], diag


def diag_rows(diag):
    wide = jnp.concatenate([diag, jnp.zeros((1, HALF), f32)], axis=1)
    return jnp.broadcast_to(wide, (8, TILE))


def unfold_tile(fold, corner, diag):
    i, j = grids(HALF, HALF)
    flip = fold.T
    a00 = jnp.where(i >= j, fold, flip)
    a11 = jnp.where(i == j, diag, jnp.where(i < j, fold, flip))
    top = jnp.concatenate([a00, corner], axis=1)
    low = jnp.concatenate([corner.T, a11], axis=1)
    return jnp.concatenate([top, low], axis=0)


def split(x):
    hi = x.astype(bf16)
    return hi, (x - hi.astype(f32)).astype(bf16)


def dot3(a_hi, a_lo, b_hi, b_lo):
    def dot(a, b):
        return jnp.dot(a, b, preferred_element_type=f32)

    return dot(a_hi, b_hi) + (dot(a_hi, b_lo) + dot(a_lo, b_hi))


def total(x):
    return jnp.sum(jnp.sum(x, axis=0, keepdims=True), axis=1, keepdims=True)


def inverse(norm):
    good = norm > 0.0
    return jnp.where(good, 1.0 / jnp.where(good, norm, 1.0), 0.0)


def put(stats, lane, value):
    _, j = grids(8, HALF)
    return jnp.where(j == lane, value, stats)


def fold_left_body(pick, src, dst):
    fold, corner, diag = fold_tile(src[0, 0])
    dst[0, :HALF, :HALF] = fold
    dst[0, :HALF, HALF:] = corner
    dst[0, HALF:, :] = diag_rows(diag)


def fold_left(left_env, pick):
    count = left_env.shape[0]
    return pl.pallas_call(
        fold_left_body,
        grid_spec=pltpu.PrefetchScalarGridSpec(
            num_scalar_prefetch=1,
            grid=(count,),
            in_specs=[pl.BlockSpec((1, 1, TILE, TILE), lambda n, pick: (n, pick[0], 0, 0))],
            out_specs=pl.BlockSpec((1, LEFT_ROWS, TILE), lambda n, pick: (n, 0, 0)),
        ),
        out_shape=jax.ShapeDtypeStruct((count, LEFT_ROWS, TILE), f32),
        compiler_params=PARAMS,
        name="fold_left",
    )(pick, left_env)


def from_rows(ids, own, other, slot, field):
    at = (slot % 8) * 3 + field
    return jnp.where(slot // 8 == ids[1], own[at], other[at])


def right_slots_body(ids, own, other, right, thin, thin_other, dst):
    slot = pl.program_id(0)
    here = slot // 8 == ids[1]
    on = from_rows(ids, own, other, slot, 1 + ids[1]).astype(f32)
    row = slot % 8
    fold, corner, diag = fold_tile(right[0, 0] * on)
    dst[0, :16, :] = jnp.where(here, thin[row], thin_other[row])
    dst[0, 16 : 16 + HALF, :HALF] = fold
    dst[0, 16 : 16 + HALF, HALF:] = corner
    dst[0, 16 + HALF :, :] = diag_rows(diag)


def right_slots(ids, own, other, right_env, thin, thin_other):
    def right_at(slot, ids, own, other):
        return (from_rows(ids, own, other, slot, 0), ids[1], 0, 0)

    whole = pl.BlockSpec((8, 16, TILE), lambda slot, ids, own, other: (0, 0, 0))
    return pl.pallas_call(
        right_slots_body,
        grid_spec=pltpu.PrefetchScalarGridSpec(
            num_scalar_prefetch=3,
            grid=(TERMS,),
            in_specs=[pl.BlockSpec((1, 1, TILE, TILE), right_at), whole, whole],
            out_specs=pl.BlockSpec(
                (1, SLOT_ROWS, TILE), lambda slot, ids, own, other: (slot, 0, 0)
            ),
        ),
        out_shape=jax.ShapeDtypeStruct((TERMS, SLOT_ROWS, TILE), f32),
        compiler_params=PARAMS,
        name="right_slots",
    )(ids, own, other, right_env, thin, thin_other)


def left_slots_body(ids, left_sector, *refs):
    pieces, dst, sem = refs[:8], refs[8], refs[9]

    def copy(src, slot):
        return pltpu.make_async_copy(src, dst.at[slot], sem.at[slot])

    def start(slot, carry):
        sector = left_sector[ids[0] * 16 + slot]
        home = sector // 4
        which = ((home // 2 - ids[0] + 4) % 4) * 2 + (home % 2 + ids[1]) % 2
        for n in range(8):

            @pl.when(which == n)
            def _():
                copy(pieces[n].at[sector % 4], slot).start()

        return carry

    def finish(slot, carry):
        copy(pieces[0].at[0], slot).wait()
        return carry

    lax.fori_loop(0, TERMS, start, 0)
    lax.fori_loop(0, TERMS, finish, 0)


def left_slots(ids, left_sector, pieces):
    smem = pl.BlockSpec(memory_space=pltpu.SMEM)
    anywhere = pl.BlockSpec(memory_space=pl.ANY)
    return pl.pallas_call(
        left_slots_body,
        in_specs=[smem, smem] + [anywhere] * 8,
        out_specs=anywhere,
        out_shape=jax.ShapeDtypeStruct((TERMS,) + pieces[0].shape[1:], f32),
        scratch_shapes=[pltpu.SemaphoreType.DMA((TERMS,))],
        name="left_slots",
    )(ids, left_sector, *pieces)


def live_sizes(ids, own, other, left_sector, left_size, right_size):
    live_left = left_size[left_sector[ids[0] * 16 + ids[2]]]
    live_right = right_size[from_rows(ids, own, other, ids[2], 0)]
    return live_right, live_left


def mask_of(live_right, live_left):
    i, j = grids(TILE, TILE)
    return (i < live_right) & (j < live_left)


def first_body(ids, own, other, sector, lsize, rsize, arrived, r_hi, r_lo, mid, q1, stats):
    live_right, live_left = live_sizes(ids, own, other, sector, lsize, rsize)
    block = jnp.concatenate([arrived[n, :16, :] for n in range(TERMS)], axis=0)
    start = jnp.where(mask_of(live_right, live_left), block, 0.0)
    norm = jnp.sqrt(total(start * start))
    vec = start * inverse(norm)
    q1[...] = vec
    stats[...] = put(jnp.zeros((8, HALF), f32), 0, norm)
    q_hi, q_lo = split(vec)

    def term(n, carry):
        full = unfold_tile(
            arrived[n, 16 : 16 + HALF, :HALF],
            arrived[n, 16 : 16 + HALF, HALF:],
            arrived[n, 16 + HALF : 17 + HALF, :HALF],
        )
        hi, lo = split(full)
        r_hi[n] = hi
        r_lo[n] = lo
        mid[n] = dot3(hi, lo, q_hi, q_lo)
        return carry

    lax.fori_loop(0, TERMS, term, 0)


def first_vector(scalars, arrived):
    smem = pl.BlockSpec(memory_space=pltpu.SMEM)
    stack = (TERMS, TILE, TILE)
    return pl.pallas_call(
        first_body,
        in_specs=[smem] * 6 + [vmem()],
        out_specs=[vmem()] * 5,
        out_shape=[
            jax.ShapeDtypeStruct(stack, bf16),
            jax.ShapeDtypeStruct(stack, bf16),
            jax.ShapeDtypeStruct(stack, f32),
            jax.ShapeDtypeStruct((TILE, TILE), f32),
            jax.ShapeDtypeStruct((8, HALF), f32),
        ],
        compiler_params=PARAMS,
        name="first_vector",
    )(*scalars, arrived)


def image_one_body(arrived, mid, l_hi, l_lo, part):
    @pl.when(pl.program_id(0) == 0)
    def _():
        part[...] = jnp.zeros_like(part)

    acc = part[...]
    for t in range(STEP):
        full = unfold_tile(
            arrived[t, :HALF, :HALF], arrived[t, :HALF, HALF:], arrived[t, HALF : HALF + 1, :HALF]
        )
        hi, lo = split(full)
        l_hi[t] = hi
        l_lo[t] = lo
        m_hi, m_lo = split(mid[t])
        acc = acc + dot3(m_hi, m_lo, hi, lo)
    part[...] = acc


def image_one(arrived, mid):
    stack = (TERMS, TILE, TILE)
    tiles = pl.BlockSpec((STEP, TILE, TILE), lambda n: (n, 0, 0))
    return pl.pallas_call(
        image_one_body,
        grid=(TERMS // STEP,),
        in_specs=[pl.BlockSpec((STEP, LEFT_ROWS, TILE), lambda n: (n, 0, 0)), tiles],
        out_specs=[tiles, tiles, pl.BlockSpec((TILE, TILE), lambda n: (0, 0))],
        out_shape=[
            jax.ShapeDtypeStruct(stack, bf16),
            jax.ShapeDtypeStruct(stack, bf16),
            jax.ShapeDtypeStruct((TILE, TILE), f32),
        ],
        compiler_params=PARAMS,
        name="image_one",
    )(arrived, mid)


def lanczos(image, last, before, beta):
    alpha = total(last * image)
    rest = image - alpha * last
    if before is not None:
        rest = rest - beta * before
    again = rest - total(last * rest) * last
    if before is not None:
        again = again - total(before * rest) * before
    norm = jnp.sqrt(total(again * again))
    return alpha, norm, again * inverse(norm)


def add_terms(q_hi, q_lo, r_hi, r_lo, l_hi, l_lo, acc):
    for t in range(STEP):
        m_hi, m_lo = split(dot3(r_hi[t], r_lo[t], q_hi, q_lo))
        acc = acc + dot3(m_hi, m_lo, l_hi[t], l_lo[t])
    return acc


def image_two_body(
    ids, own, other, sector, lsize, rsize,
    part_a, part_b, q1, stats_in, r_hi, r_lo, l_hi, l_lo,
    part, q2, stats, q_hi, q_lo,
):
    @pl.when(pl.program_id(0) == 0)
    def _():
        mask = mask_of(*live_sizes(ids, own, other, sector, lsize, rsize))
        image = jnp.where(mask, part_a[...] + part_b[...], 0.0)
        alpha, norm, vec = lanczos(image, q1[...], None, None)
        q2[...] = vec
        stats[...] = put(put(stats_in[...], 1, alpha), 2, norm)
        hi, lo = split(vec)
        q_hi[...] = hi
        q_lo[...] = lo
        part[...] = jnp.zeros_like(part)

    part[...] = add_terms(q_hi[...], q_lo[...], r_hi, r_lo, l_hi, l_lo, part[...])


def image_two(scalars, part, part_other, q1, stats, stacks):
    flat = pl.BlockSpec((TILE, TILE), lambda n, *_: (0, 0))
    line = pl.BlockSpec((8, HALF), lambda n, *_: (0, 0))
    tiles = pl.BlockSpec((STEP, TILE, TILE), lambda n, *_: (n, 0, 0))
    return pl.pallas_call(
        image_two_body,
        grid_spec=pltpu.PrefetchScalarGridSpec(
            num_scalar_prefetch=6,
            grid=(TERMS // STEP,),
            in_specs=[flat, flat, flat, line] + [tiles] * 4,
            out_specs=[flat, flat, line],
            scratch_shapes=[pltpu.VMEM((TILE, TILE), bf16)] * 2,
        ),
        out_shape=[
            jax.ShapeDtypeStruct((TILE, TILE), f32),
            jax.ShapeDtypeStruct((TILE, TILE), f32),
            jax.ShapeDtypeStruct((8, HALF), f32),
        ],
        compiler_params=PARAMS,
        name="image_two",
    )(*scalars, part, part_other, q1, stats, *stacks)


def third_body(
    ids, own, other, sector, lsize, rsize, part_a, part_b, q1, q2, stats_in, q3, sent, stats
):
    mask = mask_of(*live_sizes(ids, own, other, sector, lsize, rsize))
    image = jnp.where(mask, part_a[...] + part_b[...], 0.0)
    _, j = grids(8, HALF)
    beta = total(jnp.where((j == 2) & (grids(8, HALF)[0] == 0), stats_in[...], 0.0))
    alpha, norm, vec = lanczos(image, q2[...], q1[...], beta)
    q3[...] = vec
    pick = jnp.where(ids[1] == 0, q2[...], vec)
    for n in range(16):
        sent[n] = pick[16 * n : 16 * n + 16]
    stats[...] = put(put(stats_in[...], 3, alpha), 4, norm)


def third_vector(scalars, part, part_other, q1, q2, stats):
    smem = pl.BlockSpec(memory_space=pltpu.SMEM)
    return pl.pallas_call(
        third_body,
        in_specs=[smem] * 6 + [vmem()] * 5,
        out_specs=[vmem()] * 3,
        out_shape=[
            jax.ShapeDtypeStruct((TILE, TILE), f32),
            jax.ShapeDtypeStruct((16, 16, TILE), f32),
            jax.ShapeDtypeStruct((8, HALF), f32),
        ],
        compiler_params=PARAMS,
        name="third_vector",
    )(*scalars, part, part_other, q1, q2, stats)


def image_three_body(q3, stats_in, r_hi, r_lo, l_hi, l_lo, stats, part, q_hi, q_lo):
    @pl.when(pl.program_id(0) == 0)
    def _():
        hi, lo = split(q3[...])
        q_hi[...] = hi
        q_lo[...] = lo
        part[...] = jnp.zeros_like(part)

    part[...] = add_terms(q_hi[...], q_lo[...], r_hi, r_lo, l_hi, l_lo, part[...])

    @pl.when(pl.program_id(0) == pl.num_programs(0) - 1)
    def _():
        alpha = total(q3[...] * part[...])
        mine = put(stats_in[...], 5, alpha)
        stats[...] = jnp.broadcast_to(mine[0:1, :], (128, HALF))


def image_three(q3, stats, stacks):
    flat = pl.BlockSpec((TILE, TILE), lambda n: (0, 0))
    line = pl.BlockSpec((8, HALF), lambda n: (0, 0))
    tiles = pl.BlockSpec((STEP, TILE, TILE), lambda n: (n, 0, 0))
    return pl.pallas_call(
        image_three_body,
        grid=(TERMS // STEP,),
        in_specs=[flat, line] + [tiles] * 4,
        out_specs=pl.BlockSpec((128, HALF), lambda n: (0, 0)),
        out_shape=jax.ShapeDtypeStruct((128, HALF), f32),
        scratch_shapes=[
            pltpu.VMEM((TILE, TILE), f32),
            pltpu.VMEM((TILE, TILE), bf16),
            pltpu.VMEM((TILE, TILE), bf16),
        ],
        compiler_params=PARAMS,
        name="image_three",
    )(q3, stats, *stacks)


def ritz_pair(norm, a1, b1, a2, b2, a3):
    def apply(x):
        return [a1 * x[0] + b1 * x[1], b1 * x[0] + a2 * x[1] + b2 * x[2], b2 * x[1] + a3 * x[2]]

    def dot(x, y):
        return 0.5 * jnp.sum(x[0] * y[0] + x[1] * y[1] + x[2] * y[2], axis=1, keepdims=True)

    zero = jnp.zeros_like(norm)
    start = [norm, zero, zero]
    image = apply(start)
    norm_sq = dot(start, start)
    correlation = dot(start, image)
    inv_norm = 1.0 / jnp.sqrt(norm_sq)
    basis = [x * inv_norm for x in start]
    applied = [x * inv_norm for x in image]
    ritz = correlation / norm_sq
    for _ in range(ITERS):
        residual = [x - ritz * y for x, y in zip(applied, basis)]
        res_sq = dot(residual, residual)
        length = jnp.sqrt(res_sq)
        fresh = [x / length for x in residual]
        fresh_applied = apply(fresh)
        curvature = dot(fresh, fresh_applied)
        half_gap = 0.5 * (ritz - curvature)
        root = jnp.sqrt(half_gap * half_gap + res_sq)
        lowest = 0.5 * (ritz + curvature) - root
        first = curvature - lowest
        pair = jnp.sqrt(first * first + res_sq)
        basis = [(first * x - length * y) / pair for x, y in zip(basis, fresh)]
        applied = [(first * x - length * y) / pair for x, y in zip(applied, fresh_applied)]
        ritz = lowest
    return basis, ritz


def finish_body(
    ids, sector, rsector, lsize, rsize, stats, thin, got, back, out, energy, coef
):
    flip = stats[...].T
    norm, a1, b1, a2, b2, part = [flip[m : m + 1, :] for m in range(6)]
    _, lane = grids(1, HALF)
    core_of = (lane // 16) % 2
    a3 = part + jnp.where(core_of == 0, pltpu.roll(part, HALF - 16, 1), pltpu.roll(part, 16, 1))
    basis, ritz = ritz_pair(norm, a1, b1, a2, b2, a3)
    energy[...] = jnp.broadcast_to(ritz, (8, HALF))
    scale = jnp.sqrt(jnp.full((1, HALF), 64 * TILE * TILE, f32))
    i, _ = grids(HALF, HALF)
    c1 = basis[0] * inverse(norm) * scale
    c2 = basis[1] * scale
    c3 = basis[2] * scale
    coef[...] = jnp.where(i == 0, c1, jnp.where(i == 1, c2, jnp.where(i == 2, c3, 0.0))).T
    core = ids[1]
    own = coef[pl.ds(pl.multiple_of(ids[0] * 32 + core * 8, 8), 8), :]
    jcol, irow = grids(16, TILE)
    for b in range(8):
        live_left = lsize[sector[ids[0] * 16 + core * 8 + b]]
        live_right = rsize[rsector[b]]
        live = (jcol + ids[2] * 16 < live_right) & (irow < live_left)
        keep = got[core * 8 + b]
        recv = back[b]
        second = jnp.where(core == 0, keep, recv)
        third = jnp.where(core == 0, recv, keep)
        out[b] = (
            own[b : b + 1, 0:1] * jnp.where(live, thin[b], 0.0)
            + own[b : b + 1, 1:2] * second
            + own[b : b + 1, 2:3] * third
        )


def finish(ids, sector, rsector, lsize, rsize, stats, thin, got, back):
    smem = pl.BlockSpec(memory_space=pltpu.SMEM)
    return pl.pallas_call(
        finish_body,
        in_specs=[smem] * 5 + [vmem()] * 4,
        out_specs=[vmem()] * 2,
        out_shape=[
            jax.ShapeDtypeStruct(thin.shape, f32),
            jax.ShapeDtypeStruct((8, HALF), f32),
        ],
        scratch_shapes=[pltpu.VMEM((HALF, HALF), f32)],
        compiler_params=PARAMS,
        name="finish",
    )(ids, sector, rsector, lsize, rsize, stats, thin, got, back)


def local(theta, left_env, right_env, left_sector, right_sector, term_on, left_size, right_size):
    plane = lax.axis_index("y").astype(jnp.int32)
    core = lax.axis_index("c").astype(jnp.int32)
    place = lax.axis_index(COL).astype(jnp.int32)
    ids = jnp.stack([plane, core, place])
    thin = jnp.swapaxes(theta, 1, 2)

    theirs = lax.ppermute(fold_left(left_env, (1 - core).reshape(1)), "c", SWAP)
    mine = fold_left(left_env, core.reshape(1))
    mine_up = lax.ppermute(mine, "y", UP)
    mine_down = lax.ppermute(mine, "y", DOWN)
    theirs_up = lax.ppermute(theirs, "y", UP)
    theirs_down = lax.ppermute(theirs, "y", DOWN)
    mine_far = lax.ppermute(mine_up, "y", UP)
    theirs_far = lax.ppermute(theirs_down, "y", DOWN)
    pieces = [mine, theirs, mine_down, theirs_down, mine_far, theirs_far, mine_up, theirs_up]

    own = jnp.concatenate([right_sector[:, None], term_on], axis=1).reshape(-1)
    other = lax.ppermute(own, "c", SWAP)
    thin_other = lax.ppermute(thin, "c", SWAP)
    slots = right_slots(ids, own, other, right_env, thin, thin_other)
    arrived = lax.all_to_all(slots, COL, 0, 0, tiled=True)
    scalars = (ids, own, other, left_sector, left_size, right_size)
    r_hi, r_lo, mid, q1, stats = first_vector(scalars, arrived)

    left_arrived = lax.all_to_all(left_slots(ids, left_sector, pieces), COL, 0, 0, tiled=True)
    l_hi, l_lo, part = image_one(left_arrived, mid)
    stacks = (r_hi, r_lo, l_hi, l_lo)
    part, q2, stats = image_two(scalars, part, lax.ppermute(part, "c", SWAP), q1, stats, stacks)
    q3, sent, stats = third_vector(scalars, part, lax.ppermute(part, "c", SWAP), q1, q2, stats)

    got = lax.all_to_all(sent, COL, 0, 0, tiled=True)
    give = lax.dynamic_slice_in_dim(got, (1 - core) * 8, 8)
    back = lax.ppermute(give, "c", SWAP)

    stats = lax.all_to_all(image_three(q3, stats, stacks), ALL, 0, 0, tiled=True)
    out, energy = finish(
        ids, left_sector, right_sector, left_size, right_size, stats, thin, got, back
    )
    return jnp.swapaxes(out, 1, 2), energy[0, 0]


def solution(mesh):
    fine = Mesh(mesh.devices.reshape(4, 2, 4, 4), ALL)
    row = ("y", "c")
    placed = (
        P(row, None, COL),
        P(row, COL, None, None),
        P(None, COL, None, None),
        P(),
        P(row),
        P(row, COL),
        P(),
        P(),
    )
    return jax.shard_map(
        local, mesh=fine, in_specs=placed, out_specs=(P(row, None, COL), P()), check_vma=False
    )
```

time: 209 us -> 241 us (1.15)
  Pallas kernels: 0 us -> 119 us
  other arithmetic: 33 us -> 0.76 us
  between operations: 31.8 us -> 0.86 us
  local copies, waits for them, and re-layouts: 31.4 us -> 8.1 us
  matrix products: 18 us -> 0 us
  blocking collectives: 0 us -> 14.8 us
  starting transfers between devices: 30 us -> 34.8 us
    pallas_call x0 -> x10, Pallas kernels: none -> 119 us  [the longest x1 69.5 us: left_slots(): pl.pallas_call(left_slots_body, in_specs=[smem, smem] + [anywhere] * 8, o...]
    all_gather x1 -> x0, waiting for transfers between devices: 34.8 us -> none  [local(): every = lax.all_gather(eight, 'y', axis=0, tiled=True)]
    ppermute x5 -> x11, waiting for transfers between devices: 2.67 us -> 34.3 us  [the longest x1 11.8 us: local(): mine_far = lax.ppermute(mine_up, 'y', UP)]
    dot_general x6 -> x0, matrix products: 18 us -> none  [the longest x3 10.8 us: half_image(): middle = jnp.einsum('wjb,bi->wji', right, u, precision=high)]
    all_to_all x0 -> x1, blocking collectives: none -> 14.8 us  [local(): lax.all_to_all(image_three(q3, stats, stacks), ALL, 0, 0, tiled=True)]
    reduce_sum x12 -> x0, other arithmetic: 12.9 us -> none  [the longest x1 2.65 us: local(): b2 = jnp.sqrt(jnp.sum(w2 * w2))]
    select_n x13 -> x0, other arithmetic: 12.6 us -> none  [the longest x1 5.35 us: unpack(): a00 = jnp.where(i >= j, fold, flip)]
    ppermute x5 -> x11, starting transfers between devices: 6.13 us -> 14.7 us  [the longest x2 3.91 us: local(): lax.ppermute(part, 'c', SWAP)]
  transfers between devices with their start and end apart: 11 -> 15, of which waited for: 6 -> 9; matrix products, arithmetic and copies ran while one was open for 16% -> 0% of each run, Pallas kernels for 0% -> 36%
where the time goes in v2:
time: 241 us; the launch traced here: 240 us
  Pallas kernels  119 us (49%)
  waiting for transfers between devices  61.1 us (25%)
  starting transfers between devices  34.8 us (14%)
  blocking collectives  14.8 us (6%)
  local copies, waits for them, and re-layouts  8.1 us (3%)
    pallas_call x1, Pallas kernels, left_slots(): pl.pallas_call(left_slots_body, in_specs=[smem, smem] + [anywhere] * 8, o...  69.5 us
    all_to_all x1, waiting for transfers between devices, local(): lax.all_to_all(left_slots(ids, left_sector, pieces), COL, 0, 0, tiled=True)  19.1 us
    all_to_all x1, blocking collectives, local(): lax.all_to_all(image_three(q3, stats, stacks), ALL, 0, 0, tiled=True)  14.8 us
    ppermute x1, waiting for transfers between devices, local(): mine_far = lax.ppermute(mine_up, 'y', UP)  11.8 us
    pallas_call x1, Pallas kernels, right_slots(): pl.pallas_call(right_slots_body, grid_spec=pltpu.PrefetchScalarGridSpec(n...  10.6 us
    ppermute x1, waiting for transfers between devices, local(): mine_up = lax.ppermute(mine, 'y', UP)  10.1 us
    pallas_call x1, Pallas kernels, image_two(): pl.pallas_call(image_two_body, grid_spec=pltpu.PrefetchScalarGridSpec(num...  9.52 us
    pallas_call x1, Pallas kernels, first_vector(): pl.pallas_call(first_body, in_specs=[smem] * 6 + [vmem()], out_specs=[vme...  9.01 us
  transfers between devices with their start and end apart: 15, of which 9 were waited for; matrix products, arithmetic and copies ran while one was open for 0% of the time, Pallas kernels for 36%

profile of v2, /device:TPU:1, one launch (start us, length us, event | category | flops | bytes accessed | tf_op | source)
XLA Modules:
  0.0 239.5 jit_solution(17670982026402301469)
XLA Ops:
  0.6 1.5 collective-permute-start.8
  3.1 1.0 collective-permute-done.other
  4.1 0.9 copy-done.7
  5.0 10.6 %right_slots.1 = f32[16,152,256]{2,1,0:T(8,128)} custom-call(s32[3]{0:T(128)S(1)} %pad_add_fusion.1.ids, s32[24]{0:T(128)S(1)} %reshape.13.own, s32[24]{0:T(128)S(1)} %collective-permute-done.other, f32[8,2,256,256]{3,2,1,0:T(8,128)} %right.1, f32[8,16,256]{2,1,0:T(8,128)S(1)} %bitcast.13, f32[8,16,256]{2,1,0:T(8,128)S(1)} %collective-permute-done.8.thin_other), custom_call_target="tpu_custom_call" | custom-call | tf_op jit(solution)/shard_map/right_slots/pallas_call | solution.py:130
  15.7 7.9 %all-to-all-start.1 = ((f32[16,152,256]{2,1,0:T(8,128)}), f32[16,152,256]{2,1,0:T(8,128)}, u32[]{:S(2)}, u32[]{:S(2)}) async-start(f32[16,152,256]{2,1,0:T(8,128)} %right_slots.1), calls=%async_computation.1 | async-start | bytes 4980736 | tf_op jit(solution)/shard_map/all_to_all | solution.py:511
  24.4 0.9 collective-permute-start.4
  25.9 2.8 %collective-permute-start.3 = (f32[4,136,256]{2,1,0:T(8,128)S(1)}, f32[4,136,256]{2,1,0:T(8,128)S(1)}, u32[]{:S(2)}, u32[]{:S(2)}) collective-permute-start(f32[4,136,256]{2,1,0:T(8,128)S(1)} %collective-permute-done.1.refs_1_), channel_id=1, source_target_pairs={{0,96},{32,0},{64,32},{96,64},{1,97},{33,1},{65,33},{97,65},{2,98}... | collective-permute-start | bytes 1671176 | tf_op jit(solution)/shard_map/ppermute | solution.py:502
  29.0 1.1 collective-permute-start.7
  30.1 10.1 %collective-permute-done.4.refs_6_ = f32[4,136,256]{2,1,0:T(8,128)S(1)} collective-permute-done((f32[4,136,256]{2,1,0:T(8,128)S(1)}, f32[4,136,256]{2,1,0:T(8,128)S(1)}, u32[]{:S(2)}, u32[]{:S(2)}) %collective-permute-start.4) | collective-permute-done | bytes 557088 | tf_op jit(solution)/shard_map/ppermute | solution.py:499
  40.3 3.5 %collective-permute-start.6 = (f32[4,136,256]{2,1,0:T(8,128)S(1)}, f32[4,136,256]{2,1,0:T(8,128)}, u32[]{:S(2)}, u32[]{:S(2)}) collective-permute-start(f32[4,136,256]{2,1,0:T(8,128)S(1)} %collective-permute-done.3.refs_3_), channel_id=1, source_target_pairs={{0,96},{32,0},{64,32},{96,64},{1,97},{33,1},{65,33},{97,65},{2,98}... | collective-permute-start | bytes 1671176 | tf_op jit(solution)/shard_map/ppermute | solution.py:504
  43.8 8.4 %collective-permute-done.2.refs_2_ = f32[4,136,256]{2,1,0:T(8,128)S(1)} collective-permute-done((f32[4,136,256]{2,1,0:T(8,128)S(1)}, f32[4,136,256]{2,1,0:T(8,128)S(1)}, u32[]{:S(2)}, u32[]{:S(2)}) %collective-permute-start.2) | collective-permute-done | bytes 557088 | tf_op jit(solution)/shard_map/ppermute | solution.py:500
  52.2 11.8 %collective-permute-done.5.refs_4_ = f32[4,136,256]{2,1,0:T(8,128)S(1)} collective-permute-done((f32[4,136,256]{2,1,0:T(8,128)S(1)}, f32[4,136,256]{2,1,0:T(8,128)S(1)}, u32[]{:S(2)}, u32[]{:S(2)}) %collective-permute-start.5) | collective-permute-done | bytes 557088 | tf_op jit(solution)/shard_map/ppermute | solution.py:503
  64.8 69.5 %left_slots.1 = f32[16,136,256]{2,1,0:T(8,128)} custom-call(s32[3]{0:T(128)} %copy-done.9, s32[64]{0:T(128)} %sector.7, f32[4,136,256]{2,1,0:T(8,128)} %copy-done.6, f32[4,136,256]{2,1,0:T(8,128)} %copy-done.15, f32[4,136,256]{2,1,0:T(8,128)} %copy-done.18, f32[4,136,256]{2,1,0:T(8,128)} %copy-done.17, f32[4,136,256]{2,1,0:T(8,128)} %copy-done.20, ...), custom_call_target="tpu_custom_call" | custom-call | tf_op jit(solution)/shard_map/left_slots/pallas_call | solution.py:175
  134.4 6.9 %all-to-all-start = ((f32[16,136,256]{2,1,0:T(8,128)}), f32[16,136,256]{2,1,0:T(8,128)}, u32[]{:S(2)}, u32[]{:S(2)}) async-start(f32[16,136,256]{2,1,0:T(8,128)} %left_slots.1), calls=%async_computation | async-start | bytes 4456448 | tf_op jit(solution)/shard_map/all_to_all | solution.py:515
  141.4 9.0 %first_vector.1 = (bf16[16,256,256]{2,1,0:T(8,128)(2,1)S(1)}, bf16[16,256,256]{2,1,0:T(8,128)(2,1)S(1)}, f32[16,256,256]{2,1,0:T(8,128)}, f32[256,256]{1,0:T(8,128)S(1)}, f32[8,128]{1,0:T(8,128)S(1)}) custom-call(s32[3]{0:T(128)S(1)} %copy-done.10, s32[24]{0:T(128)S(1)} %reshape.13.own, s32[24]{0:T(128)S(1)} %collective-permute-done.other, ...), custom_call_target="tpu_custom_call" | custom-call | tf_op jit(solution)/shard_map/first_vector/pallas_call | solution.py:224
  150.4 1.4 copy-done.1
  151.7 19.1 %all-to-all-done.arrived = f32[16,136,256]{2,1,0:T(8,128)} async-done(((f32[16,136,256]{2,1,0:T(8,128)}), f32[16,136,256]{2,1,0:T(8,128)}, u32[]{:S(2)}, u32[]{:S(2)}) %all-to-all-start) | async-done | bytes 2228256 | tf_op jit(solution)/shard_map/all_to_all | solution.py:515
  170.9 7.4 %image_one.1 = (bf16[16,256,256]{2,1,0:T(8,128)(2,1)S(1)}, bf16[16,256,256]{2,1,0:T(8,128)(2,1)S(1)}, f32[256,256]{1,0:T(8,128)S(1)}) custom-call(f32[16,136,256]{2,1,0:T(8,128)} %all-to-all-done.arrived, f32[16,256,256]{2,1,0:T(8,128)} %get-tuple-element.18.mid), custom_call_target="tpu_custom_call" | custom-call | tf_op jit(solution)/shard_map/image_one/pallas_call | solution.py:261
  178.3 1.3 copy-done.4
  179.6 1.4 copy-done.5
  181.0 3.5 %collective-permute-start.9 = (f32[256,256]{1,0:T(8,128)S(1)}, f32[256,256]{1,0:T(8,128)S(1)}, u32[]{:S(2)}, u32[]{:S(2)}) collective-permute-start(f32[256,256]{1,0:T(8,128)S(1)} %get-tuple-element.19.part_a), channel_id=1, source_target_pairs={{0,16},{16,0},{1,17},{17,1},{2,18},{18,2},{3,19},{19,3},{4,20},{20... | collective-permute-start | bytes 786440 | tf_op jit(solution)/shard_map/ppermute | solution.py:518
  184.5 1.2 collective-permute-done.9.part_b
  185.6 9.5 %image_two.1 = (f32[256,256]{1,0:T(8,128)S(1)}, f32[256,256]{1,0:T(8,128)S(1)}, f32[8,128]{1,0:T(8,128)S(1)}) custom-call(s32[3]{0:T(128)S(1)} %copy-done.10, s32[24]{0:T(128)S(1)} %reshape.13.own, s32[24]{0:T(128)S(1)} %collective-permute-done.other, s32[64]{0:T(128)S(1)} %copy-done.11, s32[32]{0:T(128)S(1)} %copy-done.12, s32[8]{0:T(128)S(1)} %copy-done.13, ...), custom_call_target="tpu_custom_call" | custom-call | tf_op jit(solution)/shard_map/image_two/pallas_call | solution.py:319
  195.6 1.2 collective-permute-done.10.part_b
  196.8 1.9 third_vector.1
  198.6 3.5 %all-to-all-start.3 = ((f32[16,16,256]{2,1,0:T(8,128)}), f32[16,16,256]{2,1,0:T(8,128)S(1)}, u32[]{:S(2)}, u32[]{:S(2)}) async-start(f32[16,16,256]{2,1,0:T(8,128)} %get-tuple-element.31), calls=%async_computation.3 | async-start | bytes 524288 | tf_op jit(solution)/shard_map/all_to_all | solution.py:521
  202.2 7.7 %all-to-all-done.3.got = f32[16,16,256]{2,1,0:T(8,128)S(1)} async-done(((f32[16,16,256]{2,1,0:T(8,128)}), f32[16,16,256]{2,1,0:T(8,128)S(1)}, u32[]{:S(2)}, u32[]{:S(2)}) %all-to-all-start.3) | async-done | bytes 262176 | tf_op jit(solution)/shard_map/all_to_all | solution.py:521
  209.9 1.8 collective-permute-start.11
  211.7 1.6 copy-done.3
  213.3 8.6 %image_three.1 = f32[128,128]{1,0:T(8,128)S(1)} custom-call(f32[256,256]{1,0:T(8,128)S(1)} %get-tuple-element.29.q3, f32[8,128]{1,0:T(8,128)S(1)} %get-tuple-element.30.stats_in, bf16[16,256,256]{2,1,0:T(8,128)(2,1)S(1)} %get-tuple-element.22.r_hi, bf16[16,256,256]{2,1,0:T(8,128)(2,1)S(1)} %copy-done.3, bf16[16,256,256]{2,1,0:T(8,128)(2,1)} %copy-done.4, ...), custom_call_target="tpu_custom_call" | custom-call | tf_op jit(solution)/shard_map/image_three/pallas_call | solution.py:390
  221.9 14.8 %all_to_all.26 = f32[128,1,128]{2,1,0:T(1,128)S(1)} all-to-all(f32[128,1,128]{2,1,0:T(1,128)S(1)} %bitcast.15), channel_id=1, replica_groups=mesh['y'=4,'c'=2,'x'=4,'z'=4] {'y','c','x','z'}, dimensions={0} | all-to-all | bytes 131072 | tf_op jit(solution)/shard_map/all_to_all | solution.py:525
  236.7 2.3 finish.1
  (57 shorter events, 4.6 us)
Async XLA Ops:
  0.6 3.5 %collective-permute-start.8 = (f32[8,16,256]{2,1,0:T(8,128)}, f32[8,16,256]{2,1,0:T(8,128)S(1)}, u32[]{:S(2)}, u32[]{:S(2)}) collective-permute-start(f32[8,16,256]{2,1,0:T(8,128)} %bitcast.12), channel_id=1, source_target_pairs={{0,16},{16,0},{1,17},{17,1},{2,18},{18,2},{3,19},{19,3},{4,20},{20... | collective-permute-start | bytes 393224 | tf_op jit(solution)/shard_map/ppermute | solution.py:509
  3.0 1.1 collective-permute-start
  3.1 12.6 %copy-start.9 = (s32[3]{0:T(128)}, s32[3]{0:T(128)S(1)}, u32[]{:S(2)}) copy-start(s32[3]{0:T(128)S(1)} %pad_add_fusion.1.ids) | copy-start | bytes 40
  15.7 7.9 %copy-start = (f32[4,2,256,256]{3,2,1,0:T(8,128)S(1)}, f32[4,2,256,256]{3,2,1,0:T(8,128)}, u32[]{:S(2)}) copy-start(f32[4,2,256,256]{3,2,1,0:T(8,128)} %src.3) | copy-start | bytes 6291460
  15.7 118.7 %all-to-all-start.1 = ((f32[16,152,256]{2,1,0:T(8,128)}), f32[16,152,256]{2,1,0:T(8,128)}, u32[]{:S(2)}, u32[]{:S(2)}) async-start(f32[16,152,256]{2,1,0:T(8,128)} %right_slots.1), calls=%async_computation.1 | async-start | bytes 4980736 | tf_op jit(solution)/shard_map/all_to_all | solution.py:511
  23.7 2.2 collective-permute-start.1
  24.4 40.4 %copy-start.6 = (f32[4,136,256]{2,1,0:T(8,128)}, f32[4,136,256]{2,1,0:T(8,128)S(1)}, u32[]{:S(2)}) copy-start(f32[4,136,256]{2,1,0:T(8,128)S(1)} %fold_left.2.refs_0_) | copy-start | bytes 1671172
  24.4 15.8 %collective-permute-start.4 = (f32[4,136,256]{2,1,0:T(8,128)S(1)}, f32[4,136,256]{2,1,0:T(8,128)S(1)}, u32[]{:S(2)}, u32[]{:S(2)}) collective-permute-start(f32[4,136,256]{2,1,0:T(8,128)S(1)} %fold_left.2.refs_0_), channel_id=1, source_target_pairs={{0,32},{32,64},{64,96},{96,0},{1,33},{33,65},{65,97},{97,1},{2,34}... | collective-permute-start | bytes 1671176 | tf_op jit(solution)/shard_map/ppermute | solution.py:499
  25.8 39.0 %copy-start.15 = (f32[4,136,256]{2,1,0:T(8,128)}, f32[4,136,256]{2,1,0:T(8,128)S(1)}, u32[]{:S(2)}) copy-start(f32[4,136,256]{2,1,0:T(8,128)S(1)} %collective-permute-done.1.refs_1_) | copy-start | bytes 1671172
  25.9 14.4 %collective-permute-start.3 = (f32[4,136,256]{2,1,0:T(8,128)S(1)}, f32[4,136,256]{2,1,0:T(8,128)S(1)}, u32[]{:S(2)}, u32[]{:S(2)}) collective-permute-start(f32[4,136,256]{2,1,0:T(8,128)S(1)} %collective-permute-done.1.refs_1_), channel_id=1, source_target_pairs={{0,96},{32,0},{64,32},{96,64},{1,97},{33,1},{65,33},{97,65},{2,98}... | collective-permute-start | bytes 1671176 | tf_op jit(solution)/shard_map/ppermute | solution.py:502
  28.6 23.6 %collective-permute-start.2 = (f32[4,136,256]{2,1,0:T(8,128)S(1)}, f32[4,136,256]{2,1,0:T(8,128)S(1)}, u32[]{:S(2)}, u32[]{:S(2)}) collective-permute-start(f32[4,136,256]{2,1,0:T(8,128)S(1)} %fold_left.2.refs_0_), channel_id=1, source_target_pairs={{0,96},{32,0},{64,32},{96,64},{1,97},{33,1},{65,33},{97,65},{2,98}... | collective-permute-start | bytes 1671176 | tf_op jit(solution)/shard_map/ppermute | solution.py:500
  29.0 23.2 %collective-permute-start.7 = (f32[4,136,256]{2,1,0:T(8,128)S(1)}, f32[4,136,256]{2,1,0:T(8,128)S(1)}, u32[]{:S(2)}, u32[]{:S(2)}) collective-permute-start(f32[4,136,256]{2,1,0:T(8,128)S(1)} %collective-permute-done.1.refs_1_), channel_id=1, source_target_pairs={{0,32},{32,64},{64,96},{96,0},{1,33},{33,65},{65,97},{97,1},{2,34}... | collective-permute-start | bytes 1671176 | tf_op jit(solution)/shard_map/ppermute | solution.py:501
  40.2 24.6 %copy-start.16 = (f32[4,136,256]{2,1,0:T(8,128)}, f32[4,136,256]{2,1,0:T(8,128)S(1)}, u32[]{:S(2)}) copy-start(f32[4,136,256]{2,1,0:T(8,128)S(1)} %collective-permute-done.4.refs_6_) | copy-start | bytes 1671172
  40.2 23.8 %collective-permute-start.5 = (f32[4,136,256]{2,1,0:T(8,128)S(1)}, f32[4,136,256]{2,1,0:T(8,128)S(1)}, u32[]{:S(2)}, u32[]{:S(2)}) collective-permute-start(f32[4,136,256]{2,1,0:T(8,128)S(1)} %collective-permute-done.4.refs_6_), channel_id=1, source_target_pairs={{0,32},{32,64},{64,96},{96,0},{1,33},{33,65},{65,97},{97,1},{2,34}... | collective-permute-start | bytes 1671176 | tf_op jit(solution)/shard_map/ppermute | solution.py:503
  40.3 24.6 %copy-start.17 = (f32[4,136,256]{2,1,0:T(8,128)}, f32[4,136,256]{2,1,0:T(8,128)S(1)}, u32[]{:S(2)}) copy-start(f32[4,136,256]{2,1,0:T(8,128)S(1)} %collective-permute-done.3.refs_3_) | copy-start | bytes 1671172
  40.3 24.6 %collective-permute-start.6 = (f32[4,136,256]{2,1,0:T(8,128)S(1)}, f32[4,136,256]{2,1,0:T(8,128)}, u32[]{:S(2)}, u32[]{:S(2)}) collective-permute-start(f32[4,136,256]{2,1,0:T(8,128)S(1)} %collective-permute-done.3.refs_3_), channel_id=1, source_target_pairs={{0,96},{32,0},{64,32},{96,64},{1,97},{33,1},{65,33},{97,65},{2,98}... | collective-permute-start | bytes 1671176 | tf_op jit(solution)/shard_map/ppermute | solution.py:504
  52.2 12.6 %copy-start.18 = (f32[4,136,256]{2,1,0:T(8,128)}, f32[4,136,256]{2,1,0:T(8,128)S(1)}, u32[]{:S(2)}) copy-start(f32[4,136,256]{2,1,0:T(8,128)S(1)} %collective-permute-done.2.refs_2_) | copy-start | bytes 1671172
  52.2 11.8 %copy-start.19 = (f32[4,136,256]{2,1,0:T(8,128)}, f32[4,136,256]{2,1,0:T(8,128)S(1)}, u32[]{:S(2)}) copy-start(f32[4,136,256]{2,1,0:T(8,128)S(1)} %collective-permute-done.7.refs_7_) | copy-start | bytes 1671172
  134.3 7.0 %copy-start.10 = (s32[3]{0:T(128)S(1)}, s32[3]{0:T(128)}, u32[]{:S(2)}) copy-start(s32[3]{0:T(128)} %copy-done.9) | copy-start | bytes 40
  134.3 7.0 %copy-start.11 = (s32[64]{0:T(128)S(1)}, s32[64]{0:T(128)}, u32[]{:S(2)}) copy-start(s32[64]{0:T(128)} %sector.7) | copy-start | bytes 772
  134.3 7.0 %copy-start.12 = (s32[32]{0:T(128)S(1)}, s32[32]{0:T(128)}, u32[]{:S(2)}) copy-start(s32[32]{0:T(128)} %lsize.7) | copy-start | bytes 388
  134.3 7.0 %copy-start.13 = (s32[8]{0:T(128)S(1)}, s32[8]{0:T(128)}, u32[]{:S(2)}) copy-start(s32[8]{0:T(128)} %rsize.7) | copy-start | bytes 100
  134.4 36.5 %all-to-all-start = ((f32[16,136,256]{2,1,0:T(8,128)}), f32[16,136,256]{2,1,0:T(8,128)}, u32[]{:S(2)}, u32[]{:S(2)}) async-start(f32[16,136,256]{2,1,0:T(8,128)} %left_slots.1), calls=%async_computation | async-start | bytes 4456448 | tf_op jit(solution)/shard_map/all_to_all | solution.py:515
  170.9 14.7 %copy-start.2 = (bf16[16,256,256]{2,1,0:T(8,128)(2,1)S(1)}, bf16[16,256,256]{2,1,0:T(8,128)(2,1)}, u32[]{:S(2)}) copy-start(bf16[16,256,256]{2,1,0:T(8,128)(2,1)} %copy-done.1) | copy-start | bytes 6291460
  179.6 1.4 copy-start.5
  181.0 4.6 %collective-permute-start.9 = (f32[256,256]{1,0:T(8,128)S(1)}, f32[256,256]{1,0:T(8,128)S(1)}, u32[]{:S(2)}, u32[]{:S(2)}) collective-permute-start(f32[256,256]{1,0:T(8,128)S(1)} %get-tuple-element.19.part_a), channel_id=1, source_target_pairs={{0,16},{16,0},{1,17},{17,1},{2,18},{18,2},{3,19},{19,3},{4,20},{20... | collective-permute-start | bytes 786440 | tf_op jit(solution)/shard_map/ppermute | solution.py:518
  195.2 1.6 collective-permute-start.10
  198.6 11.2 %all-to-all-start.3 = ((f32[16,16,256]{2,1,0:T(8,128)}), f32[16,16,256]{2,1,0:T(8,128)S(1)}, u32[]{:S(2)}, u32[]{:S(2)}) async-start(f32[16,16,256]{2,1,0:T(8,128)} %get-tuple-element.31), calls=%async_computation.3 | async-start | bytes 524288 | tf_op jit(solution)/shard_map/all_to_all | solution.py:521
  209.9 26.8 %collective-permute-start.11 = (f32[8,16,256]{2,1,0:T(8,128)S(1)}, f32[8,16,256]{2,1,0:T(8,128)S(1)}, u32[]{:S(2)}, u32[]{:S(2)}) collective-permute-start(f32[8,16,256]{2,1,0:T(8,128)S(1)} %constant_dynamic-slice_fusion), channel_id=1, source_target_pairs={{0,16},{16,0},{1,17},{17,1},{2,18},{18,2},{3,19},{19,3},{4,20},{20... | collective-permute-start | bytes 393224 | tf_op jit(solution)/shard_map/ppermute | solution.py:523
  211.7 1.6 copy-start.3
  213.3 23.5 %copy-start.8 = (f32[8,256,16]{1,2,0:T(8,128)S(1)}, f32[8,256,16]{1,2,0:T(8,128)}, u32[]{:S(2)}) copy-start(f32[8,256,16]{1,2,0:T(8,128)} %param.8) | copy-start | bytes 393220
  213.3 23.5 %copy-start.14 = (s32[8]{0:T(128)S(1)}, s32[8]{0:T(128)}, u32[]{:S(2)}) copy-start(s32[8]{0:T(128)} %rsector.1) | copy-start | bytes 100
  (4 other events, 4.4 us)

commit v3 on v2

v3 whole, which is shorter than its diff:
```python
import jax
import jax.numpy as jnp
from jax import lax
from jax.experimental import pallas as pl
from jax.experimental.pallas import tpu as pltpu
from jax.sharding import Mesh, PartitionSpec as P

ITERS = 2
TILE = 256
HALF = 128
TERMS = 16
LEFT_ROWS = 136
SLOT_ROWS = 152
COL = ("x", "z")
ALL = ("y", "c", "x", "z")
SWAP = [(0, 1), (1, 0)]
UP = [(i, (i + 1) % 4) for i in range(4)]
DOWN = [(i, (i - 1) % 4) for i in range(4)]
f32 = jnp.float32
bf16 = jnp.bfloat16


def params(mib):
    return pltpu.CompilerParams(vmem_limit_bytes=mib * 1024 * 1024)


def cost(flops, nbytes):
    return pl.CostEstimate(flops=flops, transcendentals=0, bytes_accessed=nbytes)


def vmem():
    return pl.BlockSpec(memory_space=pltpu.VMEM)


def grids(rows, cols):
    i = lax.broadcasted_iota(jnp.int32, (rows, cols), 0)
    j = lax.broadcasted_iota(jnp.int32, (rows, cols), 1)
    return i, j


def fold_tile(tile):
    i, j = grids(HALF, HALF)
    a00 = tile[:HALF, :HALF]
    a11 = tile[HALF:, HALF:]
    fold = jnp.where(i >= j, a00, a11)
    diag = jnp.sum(jnp.where(i == j, a11, 0.0), axis=0, keepdims=True)
    return fold, tile[:HALF, HALF:], diag


def diag_rows(diag):
    wide = jnp.concatenate([diag, jnp.zeros((1, HALF), f32)], axis=1)
    return jnp.broadcast_to(wide, (8, TILE))


def unfold_tile(fold, corner, diag):
    i, j = grids(HALF, HALF)
    flip = fold.T
    a00 = jnp.where(i >= j, fold, flip)
    a11 = jnp.where(i == j, diag, jnp.where(i < j, fold, flip))
    top = jnp.concatenate([a00, corner], axis=1)
    low = jnp.concatenate([corner.T, a11], axis=1)
    return jnp.concatenate([top, low], axis=0)


def split(x):
    hi = x.astype(bf16)
    return hi, (x - hi.astype(f32)).astype(bf16)


def dot3(a_hi, a_lo, b_hi, b_lo):
    def dot(a, b):
        return jnp.dot(a, b, preferred_element_type=f32)

    return dot(a_hi, b_hi) + (dot(a_hi, b_lo) + dot(a_lo, b_hi))


def total(x):
    return jnp.sum(jnp.sum(x, axis=0, keepdims=True), axis=1, keepdims=True)


def inverse(norm):
    good = norm > 0.0
    return jnp.where(good, 1.0 / jnp.where(good, norm, 1.0), 0.0)


def put(stats, lane, value):
    _, j = grids(8, HALF)
    return jnp.where(j == lane, value, stats)


def fold_left_body(ids, src, keep, give):
    for dst, term in ((give, 1 - ids[1]), (keep, ids[1])):
        fold, corner, diag = fold_tile(src[0, term])
        dst[0, :HALF, :HALF] = fold
        dst[0, :HALF, HALF:] = corner
        dst[0, HALF:, :] = diag_rows(diag)


def fold_left(ids, left_env):
    count = left_env.shape[0]
    folded = pl.BlockSpec((1, LEFT_ROWS, TILE), lambda n, ids: (n, 0, 0))
    return pl.pallas_call(
        fold_left_body,
        grid_spec=pltpu.PrefetchScalarGridSpec(
            num_scalar_prefetch=1,
            grid=(count,),
            in_specs=[pl.BlockSpec((1, 2, TILE, TILE), lambda n, ids: (n, 0, 0, 0))],
            out_specs=[folded, folded],
        ),
        out_shape=[jax.ShapeDtypeStruct((count, LEFT_ROWS, TILE), f32)] * 2,
        compiler_params=params(4),
        cost_estimate=cost(1_000_000, 4_000_000),
        name="fold_left",
    )(ids, left_env)


def from_rows(ids, own, other, slot, field):
    at = (slot % 8) * 3 + field
    return jnp.where(slot // 8 == ids[1], own[at], other[at])


def right_slots_body(ids, own, other, thin, thin_other, right_env, dst, right, sem):
    def fetch(sector):
        return pltpu.make_async_copy(right_env.at[sector, ids[1]], right.at[sector], sem.at[sector])

    for sector in range(8):
        fetch(sector).start()
    for slot in range(TERMS):
        here = slot // 8 == ids[1]
        dst[slot, :16, :] = jnp.where(here, thin[slot % 8], thin_other[slot % 8])
    for sector in range(8):
        fetch(sector).wait()

    def one(slot, carry):
        on = from_rows(ids, own, other, slot, 1 + ids[1]).astype(f32)
        fold, corner, diag = fold_tile(right[from_rows(ids, own, other, slot, 0)] * on)
        dst[slot, 16 : 16 + HALF, :HALF] = fold
        dst[slot, 16 : 16 + HALF, HALF:] = corner
        dst[slot, 16 + HALF :, :] = diag_rows(diag)
        return carry

    lax.fori_loop(0, TERMS, one, 0)


def right_slots(ids, own, other, right_env, thin, thin_other):
    smem = pl.BlockSpec(memory_space=pltpu.SMEM)
    return pl.pallas_call(
        right_slots_body,
        in_specs=[smem] * 3 + [vmem()] * 2 + [pl.BlockSpec(memory_space=pl.ANY)],
        out_specs=vmem(),
        out_shape=jax.ShapeDtypeStruct((TERMS, SLOT_ROWS, TILE), f32),
        scratch_shapes=[pltpu.VMEM((8, TILE, TILE), f32), pltpu.SemaphoreType.DMA((8,))],
        compiler_params=params(10),
        cost_estimate=cost(4_000_000, 10_000_000),
        name="right_slots",
    )(ids, own, other, thin, thin_other, right_env)


def left_slots_body(ids, left_sector, *refs):
    pieces, dst = refs[:8], refs[8]

    def one(slot, carry):
        sector = left_sector[ids[0] * 16 + slot]
        home = sector // 4
        which = ((home // 2 - ids[0] + 4) % 4) * 2 + (home % 2 + ids[1]) % 2
        for n in range(8):

            @pl.when(which == n)
            def _():
                dst[slot] = pieces[n][sector % 4]

        return carry

    lax.fori_loop(0, TERMS, one, 0)


def left_slots(ids, left_sector, pieces):
    smem = pl.BlockSpec(memory_space=pltpu.SMEM)
    return pl.pallas_call(
        left_slots_body,
        in_specs=[smem, smem] + [vmem()] * 8,
        out_specs=vmem(),
        out_shape=jax.ShapeDtypeStruct((TERMS,) + pieces[0].shape[1:], f32),
        compiler_params=params(10),
        cost_estimate=cost(0, 4_000_000),
        name="left_slots",
    )(ids, left_sector, *pieces)


def live_sizes(ids, own, other, left_sector, left_size, right_size):
    live_left = left_size[left_sector[ids[0] * 16 + ids[2]]]
    live_right = right_size[from_rows(ids, own, other, ids[2], 0)]
    return live_right, live_left


def mask_of(live_right, live_left):
    i, j = grids(TILE, TILE)
    return (i < live_right) & (j < live_left)


def right_times(r_hi, r_lo, q_hi, q_lo, m_hi, m_lo):
    for n in range(TERMS):
        rows = pl.ds(n * TILE, TILE)
        hi, lo = split(dot3(r_hi[rows, :], r_lo[rows, :], q_hi, q_lo))
        m_hi[:, rows] = hi
        m_lo[:, rows] = lo


def first_body(ids, own, other, sector, lsize, rsize, arrived, r_hi, r_lo, m_hi, m_lo, q1, stats):
    live_right, live_left = live_sizes(ids, own, other, sector, lsize, rsize)
    block = jnp.concatenate([arrived[n, :16, :] for n in range(TERMS)], axis=0)
    start = jnp.where(mask_of(live_right, live_left), block, 0.0)
    norm = jnp.sqrt(total(start * start))
    vec = start * inverse(norm)
    q1[...] = vec
    stats[...] = put(jnp.zeros((8, HALF), f32), 0, norm)

    def term(n, carry):
        full = unfold_tile(
            arrived[n, 16 : 16 + HALF, :HALF],
            arrived[n, 16 : 16 + HALF, HALF:],
            arrived[n, 16 + HALF : 17 + HALF, :HALF],
        )
        hi, lo = split(full)
        rows = pl.ds(pl.multiple_of(n * TILE, TILE), TILE)
        r_hi[rows, :] = hi
        r_lo[rows, :] = lo
        return carry

    lax.fori_loop(0, TERMS, term, 0)
    q_hi, q_lo = split(vec)
    right_times(r_hi, r_lo, q_hi, q_lo, m_hi, m_lo)


def first_vector(scalars, arrived):
    smem = pl.BlockSpec(memory_space=pltpu.SMEM)
    return pl.pallas_call(
        first_body,
        in_specs=[smem] * 6 + [vmem()],
        out_specs=[vmem()] * 6,
        out_shape=[
            jax.ShapeDtypeStruct((TERMS * TILE, TILE), bf16),
            jax.ShapeDtypeStruct((TERMS * TILE, TILE), bf16),
            jax.ShapeDtypeStruct((TILE, TERMS * TILE), bf16),
            jax.ShapeDtypeStruct((TILE, TERMS * TILE), bf16),
            jax.ShapeDtypeStruct((TILE, TILE), f32),
            jax.ShapeDtypeStruct((8, HALF), f32),
        ],
        compiler_params=params(10),
        cost_estimate=cost(1_700_000_000, 12_000_000),
        name="first_vector",
    )(*scalars, arrived)


def image_one_body(arrived, m_hi, m_lo, l_hi, l_lo, part):
    for n in range(TERMS):
        full = unfold_tile(
            arrived[n, :HALF, :HALF], arrived[n, :HALF, HALF:], arrived[n, HALF : HALF + 1, :HALF]
        )
        hi, lo = split(full)
        rows = pl.ds(n * TILE, TILE)
        l_hi[rows, :] = hi
        l_lo[rows, :] = lo
    part[...] = dot3(m_hi[...], m_lo[...], l_hi[...], l_lo[...])


def image_one(arrived, m_hi, m_lo):
    return pl.pallas_call(
        image_one_body,
        in_specs=[vmem()] * 3,
        out_specs=[vmem()] * 3,
        out_shape=[
            jax.ShapeDtypeStruct((TERMS * TILE, TILE), bf16),
            jax.ShapeDtypeStruct((TERMS * TILE, TILE), bf16),
            jax.ShapeDtypeStruct((TILE, TILE), f32),
        ],
        compiler_params=params(10),
        cost_estimate=cost(1_700_000_000, 10_000_000),
        name="image_one",
    )(arrived, m_hi, m_lo)


def lanczos(image, last, before, beta):
    alpha = total(last * image)
    rest = image - alpha * last
    if before is not None:
        rest = rest - beta * before
    again = rest - total(last * rest) * last
    if before is not None:
        again = again - total(before * rest) * before
    norm = jnp.sqrt(total(again * again))
    return alpha, norm, again * inverse(norm)


def image_two_body(
    ids, own, other, sector, lsize, rsize,
    part_a, part_b, q1, stats_in, r_hi, r_lo, l_hi, l_lo,
    part, q2, stats, m_hi, m_lo,
):
    mask = mask_of(*live_sizes(ids, own, other, sector, lsize, rsize))
    image = jnp.where(mask, part_a[...] + part_b[...], 0.0)
    alpha, norm, vec = lanczos(image, q1[...], None, None)
    q2[...] = vec
    stats[...] = put(put(stats_in[...], 1, alpha), 2, norm)
    q_hi, q_lo = split(vec)
    right_times(r_hi, r_lo, q_hi, q_lo, m_hi, m_lo)
    part[...] = dot3(m_hi[...], m_lo[...], l_hi[...], l_lo[...])


def image_two(scalars, part, part_other, q1, stats, stacks):
    smem = pl.BlockSpec(memory_space=pltpu.SMEM)
    return pl.pallas_call(
        image_two_body,
        in_specs=[smem] * 6 + [vmem()] * 8,
        out_specs=[vmem()] * 3,
        out_shape=[
            jax.ShapeDtypeStruct((TILE, TILE), f32),
            jax.ShapeDtypeStruct((TILE, TILE), f32),
            jax.ShapeDtypeStruct((8, HALF), f32),
        ],
        scratch_shapes=[pltpu.VMEM((TILE, TERMS * TILE), bf16)] * 2,
        compiler_params=params(10),
        cost_estimate=cost(3_300_000_000, 9_000_000),
        name="image_two",
    )(*scalars, part, part_other, q1, stats, *stacks)


def third_body(
    ids, own, other, sector, lsize, rsize, part_a, part_b, q1, q2, stats_in, q3, sent, stats
):
    mask = mask_of(*live_sizes(ids, own, other, sector, lsize, rsize))
    image = jnp.where(mask, part_a[...] + part_b[...], 0.0)
    _, j = grids(8, HALF)
    beta = total(jnp.where((j == 2) & (grids(8, HALF)[0] == 0), stats_in[...], 0.0))
    alpha, norm, vec = lanczos(image, q2[...], q1[...], beta)
    q3[...] = vec
    pick = jnp.where(ids[1] == 0, q2[...], vec)
    for n in range(16):
        sent[n] = pick[16 * n : 16 * n + 16]
    stats[...] = put(put(stats_in[...], 3, alpha), 4, norm)


def third_vector(scalars, part, part_other, q1, q2, stats):
    smem = pl.BlockSpec(memory_space=pltpu.SMEM)
    return pl.pallas_call(
        third_body,
        in_specs=[smem] * 6 + [vmem()] * 5,
        out_specs=[vmem()] * 3,
        out_shape=[
            jax.ShapeDtypeStruct((TILE, TILE), f32),
            jax.ShapeDtypeStruct((16, 16, TILE), f32),
            jax.ShapeDtypeStruct((8, HALF), f32),
        ],
        compiler_params=params(4),
        name="third_vector",
    )(*scalars, part, part_other, q1, q2, stats)


def image_three_body(q3, stats_in, r_hi, r_lo, l_hi, l_lo, stats, m_hi, m_lo):
    vec = q3[...]
    q_hi, q_lo = split(vec)
    right_times(r_hi, r_lo, q_hi, q_lo, m_hi, m_lo)
    alpha = total(vec * dot3(m_hi[...], m_lo[...], l_hi[...], l_lo[...]))
    mine = put(stats_in[...], 5, alpha)
    stats[...] = jnp.broadcast_to(mine[0:1, :], (128, HALF))


def image_three(q3, stats, stacks):
    return pl.pallas_call(
        image_three_body,
        in_specs=[vmem()] * 6,
        out_specs=vmem(),
        out_shape=jax.ShapeDtypeStruct((128, HALF), f32),
        scratch_shapes=[pltpu.VMEM((TILE, TERMS * TILE), bf16)] * 2,
        compiler_params=params(10),
        cost_estimate=cost(3_300_000_000, 9_000_000),
        name="image_three",
    )(q3, stats, *stacks)


def ritz_pair(norm, a1, b1, a2, b2, a3):
    def apply(x):
        return [a1 * x[0] + b1 * x[1], b1 * x[0] + a2 * x[1] + b2 * x[2], b2 * x[1] + a3 * x[2]]

    def dot(x, y):
        return 0.5 * jnp.sum(x[0] * y[0] + x[1] * y[1] + x[2] * y[2], axis=1, keepdims=True)

    zero = jnp.zeros_like(norm)
    start = [norm, zero, zero]
    image = apply(start)
    norm_sq = dot(start, start)
    correlation = dot(start, image)
    inv_norm = 1.0 / jnp.sqrt(norm_sq)
    basis = [x * inv_norm for x in start]
    applied = [x * inv_norm for x in image]
    ritz = correlation / norm_sq
    for _ in range(ITERS):
        residual = [x - ritz * y for x, y in zip(applied, basis)]
        res_sq = dot(residual, residual)
        length = jnp.sqrt(res_sq)
        fresh = [x / length for x in residual]
        fresh_applied = apply(fresh)
        curvature = dot(fresh, fresh_applied)
        half_gap = 0.5 * (ritz - curvature)
        root = jnp.sqrt(half_gap * half_gap + res_sq)
        lowest = 0.5 * (ritz + curvature) - root
        first = curvature - lowest
        pair = jnp.sqrt(first * first + res_sq)
        basis = [(first * x - length * y) / pair for x, y in zip(basis, fresh)]
        applied = [(first * x - length * y) / pair for x, y in zip(applied, fresh_applied)]
        ritz = lowest
    return basis, ritz


def finish_body(
    ids, sector, rsector, lsize, rsize, stats, thin, got, back, out, energy, coef
):
    flip = stats[...].T
    norm, a1, b1, a2, b2, part = [flip[m : m + 1, :] for m in range(6)]
    _, lane = grids(1, HALF)
    core_of = (lane // 16) % 2
    a3 = part + jnp.where(core_of == 0, pltpu.roll(part, HALF - 16, 1), pltpu.roll(part, 16, 1))
    basis, ritz = ritz_pair(norm, a1, b1, a2, b2, a3)
    energy[...] = jnp.broadcast_to(ritz, (8, HALF))
    scale = jnp.sqrt(jnp.full((1, HALF), 64 * TILE * TILE, f32))
    i, _ = grids(HALF, HALF)
    c1 = basis[0] * inverse(norm) * scale
    c2 = basis[1] * scale
    c3 = basis[2] * scale
    coef[...] = jnp.where(i == 0, c1, jnp.where(i == 1, c2, jnp.where(i == 2, c3, 0.0))).T
    core = ids[1]
    own = coef[pl.ds(pl.multiple_of(ids[0] * 32 + core * 8, 8), 8), :]
    jcol, irow = grids(16, TILE)
    for b in range(8):
        live_left = lsize[sector[ids[0] * 16 + core * 8 + b]]
        live_right = rsize[rsector[b]]
        live = (jcol + ids[2] * 16 < live_right) & (irow < live_left)
        keep = got[core * 8 + b]
        recv = back[b]
        second = jnp.where(core == 0, keep, recv)
        third = jnp.where(core == 0, recv, keep)
        out[b] = (
            own[b : b + 1, 0:1] * jnp.where(live, thin[b], 0.0)
            + own[b : b + 1, 1:2] * second
            + own[b : b + 1, 2:3] * third
        )


def finish(ids, sector, rsector, lsize, rsize, stats, thin, got, back):
    smem = pl.BlockSpec(memory_space=pltpu.SMEM)
    return pl.pallas_call(
        finish_body,
        in_specs=[smem] * 5 + [vmem()] * 4,
        out_specs=[vmem()] * 2,
        out_shape=[
            jax.ShapeDtypeStruct(thin.shape, f32),
            jax.ShapeDtypeStruct((8, HALF), f32),
        ],
        scratch_shapes=[pltpu.VMEM((HALF, HALF), f32)],
        compiler_params=params(4),
        name="finish",
    )(ids, sector, rsector, lsize, rsize, stats, thin, got, back)


def local(theta, left_env, right_env, left_sector, right_sector, term_on, left_size, right_size):
    plane = lax.axis_index("y").astype(jnp.int32)
    core = lax.axis_index("c").astype(jnp.int32)
    place = lax.axis_index(COL).astype(jnp.int32)
    ids = jnp.stack([plane, core, place])
    thin = jnp.swapaxes(theta, 1, 2)

    own = jnp.concatenate([right_sector[:, None], term_on], axis=1).reshape(-1)
    mine, folded = fold_left(ids, left_env)
    theirs = lax.ppermute(folded, "c", SWAP)
    mine_up = lax.ppermute(mine, "y", UP)
    mine_down = lax.ppermute(mine, "y", DOWN)
    theirs_up = lax.ppermute(theirs, "y", UP)
    theirs_down = lax.ppermute(theirs, "y", DOWN)

    other = lax.ppermute(own, "c", SWAP)
    thin_other = lax.ppermute(thin, "c", SWAP)
    thin_late, _ = lax.optimization_barrier((thin, mine))
    slots = right_slots(ids, own, other, right_env, thin_late, thin_other)
    arrived = lax.all_to_all(slots, COL, 0, 0, tiled=True)
    scalars = (ids, own, other, left_sector, left_size, right_size)
    r_hi, r_lo, m_hi, m_lo, q1, stats = first_vector(scalars, arrived)

    mine_far = lax.ppermute(mine_up, "y", UP)
    theirs_far = lax.ppermute(theirs_down, "y", DOWN)
    pieces = [mine, theirs, mine_down, theirs_down, mine_far, theirs_far, mine_up, theirs_up]
    left_arrived = lax.all_to_all(left_slots(ids, left_sector, pieces), COL, 0, 0, tiled=True)
    l_hi, l_lo, part = image_one(left_arrived, m_hi, m_lo)
    stacks = (r_hi, r_lo, l_hi, l_lo)
    part, q2, stats = image_two(scalars, part, lax.ppermute(part, "c", SWAP), q1, stats, stacks)
    q3, sent, stats = third_vector(scalars, part, lax.ppermute(part, "c", SWAP), q1, q2, stats)

    stats = image_three(q3, stats, stacks)
    sent, stats = lax.optimization_barrier((sent, stats))
    stats = lax.all_to_all(stats, ALL, 0, 0, tiled=True)
    got = lax.all_to_all(sent, COL, 0, 0, tiled=True)
    give = lax.dynamic_slice_in_dim(got, (1 - core) * 8, 8)
    back = lax.ppermute(give, "c", SWAP)
    out, energy = finish(
        ids, left_sector, right_sector, left_size, right_size, stats, thin, got, back
    )
    return jnp.swapaxes(out, 1, 2), energy[0, 0]


def solution(mesh):
    fine = Mesh(mesh.devices.reshape(4, 2, 4, 4), ALL)
    row = ("y", "c")
    placed = (
        P(row, None, COL),
        P(row, COL, None, None),
        P(None, COL, None, None),
        P(),
        P(row),
        P(row, COL),
        P(),
        P(),
    )
    return jax.shard_map(
        local, mesh=fine, in_specs=placed, out_specs=(P(row, None, COL), P()), check_vma=False
    )
```

time: 241 us -> 160 us (0.66)
  Pallas kernels: 119 us -> 29.2 us
  local copies, waits for them, and re-layouts: 8.1 us -> 18.4 us
  waiting for transfers between devices: 61.1 us -> 56.4 us
  starting transfers between devices: 34.8 us -> 37.8 us
    pallas_call x5, Pallas kernels: 106 us -> 20 us  [the longest x1 6.92 us: image_two(): pl.pallas_call(image_two_body, in_specs=[smem] * 6 + [vmem()] * 8, out_sp...]
    unnamed x42 -> x38, local copies, waits for them, and re-layouts: 7.42 us -> 17.7 us
    pallas_call x1, Pallas kernels: 9.01 us -> 4.39 us  [first_vector(): pl.pallas_call(first_body, in_specs=[smem] * 6 + [vmem()], out_specs=[vme...]
    all_to_all x1, waiting for transfers between devices: 19.1 us -> 15.4 us  [local(): lax.all_to_all(left_slots(ids, left_sector, pieces), COL, 0, 0, tiled=True)]
  transfers between devices with their start and end apart: 15 -> 15, of which waited for: 9 -> 10; matrix products, arithmetic and copies ran while one was open for 0% -> 1% of each run, Pallas kernels for 36% -> 4%
where the time goes in v3:
time: 160 us; the launch traced here: 159 us
  waiting for transfers between devices  56.4 us (35%)
  starting transfers between devices  37.8 us (24%)
  Pallas kernels  29.2 us (18%)
  local copies, waits for them, and re-layouts  18.4 us (11%)
  blocking collectives  15.7 us (10%)
    unnamed x38, local copies, waits for them, and re-layouts  17.7 us
    all_to_all x1, blocking collectives, local(): stats = lax.all_to_all(stats, ALL, 0, 0, tiled=True)  15.7 us
    all_to_all x1, waiting for transfers between devices, local(): lax.all_to_all(left_slots(ids, left_sector, pieces), COL, 0, 0, tiled=True)  15.4 us
    ppermute x1, waiting for transfers between devices, local(): mine_far = lax.ppermute(mine_up, 'y', UP)  11.3 us
    ppermute x1, waiting for transfers between devices, local(): mine_up = lax.ppermute(mine, 'y', UP)  9.52 us
    ppermute x1, waiting for transfers between devices, local(): mine_down = lax.ppermute(mine, 'y', DOWN)  8.53 us
    all_to_all x1, starting transfers between devices, local(): arrived = lax.all_to_all(slots, COL, 0, 0, tiled=True)  7.69 us
    all_to_all x1, waiting for transfers between devices, local(): got = lax.all_to_all(sent, COL, 0, 0, tiled=True)  7.55 us
  transfers between devices with their start and end apart: 15, of which 10 were waited for; matrix products, arithmetic and copies ran while one was open for 1% of the time, Pallas kernels for 4%

profile of v3, /device:TPU:1, one launch (start us, length us, event | category | flops | bytes accessed | tf_op | source)
XLA Modules:
  0.0 159.0 jit_solution(5469040235463577690)
XLA Ops:
  0.6 1.5 collective-permute-start.8
  3.1 1.6 %copy-done.8 = f32[4,2,256,256]{3,2,1,0:T(8,128)S(1)} copy-done((f32[4,2,256,256]{3,2,1,0:T(8,128)S(1)}, f32[4,2,256,256]{3,2,1,0:T(8,128)}, u32[]{:S(2)}) %copy-start.8) | copy-done | bytes 2097176
  6.3 2.2 %copy-done.1 = f32[8,2,256,256]{3,2,1,0:T(8,128)S(1)} copy-done((f32[8,2,256,256]{3,2,1,0:T(8,128)S(1)}, f32[8,2,256,256]{3,2,1,0:T(8,128)}, u32[]{:S(2)}) %copy-start.1) | copy-done | bytes 4194328
  8.5 2.9 %right_slots.1 = f32[16,152,256]{2,1,0:T(8,128)} custom-call(s32[3]{0:T(128)S(1)} %pad_add_fusion.1.ids, s32[24]{0:T(128)S(1)} %reshape.9.own, s32[24]{0:T(128)S(1)} %collective-permute-done.other, f32[8,16,256]{2,1,0:T(8,128)S(1)} %bitcast.12, f32[8,16,256]{2,1,0:T(8,128)S(1)} %collective-permute-done.8.thin_other, f32[8,2,256,256]{3,2,1,0:T(8,128)S(1)} %copy-done.1), custom_call_target="tpu_custom_call" | custom-call | flops 4000000 | bytes 10000000 | tf_op jit(solution)/shard_map/right_slots/pallas_call | solution.py:147
  11.4 7.7 %all-to-all-start.1 = ((f32[16,152,256]{2,1,0:T(8,128)}), f32[16,152,256]{2,1,0:T(8,128)S(1)}, u32[]{:S(2)}, u32[]{:S(2)}) async-start(f32[16,152,256]{2,1,0:T(8,128)} %right_slots.1), calls=%async_computation.1 | async-start | bytes 4980736 | tf_op jit(solution)/shard_map/all_to_all | solution.py:484
  21.7 2.7 %collective-permute-start.3 = (f32[4,136,256]{2,1,0:T(8,128)S(1)}, f32[4,136,256]{2,1,0:T(8,128)S(1)}, u32[]{:S(2)}, u32[]{:S(2)}) collective-permute-start(f32[4,136,256]{2,1,0:T(8,128)S(1)} %collective-permute-done.1.refs_1_), channel_id=1, source_target_pairs={{0,96},{32,0},{64,32},{96,64},{1,97},{33,1},{65,33},{97,65},{2,98}... | collective-permute-start | bytes 1671176 | tf_op jit(solution)/shard_map/ppermute | solution.py:478
  25.9 9.5 %collective-permute-done.4.refs_6_ = f32[4,136,256]{2,1,0:T(8,128)S(1)} collective-permute-done((f32[4,136,256]{2,1,0:T(8,128)S(1)}, f32[4,136,256]{2,1,0:T(8,128)S(1)}, u32[]{:S(2)}, u32[]{:S(2)}) %collective-permute-start.4) | collective-permute-done | bytes 557088 | tf_op jit(solution)/shard_map/ppermute | solution.py:475
  36.1 3.4 %collective-permute-start.6 = (f32[4,136,256]{2,1,0:T(8,128)S(1)}, f32[4,136,256]{2,1,0:T(8,128)S(1)}, u32[]{:S(2)}, u32[]{:S(2)}) collective-permute-start(f32[4,136,256]{2,1,0:T(8,128)S(1)} %collective-permute-done.3.refs_3_), channel_id=1, source_target_pairs={{0,96},{32,0},{64,32},{96,64},{1,97},{33,1},{65,33},{97,65},{2,98}... | collective-permute-start | bytes 1671176 | tf_op jit(solution)/shard_map/ppermute | solution.py:489
  39.5 8.5 %collective-permute-done.2.refs_2_ = f32[4,136,256]{2,1,0:T(8,128)S(1)} collective-permute-done((f32[4,136,256]{2,1,0:T(8,128)S(1)}, f32[4,136,256]{2,1,0:T(8,128)S(1)}, u32[]{:S(2)}, u32[]{:S(2)}) %collective-permute-start.2) | collective-permute-done | bytes 557088 | tf_op jit(solution)/shard_map/ppermute | solution.py:476
  48.0 11.3 %collective-permute-done.5.refs_4_ = f32[4,136,256]{2,1,0:T(8,128)S(1)} collective-permute-done((f32[4,136,256]{2,1,0:T(8,128)S(1)}, f32[4,136,256]{2,1,0:T(8,128)S(1)}, u32[]{:S(2)}, u32[]{:S(2)}) %collective-permute-start.5) | collective-permute-done | bytes 557088 | tf_op jit(solution)/shard_map/ppermute | solution.py:488
  60.0 1.9 %left_slots.1 = f32[16,136,256]{2,1,0:T(8,128)S(1)} custom-call(s32[3]{0:T(128)S(1)} %pad_add_fusion.1.ids, s32[64]{0:T(128)S(1)} %copy-done.10, f32[4,136,256]{2,1,0:T(8,128)S(1)} %get-tuple-element.24.refs_0_, f32[4,136,256]{2,1,0:T(8,128)S(1)} %collective-permute-done.1.refs_1_, f32[4,136,256]{2,1,0:T(8,128)S(1)} %collective-permute-done.2.refs_2_, ...), custom_call_target="tpu_custom_call" | custom-call | bytes 4000000 | tf_op jit(solution)/shard_map/left_slots/pallas_call | solution.py:179
  61.9 1.4 copy-done
  63.3 1.5 copy-done.2
  64.7 6.9 %all-to-all-start = ((f32[16,136,256]{2,1,0:T(8,128)}), f32[16,136,256]{2,1,0:T(8,128)S(1)}, u32[]{:S(2)}, u32[]{:S(2)}) async-start(f32[16,136,256]{2,1,0:T(8,128)} %copy-done), calls=%async_computation | async-start | bytes 4456448 | tf_op jit(solution)/shard_map/all_to_all | solution.py:491
  71.6 1.7 %copy-done.3 = f32[16,152,256]{2,1,0:T(8,128)S(1)} copy-done((f32[16,152,256]{2,1,0:T(8,128)S(1)}, f32[16,152,256]{2,1,0:T(8,128)}, u32[]{:S(2)}) %copy-start.3) | copy-done | bytes 2490392
  73.3 4.4 %first_vector.1 = (bf16[4096,256]{1,0:T(8,128)(2,1)S(1)}, bf16[4096,256]{1,0:T(8,128)(2,1)S(1)}, bf16[256,4096]{1,0:T(8,128)(2,1)S(1)}, bf16[256,4096]{1,0:T(8,1...) custom-call(s32[3]{0:T(128)S(1)} %pad_add_fusion.1.ids, s32[24]{0:T(128)S(1)} %reshape.9.own, ...), custom_call_target="tpu_custom_call" | custom-call | flops 1700000000 | bytes 12000000 | tf_op jit(solution)/shard_map/first_vector/pallas_call | solution.py:237
  77.7 1.3 copy-done.4
  79.1 1.4 copy-done.6
  80.4 1.4 copy-done.15
  83.1 15.4 %all-to-all-done.arrived = f32[16,136,256]{2,1,0:T(8,128)S(1)} async-done(((f32[16,136,256]{2,1,0:T(8,128)}), f32[16,136,256]{2,1,0:T(8,128)S(1)}, u32[]{:S(2)}, u32[]{:S(2)}) %all-to-all-start) | async-done | bytes 2228256 | tf_op jit(solution)/shard_map/all_to_all | solution.py:491
  98.5 1.6 copy-done.5
  100.1 1.6 copy-done.7
  101.7 2.3 %image_one.1 = (bf16[4096,256]{1,0:T(8,128)(2,1)S(1)}, bf16[4096,256]{1,0:T(8,128)(2,1)S(1)}, f32[256,256]{1,0:T(8,128)S(1)}) custom-call(f32[16,136,256]{2,1,0:T(8,128)S(1)} %all-to-all-done.arrived, bf16[256,4096]{1,0:T(8,128)(2,1)S(1)} %copy-done.5, bf16[256,4096]{1,0:T(8,128)(2,1)S(1)} %copy-done.7), custom_call_target="tpu_custom_call" | custom-call | flops 1700000000 | bytes 10000000 | tf_op jit(solution)/shard_map/image_one/pallas_call | solution.py:268
  104.0 5.6 %collective-permute-start.9 = (f32[256,256]{1,0:T(8,128)S(1)}, f32[256,256]{1,0:T(8,128)S(1)}, u32[]{:S(2)}, u32[]{:S(2)}) collective-permute-start(f32[256,256]{1,0:T(8,128)S(1)} %get-tuple-element.29.part_a), channel_id=1, source_target_pairs={{0,16},{16,0},{1,17},{17,1},{2,18},{18,2},{3,19},{19,3},{4,20},{20... | collective-permute-start | bytes 786440 | tf_op jit(solution)/shard_map/ppermute | solution.py:494
  110.8 6.9 %image_two.1 = (f32[256,256]{1,0:T(8,128)S(1)}, f32[256,256]{1,0:T(8,128)S(1)}, f32[8,128]{1,0:T(8,128)S(1)}) custom-call(s32[3]{0:T(128)S(1)} %pad_add_fusion.1.ids, s32[24]{0:T(128)S(1)} %reshape.9.own, s32[24]{0:T(128)S(1)} %collective-permute-done.other, s32[64]{0:T(128)S(1)} %copy-done.10, s32[32]{0:T(128)S(1)} %copy-done.11, s32[8]{0:T(128)S(1)} %copy-done.12, ...), custom_call_target="tpu_custom_call" | custom-call | flops 3300000000 | bytes 9000000 | tf_op jit(solution)/shard_map/image_two/pallas_call | solution.py:312
  119.5 1.8 %third_vector.1 = (f32[256,256]{1,0:T(8,128)S(1)}, f32[16,16,256]{2,1,0:T(8,128)}, f32[8,128]{1,0:T(8,128)S(1)}) custom-call(s32[3]{0:T(128)S(1)} %pad_add_fusion.1.ids, s32[24]{0:T(128)S(1)} %reshape.9.own, s32[24]{0:T(128)S(1)} %collective-permute-done.other, s32[64]{0:T(128)S(1)} %copy-done.10, s32[32]{0:T(128)S(1)} %copy-done.11, s32[8]{0:T(128)S(1)} %copy-done.12, ...), custom_call_target="tpu_custom_call" | custom-call | tf_op jit(solution)/shard_map/third_vector/pallas_call | solution.py:345
  121.3 6.0 %image_three.1 = f32[128,128]{1,0:T(8,128)S(1)} custom-call(f32[256,256]{1,0:T(8,128)S(1)} %get-tuple-element.40.q3, f32[8,128]{1,0:T(8,128)S(1)} %get-tuple-element.41.stats_in, bf16[4096,256]{1,0:T(8,128)(2,1)S(1)} %copy-done.16, bf16[4096,256]{1,0:T(8,128)(2,1)S(1)} %copy-done.18, bf16[4096,256]{1,0:T(8,128)(2,1)S(1)} %get-tuple-element.34.l_hi, ...), custom_call_target="tpu_custom_call" | custom-call | flops 3300000000 | bytes 9000000 | tf_op jit(solution)/shard_map/image_three/pallas_call | solution.py:369
  127.3 3.7 %all-to-all-start.3 = ((f32[16,16,256]{2,1,0:T(8,128)}), f32[16,16,256]{2,1,0:T(8,128)S(1)}, u32[]{:S(2)}, u32[]{:S(2)}) async-start(f32[16,16,256]{2,1,0:T(8,128)} %get-tuple-element.43), calls=%async_computation.3 | async-start | bytes 524288 | tf_op jit(solution)/shard_map/all_to_all | solution.py:500
  131.0 7.6 %all-to-all-done.3.got = f32[16,16,256]{2,1,0:T(8,128)S(1)} async-done(((f32[16,16,256]{2,1,0:T(8,128)}), f32[16,16,256]{2,1,0:T(8,128)S(1)}, u32[]{:S(2)}, u32[]{:S(2)}) %all-to-all-start.3) | async-done | bytes 262176 | tf_op jit(solution)/shard_map/all_to_all | solution.py:500
  138.6 2.0 %collective-permute-start.11 = (f32[8,16,256]{2,1,0:T(8,128)S(1)}, f32[8,16,256]{2,1,0:T(8,128)S(1)}, u32[]{:S(2)}, u32[]{:S(2)}) collective-permute-start(f32[8,16,256]{2,1,0:T(8,128)S(1)} %constant_dynamic-slice_fusion), channel_id=1, source_target_pairs={{0,16},{16,0},{1,17},{17,1},{2,18},{18,2},{3,19},{19,3},{4,20},{20... | collective-permute-start | bytes 393224 | tf_op jit(solution)/shard_map/ppermute | solution.py:502
  140.6 15.7 %all_to_all.26 = f32[128,1,128]{2,1,0:T(1,128)S(1)} all-to-all(f32[128,1,128]{2,1,0:T(1,128)S(1)} %bitcast.15), channel_id=1, replica_groups=mesh['y'=4,'c'=2,'x'=4,'z'=4] {'y','c','x','z'}, dimensions={0} | all-to-all | bytes 131072 | tf_op jit(solution)/shard_map/all_to_all | solution.py:499
  156.2 2.3 %finish.1 = (f32[8,16,256]{2,1,0:T(8,128)}, f32[8,128]{1,0:T(8,128)S(1)}) custom-call(s32[3]{0:T(128)S(1)} %pad_add_fusion.1.ids, s32[64]{0:T(128)S(1)} %copy-done.10, s32[8]{0:T(128)S(1)} %copy-done.13, s32[32]{0:T(128)S(1)} %copy-done.11, s32[8]{0:T(128)S(1)} %copy-done.12, f32[128,128]{1,0:T(8,128)S(1)} %bitcast.14, f32[8,16,256]{2,1,0:T(8,128)S(1)} %bitcast.13, ...), custom_call_target="tpu_custom_call" | custom-call | tf_op jit(solution)/shard_map/finish/pallas_call | solution.py:451
  (52 shorter events, 12.8 us)
Async XLA Ops:
  0.6 5.6 %collective-permute-start.8 = (f32[8,16,256]{2,1,0:T(8,128)}, f32[8,16,256]{2,1,0:T(8,128)S(1)}, u32[]{:S(2)}, u32[]{:S(2)}) collective-permute-start(f32[8,16,256]{2,1,0:T(8,128)} %bitcast.11), channel_id=1, source_target_pairs={{0,16},{16,0},{1,17},{17,1},{2,18},{18,2},{3,19},{19,3},{4,20},{20... | collective-permute-start | bytes 393224 | tf_op jit(solution)/shard_map/ppermute | solution.py:481
  3.0 3.3 %collective-permute-start = (s32[24]{0:T(128)S(1)}, s32[24]{0:T(128)S(1)}, u32[]{:S(2)}, u32[]{:S(2)}) collective-permute-start(s32[24]{0:T(128)S(1)} %reshape.9.own), channel_id=1, source_target_pairs={{0,16},{16,0},{1,17},{17,1},{2,18},{18,2},{3,19},{19,3},{4,20},{20... | collective-permute-start | bytes 296 | tf_op jit(solution)/shard_map/ppermute | solution.py:480
  3.1 1.6 %copy-start.8 = (f32[4,2,256,256]{3,2,1,0:T(8,128)S(1)}, f32[4,2,256,256]{3,2,1,0:T(8,128)}, u32[]{:S(2)}) copy-start(f32[4,2,256,256]{3,2,1,0:T(8,128)} %src.1) | copy-start | bytes 6291460
  4.7 1.6 copy-start.9
  6.3 2.2 %copy-start.1 = (f32[8,2,256,256]{3,2,1,0:T(8,128)S(1)}, f32[8,2,256,256]{3,2,1,0:T(8,128)}, u32[]{:S(2)}) copy-start(f32[8,2,256,256]{3,2,1,0:T(8,128)} %right_env.1) | copy-start | bytes 12582916
  11.4 48.6 %copy-start.10 = (s32[64]{0:T(128)S(1)}, s32[64]{0:T(128)}, u32[]{:S(2)}) copy-start(s32[64]{0:T(128)} %sector.7) | copy-start | bytes 772
  11.4 51.9 %all-to-all-start.1 = ((f32[16,152,256]{2,1,0:T(8,128)}), f32[16,152,256]{2,1,0:T(8,128)S(1)}, u32[]{:S(2)}, u32[]{:S(2)}) async-start(f32[16,152,256]{2,1,0:T(8,128)} %right_slots.1), calls=%async_computation.1 | async-start | bytes 4980736 | tf_op jit(solution)/shard_map/all_to_all | solution.py:484
  19.1 2.6 %collective-permute-start.1 = (f32[4,136,256]{2,1,0:T(8,128)}, f32[4,136,256]{2,1,0:T(8,128)S(1)}, u32[]{:S(2)}, u32[]{:S(2)}) collective-permute-start(f32[4,136,256]{2,1,0:T(8,128)} %copy-done.14), channel_id=1, source_target_pairs={{0,16},{16,0},{1,17},{17,1},{2,18},{18,2},{3,19},{19,3},{4,20},{20... | collective-permute-start | bytes 1671176 | tf_op jit(solution)/shard_map/ppermute | solution.py:474
  19.9 15.5 %collective-permute-start.4 = (f32[4,136,256]{2,1,0:T(8,128)S(1)}, f32[4,136,256]{2,1,0:T(8,128)S(1)}, u32[]{:S(2)}, u32[]{:S(2)}) collective-permute-start(f32[4,136,256]{2,1,0:T(8,128)S(1)} %get-tuple-element.24.refs_0_), channel_id=1, source_target_pairs={{0,32},{32,64},{64,96},{96,0},{1,33},{33,65},{65,97},{97,1},{2,34}... | collective-permute-start | bytes 1671176 | tf_op jit(solution)/shard_map/ppermute | solution.py:475
  21.7 14.4 %collective-permute-start.3 = (f32[4,136,256]{2,1,0:T(8,128)S(1)}, f32[4,136,256]{2,1,0:T(8,128)S(1)}, u32[]{:S(2)}, u32[]{:S(2)}) collective-permute-start(f32[4,136,256]{2,1,0:T(8,128)S(1)} %collective-permute-done.1.refs_1_), channel_id=1, source_target_pairs={{0,96},{32,0},{64,32},{96,64},{1,97},{33,1},{65,33},{97,65},{2,98}... | collective-permute-start | bytes 1671176 | tf_op jit(solution)/shard_map/ppermute | solution.py:478
  24.5 23.6 %collective-permute-start.2 = (f32[4,136,256]{2,1,0:T(8,128)S(1)}, f32[4,136,256]{2,1,0:T(8,128)S(1)}, u32[]{:S(2)}, u32[]{:S(2)}) collective-permute-start(f32[4,136,256]{2,1,0:T(8,128)S(1)} %get-tuple-element.24.refs_0_), channel_id=1, source_target_pairs={{0,96},{32,0},{64,32},{96,64},{1,97},{33,1},{65,33},{97,65},{2,98}... | collective-permute-start | bytes 1671176 | tf_op jit(solution)/shard_map/ppermute | solution.py:476
  24.9 23.1 %collective-permute-start.7 = (f32[4,136,256]{2,1,0:T(8,128)S(1)}, f32[4,136,256]{2,1,0:T(8,128)S(1)}, u32[]{:S(2)}, u32[]{:S(2)}) collective-permute-start(f32[4,136,256]{2,1,0:T(8,128)S(1)} %collective-permute-done.1.refs_1_), channel_id=1, source_target_pairs={{0,32},{32,64},{64,96},{96,0},{1,33},{33,65},{65,97},{97,1},{2,34}... | collective-permute-start | bytes 1671176 | tf_op jit(solution)/shard_map/ppermute | solution.py:477
  35.4 23.9 %collective-permute-start.5 = (f32[4,136,256]{2,1,0:T(8,128)S(1)}, f32[4,136,256]{2,1,0:T(8,128)S(1)}, u32[]{:S(2)}, u32[]{:S(2)}) collective-permute-start(f32[4,136,256]{2,1,0:T(8,128)S(1)} %collective-permute-done.4.refs_6_), channel_id=1, source_target_pairs={{0,32},{32,64},{64,96},{96,0},{1,33},{33,65},{65,97},{97,1},{2,34}... | collective-permute-start | bytes 1671176 | tf_op jit(solution)/shard_map/ppermute | solution.py:488
  36.1 23.9 %collective-permute-start.6 = (f32[4,136,256]{2,1,0:T(8,128)S(1)}, f32[4,136,256]{2,1,0:T(8,128)S(1)}, u32[]{:S(2)}, u32[]{:S(2)}) collective-permute-start(f32[4,136,256]{2,1,0:T(8,128)S(1)} %collective-permute-done.3.refs_3_), channel_id=1, source_target_pairs={{0,96},{32,0},{64,32},{96,64},{1,97},{33,1},{65,33},{97,65},{2,98}... | collective-permute-start | bytes 1671176 | tf_op jit(solution)/shard_map/ppermute | solution.py:489
  61.9 1.4 copy-start
  63.3 8.4 %copy-start.11 = (s32[32]{0:T(128)S(1)}, s32[32]{0:T(128)}, u32[]{:S(2)}) copy-start(s32[32]{0:T(128)} %lsize.7) | copy-start | bytes 388
  63.3 8.4 %copy-start.12 = (s32[8]{0:T(128)S(1)}, s32[8]{0:T(128)}, u32[]{:S(2)}) copy-start(s32[8]{0:T(128)} %rsize.7) | copy-start | bytes 100
  63.3 1.5 copy-start.2
  64.7 33.8 %all-to-all-start = ((f32[16,136,256]{2,1,0:T(8,128)}), f32[16,136,256]{2,1,0:T(8,128)S(1)}, u32[]{:S(2)}, u32[]{:S(2)}) async-start(f32[16,136,256]{2,1,0:T(8,128)} %copy-done), calls=%async_computation | async-start | bytes 4456448 | tf_op jit(solution)/shard_map/all_to_all | solution.py:491
  71.6 1.7 %copy-start.3 = (f32[16,152,256]{2,1,0:T(8,128)S(1)}, f32[16,152,256]{2,1,0:T(8,128)}, u32[]{:S(2)}) copy-start(f32[16,152,256]{2,1,0:T(8,128)} %copy-done.2) | copy-start | bytes 7471108
  77.7 1.3 copy-start.4
  79.1 1.4 copy-start.6
  80.4 1.4 copy-start.15
  98.5 1.6 %copy-start.5 = (bf16[256,4096]{1,0:T(8,128)(2,1)S(1)}, bf16[256,4096]{1,0:T(8,128)(2,1)}, u32[]{:S(2)}) copy-start(bf16[256,4096]{1,0:T(8,128)(2,1)} %copy-done.4) | copy-start | bytes 6291460
  100.1 1.6 %copy-start.7 = (bf16[256,4096]{1,0:T(8,128)(2,1)S(1)}, bf16[256,4096]{1,0:T(8,128)(2,1)}, u32[]{:S(2)}) copy-start(bf16[256,4096]{1,0:T(8,128)(2,1)} %copy-done.6) | copy-start | bytes 6291460
  101.7 9.1 %copy-start.16 = (bf16[4096,256]{1,0:T(8,128)(2,1)S(1)}, bf16[4096,256]{1,0:T(8,128)(2,1)}, u32[]{:S(2)}) copy-start(bf16[4096,256]{1,0:T(8,128)(2,1)} %copy-done.15) | copy-start | bytes 6291460
  101.7 9.1 %copy-start.18 = (bf16[4096,256]{1,0:T(8,128)(2,1)S(1)}, bf16[4096,256]{1,0:T(8,128)(2,1)}, u32[]{:S(2)}) copy-start(bf16[4096,256]{1,0:T(8,128)(2,1)} %copy-done.17) | copy-start | bytes 6291460
  104.0 6.8 %collective-permute-start.9 = (f32[256,256]{1,0:T(8,128)S(1)}, f32[256,256]{1,0:T(8,128)S(1)}, u32[]{:S(2)}, u32[]{:S(2)}) collective-permute-start(f32[256,256]{1,0:T(8,128)S(1)} %get-tuple-element.29.part_a), channel_id=1, source_target_pairs={{0,16},{16,0},{1,17},{17,1},{2,18},{18,2},{3,19},{19,3},{4,20},{20... | collective-permute-start | bytes 786440 | tf_op jit(solution)/shard_map/ppermute | solution.py:494
  117.7 1.8 %collective-permute-start.10 = (f32[256,256]{1,0:T(8,128)S(1)}, f32[256,256]{1,0:T(8,128)S(1)}, u32[]{:S(2)}, u32[]{:S(2)}) collective-permute-start(f32[256,256]{1,0:T(8,128)S(1)} %get-tuple-element.36.part_a), channel_id=1, source_target_pairs={{0,16},{16,0},{1,17},{17,1},{2,18},{18,2},{3,19},{19,3},{4,20},{20... | collective-permute-start | bytes 786440 | tf_op jit(solution)/shard_map/ppermute | solution.py:495
  121.3 34.9 %copy-start.13 = (s32[8]{0:T(128)S(1)}, s32[8]{0:T(128)}, u32[]{:S(2)}) copy-start(s32[8]{0:T(128)} %rsector.1) | copy-start | bytes 100
  127.3 11.2 %all-to-all-start.3 = ((f32[16,16,256]{2,1,0:T(8,128)}), f32[16,16,256]{2,1,0:T(8,128)S(1)}, u32[]{:S(2)}, u32[]{:S(2)}) async-start(f32[16,16,256]{2,1,0:T(8,128)} %get-tuple-element.43), calls=%async_computation.3 | async-start | bytes 524288 | tf_op jit(solution)/shard_map/all_to_all | solution.py:500
  138.6 17.7 %collective-permute-start.11 = (f32[8,16,256]{2,1,0:T(8,128)S(1)}, f32[8,16,256]{2,1,0:T(8,128)S(1)}, u32[]{:S(2)}, u32[]{:S(2)}) collective-permute-start(f32[8,16,256]{2,1,0:T(8,128)S(1)} %constant_dynamic-slice_fusion), channel_id=1, source_target_pairs={{0,16},{16,0},{1,17},{17,1},{2,18},{18,2},{3,19},{19,3},{4,20},{20... | collective-permute-start | bytes 393224 | tf_op jit(solution)/shard_map/ppermute | solution.py:502
  (2 other events, 2.1 us)

commit v4 on v3

v4 whole, which is shorter than its diff:
```python
import jax
import jax.numpy as jnp
from jax import lax
from jax.experimental import pallas as pl
from jax.experimental.pallas import tpu as pltpu
from jax.sharding import Mesh, PartitionSpec as P

ITERS = 2
TILE = 256
HALF = 128
TERMS = 16
LEFT_ROWS = 136
SLOT_ROWS = 152
COL = ("x", "z")
ALL = ("y", "c", "x", "z")
SWAP = [(0, 1), (1, 0)]
UP = [(i, (i + 1) % 4) for i in range(4)]
DOWN = [(i, (i - 1) % 4) for i in range(4)]
f32 = jnp.float32
bf16 = jnp.bfloat16


def params(mib):
    return pltpu.CompilerParams(vmem_limit_bytes=mib * 1024 * 1024)


def hbm():
    return pl.BlockSpec(memory_space=pltpu.HBM)


def in_hbm(x):
    return pltpu.with_memory_space_constraint(x, pltpu.HBM)


def smem():
    return pl.BlockSpec(memory_space=pltpu.SMEM)


def cost(flops, nbytes):
    return pl.CostEstimate(flops=flops, transcendentals=0, bytes_accessed=nbytes)


def vmem():
    return pl.BlockSpec(memory_space=pltpu.VMEM)


def grids(rows, cols):
    i = lax.broadcasted_iota(jnp.int32, (rows, cols), 0)
    j = lax.broadcasted_iota(jnp.int32, (rows, cols), 1)
    return i, j


def fold_tile(tile):
    i, j = grids(HALF, HALF)
    a00 = tile[:HALF, :HALF]
    a11 = tile[HALF:, HALF:]
    fold = jnp.where(i >= j, a00, a11)
    diag = jnp.sum(jnp.where(i == j, a11, 0.0), axis=0, keepdims=True)
    return fold, tile[:HALF, HALF:], diag


def diag_rows(diag):
    wide = jnp.concatenate([diag, jnp.zeros((1, HALF), f32)], axis=1)
    return jnp.broadcast_to(wide, (8, TILE))


def unfold_tile(fold, corner, diag):
    i, j = grids(HALF, HALF)
    flip = fold.T
    a00 = jnp.where(i >= j, fold, flip)
    a11 = jnp.where(i == j, diag, jnp.where(i < j, fold, flip))
    top = jnp.concatenate([a00, corner], axis=1)
    low = jnp.concatenate([corner.T, a11], axis=1)
    return jnp.concatenate([top, low], axis=0)


def split(x):
    hi = x.astype(bf16)
    return hi, (x - hi.astype(f32)).astype(bf16)


def dot3(a_hi, a_lo, b_hi, b_lo):
    def dot(a, b):
        return jnp.dot(a, b, preferred_element_type=f32)

    return dot(a_hi, b_hi) + (dot(a_hi, b_lo) + dot(a_lo, b_hi))


def total(x):
    return jnp.sum(jnp.sum(x, axis=0, keepdims=True), axis=1, keepdims=True)


def inverse(norm):
    good = norm > 0.0
    return jnp.where(good, 1.0 / jnp.where(good, norm, 1.0), 0.0)


def put(stats, lane, value):
    _, j = grids(8, HALF)
    return jnp.where(j == lane, value, stats)


def put_folded(dst, at, row, tile):
    fold, corner, diag = fold_tile(tile)
    dst[at, row : row + HALF, :HALF] = fold
    dst[at, row : row + HALF, HALF:] = corner
    dst[at, row + HALF : row + HALF + 8, :] = diag_rows(diag)


def fold_left_body(ids, src, keep, give, tiles, folded, sem_in, sem_out):
    def fetch(t, n):
        term = ids[1] if t else 1 - ids[1]
        at = 4 * t + n
        return pltpu.make_async_copy(src.at[n, term], tiles.at[at], sem_in.at[at])

    def store(t, n):
        at = 4 * t + n
        dst = keep if t else give
        return pltpu.make_async_copy(folded.at[at], dst.at[n], sem_out.at[at])

    order = [(t, n) for t in range(2) for n in range(4)]
    for t, n in order:
        fetch(t, n).start()
    for t, n in order:
        fetch(t, n).wait()
        put_folded(folded, 4 * t + n, 0, tiles[4 * t + n])
        store(t, n).start()
    for t, n in order:
        store(t, n).wait()


def fold_left(ids, left_env):
    count = left_env.shape[0]
    return pl.pallas_call(
        fold_left_body,
        in_specs=[smem(), hbm()],
        out_specs=[hbm(), hbm()],
        out_shape=[pltpu.HBM((count, LEFT_ROWS, TILE), f32)] * 2,
        scratch_shapes=[
            pltpu.VMEM((2 * count, TILE, TILE), f32),
            pltpu.VMEM((2 * count, LEFT_ROWS, TILE), f32),
            pltpu.SemaphoreType.DMA((2 * count,)),
            pltpu.SemaphoreType.DMA((2 * count,)),
        ],
        compiler_params=params(8),
        cost_estimate=cost(1_000_000, 4_000_000),
        name="fold_left",
    )(ids, in_hbm(left_env))


def sector_of(ids, rsector, rsector_other, slot):
    return jnp.where(slot // 8 == ids[1], rsector[slot % 8], rsector_other[slot % 8])


def right_slots_body(
    ids, rsector, rsector_other, on, on_other, thin, thin_other, right_env,
    out, right, dst, sem_in, sem_out,
):
    def fetch(sector):
        return pltpu.make_async_copy(
            right_env.at[sector, ids[1]], right.at[sector], sem_in.at[sector]
        )

    def store(slot):
        return pltpu.make_async_copy(dst.at[slot], out.at[slot], sem_out.at[slot])

    for sector in range(8):
        fetch(sector).start()
    for slot in range(TERMS):
        here = slot // 8 == ids[1]
        dst[slot, :16, :] = jnp.where(here, thin[slot % 8], thin_other[slot % 8])
    for sector in range(8):
        fetch(sector).wait()

    def one(slot, carry):
        here = slot // 8 == ids[1]
        weight = jnp.where(here, on[slot % 8, ids[1]], on_other[slot % 8, ids[1]]).astype(f32)
        put_folded(dst, slot, 16, right[sector_of(ids, rsector, rsector_other, slot)] * weight)
        store(slot).start()
        return carry

    def finished(slot, carry):
        store(slot).wait()
        return carry

    lax.fori_loop(0, TERMS, one, 0)
    lax.fori_loop(0, TERMS, finished, 0)


def right_slots(ids, rsector, rsector_other, on, on_other, thin, thin_other, right_env):
    slots = (TERMS, SLOT_ROWS, TILE)
    return pl.pallas_call(
        right_slots_body,
        in_specs=[smem()] * 5 + [vmem()] * 2 + [hbm()],
        out_specs=hbm(),
        out_shape=pltpu.HBM(slots, f32),
        scratch_shapes=[
            pltpu.VMEM((8, TILE, TILE), f32),
            pltpu.VMEM(slots, f32),
            pltpu.SemaphoreType.DMA((8,)),
            pltpu.SemaphoreType.DMA((TERMS,)),
        ],
        compiler_params=params(10),
        cost_estimate=cost(4_000_000, 10_000_000),
        name="right_slots",
    )(ids, rsector, rsector_other, on, on_other, thin, thin_other, in_hbm(right_env))


def left_slots_body(ids, left_sector, kept, theirs, below, above, far_a, far_b, out, *scratch):
    dst, sem_in, sem_out = scratch

    def fetch(src, slot):
        return pltpu.make_async_copy(src, dst.at[slot], sem_in.at[slot])

    def store(slot):
        return pltpu.make_async_copy(dst.at[slot], out.at[slot], sem_out.at[slot])

    def start(slot, carry):
        sector = left_sector[ids[0] * 16 + slot]
        home = sector // 4
        tile = sector % 4
        away = (home // 2 - ids[0] + 4) % 4
        same = home % 2 == ids[1]
        cases = [
            (same, kept, (home // 2) * 4 + tile),
            (~same & (away == 0), theirs, tile),
            (~same & (away == 1), above, tile),
            (~same & (away == 2) & (tile < 2), far_a, tile),
            (~same & (away == 2) & (tile >= 2), far_b, tile - 2),
            (~same & (away == 3), below, tile),
        ]
        for case, src, at in cases:

            @pl.when(case)
            def _():
                fetch(src.at[at], slot).start()

        return carry

    def forward(slot, carry):
        fetch(kept.at[0], slot).wait()
        store(slot).start()
        return carry

    def finished(slot, carry):
        store(slot).wait()
        return carry

    lax.fori_loop(0, TERMS, start, 0)
    lax.fori_loop(0, TERMS, forward, 0)
    lax.fori_loop(0, TERMS, finished, 0)


def left_slots(ids, left_sector, pieces):
    slots = (TERMS, LEFT_ROWS, TILE)
    return pl.pallas_call(
        left_slots_body,
        in_specs=[smem(), smem()] + [hbm()] * 6,
        out_specs=hbm(),
        out_shape=pltpu.HBM(slots, f32),
        scratch_shapes=[
            pltpu.VMEM(slots, f32),
            pltpu.SemaphoreType.DMA((TERMS,)),
            pltpu.SemaphoreType.DMA((TERMS,)),
        ],
        compiler_params=params(6),
        cost_estimate=cost(0, 4_000_000),
        name="left_slots",
    )(ids, left_sector, *[in_hbm(x) for x in pieces])


def live_sizes(ids, rsector, rsector_other, left_sector, left_size, right_size):
    live_left = left_size[left_sector[ids[0] * 16 + ids[2]]]
    live_right = right_size[sector_of(ids, rsector, rsector_other, ids[2])]
    return live_right, live_left


def mask_of(live_right, live_left):
    i, j = grids(TILE, TILE)
    return (i < live_right) & (j < live_left)


def first_body(
    ids, rsector, rsector_other, sector, lsize, rsize, slots,
    r_hi, r_lo, m_hi, m_lo, q1, stats, arrived, sem,
):
    live_right, live_left = live_sizes(ids, rsector, rsector_other, sector, lsize, rsize)

    def fetch(n):
        return pltpu.make_async_copy(slots.at[n], arrived.at[n], sem.at[n])

    for n in range(TERMS):
        fetch(n).start()
    for n in range(TERMS):
        fetch(n).wait()
        full = unfold_tile(
            arrived[n, 16 : 16 + HALF, :HALF],
            arrived[n, 16 : 16 + HALF, HALF:],
            arrived[n, 16 + HALF : 17 + HALF, :HALF],
        )
        hi, lo = split(full)
        r_hi[n * TILE : (n + 1) * TILE, :] = hi
        r_lo[n * TILE : (n + 1) * TILE, :] = lo
    block = jnp.concatenate([arrived[n, :16, :] for n in range(TERMS)], axis=0)
    start = jnp.where(mask_of(live_right, live_left), block, 0.0)
    norm = jnp.sqrt(total(start * start))
    vec = start * inverse(norm)
    q1[...] = vec
    stats[...] = put(jnp.zeros((8, HALF), f32), 0, norm)
    q_hi, q_lo = split(vec)
    for n in range(TERMS):
        rows = pl.ds(n * TILE, TILE)
        hi, lo = split(dot3(r_hi[rows, :], r_lo[rows, :], q_hi, q_lo))
        m_hi[:, rows] = hi
        m_lo[:, rows] = lo


def first_vector(scalars, slots):
    return pl.pallas_call(
        first_body,
        in_specs=[smem()] * 6 + [hbm()],
        out_specs=[vmem()] * 6,
        out_shape=[
            jax.ShapeDtypeStruct((TERMS * TILE, TILE), bf16),
            jax.ShapeDtypeStruct((TERMS * TILE, TILE), bf16),
            jax.ShapeDtypeStruct((TILE, TERMS * TILE), bf16),
            jax.ShapeDtypeStruct((TILE, TERMS * TILE), bf16),
            jax.ShapeDtypeStruct((TILE, TILE), f32),
            jax.ShapeDtypeStruct((8, HALF), f32),
        ],
        scratch_shapes=[
            pltpu.VMEM((TERMS, SLOT_ROWS, TILE), f32),
            pltpu.SemaphoreType.DMA((TERMS,)),
        ],
        compiler_params=params(10),
        cost_estimate=cost(1_700_000_000, 12_000_000),
        name="first_vector",
    )(*scalars, in_hbm(slots))


def image_one_body(arrived, m_hi, m_lo, l_hi, l_lo, part, here, sem):
    chunk = TERMS // 4

    def fetch(p, c):
        cols = pl.ds(c * chunk * TILE, chunk * TILE)
        src = (m_hi, m_lo)[p]
        return pltpu.make_async_copy(src.at[:, cols], here.at[p, :, cols], sem.at[p, c])

    for c in range(4):
        for p in range(2):
            fetch(p, c).start()
    for n in range(TERMS):
        full = unfold_tile(
            arrived[n, :HALF, :HALF], arrived[n, :HALF, HALF:], arrived[n, HALF : HALF + 1, :HALF]
        )
        hi, lo = split(full)
        l_hi[n * TILE : (n + 1) * TILE, :] = hi
        l_lo[n * TILE : (n + 1) * TILE, :] = lo
    acc = jnp.zeros((TILE, TILE), f32)
    for c in range(4):
        for p in range(2):
            fetch(p, c).wait()
        cols = pl.ds(c * chunk * TILE, chunk * TILE)
        acc = acc + dot3(here[0, :, cols], here[1, :, cols], l_hi[cols, :], l_lo[cols, :])
    part[...] = acc


def image_one(arrived, m_hi, m_lo):
    return pl.pallas_call(
        image_one_body,
        in_specs=[vmem(), hbm(), hbm()],
        out_specs=[vmem()] * 3,
        out_shape=[
            jax.ShapeDtypeStruct((TERMS * TILE, TILE), bf16),
            jax.ShapeDtypeStruct((TERMS * TILE, TILE), bf16),
            jax.ShapeDtypeStruct((TILE, TILE), f32),
        ],
        scratch_shapes=[
            pltpu.VMEM((2, TILE, TERMS * TILE), bf16),
            pltpu.SemaphoreType.DMA((2, 4)),
        ],
        compiler_params=params(10),
        cost_estimate=cost(1_700_000_000, 10_000_000),
        name="image_one",
    )(arrived, in_hbm(m_hi), in_hbm(m_lo))


def lanczos(image, last, before, beta):
    alpha = total(last * image)
    rest = image - alpha * last
    if before is not None:
        rest = rest - beta * before
    again = rest - total(last * rest) * last
    if before is not None:
        again = again - total(before * rest) * before
    norm = jnp.sqrt(total(again * again))
    return alpha, norm, again * inverse(norm)


def half_image(vec, r_hi, r_lo, l_hi, l_lo):
    q_hi, q_lo = split(vec)
    acc = jnp.zeros((TILE, TILE), f32)
    for n in range(TERMS):
        rows = pl.ds(n * TILE, TILE)
        hi, lo = split(dot3(r_hi[rows, :], r_lo[rows, :], q_hi, q_lo))
        acc = acc + dot3(hi, lo, l_hi[rows, :], l_lo[rows, :])
    return acc


def image_two_body(
    ids, rsector, rsector_other, sector, lsize, rsize,
    part_a, part_b, q1, stats_in, r_hi, r_lo, l_hi, l_lo,
    part, q2, stats,
):
    mask = mask_of(*live_sizes(ids, rsector, rsector_other, sector, lsize, rsize))
    image = jnp.where(mask, part_a[...] + part_b[...], 0.0)
    alpha, norm, vec = lanczos(image, q1[...], None, None)
    q2[...] = vec
    stats[...] = put(put(stats_in[...], 1, alpha), 2, norm)
    part[...] = half_image(vec, r_hi, r_lo, l_hi, l_lo)


def image_two(scalars, part, part_other, q1, stats, stacks):
    return pl.pallas_call(
        image_two_body,
        in_specs=[smem()] * 6 + [vmem()] * 8,
        out_specs=[vmem()] * 3,
        out_shape=[
            jax.ShapeDtypeStruct((TILE, TILE), f32),
            jax.ShapeDtypeStruct((TILE, TILE), f32),
            jax.ShapeDtypeStruct((8, HALF), f32),
        ],
        compiler_params=params(6),
        cost_estimate=cost(3_300_000_000, 9_000_000),
        name="image_two",
    )(*scalars, part, part_other, q1, stats, *stacks)


def image_three_body(
    ids, rsector, rsector_other, sector, lsize, rsize,
    part_a, part_b, q1, q2, stats_in, r_hi, r_lo, l_hi, l_lo, slots,
):
    mask = mask_of(*live_sizes(ids, rsector, rsector_other, sector, lsize, rsize))
    image = jnp.where(mask, part_a[...] + part_b[...], 0.0)
    i, j = grids(8, HALF)
    beta = total(jnp.where((j == 2) & (i == 0), stats_in[...], 0.0))
    alpha, norm, vec = lanczos(image, q2[...], q1[...], beta)
    pick = jnp.where(ids[1] == 0, q2[...], vec)
    for n in range(16):
        slots[n, :16, :] = pick[16 * n : 16 * n + 16]
    stats = put(put(stats_in[...], 3, alpha), 4, norm)
    alpha = total(vec * half_image(vec, r_hi, r_lo, l_hi, l_lo))
    stats = put(stats, 5, alpha)
    wide = jnp.concatenate([stats, jnp.zeros((8, HALF), f32)], axis=1)
    for n in range(16):
        slots[n, 16:24, :] = wide


def image_three(scalars, part, part_other, q1, q2, stats, stacks):
    return pl.pallas_call(
        image_three_body,
        in_specs=[smem()] * 6 + [vmem()] * 9,
        out_specs=vmem(),
        out_shape=jax.ShapeDtypeStruct((16, 24, TILE), f32),
        compiler_params=params(6),
        cost_estimate=cost(3_300_000_000, 9_000_000),
        name="image_three",
    )(*scalars, part, part_other, q1, q2, stats, *stacks)


def ritz_pair(norm, a1, b1, a2, b2, a3):
    def apply(x):
        return [a1 * x[0] + b1 * x[1], b1 * x[0] + a2 * x[1] + b2 * x[2], b2 * x[1] + a3 * x[2]]

    def dot(x, y):
        return jnp.sum(x[0] * y[0] + x[1] * y[1] + x[2] * y[2], axis=1, keepdims=True)

    zero = jnp.zeros_like(norm)
    start = [norm, zero, zero]
    image = apply(start)
    norm_sq = dot(start, start)
    correlation = dot(start, image)
    inv_norm = 1.0 / jnp.sqrt(norm_sq)
    basis = [x * inv_norm for x in start]
    applied = [x * inv_norm for x in image]
    ritz = correlation / norm_sq
    for _ in range(ITERS):
        residual = [x - ritz * y for x, y in zip(applied, basis)]
        res_sq = dot(residual, residual)
        length = jnp.sqrt(res_sq)
        fresh = [x / length for x in residual]
        fresh_applied = apply(fresh)
        curvature = dot(fresh, fresh_applied)
        half_gap = 0.5 * (ritz - curvature)
        root = jnp.sqrt(half_gap * half_gap + res_sq)
        lowest = 0.5 * (ritz + curvature) - root
        first = curvature - lowest
        pair = jnp.sqrt(first * first + res_sq)
        basis = [(first * x - length * y) / pair for x, y in zip(basis, fresh)]
        applied = [(first * x - length * y) / pair for x, y in zip(applied, fresh_applied)]
        ritz = lowest
    return basis, ritz


def finish_body(
    ids, sector, rsector, lsize, rsize, own_stats, other_stats, thin, got, back,
    out, energy, coef,
):
    _, lane = grids(64, HALF)
    stats = own_stats[...] + jnp.where(lane == 5, other_stats[...], 0.0)
    flip = jnp.concatenate([stats, jnp.zeros((64, HALF), f32)], axis=0).T
    norm, a1, b1, a2, b2, a3 = [flip[m : m + 1, :] for m in range(6)]
    basis, ritz = ritz_pair(norm, a1, b1, a2, b2, a3)
    energy[0, 0] = jnp.sum(ritz)
    scale = jnp.sqrt(jnp.full((1, HALF), 64 * TILE * TILE, f32))
    i, _ = grids(HALF, HALF)
    c1 = basis[0] * inverse(norm) * scale
    c2 = basis[1] * scale
    c3 = basis[2] * scale
    coef[...] = jnp.where(i == 0, c1, jnp.where(i == 1, c2, jnp.where(i == 2, c3, 0.0))).T
    core = ids[1]
    own = coef[pl.ds(pl.multiple_of(core * 8, 8), 8), :]
    jcol, irow = grids(16, TILE)
    for b in range(8):
        live_left = lsize[sector[ids[0] * 16 + core * 8 + b]]
        live_right = rsize[rsector[b]]
        live = (jcol + ids[2] * 16 < live_right) & (irow < live_left)
        keep = got[core * 8 + b, :16, :]
        recv = back[b, :16, :]
        second = jnp.where(core == 0, keep, recv)
        third = jnp.where(core == 0, recv, keep)
        out[b] = (
            own[b : b + 1, 0:1] * jnp.where(live, thin[b], 0.0)
            + own[b : b + 1, 1:2] * second
            + own[b : b + 1, 2:3] * third
        )


def finish(ids, sector, rsector, lsize, rsize, own_stats, other_stats, thin, got, back):
    return pl.pallas_call(
        finish_body,
        in_specs=[smem()] * 5 + [vmem()] * 5,
        out_specs=[vmem(), smem()],
        out_shape=[
            jax.ShapeDtypeStruct(thin.shape, f32),
            jax.ShapeDtypeStruct((1, 1), f32),
        ],
        scratch_shapes=[pltpu.VMEM((HALF, HALF), f32)],
        compiler_params=params(4),
        name="finish",
    )(ids, sector, rsector, lsize, rsize, own_stats, other_stats, thin, got, back)


def local(theta, left_env, right_env, left_sector, right_sector, term_on, left_size, right_size):
    plane = lax.axis_index("y").astype(jnp.int32)
    core = lax.axis_index("c").astype(jnp.int32)
    place = lax.axis_index(COL).astype(jnp.int32)
    ids = jnp.stack([plane, core, place])
    thin = jnp.swapaxes(theta, 1, 2)

    mine, folded = fold_left(ids, left_env)
    kept = lax.all_gather(mine, "y", axis=0, tiled=True)
    theirs = lax.ppermute(folded, "c", SWAP)
    below = lax.ppermute(theirs, "y", UP)
    above = lax.ppermute(theirs, "y", DOWN)
    far_a = lax.ppermute(below[:2], "y", UP)
    far_b = lax.ppermute(above[2:], "y", DOWN)

    rsector_other = lax.ppermute(right_sector, "c", SWAP)
    on_other = lax.ppermute(term_on, "c", SWAP)
    thin_other = lax.ppermute(thin, "c", SWAP)
    thin_late, _ = lax.optimization_barrier((thin, mine))
    slots = right_slots(
        ids, right_sector, rsector_other, term_on, on_other, thin_late, thin_other, right_env
    )
    arrived = lax.all_to_all(slots, COL, 0, 0, tiled=True)
    scalars = (ids, right_sector, rsector_other, left_sector, left_size, right_size)
    r_hi, r_lo, m_hi, m_lo, q1, stats = first_vector(scalars, arrived)

    pieces = [kept, theirs, below, above, far_a, far_b]
    left_arrived = lax.all_to_all(left_slots(ids, left_sector, pieces), COL, 0, 0, tiled=True)
    l_hi, l_lo, part = image_one(left_arrived, m_hi, m_lo)
    stacks = (r_hi, r_lo, l_hi, l_lo)
    part, q2, stats = image_two(scalars, part, lax.ppermute(part, "c", SWAP), q1, stats, stacks)
    sent = image_three(scalars, part, lax.ppermute(part, "c", SWAP), q1, q2, stats, stacks)

    got = lax.all_to_all(sent, COL, 0, 0, tiled=True)
    plane_stats = got[:, 16, :HALF]
    turned = [
        lax.ppermute(plane_stats, "y", [(i, (i + k) % 4) for i in range(4)]) for k in (1, 2, 3)
    ]
    back = lax.ppermute(lax.dynamic_slice_in_dim(got, (1 - core) * 8, 8), "c", SWAP)
    own_stats = jnp.concatenate([plane_stats] + turned)
    other_stats = lax.ppermute(own_stats, "c", SWAP)
    out, energy = finish(
        ids, left_sector, right_sector, left_size, right_size,
        own_stats, other_stats, thin, got, back,
    )
    return jnp.swapaxes(out, 1, 2), energy[0, 0]


def solution(mesh):
    fine = Mesh(mesh.devices.reshape(4, 2, 4, 4), ALL)
    row = ("y", "c")
    placed = (
        P(row, None, COL),
        P(row, COL, None, None),
        P(None, COL, None, None),
        P(),
        P(row),
        P(row, COL),
        P(),
        P(),
    )
    return jax.shard_map(
        local, mesh=fine, in_specs=placed, out_specs=(P(row, None, COL), P()), check_vma=False
    )
```

time: 160 us -> 161 us (level)
  blocking collectives: 15.7 us -> 0 us
  between operations: 0.82 us -> 14.3 us
  waiting for transfers between devices: 56.4 us -> 66.9 us
  local copies, waits for them, and re-layouts: 18.4 us -> 7.94 us
  Pallas kernels: 29.2 us -> 33 us
    all_to_all x1 -> x0, blocking collectives: 15.7 us -> none  [local(): stats = lax.all_to_all(stats, ALL, 0, 0, tiled=True)]
    unnamed x38 -> x37, local copies, waits for them, and re-layouts: 17.7 us -> 7.89 us
    ppermute x8 -> x11, waiting for transfers between devices: 30.6 us -> 37.6 us  [the longest x1 23.9 us: local(): above = lax.ppermute(theirs, 'y', DOWN)]
    pallas_call x9 -> x8, Pallas kernels: 29.2 us -> 33 us  [the longest x1 5.66 us: image_three(): pl.pallas_call(image_three_body, in_specs=[smem()] * 6 + [vmem()] * 9, ou...]
    all_to_all x1, waiting for transfers between devices: 7.55 us -> 9.24 us  [local(): got = lax.all_to_all(sent, COL, 0, 0, tiled=True)]
    ppermute x8 -> x11, starting transfers between devices: 10.9 us -> 11.4 us  [the longest x1 3.59 us: local(): far_b = lax.ppermute(above[2:], 'y', DOWN)]
  transfers between devices with their start and end apart: 15 -> 19, of which waited for: 10 -> 14; matrix products, arithmetic and copies ran while one was open for 1% -> 0% of each run, Pallas kernels for 4% -> 8%
where the time goes in v4:
time: 161 us; the launch traced here: 160 us
  waiting for transfers between devices  66.9 us (42%)
  starting transfers between devices  38.2 us (24%)
  Pallas kernels  33 us (20%)
  between operations  14.3 us (9%)
  local copies, waits for them, and re-layouts  7.94 us (5%)
    ppermute x1, waiting for transfers between devices, local(): above = lax.ppermute(theirs, 'y', DOWN)  23.9 us
    all_to_all x1, waiting for transfers between devices, local(): lax.all_to_all(left_slots(ids, left_sector, pieces), COL, 0, 0, tiled=True)  16.1 us
    all_to_all x1, waiting for transfers between devices, local(): got = lax.all_to_all(sent, COL, 0, 0, tiled=True)  9.24 us
    unnamed x37, local copies, waits for them, and re-layouts  7.89 us
    all_to_all x1, starting transfers between devices, local(): arrived = lax.all_to_all(slots, COL, 0, 0, tiled=True)  7.82 us
    all_to_all x1, starting transfers between devices, local(): lax.all_to_all(left_slots(ids, left_sector, pieces), COL, 0, 0, tiled=True)  7.11 us
    ppermute x2, starting transfers between devices, local(): lax.ppermute(part, 'c', SWAP)  6.04 us
    pallas_call x1, Pallas kernels, image_three(): pl.pallas_call(image_three_body, in_specs=[smem()] * 6 + [vmem()] * 9, ou...  5.66 us
  transfers between devices with their start and end apart: 19, of which 14 were waited for; matrix products, arithmetic and copies ran while one was open for 0% of the time, Pallas kernels for 8%

profile of v4, /device:TPU:1, one launch (start us, length us, event | category | flops | bytes accessed | tf_op | source)
XLA Modules:
  0.0 160.4 jit_solution(9312918292981920014)
XLA Ops:
  7.3 2.9 %fold_left.1 = (f32[4,136,256]{2,1,0:T(8,128)}, f32[4,136,256]{2,1,0:T(8,128)}) custom-call(s32[3]{0:T(128)S(1)} %pad_add_fusion.ids, f32[4,2,256,256]{3,2,1,0:T(8,128)} %src.1), custom_call_target="tpu_custom_call" | custom-call | flops 1000000 | bytes 4000000 | tf_op jit(solution)/shard_map/fold_left/pallas_call | solution.py:134
  10.2 1.5 collective-permute-start.7
  13.2 3.9 %right_slots.1 = f32[16,152,256]{2,1,0:T(8,128)} custom-call(s32[3]{0:T(128)S(1)} %pad_add_fusion.ids, s32[8]{0:T(128)S(1)} %copy-done.4, s32[8]{0:T(128)S(1)} %collective-permute-done.rsector_other, s32[8,2]{1,0:T(8,128)S(1)} %copy.13.on, s32[8,2]{1,0:T(8,128)S(1)} %collective-permute-done.6.on_other, f32[8,16,256]{2,1,0:T(8,128)S(1)} %bitcast.8, ...), custom_call_target="tpu_custom_call" | custom-call | flops 4000000 | bytes 10000000 | tf_op jit(solution)/shard_map/right_slots/pallas_call | solution.py:192
  17.1 7.8 %all-to-all-start.1 = ((f32[16,152,256]{2,1,0:T(8,128)}), f32[16,152,256]{2,1,0:T(8,128)S(1)}, u32[]{:S(2)}, u32[]{:S(2)}) async-start(f32[16,152,256]{2,1,0:T(8,128)} %right_slots.1), calls=%async_computation.1 | async-start | bytes 4980736 | tf_op jit(solution)/shard_map/all_to_all | solution.py:576
  25.6 1.6 collective-permute-done.1.theirs
  27.2 2.7 %collective-permute-start.3 = (f32[4,136,256]{2,1,0:T(8,128)S(1)}, f32[4,136,256]{2,1,0:T(8,128)S(1)}, u32[]{:S(2)}, u32[]{:S(2)}) collective-permute-start(f32[4,136,256]{2,1,0:T(8,128)S(1)} %collective-permute-done.1.theirs), channel_id=1, source_target_pairs={{0,96},{32,0},{64,32},{96,64},{1,97},{33,1},{65,33},{97,65},{2,98}... | collective-permute-start | bytes 1671176 | tf_op jit(solution)/shard_map/ppermute | solution.py:565
  29.9 23.9 %collective-permute-done.3.above = f32[4,136,256]{2,1,0:T(8,128)S(1)} collective-permute-done((f32[4,136,256]{2,1,0:T(8,128)S(1)}, f32[4,136,256]{2,1,0:T(8,128)S(1)}, u32[]{:S(2)}, u32[]{:S(2)}) %collective-permute-start.3) | collective-permute-done | bytes 557088 | tf_op jit(solution)/shard_map/ppermute | solution.py:565
  53.8 3.6 %collective-permute-start.5 = (f32[2,136,256]{2,1,0:T(8,128)S(1)}, f32[2,136,256]{2,1,0:T(8,128)S(1)}, u32[]{:S(2)}, u32[]{:S(2)}) collective-permute-start(f32[2,136,256]{2,1,0:T(8,128)S(1)} %slice.13), channel_id=1, source_target_pairs={{0,96},{32,0},{64,32},{96,64},{1,97},{33,1},{65,33},{97,65},{2,98}... | collective-permute-start | bytes 835592 | tf_op jit(solution)/shard_map/ppermute | solution.py:567
  58.4 4.3 %collective-permute-done.5.far_b = f32[2,136,256]{2,1,0:T(8,128)S(1)} collective-permute-done((f32[2,136,256]{2,1,0:T(8,128)S(1)}, f32[2,136,256]{2,1,0:T(8,128)S(1)}, u32[]{:S(2)}, u32[]{:S(2)}) %collective-permute-start.5) | collective-permute-done | bytes 278560 | tf_op jit(solution)/shard_map/ppermute | solution.py:567
  62.7 4.2 %collective-permute-done.4.far_a = f32[2,136,256]{2,1,0:T(8,128)} collective-permute-done((f32[2,136,256]{2,1,0:T(8,128)S(1)}, f32[2,136,256]{2,1,0:T(8,128)}, u32[]{:S(2)}, u32[]{:S(2)}) %collective-permute-start.4) | collective-permute-done | bytes 278560 | tf_op jit(solution)/shard_map/ppermute | solution.py:566
  66.9 3.3 %left_slots.1 = f32[16,136,256]{2,1,0:T(8,128)} custom-call(s32[3]{0:T(128)S(1)} %pad_add_fusion.ids, s32[64]{0:T(128)S(1)} %copy-done.3, f32[16,136,256]{2,1,0:T(8,128)} %all-gather.2.cloned.1.call-done.kept, f32[4,136,256]{2,1,0:T(8,128)} %copy-done.14, f32[4,136,256]{2,1,0:T(8,128)} %copy-done.13, f32[4,136,256]{2,1,0:T(8,128)} %copy-done.12, ...), custom_call_target="tpu_custom_call" | custom-call | bytes 4000000 | tf_op jit(solution)/shard_map/left_slots/pallas_call | solution.py:256
  70.2 1.4 copy-done.11
  71.6 7.1 %all-to-all-start = ((f32[16,136,256]{2,1,0:T(8,128)}), f32[16,136,256]{2,1,0:T(8,128)S(1)}, u32[]{:S(2)}, u32[]{:S(2)}) async-start(f32[16,136,256]{2,1,0:T(8,128)} %left_slots.1), calls=%async_computation | async-start | bytes 4456448 | tf_op jit(solution)/shard_map/all_to_all | solution.py:581
  78.8 5.3 %first_vector.1 = (bf16[4096,256]{1,0:T(8,128)(2,1)S(1)}, bf16[4096,256]{1,0:T(8,128)(2,1)S(1)}, bf16[256,4096]{1,0:T(8,128)(2,1)S(1)}, bf16[256,4096]{1,0:T(8,1...) custom-call(s32[3]{0:T(128)S(1)} %pad_add_fusion.ids, s32[8]{0:T(128)S(1)} %copy-done.4, ...), custom_call_target="tpu_custom_call" | custom-call | flops 1700000000 | bytes 12000000 | tf_op jit(solution)/shard_map/first_vector/pallas_call | solution.py:319
  84.1 1.3 copy-done
  85.4 1.4 copy-done.1
  86.8 1.4 copy-done.7
  88.2 1.3 copy-done.9
  89.5 16.1 %all-to-all-done.arrived = f32[16,136,256]{2,1,0:T(8,128)S(1)} async-done(((f32[16,136,256]{2,1,0:T(8,128)}), f32[16,136,256]{2,1,0:T(8,128)S(1)}, u32[]{:S(2)}, u32[]{:S(2)}) %all-to-all-start) | async-done | bytes 2228256 | tf_op jit(solution)/shard_map/all_to_all | solution.py:581
  105.6 5.1 %image_one.1 = (bf16[4096,256]{1,0:T(8,128)(2,1)S(1)}, bf16[4096,256]{1,0:T(8,128)(2,1)S(1)}, f32[256,256]{1,0:T(8,128)S(1)}) custom-call(f32[16,136,256]{2,1,0:T(8,128)S(1)} %all-to-all-done.arrived, bf16[256,4096]{1,0:T(8,128)(2,1)} %copy-done, bf16[256,4096]{1,0:T(8,128)(2,1)} %copy-done.1), custom_call_target="tpu_custom_call" | custom-call | flops 1700000000 | bytes 10000000 | tf_op jit(solution)/shard_map/image_one/pallas_call | solution.py:369
  110.7 5.6 %collective-permute-start.8 = (f32[256,256]{1,0:T(8,128)S(1)}, f32[256,256]{1,0:T(8,128)S(1)}, u32[]{:S(2)}, u32[]{:S(2)}) collective-permute-start(f32[256,256]{1,0:T(8,128)S(1)} %get-tuple-element.24.part_a), channel_id=1, source_target_pairs={{0,16},{16,0},{1,17},{17,1},{2,18},{18,2},{3,19},{19,3},{4,20},{20... | collective-permute-start | bytes 786440 | tf_op jit(solution)/shard_map/ppermute | solution.py:584
  116.3 1.2 collective-permute-done.8.part_b
  117.4 4.7 %image_two.1 = (f32[256,256]{1,0:T(8,128)S(1)}, f32[256,256]{1,0:T(8,128)S(1)}, f32[8,128]{1,0:T(8,128)S(1)}) custom-call(s32[3]{0:T(128)S(1)} %pad_add_fusion.ids, s32[8]{0:T(128)S(1)} %copy-done.4, s32[8]{0:T(128)S(1)} %collective-permute-done.rsector_other, s32[64]{0:T(128)S(1)} %copy-done.3, s32[32]{0:T(128)S(1)} %copy-done.5, s32[8]{0:T(128)S(1)} %copy-done.6, ...), custom_call_target="tpu_custom_call" | custom-call | flops 3300000000 | bytes 9000000 | tf_op jit(solution)/shard_map/image_two/pallas_call | solution.py:424
  122.6 1.2 collective-permute-done.9.part_b
  123.8 5.7 %image_three.1 = f32[16,24,256]{2,1,0:T(8,128)} custom-call(s32[3]{0:T(128)S(1)} %pad_add_fusion.ids, s32[8]{0:T(128)S(1)} %copy-done.4, s32[8]{0:T(128)S(1)} %collective-permute-done.rsector_other, s32[64]{0:T(128)S(1)} %copy-done.3, s32[32]{0:T(128)S(1)} %copy-done.5, s32[8]{0:T(128)S(1)} %copy-done.6, f32[256,256]{1,0:T(8,128)S(1)} %get-tuple-element.31.part_a, ...), custom_call_target="tpu_custom_call" | custom-call | flops 3300000000 | bytes 9000000 | tf_op jit(solution)/shard_map/image_three/pallas_call | solution.py:460
  129.4 3.6 %all-to-all-start.2 = ((f32[16,24,256]{2,1,0:T(8,128)}), f32[16,24,256]{2,1,0:T(8,128)S(1)}, u32[]{:S(2)}, u32[]{:S(2)}) async-start(f32[16,24,256]{2,1,0:T(8,128)} %image_three.1), calls=%async_computation.2 | async-start | bytes 786432 | tf_op jit(solution)/shard_map/all_to_all | solution.py:587
  133.1 9.2 %all-to-all-done.2.got = f32[16,24,256]{2,1,0:T(8,128)S(1)} async-done(((f32[16,24,256]{2,1,0:T(8,128)}), f32[16,24,256]{2,1,0:T(8,128)S(1)}, u32[]{:S(2)}, u32[]{:S(2)}) %all-to-all-start.2) | async-done | bytes 393248 | tf_op jit(solution)/shard_map/all_to_all | solution.py:587
  142.3 1.6 %collective-permute-start.14 = (f32[8,24,256]{2,1,0:T(8,128)S(1)}, f32[8,24,256]{2,1,0:T(8,128)S(1)}, u32[]{:S(2)}, u32[]{:S(2)}) collective-permute-start(f32[8,24,256]{2,1,0:T(8,128)S(1)} %constant_dynamic-slice_fusion), channel_id=1, source_target_pairs={{0,16},{16,0},{1,17},{17,1},{2,18},{18,2},{3,19},{19,3},{4,20},{20... | collective-permute-start | bytes 589832 | tf_op jit(solution)/shard_map/ppermute | solution.py:592
  146.4 1.6 collective-permute-done.11
  148.0 1.0 collective-permute-done.10
  149.1 1.4 collective-permute-start.13
  151.3 2.2 %finish.1 = (f32[8,16,256]{2,1,0:T(8,128)}, f32[1,1]{1,0:T(1,128)}) custom-call(s32[3]{0:T(128)S(1)} %pad_add_fusion.ids, s32[64]{0:T(128)S(1)} %copy-done.3, s32[8]{0:T(128)S(1)} %copy-done.4, s32[32]{0:T(128)S(1)} %copy-done.5, s32[8]{0:T(128)S(1)} %copy-done.6, f32[64,128]{1,0:T(8,128)S(1)} %pad_maximum_fusion.own_stats, ...), custom_call_target="tpu_custom_call" | custom-call | tf_op jit(solution)/shard_map/finish/pallas_call | solution.py:540
  (58 shorter events, 7.2 us)
Async XLA Ops:
  7.2 3.1 %copy-start.2 = (f32[8,256,16]{1,2,0:T(8,128)S(1)}, f32[8,256,16]{1,2,0:T(8,128)}, u32[]{:S(2)}) copy-start(f32[8,256,16]{1,2,0:T(8,128)} %param.8) | copy-start | bytes 393220
  7.2 4.6 %copy-start.4 = (s32[8]{0:T(128)S(1)}, s32[8]{0:T(128)}, u32[]{:S(2)}) copy-start(s32[8]{0:T(128)} %rsector.9) | copy-start | bytes 100
  7.2 4.7 %copy-start.16 = (s32[8,2]{0,1:T(2,128)S(1)}, s32[8,2]{0,1:T(2,128)}, u32[]{:S(2)}) copy-start(s32[8,2]{0,1:T(2,128)} %param.13) | copy-start | bytes 196
  7.2 59.7 %all-gather.2.cloned.1.call-start = ((), (), s32[]{:S(2)}) async-start(), calls=%async_computation.3 | async-start | bytes 2785280 | tf_op jit(solution)/shard_map/all_gather | solution.py:562
  10.2 2.9 %collective-permute-start.7 = (f32[8,16,256]{2,1,0:T(8,128)S(1)}, f32[8,16,256]{2,1,0:T(8,128)S(1)}, u32[]{:S(2)}, u32[]{:S(2)}) collective-permute-start(f32[8,16,256]{2,1,0:T(8,128)S(1)} %bitcast.7), channel_id=1, source_target_pairs={{0,16},{16,0},{1,17},{17,1},{2,18},{18,2},{3,19},{19,3},{4,20},{20... | collective-permute-start | bytes 393224 | tf_op jit(solution)/shard_map/ppermute | solution.py:571
  11.7 1.1 collective-permute-start
  11.9 1.2 collective-permute-start.6
  17.1 7.9 %copy-start.17 = (f32[4,136,256]{2,1,0:T(8,128)S(1)}, f32[4,136,256]{2,1,0:T(8,128)}, u32[]{:S(2)}) copy-start(f32[4,136,256]{2,1,0:T(8,128)} %get-tuple-element.20) | copy-start | bytes 1671172
  17.1 49.8 %copy-start.3 = (s32[64]{0:T(128)S(1)}, s32[64]{0:T(128)}, u32[]{:S(2)}) copy-start(s32[64]{0:T(128)} %sector.7) | copy-start | bytes 772
  17.1 53.1 %all-to-all-start.1 = ((f32[16,152,256]{2,1,0:T(8,128)}), f32[16,152,256]{2,1,0:T(8,128)S(1)}, u32[]{:S(2)}, u32[]{:S(2)}) async-start(f32[16,152,256]{2,1,0:T(8,128)} %right_slots.1), calls=%async_computation.1 | async-start | bytes 4980736 | tf_op jit(solution)/shard_map/all_to_all | solution.py:576
  24.9 2.3 %collective-permute-start.1 = (f32[4,136,256]{2,1,0:T(8,128)S(1)}, f32[4,136,256]{2,1,0:T(8,128)S(1)}, u32[]{:S(2)}, u32[]{:S(2)}) collective-permute-start(f32[4,136,256]{2,1,0:T(8,128)S(1)} %copy-done.17), channel_id=1, source_target_pairs={{0,16},{16,0},{1,17},{17,1},{2,18},{18,2},{3,19},{19,3},{4,20},{20... | collective-permute-start | bytes 1671176 | tf_op jit(solution)/shard_map/ppermute | solution.py:563
  27.2 31.1 %copy-start.14 = (f32[4,136,256]{2,1,0:T(8,128)}, f32[4,136,256]{2,1,0:T(8,128)S(1)}, u32[]{:S(2)}) copy-start(f32[4,136,256]{2,1,0:T(8,128)S(1)} %collective-permute-done.1.theirs) | copy-start | bytes 1671172
  27.2 26.6 %collective-permute-start.3 = (f32[4,136,256]{2,1,0:T(8,128)S(1)}, f32[4,136,256]{2,1,0:T(8,128)S(1)}, u32[]{:S(2)}, u32[]{:S(2)}) collective-permute-start(f32[4,136,256]{2,1,0:T(8,128)S(1)} %collective-permute-done.1.theirs), channel_id=1, source_target_pairs={{0,96},{32,0},{64,32},{96,64},{1,97},{33,1},{65,33},{97,65},{2,98}... | collective-permute-start | bytes 1671176 | tf_op jit(solution)/shard_map/ppermute | solution.py:565
  29.9 27.5 %collective-permute-start.2 = (f32[4,136,256]{2,1,0:T(8,128)S(1)}, f32[4,136,256]{2,1,0:T(8,128)S(1)}, u32[]{:S(2)}, u32[]{:S(2)}) collective-permute-start(f32[4,136,256]{2,1,0:T(8,128)S(1)} %collective-permute-done.1.theirs), channel_id=1, source_target_pairs={{0,32},{32,64},{64,96},{96,0},{1,33},{33,65},{65,97},{97,1},{2,34}... | collective-permute-start | bytes 1671176 | tf_op jit(solution)/shard_map/ppermute | solution.py:564
  53.8 13.1 %copy-start.12 = (f32[4,136,256]{2,1,0:T(8,128)}, f32[4,136,256]{2,1,0:T(8,128)S(1)}, u32[]{:S(2)}) copy-start(f32[4,136,256]{2,1,0:T(8,128)S(1)} %collective-permute-done.3.above) | copy-start | bytes 1671172
  53.8 8.9 %collective-permute-start.5 = (f32[2,136,256]{2,1,0:T(8,128)S(1)}, f32[2,136,256]{2,1,0:T(8,128)S(1)}, u32[]{:S(2)}, u32[]{:S(2)}) collective-permute-start(f32[2,136,256]{2,1,0:T(8,128)S(1)} %slice.13), channel_id=1, source_target_pairs={{0,96},{32,0},{64,32},{96,64},{1,97},{33,1},{65,33},{97,65},{2,98}... | collective-permute-start | bytes 835592 | tf_op jit(solution)/shard_map/ppermute | solution.py:567
  58.3 8.5 %collective-permute-start.4 = (f32[2,136,256]{2,1,0:T(8,128)S(1)}, f32[2,136,256]{2,1,0:T(8,128)}, u32[]{:S(2)}, u32[]{:S(2)}) collective-permute-start(f32[2,136,256]{2,1,0:T(8,128)S(1)} %slice.12), channel_id=1, source_target_pairs={{0,32},{32,64},{64,96},{96,0},{1,33},{33,65},{65,97},{97,1},{2,34}... | collective-permute-start | bytes 835592 | tf_op jit(solution)/shard_map/ppermute | solution.py:566
  62.7 4.2 %copy-start.15 = (f32[2,136,256]{2,1,0:T(8,128)}, f32[2,136,256]{2,1,0:T(8,128)S(1)}, u32[]{:S(2)}) copy-start(f32[2,136,256]{2,1,0:T(8,128)S(1)} %collective-permute-done.5.far_b) | copy-start | bytes 835588
  70.1 8.6 %copy-start.5 = (s32[32]{0:T(128)S(1)}, s32[32]{0:T(128)}, u32[]{:S(2)}) copy-start(s32[32]{0:T(128)} %lsize.7) | copy-start | bytes 388
  70.2 8.6 %copy-start.6 = (s32[8]{0:T(128)S(1)}, s32[8]{0:T(128)}, u32[]{:S(2)}) copy-start(s32[8]{0:T(128)} %rsize.7) | copy-start | bytes 100
  70.2 1.5 copy-start.11
  71.6 34.0 %all-to-all-start = ((f32[16,136,256]{2,1,0:T(8,128)}), f32[16,136,256]{2,1,0:T(8,128)S(1)}, u32[]{:S(2)}, u32[]{:S(2)}) async-start(f32[16,136,256]{2,1,0:T(8,128)} %left_slots.1), calls=%async_computation | async-start | bytes 4456448 | tf_op jit(solution)/shard_map/all_to_all | solution.py:581
  105.6 11.8 %copy-start.8 = (bf16[4096,256]{1,0:T(8,128)(2,1)S(1)}, bf16[4096,256]{1,0:T(8,128)(2,1)}, u32[]{:S(2)}) copy-start(bf16[4096,256]{1,0:T(8,128)(2,1)} %copy-done.7) | copy-start | bytes 6291460
  105.6 11.8 %copy-start.10 = (bf16[4096,256]{1,0:T(8,128)(2,1)S(1)}, bf16[4096,256]{1,0:T(8,128)(2,1)}, u32[]{:S(2)}) copy-start(bf16[4096,256]{1,0:T(8,128)(2,1)} %copy-done.9) | copy-start | bytes 6291460
  110.7 6.8 %collective-permute-start.8 = (f32[256,256]{1,0:T(8,128)S(1)}, f32[256,256]{1,0:T(8,128)S(1)}, u32[]{:S(2)}, u32[]{:S(2)}) collective-permute-start(f32[256,256]{1,0:T(8,128)S(1)} %get-tuple-element.24.part_a), channel_id=1, source_target_pairs={{0,16},{16,0},{1,17},{17,1},{2,18},{18,2},{3,19},{19,3},{4,20},{20... | collective-permute-start | bytes 786440 | tf_op jit(solution)/shard_map/ppermute | solution.py:584
  122.1 1.6 %collective-permute-start.9 = (f32[256,256]{1,0:T(8,128)S(1)}, f32[256,256]{1,0:T(8,128)S(1)}, u32[]{:S(2)}, u32[]{:S(2)}) collective-permute-start(f32[256,256]{1,0:T(8,128)S(1)} %get-tuple-element.31.part_a), channel_id=1, source_target_pairs={{0,16},{16,0},{1,17},{17,1},{2,18},{18,2},{3,19},{19,3},{4,20},{20... | collective-permute-start | bytes 786440 | tf_op jit(solution)/shard_map/ppermute | solution.py:585
  129.4 12.9 %all-to-all-start.2 = ((f32[16,24,256]{2,1,0:T(8,128)}), f32[16,24,256]{2,1,0:T(8,128)S(1)}, u32[]{:S(2)}, u32[]{:S(2)}) async-start(f32[16,24,256]{2,1,0:T(8,128)} %image_three.1), calls=%async_computation.2 | async-start | bytes 786432 | tf_op jit(solution)/shard_map/all_to_all | solution.py:587
  142.3 9.0 %collective-permute-start.14 = (f32[8,24,256]{2,1,0:T(8,128)S(1)}, f32[8,24,256]{2,1,0:T(8,128)S(1)}, u32[]{:S(2)}, u32[]{:S(2)}) collective-permute-start(f32[8,24,256]{2,1,0:T(8,128)S(1)} %constant_dynamic-slice_fusion), channel_id=1, source_target_pairs={{0,16},{16,0},{1,17},{17,1},{2,18},{18,2},{3,19},{19,3},{4,20},{20... | collective-permute-start | bytes 589832 | tf_op jit(solution)/shard_map/ppermute | solution.py:592
  143.9 2.5 %collective-permute-start.12 = (f32[16,128]{1,0:T(8,128)S(1)}, f32[16,128]{1,0:T(8,128)S(1)}, u32[]{:S(2)}, u32[]{:S(2)}) collective-permute-start(f32[16,128]{1,0:T(8,128)S(1)} %bitcast.10), channel_id=1, source_target_pairs={{0,96},{32,0},{64,32},{96,64},{1,97},{33,1},{65,33},{97,65},{2,98}... | collective-permute-start | bytes 24584 | tf_op jit(solution)/shard_map/ppermute | solution.py:590
  143.9 4.1 %collective-permute-start.11 = (f32[16,128]{1,0:T(8,128)S(1)}, f32[16,128]{1,0:T(8,128)S(1)}, u32[]{:S(2)}, u32[]{:S(2)}) collective-permute-start(f32[16,128]{1,0:T(8,128)S(1)} %bitcast.11), channel_id=1, source_target_pairs={{0,64},{32,96},{64,0},{96,32},{1,65},{33,97},{65,1},{97,33},{2,66}... | collective-permute-start | bytes 24584 | tf_op jit(solution)/shard_map/ppermute | solution.py:590
  144.9 4.1 %collective-permute-start.10 = (f32[16,128]{1,0:T(8,128)S(1)}, f32[16,128]{1,0:T(8,128)S(1)}, u32[]{:S(2)}, u32[]{:S(2)}) collective-permute-start(f32[16,128]{1,0:T(8,128)S(1)} %bitcast.12), channel_id=1, source_target_pairs={{0,32},{32,64},{64,96},{96,0},{1,33},{33,65},{65,97},{97,1},{2,34}... | collective-permute-start | bytes 24584 | tf_op jit(solution)/shard_map/ppermute | solution.py:590
  149.1 2.2 %collective-permute-start.13 = (f32[64,128]{1,0:T(8,128)S(1)}, f32[64,128]{1,0:T(8,128)S(1)}, u32[]{:S(2)}, u32[]{:S(2)}) collective-permute-start(f32[64,128]{1,0:T(8,128)S(1)} %pad_maximum_fusion.own_stats), channel_id=1, source_target_pairs={{0,16},{16,0},{1,17},{17,1},{2,18},{18,2},{3,19},{19,3},{4,20},{20... | collective-permute-start | bytes 98312 | tf_op jit(solution)/shard_map/ppermute | solution.py:594
  (5 other events, 6.3 us)
Sparse Core Ops, SparseCore 0:
  10.3 46.1 all-gather.1

commit v5 on v4

--- a/solution.py
+++ b/solution.py
@@ -11,6 +11,7 @@
 TERMS = 16
 LEFT_ROWS = 136
 SLOT_ROWS = 152
+LEFT_BYTES = 4_000_000
 COL = ("x", "z")
 ALL = ("y", "c", "x", "z")
 SWAP = [(0, 1), (1, 0)]
@@ -107,45 +108,39 @@
     dst[at, row + HALF : row + HALF + 8, :] = diag_rows(diag)
 
 
-def fold_left_body(ids, src, keep, give, tiles, folded, sem_in, sem_out):
-    def fetch(t, n):
-        term = ids[1] if t else 1 - ids[1]
-        at = 4 * t + n
-        return pltpu.make_async_copy(src.at[n, term], tiles.at[at], sem_in.at[at])
-
-    def store(t, n):
-        at = 4 * t + n
-        dst = keep if t else give
-        return pltpu.make_async_copy(folded.at[at], dst.at[n], sem_out.at[at])
-
-    order = [(t, n) for t in range(2) for n in range(4)]
-    for t, n in order:
-        fetch(t, n).start()
-    for t, n in order:
-        fetch(t, n).wait()
-        put_folded(folded, 4 * t + n, 0, tiles[4 * t + n])
-        store(t, n).start()
-    for t, n in order:
-        store(t, n).wait()
-
-
-def fold_left(ids, left_env):
-    count = left_env.shape[0]
+def fold_left_body(term, src, dst, tiles, folded, sem_in, sem_out):
+    def fetch(n):
+        return pltpu.make_async_copy(src.at[n, term[0]], tiles.at[n], sem_in.at[n])
+
+    def store(n):
+        return pltpu.make_async_copy(folded.at[n], dst.at[n], sem_out.at[n])
+
+    for n in range(4):
+        fetch(n).start()
+    for n in range(4):
+        fetch(n).wait()
+        put_folded(folded, n, 0, tiles[n])
+        store(n).start()
+    for n in range(4):
+        store(n).wait()
+
+
+def fold_left(term, left_env):
     return pl.pallas_call(
         fold_left_body,
         in_specs=[smem(), hbm()],
-        out_specs=[hbm(), hbm()],
-        out_shape=[pltpu.HBM((count, LEFT_ROWS, TILE), f32)] * 2,
+        out_specs=hbm(),
+        out_shape=pltpu.HBM((4, LEFT_ROWS, TILE), f32),
         scratch_shapes=[
-            pltpu.VMEM((2 * count, TILE, TILE), f32),
-            pltpu.VMEM((2 * count, LEFT_ROWS, TILE), f32),
-            pltpu.SemaphoreType.DMA((2 * count,)),
-            pltpu.SemaphoreType.DMA((2 * count,)),
-        ],
-        compiler_params=params(8),
+            pltpu.VMEM((4, TILE, TILE), f32),
+            pltpu.VMEM((4, LEFT_ROWS, TILE), f32),
+            pltpu.SemaphoreType.DMA((4,)),
+            pltpu.SemaphoreType.DMA((4,)),
+        ],
+        compiler_params=params(4),
         cost_estimate=cost(1_000_000, 4_000_000),
         name="fold_left",
-    )(ids, in_hbm(left_env))
+    )(term.reshape(1), in_hbm(left_env))
 
 
 def sector_of(ids, rsector, rsector_other, slot):
@@ -206,8 +201,10 @@
     )(ids, rsector, rsector_other, on, on_other, thin, thin_other, in_hbm(right_env))
 
 
-def left_slots_body(ids, left_sector, kept, theirs, below, above, far_a, far_b, out, *scratch):
-    dst, sem_in, sem_out = scratch
+def left_slots_body(ids, left_sector, *refs):
+    mine, theirs = refs[:2]
+    above, far, below = refs[2:4], refs[4:6], refs[6:8]
+    out, dst, sem_in, sem_out = refs[8:]
 
     def fetch(src, slot):
         return pltpu.make_async_copy(src, dst.at[slot], sem_in.at[slot])
@@ -221,14 +218,12 @@
         tile = sector % 4
         away = (home // 2 - ids[0] + 4) % 4
         same = home % 2 == ids[1]
-        cases = [
-            (same, kept, (home // 2) * 4 + tile),
-            (~same & (away == 0), theirs, tile),
-            (~same & (away == 1), above, tile),
-            (~same & (away == 2) & (tile < 2), far_a, tile),
-            (~same & (away == 2) & (tile >= 2), far_b, tile - 2),
-            (~same & (away == 3), below, tile),
-        ]
+        cases = [(same, mine, tile), (~same, theirs, tile)]
+        cases = [(case & (away == 0), src, at) for case, src, at in cases]
+        for n, half in ((0, same), (1, ~same)):
+            cases.append((half & (away == 1), above[n], tile))
+            cases.append((half & (away == 2), far[n], tile))
+            cases.append((half & (away == 3), below[n], tile))
         for case, src, at in cases:
 
             @pl.when(case)
@@ -238,7 +233,7 @@
         return carry
 
     def forward(slot, carry):
-        fetch(kept.at[0], slot).wait()
+        fetch(mine.at[0], slot).wait()
         store(slot).start()
         return carry
 
@@ -255,7 +250,7 @@
     slots = (TERMS, LEFT_ROWS, TILE)
     return pl.pallas_call(
         left_slots_body,
-        in_specs=[smem(), smem()] + [hbm()] * 6,
+        in_specs=[smem(), smem()] + [hbm()] * 8,
         out_specs=hbm(),
         out_shape=pltpu.HBM(slots, f32),
         scratch_shapes=[
@@ -264,7 +259,7 @@
             pltpu.SemaphoreType.DMA((TERMS,)),
         ],
         compiler_params=params(6),
-        cost_estimate=cost(0, 4_000_000),
+        cost_estimate=cost(0, LEFT_BYTES),
         name="left_slots",
     )(ids, left_sector, *[in_hbm(x) for x in pieces])
 
@@ -558,26 +553,31 @@
     ids = jnp.stack([plane, core, place])
     thin = jnp.swapaxes(theta, 1, 2)
 
-    mine, folded = fold_left(ids, left_env)
-    kept = lax.all_gather(mine, "y", axis=0, tiled=True)
+    mine = fold_left(core, left_env)
+    other_core, mine = lax.optimization_barrier((1 - core, mine))
+    folded = fold_left(other_core, left_env)
     theirs = lax.ppermute(folded, "c", SWAP)
-    below = lax.ppermute(theirs, "y", UP)
-    above = lax.ppermute(theirs, "y", DOWN)
-    far_a = lax.ppermute(below[:2], "y", UP)
-    far_b = lax.ppermute(above[2:], "y", DOWN)
+    below = [lax.ppermute(mine, "y", UP)]
+    above = [lax.ppermute(mine, "y", DOWN)]
 
     rsector_other = lax.ppermute(right_sector, "c", SWAP)
     on_other = lax.ppermute(term_on, "c", SWAP)
     thin_other = lax.ppermute(thin, "c", SWAP)
-    thin_late, _ = lax.optimization_barrier((thin, mine))
+    thin_late, _ = lax.optimization_barrier((thin, folded))
     slots = right_slots(
         ids, right_sector, rsector_other, term_on, on_other, thin_late, thin_other, right_env
+    )
+    slots, theirs, first_below, first_above = lax.optimization_barrier(
+        (slots, theirs, below[0], above[0])
     )
     arrived = lax.all_to_all(slots, COL, 0, 0, tiled=True)
     scalars = (ids, right_sector, rsector_other, left_sector, left_size, right_size)
     r_hi, r_lo, m_hi, m_lo, q1, stats = first_vector(scalars, arrived)
 
-    pieces = [kept, theirs, below, above, far_a, far_b]
+    below = [first_below, lax.ppermute(theirs, "y", UP)]
+    above = [first_above, lax.ppermute(theirs, "y", DOWN)]
+    far = [lax.ppermute(below[0], "y", UP), lax.ppermute(above[1], "y", DOWN)]
+    pieces = [mine, theirs] + above + far + below
     left_arrived = lax.all_to_all(left_slots(ids, left_sector, pieces), COL, 0, 0, tiled=True)
     l_hi, l_lo, part = image_one(left_arrived, m_hi, m_lo)
     stacks = (r_hi, r_lo, l_hi, l_lo)

time: 161 us -> 148 us (0.919)
  between operations: 14.3 us -> 1.04 us
  waiting for transfers between devices: 66.9 us -> 64.8 us
  local copies, waits for them, and re-layouts: 7.94 us -> 9.67 us
    unnamed x37 -> x43, local copies, waits for them, and re-layouts: 7.89 us -> 9.65 us
    pallas_call x2 -> x3, Pallas kernels: 6.13 us -> 7.29 us  [the longest x2 4.01 us: fold_left(): pl.pallas_call(fold_left_body, in_specs=[smem(), hbm()], out_specs=hbm(),...]
    ppermute x4 -> x6, waiting for transfers between devices: 32.3 us -> 31.3 us  [the longest x2 11.7 us: local(): far = [lax.ppermute(below[0], 'y', UP), lax.ppermute(above[1], 'y', DOWN)]]
    ppermute x4 -> x6, starting transfers between devices: 6.4 us -> 6.47 us  [the longest x1 2.83 us: local(): above = [lax.ppermute(mine, 'y', DOWN)]]
  transfers between devices with their start and end apart: 19 -> 20, of which waited for: 14 -> 14; matrix products, arithmetic and copies ran while one was open for 0% -> 0% of each run, Pallas kernels for 8% -> 8%
where the time goes in v5:
time: 148 us
  waiting for transfers between devices  64.8 us (44%)
  starting transfers between devices  38.1 us (26%)
  Pallas kernels  34.1 us (23%)
  local copies, waits for them, and re-layouts  9.67 us (7%)
    all_to_all x1, waiting for transfers between devices, local(): lax.all_to_all(left_slots(ids, left_sector, pieces), COL, 0, 0, tiled=True)  15.8 us
    ppermute x2, waiting for transfers between devices, local(): far = [lax.ppermute(below[0], 'y', UP), lax.ppermute(above[1], 'y', DOWN)]  11.7 us
    ppermute x1, waiting for transfers between devices, local(): above = [first_above, lax.ppermute(theirs, 'y', DOWN)]  11.2 us
    unnamed x43, local copies, waits for them, and re-layouts  9.65 us
    all_to_all x1, waiting for transfers between devices, local(): got = lax.all_to_all(sent, COL, 0, 0, tiled=True)  9.23 us
    all_to_all x1, starting transfers between devices, local(): arrived = lax.all_to_all(slots, COL, 0, 0, tiled=True)  7.6 us
    ppermute x2, starting transfers between devices, local(): lax.ppermute(part, 'c', SWAP)  6.39 us
    all_to_all x1, starting transfers between devices, local(): lax.all_to_all(left_slots(ids, left_sector, pieces), COL, 0, 0, tiled=True)  6.31 us
  transfers between devices with their start and end apart: 20, of which 14 were waited for; matrix products, arithmetic and copies ran while one was open for 0% of the time, Pallas kernels for 8%

profile of v5, /device:TPU:1, one launch (start us, length us, event | category | flops | bytes accessed | tf_op | source)
XLA Modules:
  0.0 147.8 jit_solution(167539447789305074)
XLA Ops:
  0.7 2.0 %fold_left.2.refs_0_ = f32[4,136,256]{2,1,0:T(8,128)} custom-call(s32[1]{0:T(128)} %bitcast.1.term, f32[4,2,256,256]{3,2,1,0:T(8,128)} %src.3), custom_call_target="tpu_custom_call" | custom-call | flops 1000000 | bytes 4000000 | tf_op jit(solution)/shard_map/fold_left/pallas_call | solution.py:129
  2.7 2.0 %fold_left.3 = f32[4,136,256]{2,1,0:T(8,128)} custom-call(s32[1]{0:T(128)} %bitcast.4.term, f32[4,2,256,256]{3,2,1,0:T(8,128)} %src.3), custom_call_target="tpu_custom_call" | custom-call | flops 1000000 | bytes 4000000 | tf_op jit(solution)/shard_map/fold_left/pallas_call | solution.py:129
  4.7 1.5 %collective-permute-start.3 = (f32[4,136,256]{2,1,0:T(8,128)}, f32[4,136,256]{2,1,0:T(8,128)S(1)}, u32[]{:S(2)}, u32[]{:S(2)}) collective-permute-start(f32[4,136,256]{2,1,0:T(8,128)} %fold_left.3), channel_id=1, source_target_pairs={{0,16},{16,0},{1,17},{17,1},{2,18},{18,2},{3,19},{19,3},{4,20},{20... | collective-permute-start | bytes 1671176 | tf_op jit(solution)/shard_map/ppermute | solution.py:559
  6.2 2.8 %collective-permute-start.5 = (f32[4,136,256]{2,1,0:T(8,128)S(1)}, f32[4,136,256]{2,1,0:T(8,128)S(1)}, u32[]{:S(2)}, u32[]{:S(2)}) collective-permute-start(f32[4,136,256]{2,1,0:T(8,128)S(1)} %copy-done.12), channel_id=1, source_target_pairs={{0,96},{32,0},{64,32},{96,64},{1,97},{33,1},{65,33},{97,65},{2,98}... | collective-permute-start | bytes 1671176 | tf_op jit(solution)/shard_map/ppermute | solution.py:561
  11.7 3.9 %right_slots.1 = f32[16,152,256]{2,1,0:T(8,128)} custom-call(s32[3]{0:T(128)S(1)} %pad_add_fusion.ids, s32[8]{0:T(128)S(1)} %copy-done.4, s32[8]{0:T(128)S(1)} %collective-permute-done.rsector_other, s32[8,2]{1,0:T(8,128)S(1)} %copy.11.on, s32[8,2]{1,0:T(8,128)S(1)} %collective-permute-done.1.on_other, f32[8,16,256]{2,1,0:T(8,128)S(1)} %bitcast.9, ...), custom_call_target="tpu_custom_call" | custom-call | flops 4000000 | bytes 10000000 | tf_op jit(solution)/shard_map/right_slots/pallas_call | solution.py:187
  15.6 5.4 %collective-permute-done.5.refs_2_ = f32[4,136,256]{2,1,0:T(8,128)S(1)} collective-permute-done((f32[4,136,256]{2,1,0:T(8,128)S(1)}, f32[4,136,256]{2,1,0:T(8,128)S(1)}, u32[]{:S(2)}, u32[]{:S(2)}) %collective-permute-start.5) | collective-permute-done | bytes 557088 | tf_op jit(solution)/shard_map/ppermute | solution.py:561
  21.0 3.1 %collective-permute-done.4.refs_6_ = f32[4,136,256]{2,1,0:T(8,128)S(1)} collective-permute-done((f32[4,136,256]{2,1,0:T(8,128)S(1)}, f32[4,136,256]{2,1,0:T(8,128)S(1)}, u32[]{:S(2)}, u32[]{:S(2)}) %collective-permute-start.4) | collective-permute-done | bytes 557088 | tf_op jit(solution)/shard_map/ppermute | solution.py:560
  24.9 7.6 %all-to-all-start.1 = ((f32[16,152,256]{2,1,0:T(8,128)}), f32[16,152,256]{2,1,0:T(8,128)S(1)}, u32[]{:S(2)}, u32[]{:S(2)}) async-start(f32[16,152,256]{2,1,0:T(8,128)} %right_slots.1), calls=%async_computation.1 | async-start | bytes 4980736 | tf_op jit(solution)/shard_map/all_to_all | solution.py:573
  34.1 11.2 %collective-permute-done.6.refs_3_ = f32[4,136,256]{2,1,0:T(8,128)S(1)} collective-permute-done((f32[4,136,256]{2,1,0:T(8,128)S(1)}, f32[4,136,256]{2,1,0:T(8,128)S(1)}, u32[]{:S(2)}, u32[]{:S(2)}) %collective-permute-start.6) | collective-permute-done | bytes 557088 | tf_op jit(solution)/shard_map/ppermute | solution.py:578
  45.2 2.1 %collective-permute-start.8 = (f32[4,136,256]{2,1,0:T(8,128)S(1)}, f32[4,136,256]{2,1,0:T(8,128)S(1)}, u32[]{:S(2)}, u32[]{:S(2)}) collective-permute-start(f32[4,136,256]{2,1,0:T(8,128)S(1)} %collective-permute-done.6.refs_3_), channel_id=1, source_target_pairs={{0,96},{32,0},{64,32},{96,64},{1,97},{33,1},{65,33},{97,65},{2,98}... | collective-permute-start | bytes 1671176 | tf_op jit(solution)/shard_map/ppermute | solution.py:579
  47.3 11.7 %collective-permute-done.7.refs_4_ = f32[4,136,256]{2,1,0:T(8,128)S(1)} collective-permute-done((f32[4,136,256]{2,1,0:T(8,128)}, f32[4,136,256]{2,1,0:T(8,128)S(1)}, u32[]{:S(2)}, u32[]{:S(2)}) %collective-permute-start.7) | collective-permute-done | bytes 557088 | tf_op jit(solution)/shard_map/ppermute | solution.py:579
  60.9 3.3 %left_slots.1 = f32[16,136,256]{2,1,0:T(8,128)} custom-call(s32[3]{0:T(128)S(1)} %pad_add_fusion.ids, s32[64]{0:T(128)S(1)} %copy-done.3, f32[4,136,256]{2,1,0:T(8,128)} %fold_left.2.refs_0_, f32[4,136,256]{2,1,0:T(8,128)} %copy-done.13, f32[4,136,256]{2,1,0:T(8,128)} %copy-done.14, f32[4,136,256]{2,1,0:T(8,128)} %copy-done.16, f32[4,136,256]{2,1,0:T(8,128)} %copy-done.18, ...), custom_call_target="tpu_custom_call" | custom-call | bytes 4000000 | tf_op jit(solution)/shard_map/left_slots/pallas_call | solution.py:251
  64.2 1.4 copy-done.11
  65.6 6.3 %all-to-all-start = ((f32[16,136,256]{2,1,0:T(8,128)}), f32[16,136,256]{2,1,0:T(8,128)S(1)}, u32[]{:S(2)}, u32[]{:S(2)}) async-start(f32[16,136,256]{2,1,0:T(8,128)} %left_slots.1), calls=%async_computation | async-start | bytes 4456448 | tf_op jit(solution)/shard_map/all_to_all | solution.py:581
  72.0 5.3 %first_vector.1 = (bf16[4096,256]{1,0:T(8,128)(2,1)S(1)}, bf16[4096,256]{1,0:T(8,128)(2,1)S(1)}, bf16[256,4096]{1,0:T(8,128)(2,1)S(1)}, bf16[256,4096]{1,0:T(8,1...) custom-call(s32[3]{0:T(128)S(1)} %pad_add_fusion.ids, s32[8]{0:T(128)S(1)} %copy-done.4, ...), custom_call_target="tpu_custom_call" | custom-call | flops 1700000000 | bytes 12000000 | tf_op jit(solution)/shard_map/first_vector/pallas_call | solution.py:314
  77.3 1.3 copy-done
  78.6 1.4 copy-done.1
  80.0 1.4 copy-done.7
  81.4 1.3 copy-done.9
  82.7 15.8 %all-to-all-done.arrived = f32[16,136,256]{2,1,0:T(8,128)S(1)} async-done(((f32[16,136,256]{2,1,0:T(8,128)}), f32[16,136,256]{2,1,0:T(8,128)S(1)}, u32[]{:S(2)}, u32[]{:S(2)}) %all-to-all-start) | async-done | bytes 2228256 | tf_op jit(solution)/shard_map/all_to_all | solution.py:581
  98.5 5.0 %image_one.1 = (bf16[4096,256]{1,0:T(8,128)(2,1)S(1)}, bf16[4096,256]{1,0:T(8,128)(2,1)S(1)}, f32[256,256]{1,0:T(8,128)S(1)}) custom-call(f32[16,136,256]{2,1,0:T(8,128)S(1)} %all-to-all-done.arrived, bf16[256,4096]{1,0:T(8,128)(2,1)} %copy-done, bf16[256,4096]{1,0:T(8,128)(2,1)} %copy-done.1), custom_call_target="tpu_custom_call" | custom-call | flops 1700000000 | bytes 10000000 | tf_op jit(solution)/shard_map/image_one/pallas_call | solution.py:364
  103.5 5.9 %collective-permute-start.10 = (f32[256,256]{1,0:T(8,128)S(1)}, f32[256,256]{1,0:T(8,128)S(1)}, u32[]{:S(2)}, u32[]{:S(2)}) collective-permute-start(f32[256,256]{1,0:T(8,128)S(1)} %get-tuple-element.32.part_a), channel_id=1, source_target_pairs={{0,16},{16,0},{1,17},{17,1},{2,18},{18,2},{3,19},{19,3},{4,20},{20... | collective-permute-start | bytes 786440 | tf_op jit(solution)/shard_map/ppermute | solution.py:584
  110.6 4.7 %image_two.1 = (f32[256,256]{1,0:T(8,128)S(1)}, f32[256,256]{1,0:T(8,128)S(1)}, f32[8,128]{1,0:T(8,128)S(1)}) custom-call(s32[3]{0:T(128)S(1)} %pad_add_fusion.ids, s32[8]{0:T(128)S(1)} %copy-done.4, s32[8]{0:T(128)S(1)} %collective-permute-done.rsector_other, s32[64]{0:T(128)S(1)} %copy-done.3, s32[32]{0:T(128)S(1)} %copy-done.5, s32[8]{0:T(128)S(1)} %copy-done.6, ...), custom_call_target="tpu_custom_call" | custom-call | flops 3300000000 | bytes 9000000 | tf_op jit(solution)/shard_map/image_two/pallas_call | solution.py:419
  115.8 1.2 collective-permute-done.11.part_b
  116.9 5.6 %image_three.1 = f32[16,24,256]{2,1,0:T(8,128)} custom-call(s32[3]{0:T(128)S(1)} %pad_add_fusion.ids, s32[8]{0:T(128)S(1)} %copy-done.4, s32[8]{0:T(128)S(1)} %collective-permute-done.rsector_other, s32[64]{0:T(128)S(1)} %copy-done.3, s32[32]{0:T(128)S(1)} %copy-done.5, s32[8]{0:T(128)S(1)} %copy-done.6, f32[256,256]{1,0:T(8,128)S(1)} %get-tuple-element.39.part_a, ...), custom_call_target="tpu_custom_call" | custom-call | flops 3300000000 | bytes 9000000 | tf_op jit(solution)/shard_map/image_three/pallas_call | solution.py:455
  122.6 3.7 %all-to-all-start.2 = ((f32[16,24,256]{2,1,0:T(8,128)}), f32[16,24,256]{2,1,0:T(8,128)S(1)}, u32[]{:S(2)}, u32[]{:S(2)}) async-start(f32[16,24,256]{2,1,0:T(8,128)} %image_three.1), calls=%async_computation.2 | async-start | bytes 786432 | tf_op jit(solution)/shard_map/all_to_all | solution.py:587
  126.3 9.2 %all-to-all-done.2.got = f32[16,24,256]{2,1,0:T(8,128)S(1)} async-done(((f32[16,24,256]{2,1,0:T(8,128)}), f32[16,24,256]{2,1,0:T(8,128)S(1)}, u32[]{:S(2)}, u32[]{:S(2)}) %all-to-all-start.2) | async-done | bytes 393248 | tf_op jit(solution)/shard_map/all_to_all | solution.py:587
  135.5 1.6 %collective-permute-start.16 = (f32[8,24,256]{2,1,0:T(8,128)S(1)}, f32[8,24,256]{2,1,0:T(8,128)S(1)}, u32[]{:S(2)}, u32[]{:S(2)}) collective-permute-start(f32[8,24,256]{2,1,0:T(8,128)S(1)} %constant_dynamic-slice_fusion), channel_id=1, source_target_pairs={{0,16},{16,0},{1,17},{17,1},{2,18},{18,2},{3,19},{19,3},{4,20},{20... | collective-permute-start | bytes 589832 | tf_op jit(solution)/shard_map/ppermute | solution.py:592
  137.1 1.4 collective-permute-start.14
  139.7 2.9 %collective-permute-done.13 = f32[16,128]{1,0:T(8,128)S(1)} collective-permute-done((f32[16,128]{1,0:T(8,128)S(1)}, f32[16,128]{1,0:T(8,128)S(1)}, u32[]{:S(2)}, u32[]{:S(2)}) %collective-permute-start.13) | collective-permute-done | bytes 8224 | tf_op jit(solution)/shard_map/ppermute | solution.py:590
  142.7 1.8 %collective-permute-start.15 = (f32[64,128]{1,0:T(8,128)S(1)}, f32[64,128]{1,0:T(8,128)S(1)}, u32[]{:S(2)}, u32[]{:S(2)}) collective-permute-start(f32[64,128]{1,0:T(8,128)S(1)} %pad_maximum_fusion.own_stats), channel_id=1, source_target_pairs={{0,16},{16,0},{1,17},{17,1},{2,18},{18,2},{3,19},{19,3},{4,20},{20... | collective-permute-start | bytes 98312 | tf_op jit(solution)/shard_map/ppermute | solution.py:594
  145.4 2.2 %finish.1 = (f32[8,16,256]{2,1,0:T(8,128)}, f32[1,1]{1,0:T(1,128)}) custom-call(s32[3]{0:T(128)S(1)} %pad_add_fusion.ids, s32[64]{0:T(128)S(1)} %copy-done.3, s32[8]{0:T(128)S(1)} %copy-done.4, s32[32]{0:T(128)S(1)} %copy-done.5, s32[8]{0:T(128)S(1)} %copy-done.6, f32[64,128]{1,0:T(8,128)S(1)} %pad_maximum_fusion.own_stats, ...), custom_call_target="tpu_custom_call" | custom-call | tf_op jit(solution)/shard_map/finish/pallas_call | solution.py:535
  (64 shorter events, 10.8 us)
Async XLA Ops:
  0.6 8.4 %copy-start.2 = (f32[8,256,16]{1,2,0:T(8,128)S(1)}, f32[8,256,16]{1,2,0:T(8,128)}, u32[]{:S(2)}) copy-start(f32[8,256,16]{1,2,0:T(8,128)} %param.8) | copy-start | bytes 393220
  0.6 8.8 %copy-start.4 = (s32[8]{0:T(128)S(1)}, s32[8]{0:T(128)}, u32[]{:S(2)}) copy-start(s32[8]{0:T(128)} %rsector.9) | copy-start | bytes 100
  0.7 8.9 %copy-start.20 = (s32[8,2]{0,1:T(2,128)S(1)}, s32[8,2]{0,1:T(2,128)}, u32[]{:S(2)}) copy-start(s32[8,2]{0,1:T(2,128)} %param.13) | copy-start | bytes 196
  2.7 3.5 %copy-start.12 = (f32[4,136,256]{2,1,0:T(8,128)S(1)}, f32[4,136,256]{2,1,0:T(8,128)}, u32[]{:S(2)}) copy-start(f32[4,136,256]{2,1,0:T(8,128)} %fold_left.2.refs_0_) | copy-start | bytes 1671172
  4.7 10.9 %collective-permute-start.3 = (f32[4,136,256]{2,1,0:T(8,128)}, f32[4,136,256]{2,1,0:T(8,128)S(1)}, u32[]{:S(2)}, u32[]{:S(2)}) collective-permute-start(f32[4,136,256]{2,1,0:T(8,128)} %fold_left.3), channel_id=1, source_target_pairs={{0,16},{16,0},{1,17},{17,1},{2,18},{18,2},{3,19},{19,3},{4,20},{20... | collective-permute-start | bytes 1671176 | tf_op jit(solution)/shard_map/ppermute | solution.py:559
  6.2 14.8 %collective-permute-start.5 = (f32[4,136,256]{2,1,0:T(8,128)S(1)}, f32[4,136,256]{2,1,0:T(8,128)S(1)}, u32[]{:S(2)}, u32[]{:S(2)}) collective-permute-start(f32[4,136,256]{2,1,0:T(8,128)S(1)} %copy-done.12), channel_id=1, source_target_pairs={{0,96},{32,0},{64,32},{96,64},{1,97},{33,1},{65,33},{97,65},{2,98}... | collective-permute-start | bytes 1671176 | tf_op jit(solution)/shard_map/ppermute | solution.py:561
  9.0 15.1 %collective-permute-start.4 = (f32[4,136,256]{2,1,0:T(8,128)S(1)}, f32[4,136,256]{2,1,0:T(8,128)S(1)}, u32[]{:S(2)}, u32[]{:S(2)}) collective-permute-start(f32[4,136,256]{2,1,0:T(8,128)S(1)} %copy-done.12), channel_id=1, source_target_pairs={{0,32},{32,64},{64,96},{96,0},{1,33},{33,65},{65,97},{97,1},{2,34}... | collective-permute-start | bytes 1671176 | tf_op jit(solution)/shard_map/ppermute | solution.py:560
  9.0 2.6 %collective-permute-start.2 = (f32[8,16,256]{2,1,0:T(8,128)S(1)}, f32[8,16,256]{2,1,0:T(8,128)S(1)}, u32[]{:S(2)}, u32[]{:S(2)}) collective-permute-start(f32[8,16,256]{2,1,0:T(8,128)S(1)} %bitcast.8), channel_id=1, source_target_pairs={{0,16},{16,0},{1,17},{17,1},{2,18},{18,2},{3,19},{19,3},{4,20},{20... | collective-permute-start | bytes 393224 | tf_op jit(solution)/shard_map/ppermute | solution.py:565
  9.4 1.1 collective-permute-start
  10.5 1.2 collective-permute-start.1
  15.6 45.3 %copy-start.3 = (s32[64]{0:T(128)S(1)}, s32[64]{0:T(128)}, u32[]{:S(2)}) copy-start(s32[64]{0:T(128)} %sector.7) | copy-start | bytes 772
  15.6 17.5 %copy-start.13 = (f32[4,136,256]{2,1,0:T(8,128)}, f32[4,136,256]{2,1,0:T(8,128)S(1)}, u32[]{:S(2)}) copy-start(f32[4,136,256]{2,1,0:T(8,128)S(1)} %collective-permute-done.3.refs_1_) | copy-start | bytes 1671172
  21.0 3.1 %copy-start.14 = (f32[4,136,256]{2,1,0:T(8,128)}, f32[4,136,256]{2,1,0:T(8,128)S(1)}, u32[]{:S(2)}) copy-start(f32[4,136,256]{2,1,0:T(8,128)S(1)} %collective-permute-done.5.refs_2_) | copy-start | bytes 1671172
  24.9 39.3 %all-to-all-start.1 = ((f32[16,152,256]{2,1,0:T(8,128)}), f32[16,152,256]{2,1,0:T(8,128)S(1)}, u32[]{:S(2)}, u32[]{:S(2)}) async-start(f32[16,152,256]{2,1,0:T(8,128)} %right_slots.1), calls=%async_computation.1 | async-start | bytes 4980736 | tf_op jit(solution)/shard_map/all_to_all | solution.py:573
  32.5 12.7 %collective-permute-start.6 = (f32[4,136,256]{2,1,0:T(8,128)S(1)}, f32[4,136,256]{2,1,0:T(8,128)S(1)}, u32[]{:S(2)}, u32[]{:S(2)}) collective-permute-start(f32[4,136,256]{2,1,0:T(8,128)S(1)} %collective-permute-done.3.refs_1_), channel_id=1, source_target_pairs={{0,96},{32,0},{64,32},{96,64},{1,97},{33,1},{65,33},{97,65},{2,98}... | collective-permute-start | bytes 1671176 | tf_op jit(solution)/shard_map/ppermute | solution.py:578
  33.1 25.8 %collective-permute-start.9 = (f32[4,136,256]{2,1,0:T(8,128)S(1)}, f32[4,136,256]{2,1,0:T(8,128)S(1)}, u32[]{:S(2)}, u32[]{:S(2)}) collective-permute-start(f32[4,136,256]{2,1,0:T(8,128)S(1)} %collective-permute-done.3.refs_1_), channel_id=1, source_target_pairs={{0,32},{32,64},{64,96},{96,0},{1,33},{33,65},{65,97},{97,1},{2,34}... | collective-permute-start | bytes 1671176 | tf_op jit(solution)/shard_map/ppermute | solution.py:577
  34.0 24.9 %collective-permute-start.7 = (f32[4,136,256]{2,1,0:T(8,128)}, f32[4,136,256]{2,1,0:T(8,128)S(1)}, u32[]{:S(2)}, u32[]{:S(2)}) collective-permute-start(f32[4,136,256]{2,1,0:T(8,128)} %copy-done.15), channel_id=1, source_target_pairs={{0,32},{32,64},{64,96},{96,0},{1,33},{33,65},{65,97},{97,1},{2,34}... | collective-permute-start | bytes 1671176 | tf_op jit(solution)/shard_map/ppermute | solution.py:579
  45.2 13.7 %copy-start.16 = (f32[4,136,256]{2,1,0:T(8,128)}, f32[4,136,256]{2,1,0:T(8,128)S(1)}, u32[]{:S(2)}) copy-start(f32[4,136,256]{2,1,0:T(8,128)S(1)} %collective-permute-done.6.refs_3_) | copy-start | bytes 1671172
  45.2 13.7 %collective-permute-start.8 = (f32[4,136,256]{2,1,0:T(8,128)S(1)}, f32[4,136,256]{2,1,0:T(8,128)S(1)}, u32[]{:S(2)}, u32[]{:S(2)}) collective-permute-start(f32[4,136,256]{2,1,0:T(8,128)S(1)} %collective-permute-done.6.refs_3_), channel_id=1, source_target_pairs={{0,96},{32,0},{64,32},{96,64},{1,97},{33,1},{65,33},{97,65},{2,98}... | collective-permute-start | bytes 1671176 | tf_op jit(solution)/shard_map/ppermute | solution.py:579
  64.1 7.8 %copy-start.5 = (s32[32]{0:T(128)S(1)}, s32[32]{0:T(128)}, u32[]{:S(2)}) copy-start(s32[32]{0:T(128)} %lsize.7) | copy-start | bytes 388
  64.2 7.8 %copy-start.6 = (s32[8]{0:T(128)S(1)}, s32[8]{0:T(128)}, u32[]{:S(2)}) copy-start(s32[8]{0:T(128)} %rsize.7) | copy-start | bytes 100
  65.6 32.8 %all-to-all-start = ((f32[16,136,256]{2,1,0:T(8,128)}), f32[16,136,256]{2,1,0:T(8,128)S(1)}, u32[]{:S(2)}, u32[]{:S(2)}) async-start(f32[16,136,256]{2,1,0:T(8,128)} %left_slots.1), calls=%async_computation | async-start | bytes 4456448 | tf_op jit(solution)/shard_map/all_to_all | solution.py:581
  98.5 12.2 %copy-start.8 = (bf16[4096,256]{1,0:T(8,128)(2,1)S(1)}, bf16[4096,256]{1,0:T(8,128)(2,1)}, u32[]{:S(2)}) copy-start(bf16[4096,256]{1,0:T(8,128)(2,1)} %copy-done.7) | copy-start | bytes 6291460
  98.5 12.2 %copy-start.10 = (bf16[4096,256]{1,0:T(8,128)(2,1)S(1)}, bf16[4096,256]{1,0:T(8,128)(2,1)}, u32[]{:S(2)}) copy-start(bf16[4096,256]{1,0:T(8,128)(2,1)} %copy-done.9) | copy-start | bytes 6291460
  103.5 7.1 %collective-permute-start.10 = (f32[256,256]{1,0:T(8,128)S(1)}, f32[256,256]{1,0:T(8,128)S(1)}, u32[]{:S(2)}, u32[]{:S(2)}) collective-permute-start(f32[256,256]{1,0:T(8,128)S(1)} %get-tuple-element.32.part_a), channel_id=1, source_target_pairs={{0,16},{16,0},{1,17},{17,1},{2,18},{18,2},{3,19},{19,3},{4,20},{20... | collective-permute-start | bytes 786440 | tf_op jit(solution)/shard_map/ppermute | solution.py:584
  115.3 1.6 %collective-permute-start.11 = (f32[256,256]{1,0:T(8,128)S(1)}, f32[256,256]{1,0:T(8,128)S(1)}, u32[]{:S(2)}, u32[]{:S(2)}) collective-permute-start(f32[256,256]{1,0:T(8,128)S(1)} %get-tuple-element.39.part_a), channel_id=1, source_target_pairs={{0,16},{16,0},{1,17},{17,1},{2,18},{18,2},{3,19},{19,3},{4,20},{20... | collective-permute-start | bytes 786440 | tf_op jit(solution)/shard_map/ppermute | solution.py:585
  122.6 12.9 %all-to-all-start.2 = ((f32[16,24,256]{2,1,0:T(8,128)}), f32[16,24,256]{2,1,0:T(8,128)S(1)}, u32[]{:S(2)}, u32[]{:S(2)}) async-start(f32[16,24,256]{2,1,0:T(8,128)} %image_three.1), calls=%async_computation.2 | async-start | bytes 786432 | tf_op jit(solution)/shard_map/all_to_all | solution.py:587
  135.5 9.8 %collective-permute-start.16 = (f32[8,24,256]{2,1,0:T(8,128)S(1)}, f32[8,24,256]{2,1,0:T(8,128)S(1)}, u32[]{:S(2)}, u32[]{:S(2)}) collective-permute-start(f32[8,24,256]{2,1,0:T(8,128)S(1)} %constant_dynamic-slice_fusion), channel_id=1, source_target_pairs={{0,16},{16,0},{1,17},{17,1},{2,18},{18,2},{3,19},{19,3},{4,20},{20... | collective-permute-start | bytes 589832 | tf_op jit(solution)/shard_map/ppermute | solution.py:592
  137.1 2.5 %collective-permute-start.14 = (f32[16,128]{1,0:T(8,128)S(1)}, f32[16,128]{1,0:T(8,128)S(1)}, u32[]{:S(2)}, u32[]{:S(2)}) collective-permute-start(f32[16,128]{1,0:T(8,128)S(1)} %bitcast.11), channel_id=1, source_target_pairs={{0,96},{32,0},{64,32},{96,64},{1,97},{33,1},{65,33},{97,65},{2,98}... | collective-permute-start | bytes 24584 | tf_op jit(solution)/shard_map/ppermute | solution.py:590
  138.5 4.0 %collective-permute-start.13 = (f32[16,128]{1,0:T(8,128)S(1)}, f32[16,128]{1,0:T(8,128)S(1)}, u32[]{:S(2)}, u32[]{:S(2)}) collective-permute-start(f32[16,128]{1,0:T(8,128)S(1)} %bitcast.12), channel_id=1, source_target_pairs={{0,64},{32,96},{64,0},{96,32},{1,65},{33,97},{65,1},{97,33},{2,66}... | collective-permute-start | bytes 24584 | tf_op jit(solution)/shard_map/ppermute | solution.py:590
  139.0 3.7 %collective-permute-start.12 = (f32[16,128]{1,0:T(8,128)S(1)}, f32[16,128]{1,0:T(8,128)S(1)}, u32[]{:S(2)}, u32[]{:S(2)}) collective-permute-start(f32[16,128]{1,0:T(8,128)S(1)} %bitcast.13), channel_id=1, source_target_pairs={{0,32},{32,64},{64,96},{96,0},{1,33},{33,65},{65,97},{97,1},{2,34}... | collective-permute-start | bytes 24584 | tf_op jit(solution)/shard_map/ppermute | solution.py:590
  142.7 2.6 %collective-permute-start.15 = (f32[64,128]{1,0:T(8,128)S(1)}, f32[64,128]{1,0:T(8,128)S(1)}, u32[]{:S(2)}, u32[]{:S(2)}) collective-permute-start(f32[64,128]{1,0:T(8,128)S(1)} %pad_maximum_fusion.own_stats), channel_id=1, source_target_pairs={{0,16},{16,0},{1,17},{17,1},{2,18},{18,2},{3,19},{19,3},{4,20},{20... | collective-permute-start | bytes 98312 | tf_op jit(solution)/shard_map/ppermute | solution.py:594
  (9 other events, 10.4 us)

commit v6 on v4

--- a/solution.py
+++ b/solution.py
@@ -130,17 +130,16 @@
 
 
 def fold_left(ids, left_env):
-    count = left_env.shape[0]
     return pl.pallas_call(
         fold_left_body,
         in_specs=[smem(), hbm()],
         out_specs=[hbm(), hbm()],
-        out_shape=[pltpu.HBM((count, LEFT_ROWS, TILE), f32)] * 2,
+        out_shape=[pltpu.HBM((4, LEFT_ROWS, TILE), f32)] * 2,
         scratch_shapes=[
-            pltpu.VMEM((2 * count, TILE, TILE), f32),
-            pltpu.VMEM((2 * count, LEFT_ROWS, TILE), f32),
-            pltpu.SemaphoreType.DMA((2 * count,)),
-            pltpu.SemaphoreType.DMA((2 * count,)),
+            pltpu.VMEM((8, TILE, TILE), f32),
+            pltpu.VMEM((8, LEFT_ROWS, TILE), f32),
+            pltpu.SemaphoreType.DMA((8,)),
+            pltpu.SemaphoreType.DMA((8,)),
         ],
         compiler_params=params(8),
         cost_estimate=cost(1_000_000, 4_000_000),
@@ -206,8 +205,10 @@
     )(ids, rsector, rsector_other, on, on_other, thin, thin_other, in_hbm(right_env))
 
 
-def left_slots_body(ids, left_sector, kept, theirs, below, above, far_a, far_b, out, *scratch):
-    dst, sem_in, sem_out = scratch
+def left_slots_body(ids, left_sector, *refs):
+    mine, theirs = refs[:2]
+    above, far, below = refs[2:4], refs[4:6], refs[6:8]
+    out, dst, sem_in, sem_out = refs[8:]
 
     def fetch(src, slot):
         return pltpu.make_async_copy(src, dst.at[slot], sem_in.at[slot])
@@ -221,14 +222,12 @@
         tile = sector % 4
         away = (home // 2 - ids[0] + 4) % 4
         same = home % 2 == ids[1]
-        cases = [
-            (same, kept, (home // 2) * 4 + tile),
-            (~same & (away == 0), theirs, tile),
-            (~same & (away == 1), above, tile),
-            (~same & (away == 2) & (tile < 2), far_a, tile),
-            (~same & (away == 2) & (tile >= 2), far_b, tile - 2),
-            (~same & (away == 3), below, tile),
-        ]
+        cases = [(same, mine, tile), (~same, theirs, tile)]
+        cases = [(case & (away == 0), src, at) for case, src, at in cases]
+        for n, half in ((0, same), (1, ~same)):
+            cases.append((half & (away == 1), above[n], tile))
+            cases.append((half & (away == 2), far[n], tile))
+            cases.append((half & (away == 3), below[n], tile))
         for case, src, at in cases:
 
             @pl.when(case)
@@ -238,7 +237,7 @@
         return carry
 
     def forward(slot, carry):
-        fetch(kept.at[0], slot).wait()
+        fetch(mine.at[0], slot).wait()
         store(slot).start()
         return carry
 
@@ -255,7 +254,7 @@
     slots = (TERMS, LEFT_ROWS, TILE)
     return pl.pallas_call(
         left_slots_body,
-        in_specs=[smem(), smem()] + [hbm()] * 6,
+        in_specs=[smem(), smem()] + [hbm()] * 8,
         out_specs=hbm(),
         out_shape=pltpu.HBM(slots, f32),
         scratch_shapes=[
@@ -264,7 +263,7 @@
             pltpu.SemaphoreType.DMA((TERMS,)),
         ],
         compiler_params=params(6),
-        cost_estimate=cost(0, 4_000_000),
+        cost_estimate=cost(15_000_000_000, 4_000_000),
         name="left_slots",
     )(ids, left_sector, *[in_hbm(x) for x in pieces])
 
@@ -558,27 +557,28 @@
     ids = jnp.stack([plane, core, place])
     thin = jnp.swapaxes(theta, 1, 2)
 
-    mine, folded = fold_left(ids, left_env)
-    kept = lax.all_gather(mine, "y", axis=0, tiled=True)
-    theirs = lax.ppermute(folded, "c", SWAP)
-    below = lax.ppermute(theirs, "y", UP)
-    above = lax.ppermute(theirs, "y", DOWN)
-    far_a = lax.ppermute(below[:2], "y", UP)
-    far_b = lax.ppermute(above[2:], "y", DOWN)
-
     rsector_other = lax.ppermute(right_sector, "c", SWAP)
     on_other = lax.ppermute(term_on, "c", SWAP)
     thin_other = lax.ppermute(thin, "c", SWAP)
-    thin_late, _ = lax.optimization_barrier((thin, mine))
+
+    mine, folded = fold_left(ids, left_env)
+    theirs = lax.ppermute(folded, "c", SWAP)
+    below = [lax.ppermute(x, "y", UP) for x in (mine, theirs)]
+    above = [lax.ppermute(x, "y", DOWN) for x in (mine, theirs)]
+    far = [lax.ppermute(below[0], "y", UP), lax.ppermute(above[1], "y", DOWN)]
+
+    thin_late, _ = lax.optimization_barrier((thin, folded))
     slots = right_slots(
         ids, right_sector, rsector_other, term_on, on_other, thin_late, thin_other, right_env
     )
+    slots, theirs_now = lax.optimization_barrier((slots, theirs))
     arrived = lax.all_to_all(slots, COL, 0, 0, tiled=True)
     scalars = (ids, right_sector, rsector_other, left_sector, left_size, right_size)
     r_hi, r_lo, m_hi, m_lo, q1, stats = first_vector(scalars, arrived)
 
-    pieces = [kept, theirs, below, above, far_a, far_b]
-    left_arrived = lax.all_to_all(left_slots(ids, left_sector, pieces), COL, 0, 0, tiled=True)
+    pieces = [mine, theirs] + above + far + below
+    left_sent = left_slots(ids, left_sector, pieces)
+    left_arrived = lax.all_to_all(left_sent, COL, 0, 0, tiled=True)
     l_hi, l_lo, part = image_one(left_arrived, m_hi, m_lo)
     stacks = (r_hi, r_lo, l_hi, l_lo)
     part, q2, stats = image_two(scalars, part, lax.ppermute(part, "c", SWAP), q1, stats, stacks)

time: 161 us -> 140 us (0.87)
  between operations: 14.3 us -> 1.01 us
  waiting for transfers between devices: 66.9 us -> 57.5 us
    ppermute x4 -> x6, waiting for transfers between devices: 32.3 us -> 22.9 us  [the longest x2 11.9 us: local(): far = [lax.ppermute(below[0], 'y', UP), lax.ppermute(above[1], 'y', DOWN)]]
    ppermute x4 -> x6, starting transfers between devices: 6.4 us -> 8.42 us  [the longest x2 3.35 us: local(): above = [lax.ppermute(x, 'y', DOWN) for x in (mine, theirs)]]
  transfers between devices with their start and end apart: 19 -> 20, of which waited for: 14 -> 15; matrix products, arithmetic and copies ran while one was open for 0% -> 0% of each run, Pallas kernels for 8% -> 9%
where the time goes in v6:
time: 140 us
  waiting for transfers between devices  57.5 us (41%)
  starting transfers between devices  39.3 us (28%)
  Pallas kernels  33 us (24%)
  local copies, waits for them, and re-layouts  8.76 us (6%)
    all_to_all x1, waiting for transfers between devices, local(): left_arrived = lax.all_to_all(left_sent, COL, 0, 0, tiled=True)  16 us
    ppermute x2, waiting for transfers between devices, local(): far = [lax.ppermute(below[0], 'y', UP), lax.ppermute(above[1], 'y', DOWN)]  11.9 us
    ppermute x2, waiting for transfers between devices, local(): above = [lax.ppermute(x, 'y', DOWN) for x in (mine, theirs)]  9.4 us
    all_to_all x1, waiting for transfers between devices, local(): got = lax.all_to_all(sent, COL, 0, 0, tiled=True)  9.24 us
    unnamed x37, local copies, waits for them, and re-layouts  8.74 us
    all_to_all x1, starting transfers between devices, local(): arrived = lax.all_to_all(slots, COL, 0, 0, tiled=True)  7.74 us
    all_to_all x1, starting transfers between devices, local(): left_arrived = lax.all_to_all(left_sent, COL, 0, 0, tiled=True)  6.38 us
    ppermute x2, starting transfers between devices, local(): lax.ppermute(part, 'c', SWAP)  6.1 us
  transfers between devices with their start and end apart: 20, of which 15 were waited for; matrix products, arithmetic and copies ran while one was open for 0% of the time, Pallas kernels for 9%

profile of v6, /device:TPU:1, one launch (start us, length us, event | category | flops | bytes accessed | tf_op | source)
XLA Modules:
  0.0 139.7 jit_solution(11414771987023749181)
XLA Ops:
  0.7 2.9 %fold_left.1 = (f32[4,136,256]{2,1,0:T(8,128)}, f32[4,136,256]{2,1,0:T(8,128)}) custom-call(s32[3]{0:T(128)S(1)} %pad_add_fusion.ids, f32[4,2,256,256]{3,2,1,0:T(8,128)} %src.1), custom_call_target="tpu_custom_call" | custom-call | flops 1000000 | bytes 4000000 | tf_op jit(solution)/shard_map/fold_left/pallas_call | solution.py:133
  3.6 1.5 %collective-permute-start.1 = (f32[4,136,256]{2,1,0:T(8,128)}, f32[4,136,256]{2,1,0:T(8,128)}, u32[]{:S(2)}, u32[]{:S(2)}) collective-permute-start(f32[4,136,256]{2,1,0:T(8,128)} %get-tuple-element.21), channel_id=1, source_target_pairs={{0,16},{16,0},{1,17},{17,1},{2,18},{18,2},{3,19},{19,3},{4,20},{20... | collective-permute-start | bytes 1671176 | tf_op jit(solution)/shard_map/ppermute | solution.py:565
  5.1 1.4 collective-permute-start.4
  7.0 2.8 %collective-permute-start.3 = (f32[4,136,256]{2,1,0:T(8,128)}, f32[4,136,256]{2,1,0:T(8,128)}, u32[]{:S(2)}, u32[]{:S(2)}) collective-permute-start(f32[4,136,256]{2,1,0:T(8,128)} %collective-permute-done.1.refs_1_), channel_id=1, source_target_pairs={{0,96},{32,0},{64,32},{96,64},{1,97},{33,1},{65,33},{97,65},{2,98}... | collective-permute-start | bytes 1671176 | tf_op jit(solution)/shard_map/ppermute | solution.py:567
  11.9 3.9 %right_slots.1 = f32[16,152,256]{2,1,0:T(8,128)} custom-call(s32[3]{0:T(128)S(1)} %pad_add_fusion.ids, s32[8]{0:T(128)S(1)} %copy-done.3, s32[8]{0:T(128)S(1)} %collective-permute-done.rsector_other, s32[8,2]{1,0:T(8,128)S(1)} %copy.11.on, s32[8,2]{1,0:T(8,128)S(1)} %collective-permute-done.8.on_other, f32[8,16,256]{2,1,0:T(8,128)S(1)} %bitcast.8, ...), custom_call_target="tpu_custom_call" | custom-call | flops 4000000 | bytes 10000000 | tf_op jit(solution)/shard_map/right_slots/pallas_call | solution.py:191
  15.9 7.7 %all-to-all-start.1 = ((f32[16,152,256]{2,1,0:T(8,128)}), f32[16,152,256]{2,1,0:T(8,128)S(1)}, u32[]{:S(2)}, u32[]{:S(2)}) async-start(f32[16,152,256]{2,1,0:T(8,128)} %right_slots.1), calls=%async_computation.1 | async-start | bytes 4980736 | tf_op jit(solution)/shard_map/all_to_all | solution.py:575
  25.2 2.6 %collective-permute-start.6 = (f32[4,136,256]{2,1,0:T(8,128)}, f32[4,136,256]{2,1,0:T(8,128)S(1)}, u32[]{:S(2)}, u32[]{:S(2)}) collective-permute-start(f32[4,136,256]{2,1,0:T(8,128)} %collective-permute-done.3.refs_3_), channel_id=1, source_target_pairs={{0,96},{32,0},{64,32},{96,64},{1,97},{33,1},{65,33},{97,65},{2,98}... | collective-permute-start | bytes 1671176 | tf_op jit(solution)/shard_map/ppermute | solution.py:568
  27.9 9.4 %collective-permute-done.2.refs_2_ = f32[4,136,256]{2,1,0:T(8,128)S(1)} collective-permute-done((f32[4,136,256]{2,1,0:T(8,128)S(1)}, f32[4,136,256]{2,1,0:T(8,128)S(1)}, u32[]{:S(2)}, u32[]{:S(2)}) %collective-permute-start.2) | collective-permute-done | bytes 557088 | tf_op jit(solution)/shard_map/ppermute | solution.py:567
  37.3 1.6 %collective-permute-done.7.refs_7_ = f32[4,136,256]{2,1,0:T(8,128)S(1)} collective-permute-done((f32[4,136,256]{2,1,0:T(8,128)}, f32[4,136,256]{2,1,0:T(8,128)S(1)}, u32[]{:S(2)}, u32[]{:S(2)}) %collective-permute-start.7) | collective-permute-done | bytes 557088 | tf_op jit(solution)/shard_map/ppermute | solution.py:566
  38.8 11.9 %collective-permute-done.5.refs_4_ = f32[4,136,256]{2,1,0:T(8,128)S(1)} collective-permute-done((f32[4,136,256]{2,1,0:T(8,128)}, f32[4,136,256]{2,1,0:T(8,128)S(1)}, u32[]{:S(2)}, u32[]{:S(2)}) %collective-permute-start.5) | collective-permute-done | bytes 557088 | tf_op jit(solution)/shard_map/ppermute | solution.py:568
  52.5 3.3 %left_slots.1 = f32[16,136,256]{2,1,0:T(8,128)} custom-call(s32[3]{0:T(128)S(1)} %pad_add_fusion.ids, s32[64]{0:T(128)S(1)} %copy-done.4, f32[4,136,256]{2,1,0:T(8,128)} %get-tuple-element.20.refs_0_, f32[4,136,256]{2,1,0:T(8,128)} %collective-permute-done.1.refs_1_, f32[4,136,256]{2,1,0:T(8,128)} %copy-done.14, ...), custom_call_target="tpu_custom_call" | custom-call | flops 15000000512 | bytes 4000000 | tf_op jit(solution)/shard_map/left_slots/pallas_call | solution.py:255
  55.8 1.1 all-to-all-done.1.slots
  56.9 1.5 %copy-done.11 = f32[16,152,256]{2,1,0:T(8,128)} copy-done((f32[16,152,256]{2,1,0:T(8,128)}, f32[16,152,256]{2,1,0:T(8,128)S(1)}, u32[]{:S(2)}) %copy-start.11) | copy-done | bytes 2490392
  58.4 6.4 %all-to-all-start = ((f32[16,136,256]{2,1,0:T(8,128)}), f32[16,136,256]{2,1,0:T(8,128)S(1)}, u32[]{:S(2)}, u32[]{:S(2)}) async-start(f32[16,136,256]{2,1,0:T(8,128)} %left_slots.1), calls=%async_computation | async-start | bytes 4456448 | tf_op jit(solution)/shard_map/all_to_all | solution.py:581
  64.8 5.3 %first_vector.1 = (bf16[4096,256]{1,0:T(8,128)(2,1)S(1)}, bf16[4096,256]{1,0:T(8,128)(2,1)S(1)}, bf16[256,4096]{1,0:T(8,128)(2,1)S(1)}, bf16[256,4096]{1,0:T(8,1...) custom-call(s32[3]{0:T(128)S(1)} %pad_add_fusion.ids, s32[8]{0:T(128)S(1)} %copy-done.3, ...), custom_call_target="tpu_custom_call" | custom-call | flops 1700000000 | bytes 12000000 | tf_op jit(solution)/shard_map/first_vector/pallas_call | solution.py:318
  70.1 1.3 copy-done
  71.5 1.4 copy-done.1
  72.8 1.4 copy-done.7
  74.2 1.3 copy-done.9
  75.6 16.0 %all-to-all-done.arrived = f32[16,136,256]{2,1,0:T(8,128)S(1)} async-done(((f32[16,136,256]{2,1,0:T(8,128)}), f32[16,136,256]{2,1,0:T(8,128)S(1)}, u32[]{:S(2)}, u32[]{:S(2)}) %all-to-all-start) | async-done | bytes 2228256 | tf_op jit(solution)/shard_map/all_to_all | solution.py:581
  91.6 5.1 %image_one.1 = (bf16[4096,256]{1,0:T(8,128)(2,1)S(1)}, bf16[4096,256]{1,0:T(8,128)(2,1)S(1)}, f32[256,256]{1,0:T(8,128)S(1)}) custom-call(f32[16,136,256]{2,1,0:T(8,128)S(1)} %all-to-all-done.arrived, bf16[256,4096]{1,0:T(8,128)(2,1)} %copy-done, bf16[256,4096]{1,0:T(8,128)(2,1)} %copy-done.1), custom_call_target="tpu_custom_call" | custom-call | flops 1700000000 | bytes 10000000 | tf_op jit(solution)/shard_map/image_one/pallas_call | solution.py:368
  96.7 5.7 %collective-permute-start.10 = (f32[256,256]{1,0:T(8,128)S(1)}, f32[256,256]{1,0:T(8,128)S(1)}, u32[]{:S(2)}, u32[]{:S(2)}) collective-permute-start(f32[256,256]{1,0:T(8,128)S(1)} %get-tuple-element.26.part_a), channel_id=1, source_target_pairs={{0,16},{16,0},{1,17},{17,1},{2,18},{18,2},{3,19},{19,3},{4,20},{20... | collective-permute-start | bytes 786440 | tf_op jit(solution)/shard_map/ppermute | solution.py:584
  102.3 1.2 collective-permute-done.10.part_b
  103.5 4.7 %image_two.1 = (f32[256,256]{1,0:T(8,128)S(1)}, f32[256,256]{1,0:T(8,128)S(1)}, f32[8,128]{1,0:T(8,128)S(1)}) custom-call(s32[3]{0:T(128)S(1)} %pad_add_fusion.ids, s32[8]{0:T(128)S(1)} %copy-done.3, s32[8]{0:T(128)S(1)} %collective-permute-done.rsector_other, s32[64]{0:T(128)S(1)} %copy-done.4, s32[32]{0:T(128)S(1)} %copy-done.5, s32[8]{0:T(128)S(1)} %copy-done.6, ...), custom_call_target="tpu_custom_call" | custom-call | flops 3300000000 | bytes 9000000 | tf_op jit(solution)/shard_map/image_two/pallas_call | solution.py:423
  108.6 1.2 collective-permute-done.11.part_b
  109.8 5.7 %image_three.1 = f32[16,24,256]{2,1,0:T(8,128)} custom-call(s32[3]{0:T(128)S(1)} %pad_add_fusion.ids, s32[8]{0:T(128)S(1)} %copy-done.3, s32[8]{0:T(128)S(1)} %collective-permute-done.rsector_other, s32[64]{0:T(128)S(1)} %copy-done.4, s32[32]{0:T(128)S(1)} %copy-done.5, s32[8]{0:T(128)S(1)} %copy-done.6, f32[256,256]{1,0:T(8,128)S(1)} %get-tuple-element.33.part_a, ...), custom_call_target="tpu_custom_call" | custom-call | flops 3300000000 | bytes 9000000 | tf_op jit(solution)/shard_map/image_three/pallas_call | solution.py:459
  115.5 3.7 %all-to-all-start.2 = ((f32[16,24,256]{2,1,0:T(8,128)}), f32[16,24,256]{2,1,0:T(8,128)S(1)}, u32[]{:S(2)}, u32[]{:S(2)}) async-start(f32[16,24,256]{2,1,0:T(8,128)} %image_three.1), calls=%async_computation.2 | async-start | bytes 786432 | tf_op jit(solution)/shard_map/all_to_all | solution.py:587
  119.2 9.2 %all-to-all-done.2.got = f32[16,24,256]{2,1,0:T(8,128)S(1)} async-done(((f32[16,24,256]{2,1,0:T(8,128)}), f32[16,24,256]{2,1,0:T(8,128)S(1)}, u32[]{:S(2)}, u32[]{:S(2)}) %all-to-all-start.2) | async-done | bytes 393248 | tf_op jit(solution)/shard_map/all_to_all | solution.py:587
  128.4 1.6 %collective-permute-start.16 = (f32[8,24,256]{2,1,0:T(8,128)S(1)}, f32[8,24,256]{2,1,0:T(8,128)S(1)}, u32[]{:S(2)}, u32[]{:S(2)}) collective-permute-start(f32[8,24,256]{2,1,0:T(8,128)S(1)} %constant_dynamic-slice_fusion), channel_id=1, source_target_pairs={{0,16},{16,0},{1,17},{17,1},{2,18},{18,2},{3,19},{19,3},{4,20},{20... | collective-permute-start | bytes 589832 | tf_op jit(solution)/shard_map/ppermute | solution.py:592
  132.5 2.0 %collective-permute-done.13 = f32[16,128]{1,0:T(8,128)S(1)} collective-permute-done((f32[16,128]{1,0:T(8,128)S(1)}, f32[16,128]{1,0:T(8,128)S(1)}, u32[]{:S(2)}, u32[]{:S(2)}) %collective-permute-start.13) | collective-permute-done | bytes 8224 | tf_op jit(solution)/shard_map/ppermute | solution.py:590
  135.2 1.2 collective-permute-start.15
  137.3 2.2 %finish.1 = (f32[8,16,256]{2,1,0:T(8,128)}, f32[1,1]{1,0:T(1,128)}) custom-call(s32[3]{0:T(128)S(1)} %pad_add_fusion.ids, s32[64]{0:T(128)S(1)} %copy-done.4, s32[8]{0:T(128)S(1)} %copy-done.3, s32[32]{0:T(128)S(1)} %copy-done.5, s32[8]{0:T(128)S(1)} %copy-done.6, f32[64,128]{1,0:T(8,128)S(1)} %pad_maximum_fusion.own_stats, ...), custom_call_target="tpu_custom_call" | custom-call | tf_op jit(solution)/shard_map/finish/pallas_call | solution.py:539
  (57 shorter events, 10.6 us)
Async XLA Ops:
  0.6 9.2 %copy-start.2 = (f32[8,256,16]{1,2,0:T(8,128)S(1)}, f32[8,256,16]{1,2,0:T(8,128)}, u32[]{:S(2)}) copy-start(f32[8,256,16]{1,2,0:T(8,128)} %param.8) | copy-start | bytes 393220
  0.6 9.9 %copy-start.3 = (s32[8]{0:T(128)S(1)}, s32[8]{0:T(128)}, u32[]{:S(2)}) copy-start(s32[8]{0:T(128)} %rsector.9) | copy-start | bytes 100
  0.6 10.0 %copy-start.12 = (s32[8,2]{0,1:T(2,128)S(1)}, s32[8,2]{0,1:T(2,128)}, u32[]{:S(2)}) copy-start(s32[8,2]{0,1:T(2,128)} %param.13) | copy-start | bytes 196
  3.6 3.4 %collective-permute-start.1 = (f32[4,136,256]{2,1,0:T(8,128)}, f32[4,136,256]{2,1,0:T(8,128)}, u32[]{:S(2)}, u32[]{:S(2)}) collective-permute-start(f32[4,136,256]{2,1,0:T(8,128)} %get-tuple-element.21), channel_id=1, source_target_pairs={{0,16},{16,0},{1,17},{17,1},{2,18},{18,2},{3,19},{19,3},{4,20},{20... | collective-permute-start | bytes 1671176 | tf_op jit(solution)/shard_map/ppermute | solution.py:565
  5.1 20.1 %collective-permute-start.4 = (f32[4,136,256]{2,1,0:T(8,128)}, f32[4,136,256]{2,1,0:T(8,128)}, u32[]{:S(2)}, u32[]{:S(2)}) collective-permute-start(f32[4,136,256]{2,1,0:T(8,128)} %get-tuple-element.20.refs_0_), channel_id=1, source_target_pairs={{0,32},{32,64},{64,96},{96,0},{1,33},{33,65},{65,97},{97,1},{2,34}... | collective-permute-start | bytes 1671176 | tf_op jit(solution)/shard_map/ppermute | solution.py:566
  7.0 18.2 %collective-permute-start.3 = (f32[4,136,256]{2,1,0:T(8,128)}, f32[4,136,256]{2,1,0:T(8,128)}, u32[]{:S(2)}, u32[]{:S(2)}) collective-permute-start(f32[4,136,256]{2,1,0:T(8,128)} %collective-permute-done.1.refs_1_), channel_id=1, source_target_pairs={{0,96},{32,0},{64,32},{96,64},{1,97},{33,1},{65,33},{97,65},{2,98}... | collective-permute-start | bytes 1671176 | tf_op jit(solution)/shard_map/ppermute | solution.py:567
  9.9 2.1 %collective-permute-start.9 = (f32[8,16,256]{2,1,0:T(8,128)S(1)}, f32[8,16,256]{2,1,0:T(8,128)S(1)}, u32[]{:S(2)}, u32[]{:S(2)}) collective-permute-start(f32[8,16,256]{2,1,0:T(8,128)S(1)} %bitcast.7), channel_id=1, source_target_pairs={{0,16},{16,0},{1,17},{17,1},{2,18},{18,2},{3,19},{19,3},{4,20},{20... | collective-permute-start | bytes 393224 | tf_op jit(solution)/shard_map/ppermute | solution.py:562
  10.5 1.1 collective-permute-start
  10.7 1.2 collective-permute-start.8
  15.9 7.8 %copy-start.13 = (f32[4,136,256]{2,1,0:T(8,128)S(1)}, f32[4,136,256]{2,1,0:T(8,128)}, u32[]{:S(2)}) copy-start(f32[4,136,256]{2,1,0:T(8,128)} %get-tuple-element.20.refs_0_) | copy-start | bytes 1671172
  15.9 36.6 %copy-start.4 = (s32[64]{0:T(128)S(1)}, s32[64]{0:T(128)}, u32[]{:S(2)}) copy-start(s32[64]{0:T(128)} %sector.7) | copy-start | bytes 772
  15.9 41.0 %all-to-all-start.1 = ((f32[16,152,256]{2,1,0:T(8,128)}), f32[16,152,256]{2,1,0:T(8,128)S(1)}, u32[]{:S(2)}, u32[]{:S(2)}) async-start(f32[16,152,256]{2,1,0:T(8,128)} %right_slots.1), calls=%async_computation.1 | async-start | bytes 4980736 | tf_op jit(solution)/shard_map/all_to_all | solution.py:575
  23.6 13.6 %collective-permute-start.2 = (f32[4,136,256]{2,1,0:T(8,128)S(1)}, f32[4,136,256]{2,1,0:T(8,128)S(1)}, u32[]{:S(2)}, u32[]{:S(2)}) collective-permute-start(f32[4,136,256]{2,1,0:T(8,128)S(1)} %copy-done.13), channel_id=1, source_target_pairs={{0,96},{32,0},{64,32},{96,64},{1,97},{33,1},{65,33},{97,65},{2,98}... | collective-permute-start | bytes 1671176 | tf_op jit(solution)/shard_map/ppermute | solution.py:567
  24.2 14.7 %collective-permute-start.7 = (f32[4,136,256]{2,1,0:T(8,128)}, f32[4,136,256]{2,1,0:T(8,128)S(1)}, u32[]{:S(2)}, u32[]{:S(2)}) collective-permute-start(f32[4,136,256]{2,1,0:T(8,128)} %collective-permute-done.1.refs_1_), channel_id=1, source_target_pairs={{0,32},{32,64},{64,96},{96,0},{1,33},{33,65},{65,97},{97,1},{2,34}... | collective-permute-start | bytes 1671176 | tf_op jit(solution)/shard_map/ppermute | solution.py:566
  25.2 25.6 %collective-permute-start.5 = (f32[4,136,256]{2,1,0:T(8,128)}, f32[4,136,256]{2,1,0:T(8,128)S(1)}, u32[]{:S(2)}, u32[]{:S(2)}) collective-permute-start(f32[4,136,256]{2,1,0:T(8,128)} %collective-permute-done.4.refs_6_), channel_id=1, source_target_pairs={{0,32},{32,64},{64,96},{96,0},{1,33},{33,65},{65,97},{97,1},{2,34}... | collective-permute-start | bytes 1671176 | tf_op jit(solution)/shard_map/ppermute | solution.py:568
  25.2 25.6 %collective-permute-start.6 = (f32[4,136,256]{2,1,0:T(8,128)}, f32[4,136,256]{2,1,0:T(8,128)S(1)}, u32[]{:S(2)}, u32[]{:S(2)}) collective-permute-start(f32[4,136,256]{2,1,0:T(8,128)} %collective-permute-done.3.refs_3_), channel_id=1, source_target_pairs={{0,96},{32,0},{64,32},{96,64},{1,97},{33,1},{65,33},{97,65},{2,98}... | collective-permute-start | bytes 1671176 | tf_op jit(solution)/shard_map/ppermute | solution.py:568
  37.3 13.5 %copy-start.14 = (f32[4,136,256]{2,1,0:T(8,128)}, f32[4,136,256]{2,1,0:T(8,128)S(1)}, u32[]{:S(2)}) copy-start(f32[4,136,256]{2,1,0:T(8,128)S(1)} %collective-permute-done.2.refs_2_) | copy-start | bytes 1671172
  38.8 11.9 %copy-start.15 = (f32[4,136,256]{2,1,0:T(8,128)}, f32[4,136,256]{2,1,0:T(8,128)S(1)}, u32[]{:S(2)}) copy-start(f32[4,136,256]{2,1,0:T(8,128)S(1)} %collective-permute-done.7.refs_7_) | copy-start | bytes 1671172
  55.8 9.0 %copy-start.5 = (s32[32]{0:T(128)S(1)}, s32[32]{0:T(128)}, u32[]{:S(2)}) copy-start(s32[32]{0:T(128)} %lsize.7) | copy-start | bytes 388
  55.8 9.0 %copy-start.6 = (s32[8]{0:T(128)S(1)}, s32[8]{0:T(128)}, u32[]{:S(2)}) copy-start(s32[8]{0:T(128)} %rsize.7) | copy-start | bytes 100
  56.9 1.5 %copy-start.11 = (f32[16,152,256]{2,1,0:T(8,128)}, f32[16,152,256]{2,1,0:T(8,128)S(1)}, u32[]{:S(2)}) copy-start(f32[16,152,256]{2,1,0:T(8,128)S(1)} %all-to-all-done.1.slots) | copy-start | bytes 7471108
  58.4 33.2 %all-to-all-start = ((f32[16,136,256]{2,1,0:T(8,128)}), f32[16,136,256]{2,1,0:T(8,128)S(1)}, u32[]{:S(2)}, u32[]{:S(2)}) async-start(f32[16,136,256]{2,1,0:T(8,128)} %left_slots.1), calls=%async_computation | async-start | bytes 4456448 | tf_op jit(solution)/shard_map/all_to_all | solution.py:581
  91.6 11.9 %copy-start.8 = (bf16[4096,256]{1,0:T(8,128)(2,1)S(1)}, bf16[4096,256]{1,0:T(8,128)(2,1)}, u32[]{:S(2)}) copy-start(bf16[4096,256]{1,0:T(8,128)(2,1)} %copy-done.7) | copy-start | bytes 6291460
  91.6 11.9 %copy-start.10 = (bf16[4096,256]{1,0:T(8,128)(2,1)S(1)}, bf16[4096,256]{1,0:T(8,128)(2,1)}, u32[]{:S(2)}) copy-start(bf16[4096,256]{1,0:T(8,128)(2,1)} %copy-done.9) | copy-start | bytes 6291460
  96.7 6.8 %collective-permute-start.10 = (f32[256,256]{1,0:T(8,128)S(1)}, f32[256,256]{1,0:T(8,128)S(1)}, u32[]{:S(2)}, u32[]{:S(2)}) collective-permute-start(f32[256,256]{1,0:T(8,128)S(1)} %get-tuple-element.26.part_a), channel_id=1, source_target_pairs={{0,16},{16,0},{1,17},{17,1},{2,18},{18,2},{3,19},{19,3},{4,20},{20... | collective-permute-start | bytes 786440 | tf_op jit(solution)/shard_map/ppermute | solution.py:584
  108.2 1.6 %collective-permute-start.11 = (f32[256,256]{1,0:T(8,128)S(1)}, f32[256,256]{1,0:T(8,128)S(1)}, u32[]{:S(2)}, u32[]{:S(2)}) collective-permute-start(f32[256,256]{1,0:T(8,128)S(1)} %get-tuple-element.33.part_a), channel_id=1, source_target_pairs={{0,16},{16,0},{1,17},{17,1},{2,18},{18,2},{3,19},{19,3},{4,20},{20... | collective-permute-start | bytes 786440 | tf_op jit(solution)/shard_map/ppermute | solution.py:585
  115.5 12.9 %all-to-all-start.2 = ((f32[16,24,256]{2,1,0:T(8,128)}), f32[16,24,256]{2,1,0:T(8,128)S(1)}, u32[]{:S(2)}, u32[]{:S(2)}) async-start(f32[16,24,256]{2,1,0:T(8,128)} %image_three.1), calls=%async_computation.2 | async-start | bytes 786432 | tf_op jit(solution)/shard_map/all_to_all | solution.py:587
  128.4 8.9 %collective-permute-start.16 = (f32[8,24,256]{2,1,0:T(8,128)S(1)}, f32[8,24,256]{2,1,0:T(8,128)S(1)}, u32[]{:S(2)}, u32[]{:S(2)}) collective-permute-start(f32[8,24,256]{2,1,0:T(8,128)S(1)} %constant_dynamic-slice_fusion), channel_id=1, source_target_pairs={{0,16},{16,0},{1,17},{17,1},{2,18},{18,2},{3,19},{19,3},{4,20},{20... | collective-permute-start | bytes 589832 | tf_op jit(solution)/shard_map/ppermute | solution.py:592
  130.0 2.5 %collective-permute-start.14 = (f32[16,128]{1,0:T(8,128)S(1)}, f32[16,128]{1,0:T(8,128)S(1)}, u32[]{:S(2)}, u32[]{:S(2)}) collective-permute-start(f32[16,128]{1,0:T(8,128)S(1)} %bitcast.10), channel_id=1, source_target_pairs={{0,96},{32,0},{64,32},{96,64},{1,97},{33,1},{65,33},{97,65},{2,98}... | collective-permute-start | bytes 24584 | tf_op jit(solution)/shard_map/ppermute | solution.py:590
  130.5 4.0 %collective-permute-start.13 = (f32[16,128]{1,0:T(8,128)S(1)}, f32[16,128]{1,0:T(8,128)S(1)}, u32[]{:S(2)}, u32[]{:S(2)}) collective-permute-start(f32[16,128]{1,0:T(8,128)S(1)} %bitcast.11), channel_id=1, source_target_pairs={{0,64},{32,96},{64,0},{96,32},{1,65},{33,97},{65,1},{97,33},{2,66}... | collective-permute-start | bytes 24584 | tf_op jit(solution)/shard_map/ppermute | solution.py:590
  130.6 4.6 %collective-permute-start.12 = (f32[16,128]{1,0:T(8,128)S(1)}, f32[16,128]{1,0:T(8,128)S(1)}, u32[]{:S(2)}, u32[]{:S(2)}) collective-permute-start(f32[16,128]{1,0:T(8,128)S(1)} %bitcast.12), channel_id=1, source_target_pairs={{0,32},{32,64},{64,96},{96,0},{1,33},{33,65},{65,97},{97,1},{2,34}... | collective-permute-start | bytes 24584 | tf_op jit(solution)/shard_map/ppermute | solution.py:590
  135.2 2.1 %collective-permute-start.15 = (f32[64,128]{1,0:T(8,128)S(1)}, f32[64,128]{1,0:T(8,128)S(1)}, u32[]{:S(2)}, u32[]{:S(2)}) collective-permute-start(f32[64,128]{1,0:T(8,128)S(1)} %pad_maximum_fusion.own_stats), channel_id=1, source_target_pairs={{0,16},{16,0},{1,17},{17,1},{2,18},{18,2},{3,19},{19,3},{4,20},{20... | collective-permute-start | bytes 98312 | tf_op jit(solution)/shard_map/ppermute | solution.py:594
  (6 other events, 7.2 us)

commit v7 on v6

--- a/solution.py
+++ b/solution.py
@@ -6,11 +6,13 @@
 from jax.sharding import Mesh, PartitionSpec as P
 
 ITERS = 2
+LEFT_FLOPS = 15_000_000_000
 TILE = 256
 HALF = 128
 TERMS = 16
-LEFT_ROWS = 136
-SLOT_ROWS = 152
+FOLDED = 264
+THIN = 32
+SLOT = THIN + FOLDED
 COL = ("x", "z")
 ALL = ("y", "c", "x", "z")
 SWAP = [(0, 1), (1, 0)]
@@ -59,9 +61,19 @@
     return fold, tile[:HALF, HALF:], diag
 
 
-def diag_rows(diag):
-    wide = jnp.concatenate([diag, jnp.zeros((1, HALF), f32)], axis=1)
-    return jnp.broadcast_to(wide, (8, TILE))
+def put_folded(dst, at, tile):
+    fold, corner, diag = fold_tile(tile)
+    dst[at, :HALF, :] = fold
+    dst[at, HALF:TILE, :] = corner
+    dst[at, TILE:, :] = jnp.broadcast_to(diag, (FOLDED - TILE, HALF))
+
+
+def get_folded(src, at, row):
+    return unfold_tile(
+        src[at, row : row + HALF, :],
+        src[at, row + HALF : row + TILE, :],
+        src[at, row + TILE : row + TILE + 1, :],
+    )
 
 
 def unfold_tile(fold, corner, diag):
@@ -100,13 +112,6 @@
     return jnp.where(j == lane, value, stats)
 
 
-def put_folded(dst, at, row, tile):
-    fold, corner, diag = fold_tile(tile)
-    dst[at, row : row + HALF, :HALF] = fold
-    dst[at, row : row + HALF, HALF:] = corner
-    dst[at, row + HALF : row + HALF + 8, :] = diag_rows(diag)
-
-
 def fold_left_body(ids, src, keep, give, tiles, folded, sem_in, sem_out):
     def fetch(t, n):
         term = ids[1] if t else 1 - ids[1]
@@ -123,7 +128,7 @@
         fetch(t, n).start()
     for t, n in order:
         fetch(t, n).wait()
-        put_folded(folded, 4 * t + n, 0, tiles[4 * t + n])
+        put_folded(folded, 4 * t + n, tiles[4 * t + n])
         store(t, n).start()
     for t, n in order:
         store(t, n).wait()
@@ -134,10 +139,10 @@
         fold_left_body,
         in_specs=[smem(), hbm()],
         out_specs=[hbm(), hbm()],
-        out_shape=[pltpu.HBM((4, LEFT_ROWS, TILE), f32)] * 2,
+        out_shape=[pltpu.HBM((4, FOLDED, HALF), f32)] * 2,
         scratch_shapes=[
             pltpu.VMEM((8, TILE, TILE), f32),
-            pltpu.VMEM((8, LEFT_ROWS, TILE), f32),
+            pltpu.VMEM((8, FOLDED, HALF), f32),
             pltpu.SemaphoreType.DMA((8,)),
             pltpu.SemaphoreType.DMA((8,)),
         ],
@@ -153,33 +158,46 @@
 
 def right_slots_body(
     ids, rsector, rsector_other, on, on_other, thin, thin_other, right_env,
-    out, right, dst, sem_in, sem_out,
+    out, right, folded, cols, sem_in, sem_out, sem_thin,
 ):
     def fetch(sector):
         return pltpu.make_async_copy(
             right_env.at[sector, ids[1]], right.at[sector], sem_in.at[sector]
         )
 
-    def store(slot):
-        return pltpu.make_async_copy(dst.at[slot], out.at[slot], sem_out.at[slot])
+    def store_thin(slot):
+        return pltpu.make_async_copy(
+            cols.at[slot], out.at[slot, pl.ds(0, THIN), :], sem_thin.at[slot]
+        )
+
+    def store(slot, sector):
+        return pltpu.make_async_copy(
+            folded.at[sector], out.at[slot, pl.ds(THIN, FOLDED), :], sem_out.at[slot]
+        )
 
     for sector in range(8):
         fetch(sector).start()
     for slot in range(TERMS):
         here = slot // 8 == ids[1]
-        dst[slot, :16, :] = jnp.where(here, thin[slot % 8], thin_other[slot % 8])
+        block = jnp.where(here, thin[slot % 8], thin_other[slot % 8])
+        cols[slot, :16, :] = block[:, :HALF]
+        cols[slot, 16:, :] = block[:, HALF:]
+        store_thin(slot).start()
+    folded[8] = jnp.zeros((FOLDED, HALF), f32)
     for sector in range(8):
         fetch(sector).wait()
+        put_folded(folded, sector, right[sector])
 
     def one(slot, carry):
         here = slot // 8 == ids[1]
-        weight = jnp.where(here, on[slot % 8, ids[1]], on_other[slot % 8, ids[1]]).astype(f32)
-        put_folded(dst, slot, 16, right[sector_of(ids, rsector, rsector_other, slot)] * weight)
-        store(slot).start()
+        weight = jnp.where(here, on[slot % 8, ids[1]], on_other[slot % 8, ids[1]])
+        sector = sector_of(ids, rsector, rsector_other, slot)
+        store(slot, jnp.where(weight == 0, 8, sector)).start()
         return carry
 
     def finished(slot, carry):
-        store(slot).wait()
+        store_thin(slot).wait()
+        store(slot, 0).wait()
         return carry
 
     lax.fori_loop(0, TERMS, one, 0)
@@ -187,16 +205,17 @@
 
 
 def right_slots(ids, rsector, rsector_other, on, on_other, thin, thin_other, right_env):
-    slots = (TERMS, SLOT_ROWS, TILE)
     return pl.pallas_call(
         right_slots_body,
         in_specs=[smem()] * 5 + [vmem()] * 2 + [hbm()],
         out_specs=hbm(),
-        out_shape=pltpu.HBM(slots, f32),
+        out_shape=pltpu.HBM((TERMS, SLOT, HALF), f32),
         scratch_shapes=[
             pltpu.VMEM((8, TILE, TILE), f32),
-            pltpu.VMEM(slots, f32),
+            pltpu.VMEM((9, FOLDED, HALF), f32),
+            pltpu.VMEM((TERMS, THIN, HALF), f32),
             pltpu.SemaphoreType.DMA((8,)),
+            pltpu.SemaphoreType.DMA((TERMS,)),
             pltpu.SemaphoreType.DMA((TERMS,)),
         ],
         compiler_params=params(10),
@@ -208,13 +227,10 @@
 def left_slots_body(ids, left_sector, *refs):
     mine, theirs = refs[:2]
     above, far, below = refs[2:4], refs[4:6], refs[6:8]
-    out, dst, sem_in, sem_out = refs[8:]
-
-    def fetch(src, slot):
-        return pltpu.make_async_copy(src, dst.at[slot], sem_in.at[slot])
-
-    def store(slot):
-        return pltpu.make_async_copy(dst.at[slot], out.at[slot], sem_out.at[slot])
+    out, sem = refs[8:]
+
+    def store(src, slot):
+        return pltpu.make_async_copy(src, out.at[slot], sem.at[slot])
 
     def start(slot, carry):
         sector = left_sector[ids[0] * 16 + slot]
@@ -232,40 +248,29 @@
 
             @pl.when(case)
             def _():
-                fetch(src.at[at], slot).start()
+                store(src.at[at], slot).start()
 
         return carry
 
-    def forward(slot, carry):
-        fetch(mine.at[0], slot).wait()
-        store(slot).start()
+    def finished(slot, carry):
+        store(mine.at[0], slot).wait()
         return carry
 
-    def finished(slot, carry):
-        store(slot).wait()
-        return carry
-
     lax.fori_loop(0, TERMS, start, 0)
-    lax.fori_loop(0, TERMS, forward, 0)
     lax.fori_loop(0, TERMS, finished, 0)
 
 
 def left_slots(ids, left_sector, pieces):
-    slots = (TERMS, LEFT_ROWS, TILE)
     return pl.pallas_call(
         left_slots_body,
-        in_specs=[smem(), smem()] + [hbm()] * 8,
+        in_specs=[smem(), smem()] + [vmem()] * 8,
         out_specs=hbm(),
-        out_shape=pltpu.HBM(slots, f32),
-        scratch_shapes=[
-            pltpu.VMEM(slots, f32),
-            pltpu.SemaphoreType.DMA((TERMS,)),
-            pltpu.SemaphoreType.DMA((TERMS,)),
-        ],
-        compiler_params=params(6),
-        cost_estimate=cost(15_000_000_000, 4_000_000),
+        out_shape=pltpu.HBM((TERMS, FOLDED, HALF), f32),
+        scratch_shapes=[pltpu.SemaphoreType.DMA((TERMS,))],
+        compiler_params=params(8),
+        cost_estimate=cost(LEFT_FLOPS, 4_000_000),
         name="left_slots",
-    )(ids, left_sector, *[in_hbm(x) for x in pieces])
+    )(ids, left_sector, *pieces)
 
 
 def live_sizes(ids, rsector, rsector_other, left_sector, left_size, right_size):
@@ -292,15 +297,17 @@
         fetch(n).start()
     for n in range(TERMS):
         fetch(n).wait()
-        full = unfold_tile(
-            arrived[n, 16 : 16 + HALF, :HALF],
-            arrived[n, 16 : 16 + HALF, HALF:],
-            arrived[n, 16 + HALF : 17 + HALF, :HALF],
-        )
+        full = get_folded(arrived, n, THIN)
         hi, lo = split(full)
         r_hi[n * TILE : (n + 1) * TILE, :] = hi
         r_lo[n * TILE : (n + 1) * TILE, :] = lo
-    block = jnp.concatenate([arrived[n, :16, :] for n in range(TERMS)], axis=0)
+    block = jnp.concatenate(
+        [
+            jnp.concatenate([arrived[n, :16, :], arrived[n, 16:THIN, :]], axis=1)
+            for n in range(TERMS)
+        ],
+        axis=0,
+    )
     start = jnp.where(mask_of(live_right, live_left), block, 0.0)
     norm = jnp.sqrt(total(start * start))
     vec = start * inverse(norm)
@@ -328,7 +335,7 @@
             jax.ShapeDtypeStruct((8, HALF), f32),
         ],
         scratch_shapes=[
-            pltpu.VMEM((TERMS, SLOT_ROWS, TILE), f32),
+            pltpu.VMEM((TERMS, SLOT, HALF), f32),
             pltpu.SemaphoreType.DMA((TERMS,)),
         ],
         compiler_params=params(10),
@@ -337,7 +344,9 @@
     )(*scalars, in_hbm(slots))
 
 
-def image_one_body(arrived, m_hi, m_lo, l_hi, l_lo, part, here, sem):
+def image_one_body(
+    arrived, m_hi, m_lo, r_hi_in, r_lo_in, l_hi, l_lo, part, r_hi, r_lo, here, sem, sem_r
+):
     chunk = TERMS // 4
 
     def fetch(p, c):
@@ -345,43 +354,46 @@
         src = (m_hi, m_lo)[p]
         return pltpu.make_async_copy(src.at[:, cols], here.at[p, :, cols], sem.at[p, c])
 
+    def fetch_right(p):
+        src, dst = ((r_hi_in, r_hi), (r_lo_in, r_lo))[p]
+        return pltpu.make_async_copy(src, dst, sem_r.at[p])
+
     for c in range(4):
         for p in range(2):
             fetch(p, c).start()
-    for n in range(TERMS):
-        full = unfold_tile(
-            arrived[n, :HALF, :HALF], arrived[n, :HALF, HALF:], arrived[n, HALF : HALF + 1, :HALF]
-        )
-        hi, lo = split(full)
-        l_hi[n * TILE : (n + 1) * TILE, :] = hi
-        l_lo[n * TILE : (n + 1) * TILE, :] = lo
+    for p in range(2):
+        fetch_right(p).start()
     acc = jnp.zeros((TILE, TILE), f32)
     for c in range(4):
+        for n in range(c * chunk, (c + 1) * chunk):
+            hi, lo = split(get_folded(arrived, n, 0))
+            l_hi[n * TILE : (n + 1) * TILE, :] = hi
+            l_lo[n * TILE : (n + 1) * TILE, :] = lo
         for p in range(2):
             fetch(p, c).wait()
         cols = pl.ds(c * chunk * TILE, chunk * TILE)
         acc = acc + dot3(here[0, :, cols], here[1, :, cols], l_hi[cols, :], l_lo[cols, :])
     part[...] = acc
-
-
-def image_one(arrived, m_hi, m_lo):
+    for p in range(2):
+        fetch_right(p).wait()
+
+
+def image_one(arrived, m_hi, m_lo, r_hi, r_lo):
+    stack = jax.ShapeDtypeStruct((TERMS * TILE, TILE), bf16)
     return pl.pallas_call(
         image_one_body,
-        in_specs=[vmem(), hbm(), hbm()],
-        out_specs=[vmem()] * 3,
-        out_shape=[
-            jax.ShapeDtypeStruct((TERMS * TILE, TILE), bf16),
-            jax.ShapeDtypeStruct((TERMS * TILE, TILE), bf16),
-            jax.ShapeDtypeStruct((TILE, TILE), f32),
-        ],
+        in_specs=[vmem()] + [hbm()] * 4,
+        out_specs=[vmem()] * 5,
+        out_shape=[stack, stack, jax.ShapeDtypeStruct((TILE, TILE), f32), stack, stack],
         scratch_shapes=[
             pltpu.VMEM((2, TILE, TERMS * TILE), bf16),
             pltpu.SemaphoreType.DMA((2, 4)),
+            pltpu.SemaphoreType.DMA((2,)),
         ],
         compiler_params=params(10),
         cost_estimate=cost(1_700_000_000, 10_000_000),
         name="image_one",
-    )(arrived, in_hbm(m_hi), in_hbm(m_lo))
+    )(arrived, in_hbm(m_hi), in_hbm(m_lo), in_hbm(r_hi), in_hbm(r_lo))
 
 
 def lanczos(image, last, before, beta):
@@ -579,7 +591,7 @@
     pieces = [mine, theirs] + above + far + below
     left_sent = left_slots(ids, left_sector, pieces)
     left_arrived = lax.all_to_all(left_sent, COL, 0, 0, tiled=True)
-    l_hi, l_lo, part = image_one(left_arrived, m_hi, m_lo)
+    l_hi, l_lo, part, r_hi, r_lo = image_one(left_arrived, m_hi, m_lo, r_hi, r_lo)
     stacks = (r_hi, r_lo, l_hi, l_lo)
     part, q2, stats = image_two(scalars, part, lax.ppermute(part, "c", SWAP), q1, stats, stacks)
     sent = image_three(scalars, part, lax.ppermute(part, "c", SWAP), q1, q2, stats, stacks)

time: 140 us -> 138 us (0.986)
  local copies, waits for them, and re-layouts: 8.76 us -> 5.59 us
  waiting for transfers between devices: 57.5 us -> 59 us
    unnamed x37 -> x23, local copies, waits for them, and re-layouts: 8.74 us -> 5.57 us
    all_to_all x1, waiting for transfers between devices: 1.1 us -> 4.18 us  [local(): arrived = lax.all_to_all(slots, COL, 0, 0, tiled=True)]
  transfers between devices with their start and end apart: 20 -> 20, of which waited for: 15 -> 15; matrix products, arithmetic and copies ran while one was open for 0% -> 0% of each run, Pallas kernels for 9% -> 8%
where the time goes in v7:
time: 138 us
  waiting for transfers between devices  59 us (43%)
  starting transfers between devices  38.7 us (28%)
  Pallas kernels  33.3 us (24%)
  local copies, waits for them, and re-layouts  5.59 us (4%)
    all_to_all x1, waiting for transfers between devices, local(): left_arrived = lax.all_to_all(left_sent, COL, 0, 0, tiled=True)  15.4 us
    ppermute x2, waiting for transfers between devices, local(): far = [lax.ppermute(below[0], 'y', UP), lax.ppermute(above[1], 'y', DOWN)]  11.6 us
    all_to_all x1, waiting for transfers between devices, local(): got = lax.all_to_all(sent, COL, 0, 0, tiled=True)  9.23 us
    ppermute x2, waiting for transfers between devices, local(): above = [lax.ppermute(x, 'y', DOWN) for x in (mine, theirs)]  9.15 us
    all_to_all x1, starting transfers between devices, local(): arrived = lax.all_to_all(slots, COL, 0, 0, tiled=True)  7.79 us
    pallas_call x1, Pallas kernels, image_one(): pl.pallas_call(image_one_body, in_specs=[vmem()] + [hbm()] * 4, out_specs...  6.31 us
    ppermute x2, starting transfers between devices, local(): lax.ppermute(part, 'c', SWAP)  5.99 us
    all_to_all x1, starting transfers between devices, local(): left_arrived = lax.all_to_all(left_sent, COL, 0, 0, tiled=True)  5.95 us
  transfers between devices with their start and end apart: 20, of which 15 were waited for; matrix products, arithmetic and copies ran while one was open for 0% of the time, Pallas kernels for 8%

profile of v7, /device:TPU:1, one launch (start us, length us, event | category | flops | bytes accessed | tf_op | source)
XLA Modules:
  0.0 137.7 jit_solution(18344305332036065195)
XLA Ops:
  0.7 2.9 %fold_left.1 = (f32[4,264,128]{2,1,0:T(8,128)}, f32[4,264,128]{2,1,0:T(8,128)}) custom-call(s32[3]{0:T(128)S(1)} %pad_add_fusion.ids, f32[4,2,256,256]{3,2,1,0:T(8,128)} %src.1), custom_call_target="tpu_custom_call" | custom-call | flops 1000000 | bytes 4000000 | tf_op jit(solution)/shard_map/fold_left/pallas_call | solution.py:138
  3.6 1.5 %collective-permute-start.1 = (f32[4,264,128]{2,1,0:T(8,128)}, f32[4,264,128]{2,1,0:T(8,128)S(1)}, u32[]{:S(2)}, u32[]{:S(2)}) collective-permute-start(f32[4,264,128]{2,1,0:T(8,128)} %get-tuple-element.23), channel_id=1, source_target_pairs={{0,16},{16,0},{1,17},{17,1},{2,18},{18,2},{3,19},{19,3},{4,20},{20... | collective-permute-start | bytes 1622024 | tf_op jit(solution)/shard_map/ppermute | solution.py:577
  5.1 1.4 %collective-permute-start.4 = (f32[4,264,128]{2,1,0:T(8,128)}, f32[4,264,128]{2,1,0:T(8,128)S(1)}, u32[]{:S(2)}, u32[]{:S(2)}) collective-permute-start(f32[4,264,128]{2,1,0:T(8,128)} %get-tuple-element.22.refs_0_), channel_id=1, source_target_pairs={{0,32},{32,64},{64,96},{96,0},{1,33},{33,65},{65,97},{97,1},{2,34}... | collective-permute-start | bytes 1622024 | tf_op jit(solution)/shard_map/ppermute | solution.py:578
  6.9 2.8 %collective-permute-start.3 = (f32[4,264,128]{2,1,0:T(8,128)S(1)}, f32[4,264,128]{2,1,0:T(8,128)S(1)}, u32[]{:S(2)}, u32[]{:S(2)}) collective-permute-start(f32[4,264,128]{2,1,0:T(8,128)S(1)} %collective-permute-done.1.refs_1_), channel_id=1, source_target_pairs={{0,96},{32,0},{64,32},{96,64},{1,97},{33,1},{65,33},{97,65},{2,98}... | collective-permute-start | bytes 1622024 | tf_op jit(solution)/shard_map/ppermute | solution.py:579
  11.8 4.1 %right_slots.1 = f32[16,296,128]{2,1,0:T(8,128)} custom-call(s32[3]{0:T(128)S(1)} %pad_add_fusion.ids, s32[8]{0:T(128)S(1)} %copy-done.5, s32[8]{0:T(128)S(1)} %collective-permute-done.rsector_other, s32[8,2]{1,0:T(8,128)S(1)} %copy.11.on, s32[8,2]{1,0:T(8,128)S(1)} %collective-permute-done.8.on_other, f32[8,16,256]{2,1,0:T(8,128)S(1)} %bitcast.8, ...), custom_call_target="tpu_custom_call" | custom-call | flops 4000000 | bytes 10000000 | tf_op jit(solution)/shard_map/right_slots/pallas_call | solution.py:208
  15.9 7.8 %all-to-all-start.1 = ((f32[16,296,128]{2,1,0:T(8,128)}), f32[16,296,128]{2,1,0:T(8,128)}, u32[]{:S(2)}, u32[]{:S(2)}) async-start(f32[16,296,128]{2,1,0:T(8,128)} %right_slots.1), calls=%async_computation.1 | async-start | bytes 4849664 | tf_op jit(solution)/shard_map/all_to_all | solution.py:587
  25.3 2.6 %collective-permute-start.6 = (f32[4,264,128]{2,1,0:T(8,128)S(1)}, f32[4,264,128]{2,1,0:T(8,128)S(1)}, u32[]{:S(2)}, u32[]{:S(2)}) collective-permute-start(f32[4,264,128]{2,1,0:T(8,128)S(1)} %collective-permute-done.3.refs_3_), channel_id=1, source_target_pairs={{0,96},{32,0},{64,32},{96,64},{1,97},{33,1},{65,33},{97,65},{2,98}... | collective-permute-start | bytes 1622024 | tf_op jit(solution)/shard_map/ppermute | solution.py:580
  27.9 9.2 %collective-permute-done.2.refs_2_ = f32[4,264,128]{2,1,0:T(8,128)S(1)} collective-permute-done((f32[4,264,128]{2,1,0:T(8,128)S(1)}, f32[4,264,128]{2,1,0:T(8,128)S(1)}, u32[]{:S(2)}, u32[]{:S(2)}) %collective-permute-start.2) | collective-permute-done | bytes 540704 | tf_op jit(solution)/shard_map/ppermute | solution.py:579
  37.1 1.4 collective-permute-done.7.refs_7_
  38.4 11.6 %collective-permute-done.5.refs_4_ = f32[4,264,128]{2,1,0:T(8,128)S(1)} collective-permute-done((f32[4,264,128]{2,1,0:T(8,128)S(1)}, f32[4,264,128]{2,1,0:T(8,128)S(1)}, u32[]{:S(2)}, u32[]{:S(2)}) %collective-permute-start.5) | collective-permute-done | bytes 540704 | tf_op jit(solution)/shard_map/ppermute | solution.py:580
  50.0 2.1 %left_slots.1 = f32[16,264,128]{2,1,0:T(8,128)} custom-call(s32[3]{0:T(128)S(1)} %pad_add_fusion.ids, s32[64]{0:T(128)S(1)} %copy-done.6, f32[4,264,128]{2,1,0:T(8,128)S(1)} %copy-done.9, f32[4,264,128]{2,1,0:T(8,128)S(1)} %collective-permute-done.1.refs_1_, f32[4,264,128]{2,1,0:T(8,128)S(1)} %collective-permute-done.2.refs_2_, ...), custom_call_target="tpu_custom_call" | custom-call | flops 15000000512 | bytes 4000000 | tf_op jit(solution)/shard_map/left_slots/pallas_call | solution.py:264
  52.2 4.2 %all-to-all-done.1.slots = f32[16,296,128]{2,1,0:T(8,128)} async-done(((f32[16,296,128]{2,1,0:T(8,128)}), f32[16,296,128]{2,1,0:T(8,128)}, u32[]{:S(2)}, u32[]{:S(2)}) %all-to-all-start.1) | async-done | bytes 2424864 | tf_op jit(solution)/shard_map/all_to_all | solution.py:587
  56.4 5.9 %all-to-all-start = ((f32[16,264,128]{2,1,0:T(8,128)}), f32[16,264,128]{2,1,0:T(8,128)S(1)}, u32[]{:S(2)}, u32[]{:S(2)}) async-start(f32[16,264,128]{2,1,0:T(8,128)} %left_slots.1), calls=%async_computation | async-start | bytes 4325376 | tf_op jit(solution)/shard_map/all_to_all | solution.py:593
  62.3 5.3 %first_vector.1 = (bf16[4096,256]{1,0:T(8,128)(2,1)S(1)}, bf16[4096,256]{1,0:T(8,128)(2,1)S(1)}, bf16[256,4096]{1,0:T(8,128)(2,1)S(1)}, bf16[256,4096]{1,0:T(8,1...) custom-call(s32[3]{0:T(128)S(1)} %pad_add_fusion.ids, s32[8]{0:T(128)S(1)} %copy-done.5, ...), custom_call_target="tpu_custom_call" | custom-call | flops 1700000000 | bytes 12000000 | tf_op jit(solution)/shard_map/first_vector/pallas_call | solution.py:325
  67.7 1.4 %copy-done = bf16[4096,256]{1,0:T(8,128)(2,1)} copy-done((bf16[4096,256]{1,0:T(8,128)(2,1)}, bf16[4096,256]{1,0:T(8,128)(2,1)S(1)}, u32[]{:S(2)}) %copy-start) | copy-done | bytes 2097176
  69.1 1.4 copy-done.1
  70.4 1.3 copy-done.2
  71.8 1.4 copy-done.3
  73.1 15.4 %all-to-all-done.arrived = f32[16,264,128]{2,1,0:T(8,128)S(1)} async-done(((f32[16,264,128]{2,1,0:T(8,128)}), f32[16,264,128]{2,1,0:T(8,128)S(1)}, u32[]{:S(2)}, u32[]{:S(2)}) %all-to-all-start) | async-done | bytes 2162720 | tf_op jit(solution)/shard_map/all_to_all | solution.py:593
  88.5 6.3 %image_one.1 = (bf16[4096,256]{1,0:T(8,128)(2,1)S(1)}, bf16[4096,256]{1,0:T(8,128)(2,1)S(1)}, f32[256,256]{1,0:T(8,128)S(1)}, bf16[4096,256]{1,0:T(8,128)(2,1)S(1)}, bf16[4096,256]{1,0:T(8,128)(2,1)S(1)}) custom-call(f32[16,264,128]{2,1,0:T(8,128)S(1)} %all-to-all-done.arrived, bf16[256,4096]{1,0:T(8,128)(2,1)} %copy-done.2, bf16[256,4096]{1,0:T(8,128)(2,1)} %copy-done.3, ...), custom_call_target="tpu_custom_call" | custom-call | flops 1700000000 | bytes 10000000 | tf_op jit(solution)/shard_map/image_one/pallas_call | solution.py:383
  94.8 5.5 %collective-permute-start.10 = (f32[256,256]{1,0:T(8,128)S(1)}, f32[256,256]{1,0:T(8,128)S(1)}, u32[]{:S(2)}, u32[]{:S(2)}) collective-permute-start(f32[256,256]{1,0:T(8,128)S(1)} %get-tuple-element.30.part_a), channel_id=1, source_target_pairs={{0,16},{16,0},{1,17},{17,1},{2,18},{18,2},{3,19},{19,3},{4,20},{20... | collective-permute-start | bytes 786440 | tf_op jit(solution)/shard_map/ppermute | solution.py:596
  100.3 1.2 collective-permute-done.10.part_b
  101.5 4.7 %image_two.1 = (f32[256,256]{1,0:T(8,128)S(1)}, f32[256,256]{1,0:T(8,128)S(1)}, f32[8,128]{1,0:T(8,128)S(1)}) custom-call(s32[3]{0:T(128)S(1)} %pad_add_fusion.ids, s32[8]{0:T(128)S(1)} %copy-done.5, s32[8]{0:T(128)S(1)} %collective-permute-done.rsector_other, s32[64]{0:T(128)S(1)} %copy-done.6, s32[32]{0:T(128)S(1)} %copy-done.7, s32[8]{0:T(128)S(1)} %copy-done.8, ...), custom_call_target="tpu_custom_call" | custom-call | flops 3300000000 | bytes 9000000 | tf_op jit(solution)/shard_map/image_two/pallas_call | solution.py:435
  106.7 1.2 collective-permute-done.11.part_b
  107.8 5.7 %image_three.1 = f32[16,24,256]{2,1,0:T(8,128)} custom-call(s32[3]{0:T(128)S(1)} %pad_add_fusion.ids, s32[8]{0:T(128)S(1)} %copy-done.5, s32[8]{0:T(128)S(1)} %collective-permute-done.rsector_other, s32[64]{0:T(128)S(1)} %copy-done.6, s32[32]{0:T(128)S(1)} %copy-done.7, s32[8]{0:T(128)S(1)} %copy-done.8, f32[256,256]{1,0:T(8,128)S(1)} %get-tuple-element.37.part_a, ...), custom_call_target="tpu_custom_call" | custom-call | flops 3300000000 | bytes 9000000 | tf_op jit(solution)/shard_map/image_three/pallas_call | solution.py:471
  113.5 3.6 %all-to-all-start.2 = ((f32[16,24,256]{2,1,0:T(8,128)}), f32[16,24,256]{2,1,0:T(8,128)S(1)}, u32[]{:S(2)}, u32[]{:S(2)}) async-start(f32[16,24,256]{2,1,0:T(8,128)} %image_three.1), calls=%async_computation.2 | async-start | bytes 786432 | tf_op jit(solution)/shard_map/all_to_all | solution.py:599
  117.1 9.2 %all-to-all-done.2.got = f32[16,24,256]{2,1,0:T(8,128)S(1)} async-done(((f32[16,24,256]{2,1,0:T(8,128)}), f32[16,24,256]{2,1,0:T(8,128)S(1)}, u32[]{:S(2)}, u32[]{:S(2)}) %all-to-all-start.2) | async-done | bytes 393248 | tf_op jit(solution)/shard_map/all_to_all | solution.py:599
  126.4 1.6 %collective-permute-start.16 = (f32[8,24,256]{2,1,0:T(8,128)S(1)}, f32[8,24,256]{2,1,0:T(8,128)S(1)}, u32[]{:S(2)}, u32[]{:S(2)}) collective-permute-start(f32[8,24,256]{2,1,0:T(8,128)S(1)} %constant_dynamic-slice_fusion), channel_id=1, source_target_pairs={{0,16},{16,0},{1,17},{17,1},{2,18},{18,2},{3,19},{19,3},{4,20},{20... | collective-permute-start | bytes 589832 | tf_op jit(solution)/shard_map/ppermute | solution.py:604
  129.5 1.0 collective-permute-done.14
  130.5 2.0 %collective-permute-done.13 = f32[16,128]{1,0:T(8,128)S(1)} collective-permute-done((f32[16,128]{1,0:T(8,128)S(1)}, f32[16,128]{1,0:T(8,128)S(1)}, u32[]{:S(2)}, u32[]{:S(2)}) %collective-permute-start.13) | collective-permute-done | bytes 8224 | tf_op jit(solution)/shard_map/ppermute | solution.py:602
  133.2 1.2 collective-permute-start.15
  135.3 2.2 %finish.1 = (f32[8,16,256]{2,1,0:T(8,128)}, f32[1,1]{1,0:T(1,128)}) custom-call(s32[3]{0:T(128)S(1)} %pad_add_fusion.ids, s32[64]{0:T(128)S(1)} %copy-done.6, s32[8]{0:T(128)S(1)} %copy-done.5, s32[32]{0:T(128)S(1)} %copy-done.7, s32[8]{0:T(128)S(1)} %copy-done.8, f32[64,128]{1,0:T(8,128)S(1)} %pad_maximum_fusion.own_stats, ...), custom_call_target="tpu_custom_call" | custom-call | tf_op jit(solution)/shard_map/finish/pallas_call | solution.py:551
  (43 shorter events, 7.7 us)
Async XLA Ops:
  0.6 9.1 %copy-start.4 = (f32[8,256,16]{1,2,0:T(8,128)S(1)}, f32[8,256,16]{1,2,0:T(8,128)}, u32[]{:S(2)}) copy-start(f32[8,256,16]{1,2,0:T(8,128)} %param.8) | copy-start | bytes 393220
  0.6 9.7 %copy-start.5 = (s32[8]{0:T(128)S(1)}, s32[8]{0:T(128)}, u32[]{:S(2)}) copy-start(s32[8]{0:T(128)} %rsector.9) | copy-start | bytes 100
  0.6 9.8 %copy-start.10 = (s32[8,2]{0,1:T(2,128)S(1)}, s32[8,2]{0,1:T(2,128)}, u32[]{:S(2)}) copy-start(s32[8,2]{0,1:T(2,128)} %param.13) | copy-start | bytes 196
  3.6 3.3 %collective-permute-start.1 = (f32[4,264,128]{2,1,0:T(8,128)}, f32[4,264,128]{2,1,0:T(8,128)S(1)}, u32[]{:S(2)}, u32[]{:S(2)}) collective-permute-start(f32[4,264,128]{2,1,0:T(8,128)} %get-tuple-element.23), channel_id=1, source_target_pairs={{0,16},{16,0},{1,17},{17,1},{2,18},{18,2},{3,19},{19,3},{4,20},{20... | collective-permute-start | bytes 1622024 | tf_op jit(solution)/shard_map/ppermute | solution.py:577
  5.1 20.1 %collective-permute-start.4 = (f32[4,264,128]{2,1,0:T(8,128)}, f32[4,264,128]{2,1,0:T(8,128)S(1)}, u32[]{:S(2)}, u32[]{:S(2)}) collective-permute-start(f32[4,264,128]{2,1,0:T(8,128)} %get-tuple-element.22.refs_0_), channel_id=1, source_target_pairs={{0,32},{32,64},{64,96},{96,0},{1,33},{33,65},{65,97},{97,1},{2,34}... | collective-permute-start | bytes 1622024 | tf_op jit(solution)/shard_map/ppermute | solution.py:578
  6.9 18.4 %collective-permute-start.3 = (f32[4,264,128]{2,1,0:T(8,128)S(1)}, f32[4,264,128]{2,1,0:T(8,128)S(1)}, u32[]{:S(2)}, u32[]{:S(2)}) collective-permute-start(f32[4,264,128]{2,1,0:T(8,128)S(1)} %collective-permute-done.1.refs_1_), channel_id=1, source_target_pairs={{0,96},{32,0},{64,32},{96,64},{1,97},{33,1},{65,33},{97,65},{2,98}... | collective-permute-start | bytes 1622024 | tf_op jit(solution)/shard_map/ppermute | solution.py:579
  9.7 2.1 %collective-permute-start.9 = (f32[8,16,256]{2,1,0:T(8,128)S(1)}, f32[8,16,256]{2,1,0:T(8,128)S(1)}, u32[]{:S(2)}, u32[]{:S(2)}) collective-permute-start(f32[8,16,256]{2,1,0:T(8,128)S(1)} %bitcast.7), channel_id=1, source_target_pairs={{0,16},{16,0},{1,17},{17,1},{2,18},{18,2},{3,19},{19,3},{4,20},{20... | collective-permute-start | bytes 393224 | tf_op jit(solution)/shard_map/ppermute | solution.py:574
  10.4 1.1 collective-permute-start
  10.5 1.2 collective-permute-start.8
  15.9 7.8 %copy-start.9 = (f32[4,264,128]{2,1,0:T(8,128)S(1)}, f32[4,264,128]{2,1,0:T(8,128)}, u32[]{:S(2)}) copy-start(f32[4,264,128]{2,1,0:T(8,128)} %get-tuple-element.22.refs_0_) | copy-start | bytes 1622020
  15.9 34.1 %copy-start.6 = (s32[64]{0:T(128)S(1)}, s32[64]{0:T(128)}, u32[]{:S(2)}) copy-start(s32[64]{0:T(128)} %sector.7) | copy-start | bytes 772
  15.9 40.4 %all-to-all-start.1 = ((f32[16,296,128]{2,1,0:T(8,128)}), f32[16,296,128]{2,1,0:T(8,128)}, u32[]{:S(2)}, u32[]{:S(2)}) async-start(f32[16,296,128]{2,1,0:T(8,128)} %right_slots.1), calls=%async_computation.1 | async-start | bytes 4849664 | tf_op jit(solution)/shard_map/all_to_all | solution.py:587
  23.7 13.4 %collective-permute-start.2 = (f32[4,264,128]{2,1,0:T(8,128)S(1)}, f32[4,264,128]{2,1,0:T(8,128)S(1)}, u32[]{:S(2)}, u32[]{:S(2)}) collective-permute-start(f32[4,264,128]{2,1,0:T(8,128)S(1)} %copy-done.9), channel_id=1, source_target_pairs={{0,96},{32,0},{64,32},{96,64},{1,97},{33,1},{65,33},{97,65},{2,98}... | collective-permute-start | bytes 1622024 | tf_op jit(solution)/shard_map/ppermute | solution.py:579
  24.3 14.2 %collective-permute-start.7 = (f32[4,264,128]{2,1,0:T(8,128)S(1)}, f32[4,264,128]{2,1,0:T(8,128)S(1)}, u32[]{:S(2)}, u32[]{:S(2)}) collective-permute-start(f32[4,264,128]{2,1,0:T(8,128)S(1)} %collective-permute-done.1.refs_1_), channel_id=1, source_target_pairs={{0,32},{32,64},{64,96},{96,0},{1,33},{33,65},{65,97},{97,1},{2,34}... | collective-permute-start | bytes 1622024 | tf_op jit(solution)/shard_map/ppermute | solution.py:578
  25.3 24.8 %collective-permute-start.5 = (f32[4,264,128]{2,1,0:T(8,128)S(1)}, f32[4,264,128]{2,1,0:T(8,128)S(1)}, u32[]{:S(2)}, u32[]{:S(2)}) collective-permute-start(f32[4,264,128]{2,1,0:T(8,128)S(1)} %collective-permute-done.4.refs_6_), channel_id=1, source_target_pairs={{0,32},{32,64},{64,96},{96,0},{1,33},{33,65},{65,97},{97,1},{2,34}... | collective-permute-start | bytes 1622024 | tf_op jit(solution)/shard_map/ppermute | solution.py:580
  25.3 24.7 %collective-permute-start.6 = (f32[4,264,128]{2,1,0:T(8,128)S(1)}, f32[4,264,128]{2,1,0:T(8,128)S(1)}, u32[]{:S(2)}, u32[]{:S(2)}) collective-permute-start(f32[4,264,128]{2,1,0:T(8,128)S(1)} %collective-permute-done.3.refs_3_), channel_id=1, source_target_pairs={{0,96},{32,0},{64,32},{96,64},{1,97},{33,1},{65,33},{97,65},{2,98}... | collective-permute-start | bytes 1622024 | tf_op jit(solution)/shard_map/ppermute | solution.py:580
  52.2 10.2 %copy-start.7 = (s32[32]{0:T(128)S(1)}, s32[32]{0:T(128)}, u32[]{:S(2)}) copy-start(s32[32]{0:T(128)} %lsize.7) | copy-start | bytes 388
  52.2 10.2 %copy-start.8 = (s32[8]{0:T(128)S(1)}, s32[8]{0:T(128)}, u32[]{:S(2)}) copy-start(s32[8]{0:T(128)} %rsize.7) | copy-start | bytes 100
  56.4 32.1 %all-to-all-start = ((f32[16,264,128]{2,1,0:T(8,128)}), f32[16,264,128]{2,1,0:T(8,128)S(1)}, u32[]{:S(2)}, u32[]{:S(2)}) async-start(f32[16,264,128]{2,1,0:T(8,128)} %left_slots.1), calls=%async_computation | async-start | bytes 4325376 | tf_op jit(solution)/shard_map/all_to_all | solution.py:593
  67.7 1.4 %copy-start = (bf16[4096,256]{1,0:T(8,128)(2,1)}, bf16[4096,256]{1,0:T(8,128)(2,1)S(1)}, u32[]{:S(2)}) copy-start(bf16[4096,256]{1,0:T(8,128)(2,1)S(1)} %get-tuple-element.28.r_hi_in) | copy-start | bytes 6291460
  69.1 1.4 copy-start.1
  70.4 1.3 copy-start.2
  71.8 1.4 copy-start.3
  94.8 6.7 %collective-permute-start.10 = (f32[256,256]{1,0:T(8,128)S(1)}, f32[256,256]{1,0:T(8,128)S(1)}, u32[]{:S(2)}, u32[]{:S(2)}) collective-permute-start(f32[256,256]{1,0:T(8,128)S(1)} %get-tuple-element.30.part_a), channel_id=1, source_target_pairs={{0,16},{16,0},{1,17},{17,1},{2,18},{18,2},{3,19},{19,3},{4,20},{20... | collective-permute-start | bytes 786440 | tf_op jit(solution)/shard_map/ppermute | solution.py:596
  106.2 1.6 %collective-permute-start.11 = (f32[256,256]{1,0:T(8,128)S(1)}, f32[256,256]{1,0:T(8,128)S(1)}, u32[]{:S(2)}, u32[]{:S(2)}) collective-permute-start(f32[256,256]{1,0:T(8,128)S(1)} %get-tuple-element.37.part_a), channel_id=1, source_target_pairs={{0,16},{16,0},{1,17},{17,1},{2,18},{18,2},{3,19},{19,3},{4,20},{20... | collective-permute-start | bytes 786440 | tf_op jit(solution)/shard_map/ppermute | solution.py:597
  113.5 12.8 %all-to-all-start.2 = ((f32[16,24,256]{2,1,0:T(8,128)}), f32[16,24,256]{2,1,0:T(8,128)S(1)}, u32[]{:S(2)}, u32[]{:S(2)}) async-start(f32[16,24,256]{2,1,0:T(8,128)} %image_three.1), calls=%async_computation.2 | async-start | bytes 786432 | tf_op jit(solution)/shard_map/all_to_all | solution.py:599
  126.4 8.9 %collective-permute-start.16 = (f32[8,24,256]{2,1,0:T(8,128)S(1)}, f32[8,24,256]{2,1,0:T(8,128)S(1)}, u32[]{:S(2)}, u32[]{:S(2)}) collective-permute-start(f32[8,24,256]{2,1,0:T(8,128)S(1)} %constant_dynamic-slice_fusion), channel_id=1, source_target_pairs={{0,16},{16,0},{1,17},{17,1},{2,18},{18,2},{3,19},{19,3},{4,20},{20... | collective-permute-start | bytes 589832 | tf_op jit(solution)/shard_map/ppermute | solution.py:604
  128.0 2.5 %collective-permute-start.14 = (f32[16,128]{1,0:T(8,128)S(1)}, f32[16,128]{1,0:T(8,128)S(1)}, u32[]{:S(2)}, u32[]{:S(2)}) collective-permute-start(f32[16,128]{1,0:T(8,128)S(1)} %bitcast.10), channel_id=1, source_target_pairs={{0,96},{32,0},{64,32},{96,64},{1,97},{33,1},{65,33},{97,65},{2,98}... | collective-permute-start | bytes 24584 | tf_op jit(solution)/shard_map/ppermute | solution.py:602
  128.5 4.0 %collective-permute-start.13 = (f32[16,128]{1,0:T(8,128)S(1)}, f32[16,128]{1,0:T(8,128)S(1)}, u32[]{:S(2)}, u32[]{:S(2)}) collective-permute-start(f32[16,128]{1,0:T(8,128)S(1)} %bitcast.11), channel_id=1, source_target_pairs={{0,64},{32,96},{64,0},{96,32},{1,65},{33,97},{65,1},{97,33},{2,66}... | collective-permute-start | bytes 24584 | tf_op jit(solution)/shard_map/ppermute | solution.py:602
  128.5 4.7 %collective-permute-start.12 = (f32[16,128]{1,0:T(8,128)S(1)}, f32[16,128]{1,0:T(8,128)S(1)}, u32[]{:S(2)}, u32[]{:S(2)}) collective-permute-start(f32[16,128]{1,0:T(8,128)S(1)} %bitcast.12), channel_id=1, source_target_pairs={{0,32},{32,64},{64,96},{96,0},{1,33},{33,65},{65,97},{97,1},{2,34}... | collective-permute-start | bytes 24584 | tf_op jit(solution)/shard_map/ppermute | solution.py:602
  133.2 2.1 %collective-permute-start.15 = (f32[64,128]{1,0:T(8,128)S(1)}, f32[64,128]{1,0:T(8,128)S(1)}, u32[]{:S(2)}, u32[]{:S(2)}) collective-permute-start(f32[64,128]{1,0:T(8,128)S(1)} %pad_maximum_fusion.own_stats), channel_id=1, source_target_pairs={{0,16},{16,0},{1,17},{17,1},{2,18},{18,2},{3,19},{19,3},{4,20},{20... | collective-permute-start | bytes 98312 | tf_op jit(solution)/shard_map/ppermute | solution.py:606

commit v8 on v7

--- a/solution.py
+++ b/solution.py
@@ -12,6 +12,7 @@
 TERMS = 16
 FOLDED = 264
 THIN = 32
+GROUP = 4
 SLOT = THIN + FOLDED
 COL = ("x", "z")
 ALL = ("y", "c", "x", "z")
@@ -188,19 +189,22 @@
         fetch(sector).wait()
         put_folded(folded, sector, right[sector])
 
-    def one(slot, carry):
-        here = slot // 8 == ids[1]
-        weight = jnp.where(here, on[slot % 8, ids[1]], on_other[slot % 8, ids[1]])
-        sector = sector_of(ids, rsector, rsector_other, slot)
-        store(slot, jnp.where(weight == 0, 8, sector)).start()
-        return carry
+        def one(slot, carry):
+            @pl.when(sector_of(ids, rsector, rsector_other, slot) == sector)
+            def _():
+                here = slot // 8 == ids[1]
+                weight = jnp.where(here, on[slot % 8, ids[1]], on_other[slot % 8, ids[1]])
+                store(slot, jnp.where(weight == 0, 8, sector)).start()
+
+            return carry
+
+        lax.fori_loop(0, TERMS, one, 0)
 
     def finished(slot, carry):
         store_thin(slot).wait()
         store(slot, 0).wait()
         return carry
 
-    lax.fori_loop(0, TERMS, one, 0)
     lax.fori_loop(0, TERMS, finished, 0)
 
 
@@ -286,7 +290,7 @@
 
 def first_body(
     ids, rsector, rsector_other, sector, lsize, rsize, slots,
-    r_hi, r_lo, m_hi, m_lo, q1, stats, arrived, sem,
+    r_hi, r_lo, q1, stats, arrived, sem,
 ):
     live_right, live_left = live_sizes(ids, rsector, rsector_other, sector, lsize, rsize)
 
@@ -313,24 +317,16 @@
     vec = start * inverse(norm)
     q1[...] = vec
     stats[...] = put(jnp.zeros((8, HALF), f32), 0, norm)
-    q_hi, q_lo = split(vec)
-    for n in range(TERMS):
-        rows = pl.ds(n * TILE, TILE)
-        hi, lo = split(dot3(r_hi[rows, :], r_lo[rows, :], q_hi, q_lo))
-        m_hi[:, rows] = hi
-        m_lo[:, rows] = lo
 
 
 def first_vector(scalars, slots):
     return pl.pallas_call(
         first_body,
         in_specs=[smem()] * 6 + [hbm()],
-        out_specs=[vmem()] * 6,
+        out_specs=[vmem()] * 4,
         out_shape=[
             jax.ShapeDtypeStruct((TERMS * TILE, TILE), bf16),
             jax.ShapeDtypeStruct((TERMS * TILE, TILE), bf16),
-            jax.ShapeDtypeStruct((TILE, TERMS * TILE), bf16),
-            jax.ShapeDtypeStruct((TILE, TERMS * TILE), bf16),
             jax.ShapeDtypeStruct((TILE, TILE), f32),
             jax.ShapeDtypeStruct((8, HALF), f32),
         ],
@@ -339,61 +335,48 @@
             pltpu.SemaphoreType.DMA((TERMS,)),
         ],
         compiler_params=params(10),
-        cost_estimate=cost(1_700_000_000, 12_000_000),
+        cost_estimate=cost(1_700_000_000, 8_000_000),
         name="first_vector",
     )(*scalars, in_hbm(slots))
 
 
-def image_one_body(
-    arrived, m_hi, m_lo, r_hi_in, r_lo_in, l_hi, l_lo, part, r_hi, r_lo, here, sem, sem_r
-):
-    chunk = TERMS // 4
-
-    def fetch(p, c):
-        cols = pl.ds(c * chunk * TILE, chunk * TILE)
-        src = (m_hi, m_lo)[p]
-        return pltpu.make_async_copy(src.at[:, cols], here.at[p, :, cols], sem.at[p, c])
-
-    def fetch_right(p):
+def image_one_body(arrived, q1, r_hi_in, r_lo_in, l_hi, l_lo, part, r_hi, r_lo, sem):
+    def fetch(n, p):
+        rows = pl.ds(n * TILE, TILE)
         src, dst = ((r_hi_in, r_hi), (r_lo_in, r_lo))[p]
-        return pltpu.make_async_copy(src, dst, sem_r.at[p])
-
-    for c in range(4):
-        for p in range(2):
-            fetch(p, c).start()
-    for p in range(2):
-        fetch_right(p).start()
+        return pltpu.make_async_copy(src.at[rows, :], dst.at[rows, :], sem.at[n, p])
+
+    pairs = [(n, p) for n in range(TERMS) for p in range(2)]
+    for n, p in pairs:
+        fetch(n, p).start()
+    q_hi, q_lo = split(q1[...])
     acc = jnp.zeros((TILE, TILE), f32)
-    for c in range(4):
-        for n in range(c * chunk, (c + 1) * chunk):
-            hi, lo = split(get_folded(arrived, n, 0))
-            l_hi[n * TILE : (n + 1) * TILE, :] = hi
-            l_lo[n * TILE : (n + 1) * TILE, :] = lo
-        for p in range(2):
-            fetch(p, c).wait()
-        cols = pl.ds(c * chunk * TILE, chunk * TILE)
-        acc = acc + dot3(here[0, :, cols], here[1, :, cols], l_hi[cols, :], l_lo[cols, :])
+    for c in range(0, TERMS, GROUP):
+        for n in range(c, c + GROUP):
+            for p in range(2):
+                fetch(n, p).wait()
+        for n in range(c, c + GROUP):
+            rows = pl.ds(n * TILE, TILE)
+            left_hi, left_lo = split(get_folded(arrived, n, 0))
+            l_hi[rows, :] = left_hi
+            l_lo[rows, :] = left_lo
+            hi, lo = split(dot3(r_hi[rows, :], r_lo[rows, :], q_hi, q_lo))
+            acc = acc + dot3(hi, lo, left_hi, left_lo)
     part[...] = acc
-    for p in range(2):
-        fetch_right(p).wait()
-
-
-def image_one(arrived, m_hi, m_lo, r_hi, r_lo):
+
+
+def image_one(arrived, q1, r_hi, r_lo):
     stack = jax.ShapeDtypeStruct((TERMS * TILE, TILE), bf16)
     return pl.pallas_call(
         image_one_body,
-        in_specs=[vmem()] + [hbm()] * 4,
+        in_specs=[vmem(), vmem(), hbm(), hbm()],
         out_specs=[vmem()] * 5,
         out_shape=[stack, stack, jax.ShapeDtypeStruct((TILE, TILE), f32), stack, stack],
-        scratch_shapes=[
-            pltpu.VMEM((2, TILE, TERMS * TILE), bf16),
-            pltpu.SemaphoreType.DMA((2, 4)),
-            pltpu.SemaphoreType.DMA((2,)),
-        ],
+        scratch_shapes=[pltpu.SemaphoreType.DMA((TERMS, 2))],
         compiler_params=params(10),
-        cost_estimate=cost(1_700_000_000, 10_000_000),
+        cost_estimate=cost(3_300_000_000, 10_000_000),
         name="image_one",
-    )(arrived, in_hbm(m_hi), in_hbm(m_lo), in_hbm(r_hi), in_hbm(r_lo))
+    )(arrived, q1, in_hbm(r_hi), in_hbm(r_lo))
 
 
 def lanczos(image, last, before, beta):
@@ -586,12 +569,12 @@
     slots, theirs_now = lax.optimization_barrier((slots, theirs))
     arrived = lax.all_to_all(slots, COL, 0, 0, tiled=True)
     scalars = (ids, right_sector, rsector_other, left_sector, left_size, right_size)
-    r_hi, r_lo, m_hi, m_lo, q1, stats = first_vector(scalars, arrived)
+    r_hi, r_lo, q1, stats = first_vector(scalars, arrived)
 
     pieces = [mine, theirs] + above + far + below
     left_sent = left_slots(ids, left_sector, pieces)
     left_arrived = lax.all_to_all(left_sent, COL, 0, 0, tiled=True)
-    l_hi, l_lo, part, r_hi, r_lo = image_one(left_arrived, m_hi, m_lo, r_hi, r_lo)
+    l_hi, l_lo, part, r_hi, r_lo = image_one(left_arrived, q1, r_hi, r_lo)
     stacks = (r_hi, r_lo, l_hi, l_lo)
     part, q2, stats = image_two(scalars, part, lax.ppermute(part, "c", SWAP), q1, stats, stacks)
     sent = image_three(scalars, part, lax.ppermute(part, "c", SWAP), q1, q2, stats, stacks)

time: 138 us -> 139 us (level)
  waiting for transfers between devices: 59 us -> 63.3 us
  local copies, waits for them, and re-layouts: 5.59 us -> 2.79 us
    all_to_all x1, waiting for transfers between devices: 15.4 us -> 20 us  [local(): left_arrived = lax.all_to_all(left_sent, COL, 0, 0, tiled=True)]
    unnamed x23 -> x19, local copies, waits for them, and re-layouts: 5.57 us -> 2.77 us
    pallas_call x1, Pallas kernels: 5.32 us -> 3.52 us  [first_vector(): pl.pallas_call(first_body, in_specs=[smem()] * 6 + [hbm()], out_specs=[vm...]
where the time goes in v8:
time: 139 us
  waiting for transfers between devices  63.3 us (46%)
  starting transfers between devices  39 us (28%)
  Pallas kernels  32.8 us (24%)
  local copies, waits for them, and re-layouts  2.79 us (2%)
    all_to_all x1, waiting for transfers between devices, local(): left_arrived = lax.all_to_all(left_sent, COL, 0, 0, tiled=True)  20 us
    ppermute x2, waiting for transfers between devices, local(): far = [lax.ppermute(below[0], 'y', UP), lax.ppermute(above[1], 'y', DOWN)]  11.6 us
    all_to_all x1, waiting for transfers between devices, local(): got = lax.all_to_all(sent, COL, 0, 0, tiled=True)  9.24 us
    ppermute x2, waiting for transfers between devices, local(): above = [lax.ppermute(x, 'y', DOWN) for x in (mine, theirs)]  9.15 us
    all_to_all x1, starting transfers between devices, local(): arrived = lax.all_to_all(slots, COL, 0, 0, tiled=True)  7.79 us
    pallas_call x1, Pallas kernels, image_one(): pl.pallas_call(image_one_body, in_specs=[vmem(), vmem(), hbm(), hbm()], o...  6.33 us
    ppermute x2, starting transfers between devices, local(): lax.ppermute(part, 'c', SWAP)  5.99 us
    all_to_all x1, starting transfers between devices, local(): left_arrived = lax.all_to_all(left_sent, COL, 0, 0, tiled=True)  5.96 us
  transfers between devices with their start and end apart: 20, of which 15 were waited for; matrix products, arithmetic and copies ran while one was open for 0% of the time, Pallas kernels for 8%

profile of v8, /device:TPU:1, one launch (start us, length us, event | category | flops | bytes accessed | tf_op | source)
XLA Modules:
  0.0 139.0 jit_solution(3371255439915299995)
XLA Ops:
  0.7 2.9 %fold_left.1 = (f32[4,264,128]{2,1,0:T(8,128)}, f32[4,264,128]{2,1,0:T(8,128)}) custom-call(s32[3]{0:T(128)S(1)} %pad_add_fusion.ids, f32[4,2,256,256]{3,2,1,0:T(8,128)} %src.1), custom_call_target="tpu_custom_call" | custom-call | flops 1000000 | bytes 4000000 | tf_op jit(solution)/shard_map/fold_left/pallas_call | solution.py:139
  3.6 1.5 %collective-permute-start.1 = (f32[4,264,128]{2,1,0:T(8,128)}, f32[4,264,128]{2,1,0:T(8,128)S(1)}, u32[]{:S(2)}, u32[]{:S(2)}) collective-permute-start(f32[4,264,128]{2,1,0:T(8,128)} %get-tuple-element.21), channel_id=1, source_target_pairs={{0,16},{16,0},{1,17},{17,1},{2,18},{18,2},{3,19},{19,3},{4,20},{20... | collective-permute-start | bytes 1622024 | tf_op jit(solution)/shard_map/ppermute | solution.py:560
  5.1 1.4 %collective-permute-start.4 = (f32[4,264,128]{2,1,0:T(8,128)}, f32[4,264,128]{2,1,0:T(8,128)S(1)}, u32[]{:S(2)}, u32[]{:S(2)}) collective-permute-start(f32[4,264,128]{2,1,0:T(8,128)} %get-tuple-element.20.refs_0_), channel_id=1, source_target_pairs={{0,32},{32,64},{64,96},{96,0},{1,33},{33,65},{65,97},{97,1},{2,34}... | collective-permute-start | bytes 1622024 | tf_op jit(solution)/shard_map/ppermute | solution.py:561
  6.9 2.8 %collective-permute-start.3 = (f32[4,264,128]{2,1,0:T(8,128)S(1)}, f32[4,264,128]{2,1,0:T(8,128)S(1)}, u32[]{:S(2)}, u32[]{:S(2)}) collective-permute-start(f32[4,264,128]{2,1,0:T(8,128)S(1)} %collective-permute-done.1.refs_1_), channel_id=1, source_target_pairs={{0,96},{32,0},{64,32},{96,64},{1,97},{33,1},{65,33},{97,65},{2,98}... | collective-permute-start | bytes 1622024 | tf_op jit(solution)/shard_map/ppermute | solution.py:562
  11.8 5.4 %right_slots.1 = f32[16,296,128]{2,1,0:T(8,128)} custom-call(s32[3]{0:T(128)S(1)} %pad_add_fusion.ids, s32[8]{0:T(128)S(1)} %copy-done.1, s32[8]{0:T(128)S(1)} %collective-permute-done.rsector_other, s32[8,2]{1,0:T(8,128)S(1)} %copy.11.on, s32[8,2]{1,0:T(8,128)S(1)} %collective-permute-done.8.on_other, f32[8,16,256]{2,1,0:T(8,128)S(1)} %bitcast.8, ...), custom_call_target="tpu_custom_call" | custom-call | flops 4000000 | bytes 10000000 | tf_op jit(solution)/shard_map/right_slots/pallas_call | solution.py:212
  17.2 7.8 %all-to-all-start.1 = ((f32[16,296,128]{2,1,0:T(8,128)}), f32[16,296,128]{2,1,0:T(8,128)}, u32[]{:S(2)}, u32[]{:S(2)}) async-start(f32[16,296,128]{2,1,0:T(8,128)} %right_slots.1), calls=%async_computation.1 | async-start | bytes 4849664 | tf_op jit(solution)/shard_map/all_to_all | solution.py:570
  25.8 0.8 collective-permute-start.7
  26.6 2.7 %collective-permute-start.6 = (f32[4,264,128]{2,1,0:T(8,128)S(1)}, f32[4,264,128]{2,1,0:T(8,128)S(1)}, u32[]{:S(2)}, u32[]{:S(2)}) collective-permute-start(f32[4,264,128]{2,1,0:T(8,128)S(1)} %collective-permute-done.3.refs_3_), channel_id=1, source_target_pairs={{0,96},{32,0},{64,32},{96,64},{1,97},{33,1},{65,33},{97,65},{2,98}... | collective-permute-start | bytes 1622024 | tf_op jit(solution)/shard_map/ppermute | solution.py:563
  29.3 9.1 %collective-permute-done.2.refs_2_ = f32[4,264,128]{2,1,0:T(8,128)S(1)} collective-permute-done((f32[4,264,128]{2,1,0:T(8,128)S(1)}, f32[4,264,128]{2,1,0:T(8,128)S(1)}, u32[]{:S(2)}, u32[]{:S(2)}) %collective-permute-start.2) | collective-permute-done | bytes 540704 | tf_op jit(solution)/shard_map/ppermute | solution.py:562
  38.4 1.5 %collective-permute-done.7.refs_7_ = f32[4,264,128]{2,1,0:T(8,128)S(1)} collective-permute-done((f32[4,264,128]{2,1,0:T(8,128)S(1)}, f32[4,264,128]{2,1,0:T(8,128)S(1)}, u32[]{:S(2)}, u32[]{:S(2)}) %collective-permute-start.7) | collective-permute-done | bytes 540704 | tf_op jit(solution)/shard_map/ppermute | solution.py:561
  40.0 11.6 %collective-permute-done.5.refs_4_ = f32[4,264,128]{2,1,0:T(8,128)S(1)} collective-permute-done((f32[4,264,128]{2,1,0:T(8,128)S(1)}, f32[4,264,128]{2,1,0:T(8,128)S(1)}, u32[]{:S(2)}, u32[]{:S(2)}) %collective-permute-start.5) | collective-permute-done | bytes 540704 | tf_op jit(solution)/shard_map/ppermute | solution.py:563
  51.5 2.1 %left_slots.1 = f32[16,264,128]{2,1,0:T(8,128)} custom-call(s32[3]{0:T(128)S(1)} %pad_add_fusion.ids, s32[64]{0:T(128)S(1)} %copy-done.2, f32[4,264,128]{2,1,0:T(8,128)S(1)} %copy-done.5, f32[4,264,128]{2,1,0:T(8,128)S(1)} %collective-permute-done.1.refs_1_, f32[4,264,128]{2,1,0:T(8,128)S(1)} %collective-permute-done.2.refs_2_, ...), custom_call_target="tpu_custom_call" | custom-call | flops 15000000512 | bytes 4000000 | tf_op jit(solution)/shard_map/left_slots/pallas_call | solution.py:268
  53.7 4.0 %all-to-all-done.1.slots = f32[16,296,128]{2,1,0:T(8,128)} async-done(((f32[16,296,128]{2,1,0:T(8,128)}), f32[16,296,128]{2,1,0:T(8,128)}, u32[]{:S(2)}, u32[]{:S(2)}) %all-to-all-start.1) | async-done | bytes 2424864 | tf_op jit(solution)/shard_map/all_to_all | solution.py:570
  57.7 6.0 %all-to-all-start = ((f32[16,264,128]{2,1,0:T(8,128)}), f32[16,264,128]{2,1,0:T(8,128)S(1)}, u32[]{:S(2)}, u32[]{:S(2)}) async-start(f32[16,264,128]{2,1,0:T(8,128)} %left_slots.1), calls=%async_computation | async-start | bytes 4325376 | tf_op jit(solution)/shard_map/all_to_all | solution.py:576
  63.7 3.5 %first_vector.1 = (bf16[4096,256]{1,0:T(8,128)(2,1)S(1)}, bf16[4096,256]{1,0:T(8,128)(2,1)S(1)}, f32[256,256]{1,0:T(8,128)S(1)}, f32[8,128]{1,0:T(8,128)S(1)}) custom-call(s32[3]{0:T(128)S(1)} %pad_add_fusion.ids, s32[8]{0:T(128)S(1)} %copy-done.1, s32[8]{0:T(128)S(1)} %collective-permute-done.rsector_other, s32[64]{0:T(128)S(1)} %copy-done.2, ...), custom_call_target="tpu_custom_call" | custom-call | flops 1700000000 | bytes 8000000 | tf_op jit(solution)/shard_map/first_vector/pallas_call | solution.py:323
  67.2 1.3 copy-done.6
  68.5 1.3 copy-done.7
  69.9 20.0 %all-to-all-done.arrived = f32[16,264,128]{2,1,0:T(8,128)S(1)} async-done(((f32[16,264,128]{2,1,0:T(8,128)}), f32[16,264,128]{2,1,0:T(8,128)S(1)}, u32[]{:S(2)}, u32[]{:S(2)}) %all-to-all-start) | async-done | bytes 2162720 | tf_op jit(solution)/shard_map/all_to_all | solution.py:576
  89.8 6.3 %image_one.1 = (bf16[4096,256]{1,0:T(8,128)(2,1)S(1)}, bf16[4096,256]{1,0:T(8,128)(2,1)S(1)}, f32[256,256]{1,0:T(8,128)S(1)}, bf16[4096,256]{1,0:T(8,128)(2,1)S(1)}, bf16[4096,256]{1,0:T(8,128)(2,1)S(1)}) custom-call(f32[16,264,128]{2,1,0:T(8,128)S(1)} %all-to-all-done.arrived, f32[256,256]{1,0:T(8,128)S(1)} %get-tuple-element.24.q1, ...), custom_call_target="tpu_custom_call" | custom-call | flops 3300000000 | bytes 10000000 | tf_op jit(solution)/shard_map/image_one/pallas_call | solution.py:370
  96.2 5.5 %collective-permute-start.10 = (f32[256,256]{1,0:T(8,128)S(1)}, f32[256,256]{1,0:T(8,128)S(1)}, u32[]{:S(2)}, u32[]{:S(2)}) collective-permute-start(f32[256,256]{1,0:T(8,128)S(1)} %get-tuple-element.27.part_a), channel_id=1, source_target_pairs={{0,16},{16,0},{1,17},{17,1},{2,18},{18,2},{3,19},{19,3},{4,20},{20... | collective-permute-start | bytes 786440 | tf_op jit(solution)/shard_map/ppermute | solution.py:579
  101.7 1.2 collective-permute-done.10.part_b
  102.9 4.7 %image_two.1 = (f32[256,256]{1,0:T(8,128)S(1)}, f32[256,256]{1,0:T(8,128)S(1)}, f32[8,128]{1,0:T(8,128)S(1)}) custom-call(s32[3]{0:T(128)S(1)} %pad_add_fusion.ids, s32[8]{0:T(128)S(1)} %copy-done.1, s32[8]{0:T(128)S(1)} %collective-permute-done.rsector_other, s32[64]{0:T(128)S(1)} %copy-done.2, s32[32]{0:T(128)S(1)} %copy-done.3, s32[8]{0:T(128)S(1)} %copy-done.4, ...), custom_call_target="tpu_custom_call" | custom-call | flops 3300000000 | bytes 9000000 | tf_op jit(solution)/shard_map/image_two/pallas_call | solution.py:418
  108.0 1.2 collective-permute-done.11.part_b
  109.2 5.7 %image_three.1 = f32[16,24,256]{2,1,0:T(8,128)} custom-call(s32[3]{0:T(128)S(1)} %pad_add_fusion.ids, s32[8]{0:T(128)S(1)} %copy-done.1, s32[8]{0:T(128)S(1)} %collective-permute-done.rsector_other, s32[64]{0:T(128)S(1)} %copy-done.2, s32[32]{0:T(128)S(1)} %copy-done.3, s32[8]{0:T(128)S(1)} %copy-done.4, f32[256,256]{1,0:T(8,128)S(1)} %get-tuple-element.33.part_a, ...), custom_call_target="tpu_custom_call" | custom-call | flops 3300000000 | bytes 9000000 | tf_op jit(solution)/shard_map/image_three/pallas_call | solution.py:454
  114.8 3.6 %all-to-all-start.2 = ((f32[16,24,256]{2,1,0:T(8,128)}), f32[16,24,256]{2,1,0:T(8,128)S(1)}, u32[]{:S(2)}, u32[]{:S(2)}) async-start(f32[16,24,256]{2,1,0:T(8,128)} %image_three.1), calls=%async_computation.2 | async-start | bytes 786432 | tf_op jit(solution)/shard_map/all_to_all | solution.py:582
  118.4 9.2 %all-to-all-done.2.got = f32[16,24,256]{2,1,0:T(8,128)S(1)} async-done(((f32[16,24,256]{2,1,0:T(8,128)}), f32[16,24,256]{2,1,0:T(8,128)S(1)}, u32[]{:S(2)}, u32[]{:S(2)}) %all-to-all-start.2) | async-done | bytes 393248 | tf_op jit(solution)/shard_map/all_to_all | solution.py:582
  127.7 1.6 %collective-permute-start.16 = (f32[8,24,256]{2,1,0:T(8,128)S(1)}, f32[8,24,256]{2,1,0:T(8,128)S(1)}, u32[]{:S(2)}, u32[]{:S(2)}) collective-permute-start(f32[8,24,256]{2,1,0:T(8,128)S(1)} %constant_dynamic-slice_fusion), channel_id=1, source_target_pairs={{0,16},{16,0},{1,17},{17,1},{2,18},{18,2},{3,19},{19,3},{4,20},{20... | collective-permute-start | bytes 589832 | tf_op jit(solution)/shard_map/ppermute | solution.py:587
  130.8 1.0 collective-permute-done.14
  131.8 2.2 %collective-permute-done.13 = f32[16,128]{1,0:T(8,128)S(1)} collective-permute-done((f32[16,128]{1,0:T(8,128)S(1)}, f32[16,128]{1,0:T(8,128)S(1)}, u32[]{:S(2)}, u32[]{:S(2)}) %collective-permute-start.13) | collective-permute-done | bytes 8224 | tf_op jit(solution)/shard_map/ppermute | solution.py:585
  134.2 1.5 %collective-permute-start.15 = (f32[64,128]{1,0:T(8,128)S(1)}, f32[64,128]{1,0:T(8,128)S(1)}, u32[]{:S(2)}, u32[]{:S(2)}) collective-permute-start(f32[64,128]{1,0:T(8,128)S(1)} %pad_maximum_fusion.own_stats), channel_id=1, source_target_pairs={{0,16},{16,0},{1,17},{17,1},{2,18},{18,2},{3,19},{19,3},{4,20},{20... | collective-permute-start | bytes 98312 | tf_op jit(solution)/shard_map/ppermute | solution.py:589
  135.7 0.9 collective-permute-done.15.other_stats
  136.6 2.2 %finish.1 = (f32[8,16,256]{2,1,0:T(8,128)}, f32[1,1]{1,0:T(1,128)}) custom-call(s32[3]{0:T(128)S(1)} %pad_add_fusion.ids, s32[64]{0:T(128)S(1)} %copy-done.2, s32[8]{0:T(128)S(1)} %copy-done.1, s32[32]{0:T(128)S(1)} %copy-done.3, s32[8]{0:T(128)S(1)} %copy-done.4, f32[64,128]{1,0:T(8,128)S(1)} %pad_maximum_fusion.own_stats, ...), custom_call_target="tpu_custom_call" | custom-call | tf_op jit(solution)/shard_map/finish/pallas_call | solution.py:534
  (39 shorter events, 5.5 us)
Async XLA Ops:
  0.6 9.1 %copy-start = (f32[8,256,16]{1,2,0:T(8,128)S(1)}, f32[8,256,16]{1,2,0:T(8,128)}, u32[]{:S(2)}) copy-start(f32[8,256,16]{1,2,0:T(8,128)} %param.8) | copy-start | bytes 393220
  0.6 9.7 %copy-start.1 = (s32[8]{0:T(128)S(1)}, s32[8]{0:T(128)}, u32[]{:S(2)}) copy-start(s32[8]{0:T(128)} %rsector.9) | copy-start | bytes 100
  0.6 9.8 %copy-start.8 = (s32[8,2]{0,1:T(2,128)S(1)}, s32[8,2]{0,1:T(2,128)}, u32[]{:S(2)}) copy-start(s32[8,2]{0,1:T(2,128)} %param.13) | copy-start | bytes 196
  3.6 3.3 %collective-permute-start.1 = (f32[4,264,128]{2,1,0:T(8,128)}, f32[4,264,128]{2,1,0:T(8,128)S(1)}, u32[]{:S(2)}, u32[]{:S(2)}) collective-permute-start(f32[4,264,128]{2,1,0:T(8,128)} %get-tuple-element.21), channel_id=1, source_target_pairs={{0,16},{16,0},{1,17},{17,1},{2,18},{18,2},{3,19},{19,3},{4,20},{20... | collective-permute-start | bytes 1622024 | tf_op jit(solution)/shard_map/ppermute | solution.py:560
  5.1 21.5 %collective-permute-start.4 = (f32[4,264,128]{2,1,0:T(8,128)}, f32[4,264,128]{2,1,0:T(8,128)S(1)}, u32[]{:S(2)}, u32[]{:S(2)}) collective-permute-start(f32[4,264,128]{2,1,0:T(8,128)} %get-tuple-element.20.refs_0_), channel_id=1, source_target_pairs={{0,32},{32,64},{64,96},{96,0},{1,33},{33,65},{65,97},{97,1},{2,34}... | collective-permute-start | bytes 1622024 | tf_op jit(solution)/shard_map/ppermute | solution.py:561
  6.9 19.7 %collective-permute-start.3 = (f32[4,264,128]{2,1,0:T(8,128)S(1)}, f32[4,264,128]{2,1,0:T(8,128)S(1)}, u32[]{:S(2)}, u32[]{:S(2)}) collective-permute-start(f32[4,264,128]{2,1,0:T(8,128)S(1)} %collective-permute-done.1.refs_1_), channel_id=1, source_target_pairs={{0,96},{32,0},{64,32},{96,64},{1,97},{33,1},{65,33},{97,65},{2,98}... | collective-permute-start | bytes 1622024 | tf_op jit(solution)/shard_map/ppermute | solution.py:562
  9.7 2.1 %collective-permute-start.9 = (f32[8,16,256]{2,1,0:T(8,128)S(1)}, f32[8,16,256]{2,1,0:T(8,128)S(1)}, u32[]{:S(2)}, u32[]{:S(2)}) collective-permute-start(f32[8,16,256]{2,1,0:T(8,128)S(1)} %bitcast.7), channel_id=1, source_target_pairs={{0,16},{16,0},{1,17},{17,1},{2,18},{18,2},{3,19},{19,3},{4,20},{20... | collective-permute-start | bytes 393224 | tf_op jit(solution)/shard_map/ppermute | solution.py:557
  10.4 1.1 collective-permute-start
  10.5 1.2 collective-permute-start.8
  17.2 7.8 %copy-start.5 = (f32[4,264,128]{2,1,0:T(8,128)S(1)}, f32[4,264,128]{2,1,0:T(8,128)}, u32[]{:S(2)}) copy-start(f32[4,264,128]{2,1,0:T(8,128)} %get-tuple-element.20.refs_0_) | copy-start | bytes 1622020
  17.2 34.3 %copy-start.2 = (s32[64]{0:T(128)S(1)}, s32[64]{0:T(128)}, u32[]{:S(2)}) copy-start(s32[64]{0:T(128)} %sector.7) | copy-start | bytes 772
  17.2 40.4 %all-to-all-start.1 = ((f32[16,296,128]{2,1,0:T(8,128)}), f32[16,296,128]{2,1,0:T(8,128)}, u32[]{:S(2)}, u32[]{:S(2)}) async-start(f32[16,296,128]{2,1,0:T(8,128)} %right_slots.1), calls=%async_computation.1 | async-start | bytes 4849664 | tf_op jit(solution)/shard_map/all_to_all | solution.py:570
  25.0 13.4 %collective-permute-start.2 = (f32[4,264,128]{2,1,0:T(8,128)S(1)}, f32[4,264,128]{2,1,0:T(8,128)S(1)}, u32[]{:S(2)}, u32[]{:S(2)}) collective-permute-start(f32[4,264,128]{2,1,0:T(8,128)S(1)} %copy-done.5), channel_id=1, source_target_pairs={{0,96},{32,0},{64,32},{96,64},{1,97},{33,1},{65,33},{97,65},{2,98}... | collective-permute-start | bytes 1622024 | tf_op jit(solution)/shard_map/ppermute | solution.py:562
  25.8 14.2 %collective-permute-start.7 = (f32[4,264,128]{2,1,0:T(8,128)S(1)}, f32[4,264,128]{2,1,0:T(8,128)S(1)}, u32[]{:S(2)}, u32[]{:S(2)}) collective-permute-start(f32[4,264,128]{2,1,0:T(8,128)S(1)} %collective-permute-done.1.refs_1_), channel_id=1, source_target_pairs={{0,32},{32,64},{64,96},{96,0},{1,33},{33,65},{65,97},{97,1},{2,34}... | collective-permute-start | bytes 1622024 | tf_op jit(solution)/shard_map/ppermute | solution.py:561
  26.6 25.0 %collective-permute-start.5 = (f32[4,264,128]{2,1,0:T(8,128)S(1)}, f32[4,264,128]{2,1,0:T(8,128)S(1)}, u32[]{:S(2)}, u32[]{:S(2)}) collective-permute-start(f32[4,264,128]{2,1,0:T(8,128)S(1)} %collective-permute-done.4.refs_6_), channel_id=1, source_target_pairs={{0,32},{32,64},{64,96},{96,0},{1,33},{33,65},{65,97},{97,1},{2,34}... | collective-permute-start | bytes 1622024 | tf_op jit(solution)/shard_map/ppermute | solution.py:563
  26.6 24.9 %collective-permute-start.6 = (f32[4,264,128]{2,1,0:T(8,128)S(1)}, f32[4,264,128]{2,1,0:T(8,128)S(1)}, u32[]{:S(2)}, u32[]{:S(2)}) collective-permute-start(f32[4,264,128]{2,1,0:T(8,128)S(1)} %collective-permute-done.3.refs_3_), channel_id=1, source_target_pairs={{0,96},{32,0},{64,32},{96,64},{1,97},{33,1},{65,33},{97,65},{2,98}... | collective-permute-start | bytes 1622024 | tf_op jit(solution)/shard_map/ppermute | solution.py:563
  53.7 10.0 %copy-start.3 = (s32[32]{0:T(128)S(1)}, s32[32]{0:T(128)}, u32[]{:S(2)}) copy-start(s32[32]{0:T(128)} %lsize.7) | copy-start | bytes 388
  53.7 10.0 %copy-start.4 = (s32[8]{0:T(128)S(1)}, s32[8]{0:T(128)}, u32[]{:S(2)}) copy-start(s32[8]{0:T(128)} %rsize.7) | copy-start | bytes 100
  57.7 32.1 %all-to-all-start = ((f32[16,264,128]{2,1,0:T(8,128)}), f32[16,264,128]{2,1,0:T(8,128)S(1)}, u32[]{:S(2)}, u32[]{:S(2)}) async-start(f32[16,264,128]{2,1,0:T(8,128)} %left_slots.1), calls=%async_computation | async-start | bytes 4325376 | tf_op jit(solution)/shard_map/all_to_all | solution.py:576
  67.2 1.3 copy-start.6
  68.5 1.3 copy-start.7
  96.2 6.7 %collective-permute-start.10 = (f32[256,256]{1,0:T(8,128)S(1)}, f32[256,256]{1,0:T(8,128)S(1)}, u32[]{:S(2)}, u32[]{:S(2)}) collective-permute-start(f32[256,256]{1,0:T(8,128)S(1)} %get-tuple-element.27.part_a), channel_id=1, source_target_pairs={{0,16},{16,0},{1,17},{17,1},{2,18},{18,2},{3,19},{19,3},{4,20},{20... | collective-permute-start | bytes 786440 | tf_op jit(solution)/shard_map/ppermute | solution.py:579
  107.6 1.6 %collective-permute-start.11 = (f32[256,256]{1,0:T(8,128)S(1)}, f32[256,256]{1,0:T(8,128)S(1)}, u32[]{:S(2)}, u32[]{:S(2)}) collective-permute-start(f32[256,256]{1,0:T(8,128)S(1)} %get-tuple-element.33.part_a), channel_id=1, source_target_pairs={{0,16},{16,0},{1,17},{17,1},{2,18},{18,2},{3,19},{19,3},{4,20},{20... | collective-permute-start | bytes 786440 | tf_op jit(solution)/shard_map/ppermute | solution.py:580
  114.8 12.8 %all-to-all-start.2 = ((f32[16,24,256]{2,1,0:T(8,128)}), f32[16,24,256]{2,1,0:T(8,128)S(1)}, u32[]{:S(2)}, u32[]{:S(2)}) async-start(f32[16,24,256]{2,1,0:T(8,128)} %image_three.1), calls=%async_computation.2 | async-start | bytes 786432 | tf_op jit(solution)/shard_map/all_to_all | solution.py:582
  127.7 8.9 %collective-permute-start.16 = (f32[8,24,256]{2,1,0:T(8,128)S(1)}, f32[8,24,256]{2,1,0:T(8,128)S(1)}, u32[]{:S(2)}, u32[]{:S(2)}) collective-permute-start(f32[8,24,256]{2,1,0:T(8,128)S(1)} %constant_dynamic-slice_fusion), channel_id=1, source_target_pairs={{0,16},{16,0},{1,17},{17,1},{2,18},{18,2},{3,19},{19,3},{4,20},{20... | collective-permute-start | bytes 589832 | tf_op jit(solution)/shard_map/ppermute | solution.py:587
  129.3 2.5 %collective-permute-start.14 = (f32[16,128]{1,0:T(8,128)S(1)}, f32[16,128]{1,0:T(8,128)S(1)}, u32[]{:S(2)}, u32[]{:S(2)}) collective-permute-start(f32[16,128]{1,0:T(8,128)S(1)} %bitcast.10), channel_id=1, source_target_pairs={{0,96},{32,0},{64,32},{96,64},{1,97},{33,1},{65,33},{97,65},{2,98}... | collective-permute-start | bytes 24584 | tf_op jit(solution)/shard_map/ppermute | solution.py:585
  130.0 4.0 %collective-permute-start.13 = (f32[16,128]{1,0:T(8,128)S(1)}, f32[16,128]{1,0:T(8,128)S(1)}, u32[]{:S(2)}, u32[]{:S(2)}) collective-permute-start(f32[16,128]{1,0:T(8,128)S(1)} %bitcast.11), channel_id=1, source_target_pairs={{0,64},{32,96},{64,0},{96,32},{1,65},{33,97},{65,1},{97,33},{2,66}... | collective-permute-start | bytes 24584 | tf_op jit(solution)/shard_map/ppermute | solution.py:585
  130.1 4.2 %collective-permute-start.12 = (f32[16,128]{1,0:T(8,128)S(1)}, f32[16,128]{1,0:T(8,128)S(1)}, u32[]{:S(2)}, u32[]{:S(2)}) collective-permute-start(f32[16,128]{1,0:T(8,128)S(1)} %bitcast.12), channel_id=1, source_target_pairs={{0,32},{32,64},{64,96},{96,0},{1,33},{33,65},{65,97},{97,1},{2,34}... | collective-permute-start | bytes 24584 | tf_op jit(solution)/shard_map/ppermute | solution.py:585
  134.2 2.4 %collective-permute-start.15 = (f32[64,128]{1,0:T(8,128)S(1)}, f32[64,128]{1,0:T(8,128)S(1)}, u32[]{:S(2)}, u32[]{:S(2)}) collective-permute-start(f32[64,128]{1,0:T(8,128)S(1)} %pad_maximum_fusion.own_stats), channel_id=1, source_target_pairs={{0,16},{16,0},{1,17},{17,1},{2,18},{18,2},{3,19},{19,3},{4,20},{20... | collective-permute-start | bytes 98312 | tf_op jit(solution)/shard_map/ppermute | solution.py:589

commit v9 on v7

--- a/solution.py
+++ b/solution.py
@@ -112,11 +112,16 @@
     return jnp.where(j == lane, value, stats)
 
 
-def fold_left_body(ids, src, keep, give, tiles, folded, sem_in, sem_out):
+def fold_body(
+    ids, left_env, right_env, keep, give, right, tiles, folded, others, sem_in, sem_out, sem_right
+):
     def fetch(t, n):
         term = ids[1] if t else 1 - ids[1]
         at = 4 * t + n
-        return pltpu.make_async_copy(src.at[n, term], tiles.at[at], sem_in.at[at])
+        return pltpu.make_async_copy(left_env.at[n, term], tiles.at[at], sem_in.at[at])
+
+    def fetch_right(n):
+        return pltpu.make_async_copy(right_env.at[n, ids[1]], others.at[n], sem_right.at[n])
 
     def store(t, n):
         at = 4 * t + n
@@ -126,30 +131,39 @@
     order = [(t, n) for t in range(2) for n in range(4)]
     for t, n in order:
         fetch(t, n).start()
+    for n in range(8):
+        fetch_right(n).start()
+    right[8] = jnp.zeros((FOLDED, HALF), f32)
     for t, n in order:
         fetch(t, n).wait()
         put_folded(folded, 4 * t + n, tiles[4 * t + n])
         store(t, n).start()
+    for n in range(8):
+        fetch_right(n).wait()
+        put_folded(right, n, others[n])
     for t, n in order:
         store(t, n).wait()
 
 
-def fold_left(ids, left_env):
-    return pl.pallas_call(
-        fold_left_body,
-        in_specs=[smem(), hbm()],
-        out_specs=[hbm(), hbm()],
-        out_shape=[pltpu.HBM((4, FOLDED, HALF), f32)] * 2,
+def fold(ids, left_env, right_env):
+    return pl.pallas_call(
+        fold_body,
+        in_specs=[smem(), hbm(), hbm()],
+        out_specs=[hbm(), hbm(), vmem()],
+        out_shape=[pltpu.HBM((4, FOLDED, HALF), f32)] * 2
+        + [jax.ShapeDtypeStruct((9, FOLDED, HALF), f32)],
         scratch_shapes=[
             pltpu.VMEM((8, TILE, TILE), f32),
             pltpu.VMEM((8, FOLDED, HALF), f32),
+            pltpu.VMEM((8, TILE, TILE), f32),
             pltpu.SemaphoreType.DMA((8,)),
             pltpu.SemaphoreType.DMA((8,)),
-        ],
-        compiler_params=params(8),
-        cost_estimate=cost(1_000_000, 4_000_000),
-        name="fold_left",
-    )(ids, in_hbm(left_env))
+            pltpu.SemaphoreType.DMA((8,)),
+        ],
+        compiler_params=params(10),
+        cost_estimate=cost(1_000_000, 6_000_000),
+        name="fold",
+    )(ids, in_hbm(left_env), in_hbm(right_env))
 
 
 def sector_of(ids, rsector, rsector_other, slot):
@@ -157,14 +171,8 @@
 
 
 def right_slots_body(
-    ids, rsector, rsector_other, on, on_other, thin, thin_other, right_env,
-    out, right, folded, cols, sem_in, sem_out, sem_thin,
+    ids, rsector, rsector_other, on, on_other, thin, thin_other, folded, out, cols, sem_out, sem_thin
 ):
-    def fetch(sector):
-        return pltpu.make_async_copy(
-            right_env.at[sector, ids[1]], right.at[sector], sem_in.at[sector]
-        )
-
     def store_thin(slot):
         return pltpu.make_async_copy(
             cols.at[slot], out.at[slot, pl.ds(0, THIN), :], sem_thin.at[slot]
@@ -175,53 +183,37 @@
             folded.at[sector], out.at[slot, pl.ds(THIN, FOLDED), :], sem_out.at[slot]
         )
 
-    for sector in range(8):
-        fetch(sector).start()
+    for slot in range(TERMS):
+        here = slot // 8 == ids[1]
+        weight = jnp.where(here, on[slot % 8, ids[1]], on_other[slot % 8, ids[1]])
+        sector = sector_of(ids, rsector, rsector_other, slot)
+        store(slot, jnp.where(weight == 0, 8, sector)).start()
     for slot in range(TERMS):
         here = slot // 8 == ids[1]
         block = jnp.where(here, thin[slot % 8], thin_other[slot % 8])
         cols[slot, :16, :] = block[:, :HALF]
         cols[slot, 16:, :] = block[:, HALF:]
         store_thin(slot).start()
-    folded[8] = jnp.zeros((FOLDED, HALF), f32)
-    for sector in range(8):
-        fetch(sector).wait()
-        put_folded(folded, sector, right[sector])
-
-    def one(slot, carry):
-        here = slot // 8 == ids[1]
-        weight = jnp.where(here, on[slot % 8, ids[1]], on_other[slot % 8, ids[1]])
-        sector = sector_of(ids, rsector, rsector_other, slot)
-        store(slot, jnp.where(weight == 0, 8, sector)).start()
-        return carry
-
-    def finished(slot, carry):
+    for slot in range(TERMS):
         store_thin(slot).wait()
         store(slot, 0).wait()
-        return carry
-
-    lax.fori_loop(0, TERMS, one, 0)
-    lax.fori_loop(0, TERMS, finished, 0)
-
-
-def right_slots(ids, rsector, rsector_other, on, on_other, thin, thin_other, right_env):
+
+
+def right_slots(ids, rsector, rsector_other, on, on_other, thin, thin_other, folded):
     return pl.pallas_call(
         right_slots_body,
-        in_specs=[smem()] * 5 + [vmem()] * 2 + [hbm()],
+        in_specs=[smem()] * 5 + [vmem()] * 3,
         out_specs=hbm(),
         out_shape=pltpu.HBM((TERMS, SLOT, HALF), f32),
         scratch_shapes=[
-            pltpu.VMEM((8, TILE, TILE), f32),
-            pltpu.VMEM((9, FOLDED, HALF), f32),
             pltpu.VMEM((TERMS, THIN, HALF), f32),
-            pltpu.SemaphoreType.DMA((8,)),
             pltpu.SemaphoreType.DMA((TERMS,)),
             pltpu.SemaphoreType.DMA((TERMS,)),
         ],
-        compiler_params=params(10),
-        cost_estimate=cost(4_000_000, 10_000_000),
+        compiler_params=params(6),
+        cost_estimate=cost(4_000_000, 6_000_000),
         name="right_slots",
-    )(ids, rsector, rsector_other, on, on_other, thin, thin_other, in_hbm(right_env))
+    )(ids, rsector, rsector_other, on, on_other, thin, thin_other, folded)
 
 
 def left_slots_body(ids, left_sector, *refs):
@@ -344,9 +336,7 @@
     )(*scalars, in_hbm(slots))
 
 
-def image_one_body(
-    arrived, m_hi, m_lo, r_hi_in, r_lo_in, l_hi, l_lo, part, r_hi, r_lo, here, sem, sem_r
-):
+def image_one_body(arrived, m_hi, m_lo, l_hi, l_lo, part, here, sem):
     chunk = TERMS // 4
 
     def fetch(p, c):
@@ -354,46 +344,37 @@
         src = (m_hi, m_lo)[p]
         return pltpu.make_async_copy(src.at[:, cols], here.at[p, :, cols], sem.at[p, c])
 
-    def fetch_right(p):
-        src, dst = ((r_hi_in, r_hi), (r_lo_in, r_lo))[p]
-        return pltpu.make_async_copy(src, dst, sem_r.at[p])
-
     for c in range(4):
         for p in range(2):
             fetch(p, c).start()
-    for p in range(2):
-        fetch_right(p).start()
+    for n in range(TERMS):
+        hi, lo = split(get_folded(arrived, n, 0))
+        l_hi[n * TILE : (n + 1) * TILE, :] = hi
+        l_lo[n * TILE : (n + 1) * TILE, :] = lo
     acc = jnp.zeros((TILE, TILE), f32)
     for c in range(4):
-        for n in range(c * chunk, (c + 1) * chunk):
-            hi, lo = split(get_folded(arrived, n, 0))
-            l_hi[n * TILE : (n + 1) * TILE, :] = hi
-            l_lo[n * TILE : (n + 1) * TILE, :] = lo
         for p in range(2):
             fetch(p, c).wait()
         cols = pl.ds(c * chunk * TILE, chunk * TILE)
         acc = acc + dot3(here[0, :, cols], here[1, :, cols], l_hi[cols, :], l_lo[cols, :])
     part[...] = acc
-    for p in range(2):
-        fetch_right(p).wait()
-
-
-def image_one(arrived, m_hi, m_lo, r_hi, r_lo):
+
+
+def image_one(arrived, m_hi, m_lo):
     stack = jax.ShapeDtypeStruct((TERMS * TILE, TILE), bf16)
     return pl.pallas_call(
         image_one_body,
-        in_specs=[vmem()] + [hbm()] * 4,
-        out_specs=[vmem()] * 5,
-        out_shape=[stack, stack, jax.ShapeDtypeStruct((TILE, TILE), f32), stack, stack],
+        in_specs=[vmem(), hbm(), hbm()],
+        out_specs=[vmem()] * 3,
+        out_shape=[stack, stack, jax.ShapeDtypeStruct((TILE, TILE), f32)],
         scratch_shapes=[
             pltpu.VMEM((2, TILE, TERMS * TILE), bf16),
             pltpu.SemaphoreType.DMA((2, 4)),
-            pltpu.SemaphoreType.DMA((2,)),
         ],
         compiler_params=params(10),
         cost_estimate=cost(1_700_000_000, 10_000_000),
         name="image_one",
-    )(arrived, in_hbm(m_hi), in_hbm(m_lo), in_hbm(r_hi), in_hbm(r_lo))
+    )(arrived, in_hbm(m_hi), in_hbm(m_lo))
 
 
 def lanczos(image, last, before, beta):
@@ -573,15 +554,14 @@
     on_other = lax.ppermute(term_on, "c", SWAP)
     thin_other = lax.ppermute(thin, "c", SWAP)
 
-    mine, folded = fold_left(ids, left_env)
+    mine, folded, right_folded = fold(ids, left_env, right_env)
     theirs = lax.ppermute(folded, "c", SWAP)
     below = [lax.ppermute(x, "y", UP) for x in (mine, theirs)]
     above = [lax.ppermute(x, "y", DOWN) for x in (mine, theirs)]
     far = [lax.ppermute(below[0], "y", UP), lax.ppermute(above[1], "y", DOWN)]
 
-    thin_late, _ = lax.optimization_barrier((thin, folded))
     slots = right_slots(
-        ids, right_sector, rsector_other, term_on, on_other, thin_late, thin_other, right_env
+        ids, right_sector, rsector_other, term_on, on_other, thin, thin_other, right_folded
     )
     slots, theirs_now = lax.optimization_barrier((slots, theirs))
     arrived = lax.all_to_all(slots, COL, 0, 0, tiled=True)
@@ -591,7 +571,7 @@
     pieces = [mine, theirs] + above + far + below
     left_sent = left_slots(ids, left_sector, pieces)
     left_arrived = lax.all_to_all(left_sent, COL, 0, 0, tiled=True)
-    l_hi, l_lo, part, r_hi, r_lo = image_one(left_arrived, m_hi, m_lo, r_hi, r_lo)
+    l_hi, l_lo, part = image_one(left_arrived, m_hi, m_lo)
     stacks = (r_hi, r_lo, l_hi, l_lo)
     part, q2, stats = image_two(scalars, part, lax.ppermute(part, "c", SWAP), q1, stats, stacks)
     sent = image_three(scalars, part, lax.ppermute(part, "c", SWAP), q1, q2, stats, stacks)

time: 138 us -> 136 us (0.986)
  Pallas kernels: 33.3 us -> 31.1 us
    pallas_call x3, Pallas kernels: 13.3 us -> 11.1 us  [the longest x1 5.05 us: image_one(): pl.pallas_call(image_one_body, in_specs=[vmem(), hbm(), hbm()], out_specs...]
    unnamed x23 -> x27, local copies, waits for them, and re-layouts: 5.57 us -> 5.55 us
  transfers between devices with their start and end apart: 20 -> 20, of which waited for: 15 -> 15; matrix products, arithmetic and copies ran while one was open for 0% -> 0% of each run, Pallas kernels for 8% -> 7%
where the time goes in v9:
time: 136 us; the launch traced here: 135 us
  waiting for transfers between devices  59 us (43%)
  starting transfers between devices  38.7 us (28%)
  Pallas kernels  31.1 us (23%)
  local copies, waits for them, and re-layouts  5.57 us (4%)
    all_to_all x1, waiting for transfers between devices, local(): left_arrived = lax.all_to_all(left_sent, COL, 0, 0, tiled=True)  15.4 us
    ppermute x2, waiting for transfers between devices, local(): far = [lax.ppermute(below[0], 'y', UP), lax.ppermute(above[1], 'y', DOWN)]  11.6 us
    all_to_all x1, waiting for transfers between devices, local(): got = lax.all_to_all(sent, COL, 0, 0, tiled=True)  9.24 us
    ppermute x2, waiting for transfers between devices, local(): above = [lax.ppermute(x, 'y', DOWN) for x in (mine, theirs)]  9.15 us
    all_to_all x1, starting transfers between devices, local(): arrived = lax.all_to_all(slots, COL, 0, 0, tiled=True)  7.79 us
    ppermute x2, starting transfers between devices, local(): lax.ppermute(part, 'c', SWAP)  5.99 us
    all_to_all x1, starting transfers between devices, local(): left_arrived = lax.all_to_all(left_sent, COL, 0, 0, tiled=True)  5.95 us
    pallas_call x1, Pallas kernels, image_three(): pl.pallas_call(image_three_body, in_specs=[smem()] * 6 + [vmem()] * 9, ou...  5.66 us
  transfers between devices with their start and end apart: 20, of which 15 were waited for; matrix products, arithmetic and copies ran while one was open for 0% of the time, Pallas kernels for 7%

profile of v9, /device:TPU:1, one launch (start us, length us, event | category | flops | bytes accessed | tf_op | source)
XLA Modules:
  0.0 135.5 jit_solution(7814892349610727384)
XLA Ops:
  0.7 3.6 %fold.1 = (f32[4,264,128]{2,1,0:T(8,128)}, f32[4,264,128]{2,1,0:T(8,128)}, f32[9,264,128]{2,1,0:T(8,128)S(1)}) custom-call(s32[3]{0:T(128)S(1)} %pad_add_fusion.ids, f32[4,2,256,256]{3,2,1,0:T(8,128)} %left_env.1, f32[8,2,256,256]{3,2,1,0:T(8,128)} %right_env.1), custom_call_target="tpu_custom_call" | custom-call | flops 1000000 | bytes 6000000 | tf_op jit(solution)/shard_map/fold/pallas_call | solution.py:149
  4.3 1.5 %collective-permute-start.1 = (f32[4,264,128]{2,1,0:T(8,128)}, f32[4,264,128]{2,1,0:T(8,128)S(1)}, u32[]{:S(2)}, u32[]{:S(2)}) collective-permute-start(f32[4,264,128]{2,1,0:T(8,128)} %get-tuple-element.21), channel_id=1, source_target_pairs={{0,16},{16,0},{1,17},{17,1},{2,18},{18,2},{3,19},{19,3},{4,20},{20... | collective-permute-start | bytes 1622024 | tf_op jit(solution)/shard_map/ppermute | solution.py:558
  5.8 1.4 %collective-permute-start.4 = (f32[4,264,128]{2,1,0:T(8,128)}, f32[4,264,128]{2,1,0:T(8,128)S(1)}, u32[]{:S(2)}, u32[]{:S(2)}) collective-permute-start(f32[4,264,128]{2,1,0:T(8,128)} %get-tuple-element.20.refs_0_), channel_id=1, source_target_pairs={{0,32},{32,64},{64,96},{96,0},{1,33},{33,65},{65,97},{97,1},{2,34}... | collective-permute-start | bytes 1622024 | tf_op jit(solution)/shard_map/ppermute | solution.py:559
  7.6 2.8 %collective-permute-start.3 = (f32[4,264,128]{2,1,0:T(8,128)S(1)}, f32[4,264,128]{2,1,0:T(8,128)S(1)}, u32[]{:S(2)}, u32[]{:S(2)}) collective-permute-start(f32[4,264,128]{2,1,0:T(8,128)S(1)} %collective-permute-done.1.refs_1_), channel_id=1, source_target_pairs={{0,96},{32,0},{64,32},{96,64},{1,97},{33,1},{65,33},{97,65},{2,98}... | collective-permute-start | bytes 1622024 | tf_op jit(solution)/shard_map/ppermute | solution.py:560
  12.5 2.4 %right_slots.1 = f32[16,296,128]{2,1,0:T(8,128)} custom-call(s32[3]{0:T(128)S(1)} %pad_add_fusion.ids, s32[8]{0:T(128)S(1)} %copy-done.3, s32[8]{0:T(128)S(1)} %collective-permute-done.rsector_other, s32[8,2]{1,0:T(8,128)S(1)} %copy.11.on, s32[8,2]{1,0:T(8,128)S(1)} %collective-permute-done.8.on_other, f32[8,16,256]{2,1,0:T(8,128)S(1)} %bitcast.8, ...), custom_call_target="tpu_custom_call" | custom-call | flops 4000000 | bytes 6000000 | tf_op jit(solution)/shard_map/right_slots/pallas_call | solution.py:203
  15.0 7.8 %all-to-all-start.1 = ((f32[16,296,128]{2,1,0:T(8,128)}), f32[16,296,128]{2,1,0:T(8,128)}, u32[]{:S(2)}, u32[]{:S(2)}) async-start(f32[16,296,128]{2,1,0:T(8,128)} %right_slots.1), calls=%async_computation.1 | async-start | bytes 4849664 | tf_op jit(solution)/shard_map/all_to_all | solution.py:567
  24.3 2.6 %collective-permute-start.6 = (f32[4,264,128]{2,1,0:T(8,128)S(1)}, f32[4,264,128]{2,1,0:T(8,128)S(1)}, u32[]{:S(2)}, u32[]{:S(2)}) collective-permute-start(f32[4,264,128]{2,1,0:T(8,128)S(1)} %collective-permute-done.3.refs_3_), channel_id=1, source_target_pairs={{0,96},{32,0},{64,32},{96,64},{1,97},{33,1},{65,33},{97,65},{2,98}... | collective-permute-start | bytes 1622024 | tf_op jit(solution)/shard_map/ppermute | solution.py:561
  27.0 9.2 %collective-permute-done.2.refs_2_ = f32[4,264,128]{2,1,0:T(8,128)S(1)} collective-permute-done((f32[4,264,128]{2,1,0:T(8,128)S(1)}, f32[4,264,128]{2,1,0:T(8,128)S(1)}, u32[]{:S(2)}, u32[]{:S(2)}) %collective-permute-start.2) | collective-permute-done | bytes 540704 | tf_op jit(solution)/shard_map/ppermute | solution.py:560
  36.1 1.4 %collective-permute-done.7.refs_7_ = f32[4,264,128]{2,1,0:T(8,128)S(1)} collective-permute-done((f32[4,264,128]{2,1,0:T(8,128)S(1)}, f32[4,264,128]{2,1,0:T(8,128)S(1)}, u32[]{:S(2)}, u32[]{:S(2)}) %collective-permute-start.7) | collective-permute-done | bytes 540704 | tf_op jit(solution)/shard_map/ppermute | solution.py:559
  37.5 11.6 %collective-permute-done.5.refs_4_ = f32[4,264,128]{2,1,0:T(8,128)S(1)} collective-permute-done((f32[4,264,128]{2,1,0:T(8,128)S(1)}, f32[4,264,128]{2,1,0:T(8,128)S(1)}, u32[]{:S(2)}, u32[]{:S(2)}) %collective-permute-start.5) | collective-permute-done | bytes 540704 | tf_op jit(solution)/shard_map/ppermute | solution.py:561
  49.1 2.1 %left_slots.1 = f32[16,264,128]{2,1,0:T(8,128)} custom-call(s32[3]{0:T(128)S(1)} %pad_add_fusion.ids, s32[64]{0:T(128)S(1)} %copy-done.4, f32[4,264,128]{2,1,0:T(8,128)S(1)} %copy-done.7, f32[4,264,128]{2,1,0:T(8,128)S(1)} %collective-permute-done.1.refs_1_, f32[4,264,128]{2,1,0:T(8,128)S(1)} %collective-permute-done.2.refs_2_, ...), custom_call_target="tpu_custom_call" | custom-call | flops 15000000512 | bytes 4000000 | tf_op jit(solution)/shard_map/left_slots/pallas_call | solution.py:256
  51.2 4.2 %all-to-all-done.1.slots = f32[16,296,128]{2,1,0:T(8,128)} async-done(((f32[16,296,128]{2,1,0:T(8,128)}), f32[16,296,128]{2,1,0:T(8,128)}, u32[]{:S(2)}, u32[]{:S(2)}) %all-to-all-start.1) | async-done | bytes 2424864 | tf_op jit(solution)/shard_map/all_to_all | solution.py:567
  55.4 5.9 %all-to-all-start = ((f32[16,264,128]{2,1,0:T(8,128)}), f32[16,264,128]{2,1,0:T(8,128)S(1)}, u32[]{:S(2)}, u32[]{:S(2)}) async-start(f32[16,264,128]{2,1,0:T(8,128)} %left_slots.1), calls=%async_computation | async-start | bytes 4325376 | tf_op jit(solution)/shard_map/all_to_all | solution.py:573
  61.4 5.3 %first_vector.1 = (bf16[4096,256]{1,0:T(8,128)(2,1)S(1)}, bf16[4096,256]{1,0:T(8,128)(2,1)S(1)}, bf16[256,4096]{1,0:T(8,128)(2,1)S(1)}, bf16[256,4096]{1,0:T(8,1...) custom-call(s32[3]{0:T(128)S(1)} %pad_add_fusion.ids, s32[8]{0:T(128)S(1)} %copy-done.3, ...), custom_call_target="tpu_custom_call" | custom-call | flops 1700000000 | bytes 12000000 | tf_op jit(solution)/shard_map/first_vector/pallas_call | solution.py:317
  66.7 1.3 copy-done
  68.0 1.4 %copy-done.1 = bf16[256,4096]{1,0:T(8,128)(2,1)} copy-done((bf16[256,4096]{1,0:T(8,128)(2,1)}, bf16[256,4096]{1,0:T(8,128)(2,1)S(1)}, u32[]{:S(2)}) %copy-start.1) | copy-done | bytes 2097176
  69.4 1.4 %copy-done.8 = bf16[4096,256]{1,0:T(8,128)(2,1)} copy-done((bf16[4096,256]{1,0:T(8,128)(2,1)}, bf16[4096,256]{1,0:T(8,128)(2,1)S(1)}, u32[]{:S(2)}) %copy-start.8) | copy-done | bytes 2097176
  70.8 1.3 copy-done.10
  72.1 15.4 %all-to-all-done.arrived = f32[16,264,128]{2,1,0:T(8,128)S(1)} async-done(((f32[16,264,128]{2,1,0:T(8,128)}), f32[16,264,128]{2,1,0:T(8,128)S(1)}, u32[]{:S(2)}, u32[]{:S(2)}) %all-to-all-start) | async-done | bytes 2162720 | tf_op jit(solution)/shard_map/all_to_all | solution.py:573
  87.5 5.1 %image_one.1 = (bf16[4096,256]{1,0:T(8,128)(2,1)S(1)}, bf16[4096,256]{1,0:T(8,128)(2,1)S(1)}, f32[256,256]{1,0:T(8,128)S(1)}) custom-call(f32[16,264,128]{2,1,0:T(8,128)S(1)} %all-to-all-done.arrived, bf16[256,4096]{1,0:T(8,128)(2,1)} %copy-done, bf16[256,4096]{1,0:T(8,128)(2,1)} %copy-done.1), custom_call_target="tpu_custom_call" | custom-call | flops 1700000000 | bytes 10000000 | tf_op jit(solution)/shard_map/image_one/pallas_call | solution.py:365
  92.6 5.5 %collective-permute-start.10 = (f32[256,256]{1,0:T(8,128)S(1)}, f32[256,256]{1,0:T(8,128)S(1)}, u32[]{:S(2)}, u32[]{:S(2)}) collective-permute-start(f32[256,256]{1,0:T(8,128)S(1)} %get-tuple-element.26.part_a), channel_id=1, source_target_pairs={{0,16},{16,0},{1,17},{17,1},{2,18},{18,2},{3,19},{19,3},{4,20},{20... | collective-permute-start | bytes 786440 | tf_op jit(solution)/shard_map/ppermute | solution.py:576
  98.1 1.2 collective-permute-done.10.part_b
  99.3 4.7 %image_two.1 = (f32[256,256]{1,0:T(8,128)S(1)}, f32[256,256]{1,0:T(8,128)S(1)}, f32[8,128]{1,0:T(8,128)S(1)}) custom-call(s32[3]{0:T(128)S(1)} %pad_add_fusion.ids, s32[8]{0:T(128)S(1)} %copy-done.3, s32[8]{0:T(128)S(1)} %collective-permute-done.rsector_other, s32[64]{0:T(128)S(1)} %copy-done.4, s32[32]{0:T(128)S(1)} %copy-done.5, s32[8]{0:T(128)S(1)} %copy-done.6, ...), custom_call_target="tpu_custom_call" | custom-call | flops 3300000000 | bytes 9000000 | tf_op jit(solution)/shard_map/image_two/pallas_call | solution.py:416
  104.5 1.2 collective-permute-done.11.part_b
  105.6 5.7 %image_three.1 = f32[16,24,256]{2,1,0:T(8,128)} custom-call(s32[3]{0:T(128)S(1)} %pad_add_fusion.ids, s32[8]{0:T(128)S(1)} %copy-done.3, s32[8]{0:T(128)S(1)} %collective-permute-done.rsector_other, s32[64]{0:T(128)S(1)} %copy-done.4, s32[32]{0:T(128)S(1)} %copy-done.5, s32[8]{0:T(128)S(1)} %copy-done.6, f32[256,256]{1,0:T(8,128)S(1)} %get-tuple-element.33.part_a, ...), custom_call_target="tpu_custom_call" | custom-call | flops 3300000000 | bytes 9000000 | tf_op jit(solution)/shard_map/image_three/pallas_call | solution.py:452
  111.3 3.6 %all-to-all-start.2 = ((f32[16,24,256]{2,1,0:T(8,128)}), f32[16,24,256]{2,1,0:T(8,128)S(1)}, u32[]{:S(2)}, u32[]{:S(2)}) async-start(f32[16,24,256]{2,1,0:T(8,128)} %image_three.1), calls=%async_computation.2 | async-start | bytes 786432 | tf_op jit(solution)/shard_map/all_to_all | solution.py:579
  114.9 9.2 %all-to-all-done.2.got = f32[16,24,256]{2,1,0:T(8,128)S(1)} async-done(((f32[16,24,256]{2,1,0:T(8,128)}), f32[16,24,256]{2,1,0:T(8,128)S(1)}, u32[]{:S(2)}, u32[]{:S(2)}) %all-to-all-start.2) | async-done | bytes 393248 | tf_op jit(solution)/shard_map/all_to_all | solution.py:579
  124.2 1.6 %collective-permute-start.16 = (f32[8,24,256]{2,1,0:T(8,128)S(1)}, f32[8,24,256]{2,1,0:T(8,128)S(1)}, u32[]{:S(2)}, u32[]{:S(2)}) collective-permute-start(f32[8,24,256]{2,1,0:T(8,128)S(1)} %constant_dynamic-slice_fusion), channel_id=1, source_target_pairs={{0,16},{16,0},{1,17},{17,1},{2,18},{18,2},{3,19},{19,3},{4,20},{20... | collective-permute-start | bytes 589832 | tf_op jit(solution)/shard_map/ppermute | solution.py:584
  127.3 1.0 collective-permute-done.14
  128.3 2.0 %collective-permute-done.13 = f32[16,128]{1,0:T(8,128)S(1)} collective-permute-done((f32[16,128]{1,0:T(8,128)S(1)}, f32[16,128]{1,0:T(8,128)S(1)}, u32[]{:S(2)}, u32[]{:S(2)}) %collective-permute-start.13) | collective-permute-done | bytes 8224 | tf_op jit(solution)/shard_map/ppermute | solution.py:582
  131.0 1.2 collective-permute-start.15
  133.1 2.2 %finish.1 = (f32[8,16,256]{2,1,0:T(8,128)}, f32[1,1]{1,0:T(1,128)}) custom-call(s32[3]{0:T(128)S(1)} %pad_add_fusion.ids, s32[64]{0:T(128)S(1)} %copy-done.4, s32[8]{0:T(128)S(1)} %copy-done.3, s32[32]{0:T(128)S(1)} %copy-done.5, s32[8]{0:T(128)S(1)} %copy-done.6, f32[64,128]{1,0:T(8,128)S(1)} %pad_maximum_fusion.own_stats, ...), custom_call_target="tpu_custom_call" | custom-call | tf_op jit(solution)/shard_map/finish/pallas_call | solution.py:532
  (47 shorter events, 7.7 us)
Async XLA Ops:
  0.7 9.7 %copy-start.2 = (f32[8,256,16]{1,2,0:T(8,128)S(1)}, f32[8,256,16]{1,2,0:T(8,128)}, u32[]{:S(2)}) copy-start(f32[8,256,16]{1,2,0:T(8,128)} %param.8) | copy-start | bytes 393220
  0.7 10.3 %copy-start.3 = (s32[8]{0:T(128)S(1)}, s32[8]{0:T(128)}, u32[]{:S(2)}) copy-start(s32[8]{0:T(128)} %rsector.9) | copy-start | bytes 100
  0.7 10.4 %copy-start.12 = (s32[8,2]{0,1:T(2,128)S(1)}, s32[8,2]{0,1:T(2,128)}, u32[]{:S(2)}) copy-start(s32[8,2]{0,1:T(2,128)} %param.13) | copy-start | bytes 196
  4.3 3.3 %collective-permute-start.1 = (f32[4,264,128]{2,1,0:T(8,128)}, f32[4,264,128]{2,1,0:T(8,128)S(1)}, u32[]{:S(2)}, u32[]{:S(2)}) collective-permute-start(f32[4,264,128]{2,1,0:T(8,128)} %get-tuple-element.21), channel_id=1, source_target_pairs={{0,16},{16,0},{1,17},{17,1},{2,18},{18,2},{3,19},{19,3},{4,20},{20... | collective-permute-start | bytes 1622024 | tf_op jit(solution)/shard_map/ppermute | solution.py:558
  5.8 18.5 %collective-permute-start.4 = (f32[4,264,128]{2,1,0:T(8,128)}, f32[4,264,128]{2,1,0:T(8,128)S(1)}, u32[]{:S(2)}, u32[]{:S(2)}) collective-permute-start(f32[4,264,128]{2,1,0:T(8,128)} %get-tuple-element.20.refs_0_), channel_id=1, source_target_pairs={{0,32},{32,64},{64,96},{96,0},{1,33},{33,65},{65,97},{97,1},{2,34}... | collective-permute-start | bytes 1622024 | tf_op jit(solution)/shard_map/ppermute | solution.py:559
  7.6 16.8 %collective-permute-start.3 = (f32[4,264,128]{2,1,0:T(8,128)S(1)}, f32[4,264,128]{2,1,0:T(8,128)S(1)}, u32[]{:S(2)}, u32[]{:S(2)}) collective-permute-start(f32[4,264,128]{2,1,0:T(8,128)S(1)} %collective-permute-done.1.refs_1_), channel_id=1, source_target_pairs={{0,96},{32,0},{64,32},{96,64},{1,97},{33,1},{65,33},{97,65},{2,98}... | collective-permute-start | bytes 1622024 | tf_op jit(solution)/shard_map/ppermute | solution.py:560
  10.4 2.1 %collective-permute-start.9 = (f32[8,16,256]{2,1,0:T(8,128)S(1)}, f32[8,16,256]{2,1,0:T(8,128)S(1)}, u32[]{:S(2)}, u32[]{:S(2)}) collective-permute-start(f32[8,16,256]{2,1,0:T(8,128)S(1)} %bitcast.7), channel_id=1, source_target_pairs={{0,16},{16,0},{1,17},{17,1},{2,18},{18,2},{3,19},{19,3},{4,20},{20... | collective-permute-start | bytes 393224 | tf_op jit(solution)/shard_map/ppermute | solution.py:555
  11.1 1.1 collective-permute-start
  11.2 1.2 collective-permute-start.8
  14.9 7.8 %copy-start.7 = (f32[4,264,128]{2,1,0:T(8,128)S(1)}, f32[4,264,128]{2,1,0:T(8,128)}, u32[]{:S(2)}) copy-start(f32[4,264,128]{2,1,0:T(8,128)} %get-tuple-element.20.refs_0_) | copy-start | bytes 1622020
  14.9 34.1 %copy-start.4 = (s32[64]{0:T(128)S(1)}, s32[64]{0:T(128)}, u32[]{:S(2)}) copy-start(s32[64]{0:T(128)} %sector.7) | copy-start | bytes 772
  15.0 40.4 %all-to-all-start.1 = ((f32[16,296,128]{2,1,0:T(8,128)}), f32[16,296,128]{2,1,0:T(8,128)}, u32[]{:S(2)}, u32[]{:S(2)}) async-start(f32[16,296,128]{2,1,0:T(8,128)} %right_slots.1), calls=%async_computation.1 | async-start | bytes 4849664 | tf_op jit(solution)/shard_map/all_to_all | solution.py:567
  22.8 13.4 %collective-permute-start.2 = (f32[4,264,128]{2,1,0:T(8,128)S(1)}, f32[4,264,128]{2,1,0:T(8,128)S(1)}, u32[]{:S(2)}, u32[]{:S(2)}) collective-permute-start(f32[4,264,128]{2,1,0:T(8,128)S(1)} %copy-done.7), channel_id=1, source_target_pairs={{0,96},{32,0},{64,32},{96,64},{1,97},{33,1},{65,33},{97,65},{2,98}... | collective-permute-start | bytes 1622024 | tf_op jit(solution)/shard_map/ppermute | solution.py:560
  23.3 14.2 %collective-permute-start.7 = (f32[4,264,128]{2,1,0:T(8,128)S(1)}, f32[4,264,128]{2,1,0:T(8,128)S(1)}, u32[]{:S(2)}, u32[]{:S(2)}) collective-permute-start(f32[4,264,128]{2,1,0:T(8,128)S(1)} %collective-permute-done.1.refs_1_), channel_id=1, source_target_pairs={{0,32},{32,64},{64,96},{96,0},{1,33},{33,65},{65,97},{97,1},{2,34}... | collective-permute-start | bytes 1622024 | tf_op jit(solution)/shard_map/ppermute | solution.py:559
  24.3 24.8 %collective-permute-start.5 = (f32[4,264,128]{2,1,0:T(8,128)S(1)}, f32[4,264,128]{2,1,0:T(8,128)S(1)}, u32[]{:S(2)}, u32[]{:S(2)}) collective-permute-start(f32[4,264,128]{2,1,0:T(8,128)S(1)} %collective-permute-done.4.refs_6_), channel_id=1, source_target_pairs={{0,32},{32,64},{64,96},{96,0},{1,33},{33,65},{65,97},{97,1},{2,34}... | collective-permute-start | bytes 1622024 | tf_op jit(solution)/shard_map/ppermute | solution.py:561
  24.3 24.7 %collective-permute-start.6 = (f32[4,264,128]{2,1,0:T(8,128)S(1)}, f32[4,264,128]{2,1,0:T(8,128)S(1)}, u32[]{:S(2)}, u32[]{:S(2)}) collective-permute-start(f32[4,264,128]{2,1,0:T(8,128)S(1)} %collective-permute-done.3.refs_3_), channel_id=1, source_target_pairs={{0,96},{32,0},{64,32},{96,64},{1,97},{33,1},{65,33},{97,65},{2,98}... | collective-permute-start | bytes 1622024 | tf_op jit(solution)/shard_map/ppermute | solution.py:561
  51.2 10.2 %copy-start.5 = (s32[32]{0:T(128)S(1)}, s32[32]{0:T(128)}, u32[]{:S(2)}) copy-start(s32[32]{0:T(128)} %lsize.7) | copy-start | bytes 388
  51.2 10.2 %copy-start.6 = (s32[8]{0:T(128)S(1)}, s32[8]{0:T(128)}, u32[]{:S(2)}) copy-start(s32[8]{0:T(128)} %rsize.7) | copy-start | bytes 100
  55.4 32.1 %all-to-all-start = ((f32[16,264,128]{2,1,0:T(8,128)}), f32[16,264,128]{2,1,0:T(8,128)S(1)}, u32[]{:S(2)}, u32[]{:S(2)}) async-start(f32[16,264,128]{2,1,0:T(8,128)} %left_slots.1), calls=%async_computation | async-start | bytes 4325376 | tf_op jit(solution)/shard_map/all_to_all | solution.py:573
  68.0 1.4 %copy-start.1 = (bf16[256,4096]{1,0:T(8,128)(2,1)}, bf16[256,4096]{1,0:T(8,128)(2,1)S(1)}, u32[]{:S(2)}) copy-start(bf16[256,4096]{1,0:T(8,128)(2,1)S(1)} %get-tuple-element.25.m_lo) | copy-start | bytes 6291460
  69.4 1.4 %copy-start.8 = (bf16[4096,256]{1,0:T(8,128)(2,1)}, bf16[4096,256]{1,0:T(8,128)(2,1)S(1)}, u32[]{:S(2)}) copy-start(bf16[4096,256]{1,0:T(8,128)(2,1)S(1)} %get-tuple-element.29.r_hi) | copy-start | bytes 6291460
  70.8 1.3 copy-start.10
  87.5 11.8 %copy-start.9 = (bf16[4096,256]{1,0:T(8,128)(2,1)S(1)}, bf16[4096,256]{1,0:T(8,128)(2,1)}, u32[]{:S(2)}) copy-start(bf16[4096,256]{1,0:T(8,128)(2,1)} %copy-done.8) | copy-start | bytes 6291460
  87.5 11.8 %copy-start.11 = (bf16[4096,256]{1,0:T(8,128)(2,1)S(1)}, bf16[4096,256]{1,0:T(8,128)(2,1)}, u32[]{:S(2)}) copy-start(bf16[4096,256]{1,0:T(8,128)(2,1)} %copy-done.10) | copy-start | bytes 6291460
  92.6 6.7 %collective-permute-start.10 = (f32[256,256]{1,0:T(8,128)S(1)}, f32[256,256]{1,0:T(8,128)S(1)}, u32[]{:S(2)}, u32[]{:S(2)}) collective-permute-start(f32[256,256]{1,0:T(8,128)S(1)} %get-tuple-element.26.part_a), channel_id=1, source_target_pairs={{0,16},{16,0},{1,17},{17,1},{2,18},{18,2},{3,19},{19,3},{4,20},{20... | collective-permute-start | bytes 786440 | tf_op jit(solution)/shard_map/ppermute | solution.py:576
  104.0 1.6 %collective-permute-start.11 = (f32[256,256]{1,0:T(8,128)S(1)}, f32[256,256]{1,0:T(8,128)S(1)}, u32[]{:S(2)}, u32[]{:S(2)}) collective-permute-start(f32[256,256]{1,0:T(8,128)S(1)} %get-tuple-element.33.part_a), channel_id=1, source_target_pairs={{0,16},{16,0},{1,17},{17,1},{2,18},{18,2},{3,19},{19,3},{4,20},{20... | collective-permute-start | bytes 786440 | tf_op jit(solution)/shard_map/ppermute | solution.py:577
  111.3 12.9 %all-to-all-start.2 = ((f32[16,24,256]{2,1,0:T(8,128)}), f32[16,24,256]{2,1,0:T(8,128)S(1)}, u32[]{:S(2)}, u32[]{:S(2)}) async-start(f32[16,24,256]{2,1,0:T(8,128)} %image_three.1), calls=%async_computation.2 | async-start | bytes 786432 | tf_op jit(solution)/shard_map/all_to_all | solution.py:579
  124.2 8.9 %collective-permute-start.16 = (f32[8,24,256]{2,1,0:T(8,128)S(1)}, f32[8,24,256]{2,1,0:T(8,128)S(1)}, u32[]{:S(2)}, u32[]{:S(2)}) collective-permute-start(f32[8,24,256]{2,1,0:T(8,128)S(1)} %constant_dynamic-slice_fusion), channel_id=1, source_target_pairs={{0,16},{16,0},{1,17},{17,1},{2,18},{18,2},{3,19},{19,3},{4,20},{20... | collective-permute-start | bytes 589832 | tf_op jit(solution)/shard_map/ppermute | solution.py:584
  125.8 2.5 %collective-permute-start.14 = (f32[16,128]{1,0:T(8,128)S(1)}, f32[16,128]{1,0:T(8,128)S(1)}, u32[]{:S(2)}, u32[]{:S(2)}) collective-permute-start(f32[16,128]{1,0:T(8,128)S(1)} %bitcast.10), channel_id=1, source_target_pairs={{0,96},{32,0},{64,32},{96,64},{1,97},{33,1},{65,33},{97,65},{2,98}... | collective-permute-start | bytes 24584 | tf_op jit(solution)/shard_map/ppermute | solution.py:582
  126.3 4.0 %collective-permute-start.13 = (f32[16,128]{1,0:T(8,128)S(1)}, f32[16,128]{1,0:T(8,128)S(1)}, u32[]{:S(2)}, u32[]{:S(2)}) collective-permute-start(f32[16,128]{1,0:T(8,128)S(1)} %bitcast.11), channel_id=1, source_target_pairs={{0,64},{32,96},{64,0},{96,32},{1,65},{33,97},{65,1},{97,33},{2,66}... | collective-permute-start | bytes 24584 | tf_op jit(solution)/shard_map/ppermute | solution.py:582
  126.3 4.7 %collective-permute-start.12 = (f32[16,128]{1,0:T(8,128)S(1)}, f32[16,128]{1,0:T(8,128)S(1)}, u32[]{:S(2)}, u32[]{:S(2)}) collective-permute-start(f32[16,128]{1,0:T(8,128)S(1)} %bitcast.12), channel_id=1, source_target_pairs={{0,32},{32,64},{64,96},{96,0},{1,33},{33,65},{65,97},{97,1},{2,34}... | collective-permute-start | bytes 24584 | tf_op jit(solution)/shard_map/ppermute | solution.py:582
  131.0 2.1 %collective-permute-start.15 = (f32[64,128]{1,0:T(8,128)S(1)}, f32[64,128]{1,0:T(8,128)S(1)}, u32[]{:S(2)}, u32[]{:S(2)}) collective-permute-start(f32[64,128]{1,0:T(8,128)S(1)} %pad_maximum_fusion.own_stats), channel_id=1, source_target_pairs={{0,16},{16,0},{1,17},{17,1},{2,18},{18,2},{3,19},{19,3},{4,20},{20... | collective-permute-start | bytes 98312 | tf_op jit(solution)/shard_map/ppermute | solution.py:586
  (1 other events, 1.3 us)

commit v10 on v9

--- a/solution.py
+++ b/solution.py
@@ -115,34 +115,29 @@
 def fold_body(
     ids, left_env, right_env, keep, give, right, tiles, folded, others, sem_in, sem_out, sem_right
 ):
-    def fetch(t, n):
+    def fetch(t):
         term = ids[1] if t else 1 - ids[1]
-        at = 4 * t + n
-        return pltpu.make_async_copy(left_env.at[n, term], tiles.at[at], sem_in.at[at])
-
-    def fetch_right(n):
-        return pltpu.make_async_copy(right_env.at[n, ids[1]], others.at[n], sem_right.at[n])
-
-    def store(t, n):
-        at = 4 * t + n
+        return pltpu.make_async_copy(left_env.at[:, term], tiles.at[t], sem_in.at[t])
+
+    def store(t):
         dst = keep if t else give
-        return pltpu.make_async_copy(folded.at[at], dst.at[n], sem_out.at[at])
-
-    order = [(t, n) for t in range(2) for n in range(4)]
-    for t, n in order:
-        fetch(t, n).start()
+        return pltpu.make_async_copy(folded.at[t], dst, sem_out.at[t])
+
+    rights = pltpu.make_async_copy(right_env.at[:, ids[1]], others, sem_right)
+    for t in range(2):
+        fetch(t).start()
+    rights.start()
+    right[8] = jnp.zeros((FOLDED, HALF), f32)
+    for t in range(2):
+        fetch(t).wait()
+        for n in range(4):
+            put_folded(folded.at[t], n, tiles[t, n])
+        store(t).start()
+    rights.wait()
     for n in range(8):
-        fetch_right(n).start()
-    right[8] = jnp.zeros((FOLDED, HALF), f32)
-    for t, n in order:
-        fetch(t, n).wait()
-        put_folded(folded, 4 * t + n, tiles[4 * t + n])
-        store(t, n).start()
-    for n in range(8):
-        fetch_right(n).wait()
         put_folded(right, n, others[n])
-    for t, n in order:
-        store(t, n).wait()
+    for t in range(2):
+        store(t).wait()
 
 
 def fold(ids, left_env, right_env):
@@ -153,12 +148,12 @@
         out_shape=[pltpu.HBM((4, FOLDED, HALF), f32)] * 2
         + [jax.ShapeDtypeStruct((9, FOLDED, HALF), f32)],
         scratch_shapes=[
+            pltpu.VMEM((2, 4, TILE, TILE), f32),
+            pltpu.VMEM((2, 4, FOLDED, HALF), f32),
             pltpu.VMEM((8, TILE, TILE), f32),
-            pltpu.VMEM((8, FOLDED, HALF), f32),
-            pltpu.VMEM((8, TILE, TILE), f32),
-            pltpu.SemaphoreType.DMA((8,)),
-            pltpu.SemaphoreType.DMA((8,)),
-            pltpu.SemaphoreType.DMA((8,)),
+            pltpu.SemaphoreType.DMA((2,)),
+            pltpu.SemaphoreType.DMA((2,)),
+            pltpu.SemaphoreType.DMA(()),
         ],
         compiler_params=params(10),
         cost_estimate=cost(1_000_000, 6_000_000),
@@ -171,32 +166,21 @@
 
 
 def right_slots_body(
-    ids, rsector, rsector_other, on, on_other, thin, thin_other, folded, out, cols, sem_out, sem_thin
+    ids, rsector, rsector_other, on, on_other, thin, thin_other, folded, out, cols, sem
 ):
-    def store_thin(slot):
-        return pltpu.make_async_copy(
-            cols.at[slot], out.at[slot, pl.ds(0, THIN), :], sem_thin.at[slot]
-        )
-
-    def store(slot, sector):
-        return pltpu.make_async_copy(
-            folded.at[sector], out.at[slot, pl.ds(THIN, FOLDED), :], sem_out.at[slot]
-        )
-
     for slot in range(TERMS):
         here = slot // 8 == ids[1]
         weight = jnp.where(here, on[slot % 8, ids[1]], on_other[slot % 8, ids[1]])
         sector = sector_of(ids, rsector, rsector_other, slot)
-        store(slot, jnp.where(weight == 0, 8, sector)).start()
+        src = folded.at[jnp.where(weight == 0, 8, sector)]
+        pltpu.make_async_copy(src, out.at[slot, pl.ds(THIN, FOLDED), :], sem).start()
     for slot in range(TERMS):
         here = slot // 8 == ids[1]
         block = jnp.where(here, thin[slot % 8], thin_other[slot % 8])
         cols[slot, :16, :] = block[:, :HALF]
         cols[slot, 16:, :] = block[:, HALF:]
-        store_thin(slot).start()
-    for slot in range(TERMS):
-        store_thin(slot).wait()
-        store(slot, 0).wait()
+    pltpu.make_async_copy(cols, out.at[:, pl.ds(0, THIN), :], sem).start()
+    pltpu.make_async_copy(out, out, sem).wait()
 
 
 def right_slots(ids, rsector, rsector_other, on, on_other, thin, thin_other, folded):
@@ -207,8 +191,7 @@
         out_shape=pltpu.HBM((TERMS, SLOT, HALF), f32),
         scratch_shapes=[
             pltpu.VMEM((TERMS, THIN, HALF), f32),
-            pltpu.SemaphoreType.DMA((TERMS,)),
-            pltpu.SemaphoreType.DMA((TERMS,)),
+            pltpu.SemaphoreType.DMA(()),
         ],
         compiler_params=params(6),
         cost_estimate=cost(4_000_000, 6_000_000),
@@ -222,7 +205,7 @@
     out, sem = refs[8:]
 
     def store(src, slot):
-        return pltpu.make_async_copy(src, out.at[slot], sem.at[slot])
+        return pltpu.make_async_copy(src, out.at[slot], sem)
 
     def start(slot, carry):
         sector = left_sector[ids[0] * 16 + slot]
@@ -244,12 +227,8 @@
 
         return carry
 
-    def finished(slot, carry):
-        store(mine.at[0], slot).wait()
-        return carry
-
     lax.fori_loop(0, TERMS, start, 0)
-    lax.fori_loop(0, TERMS, finished, 0)
+    pltpu.make_async_copy(out, out, sem).wait()
 
 
 def left_slots(ids, left_sector, pieces):
@@ -258,7 +237,7 @@
         in_specs=[smem(), smem()] + [vmem()] * 8,
         out_specs=hbm(),
         out_shape=pltpu.HBM((TERMS, FOLDED, HALF), f32),
-        scratch_shapes=[pltpu.SemaphoreType.DMA((TERMS,))],
+        scratch_shapes=[pltpu.SemaphoreType.DMA(())],
         compiler_params=params(8),
         cost_estimate=cost(LEFT_FLOPS, 4_000_000),
         name="left_slots",
@@ -336,28 +315,20 @@
     )(*scalars, in_hbm(slots))
 
 
-def image_one_body(arrived, m_hi, m_lo, l_hi, l_lo, part, here, sem):
-    chunk = TERMS // 4
-
-    def fetch(p, c):
-        cols = pl.ds(c * chunk * TILE, chunk * TILE)
-        src = (m_hi, m_lo)[p]
-        return pltpu.make_async_copy(src.at[:, cols], here.at[p, :, cols], sem.at[p, c])
-
-    for c in range(4):
-        for p in range(2):
-            fetch(p, c).start()
+def image_one_body(arrived, m_hi, m_lo, l_hi, l_lo, part, here_hi, here_lo, sem):
+    fetches = [
+        pltpu.make_async_copy(m_hi, here_hi, sem.at[0]),
+        pltpu.make_async_copy(m_lo, here_lo, sem.at[1]),
+    ]
+    for fetch in fetches:
+        fetch.start()
     for n in range(TERMS):
         hi, lo = split(get_folded(arrived, n, 0))
         l_hi[n * TILE : (n + 1) * TILE, :] = hi
         l_lo[n * TILE : (n + 1) * TILE, :] = lo
-    acc = jnp.zeros((TILE, TILE), f32)
-    for c in range(4):
-        for p in range(2):
-            fetch(p, c).wait()
-        cols = pl.ds(c * chunk * TILE, chunk * TILE)
-        acc = acc + dot3(here[0, :, cols], here[1, :, cols], l_hi[cols, :], l_lo[cols, :])
-    part[...] = acc
+    for fetch in fetches:
+        fetch.wait()
+    part[...] = dot3(here_hi[...], here_lo[...], l_hi[...], l_lo[...])
 
 
 def image_one(arrived, m_hi, m_lo):
@@ -368,8 +339,9 @@
         out_specs=[vmem()] * 3,
         out_shape=[stack, stack, jax.ShapeDtypeStruct((TILE, TILE), f32)],
         scratch_shapes=[
-            pltpu.VMEM((2, TILE, TERMS * TILE), bf16),
-            pltpu.SemaphoreType.DMA((2, 4)),
+            pltpu.VMEM((TILE, TERMS * TILE), bf16),
+            pltpu.VMEM((TILE, TERMS * TILE), bf16),
+            pltpu.SemaphoreType.DMA((2,)),
         ],
         compiler_params=params(10),
         cost_estimate=cost(1_700_000_000, 10_000_000),

time: 136 us -> 134 us (0.985)
  Pallas kernels: 31.1 us -> 29.3 us
where the time goes in v10:
time: 134 us
  waiting for transfers between devices  59.2 us (44%)
  starting transfers between devices  38.7 us (29%)
  Pallas kernels  29.3 us (22%)
  local copies, waits for them, and re-layouts  5.57 us (4%)
    all_to_all x1, waiting for transfers between devices, local(): left_arrived = lax.all_to_all(left_sent, COL, 0, 0, tiled=True)  15.4 us
    ppermute x2, waiting for transfers between devices, local(): far = [lax.ppermute(below[0], 'y', UP), lax.ppermute(above[1], 'y', DOWN)]  11.6 us
    all_to_all x1, waiting for transfers between devices, local(): got = lax.all_to_all(sent, COL, 0, 0, tiled=True)  9.24 us
    ppermute x2, waiting for transfers between devices, local(): above = [lax.ppermute(x, 'y', DOWN) for x in (mine, theirs)]  9.15 us
    all_to_all x1, starting transfers between devices, local(): arrived = lax.all_to_all(slots, COL, 0, 0, tiled=True)  7.79 us
    ppermute x2, starting transfers between devices, local(): lax.ppermute(part, 'c', SWAP)  5.99 us
    all_to_all x1, starting transfers between devices, local(): left_arrived = lax.all_to_all(left_sent, COL, 0, 0, tiled=True)  5.95 us
    pallas_call x1, Pallas kernels, image_three(): pl.pallas_call(image_three_body, in_specs=[smem()] * 6 + [vmem()] * 9, ou...  5.66 us
  transfers between devices with their start and end apart: 20, of which 15 were waited for; matrix products, arithmetic and copies ran while one was open for 0% of the time, Pallas kernels for 7%

profile of v10, /device:TPU:1, one launch (start us, length us, event | category | flops | bytes accessed | tf_op | source)
XLA Modules:
  0.0 133.8 jit_solution(23219524534837167)
XLA Ops:
  0.7 3.0 %fold.1 = (f32[4,264,128]{2,1,0:T(8,128)}, f32[4,264,128]{2,1,0:T(8,128)}, f32[9,264,128]{2,1,0:T(8,128)S(1)}) custom-call(s32[3]{0:T(128)S(1)} %pad_add_fusion.ids, f32[4,2,256,256]{3,2,1,0:T(8,128)} %left_env.1, f32[8,2,256,256]{3,2,1,0:T(8,128)} %right_env.1), custom_call_target="tpu_custom_call" | custom-call | flops 1000000 | bytes 6000000 | tf_op jit(solution)/shard_map/fold/pallas_call | solution.py:144
  3.7 1.5 %collective-permute-start.1 = (f32[4,264,128]{2,1,0:T(8,128)}, f32[4,264,128]{2,1,0:T(8,128)S(1)}, u32[]{:S(2)}, u32[]{:S(2)}) collective-permute-start(f32[4,264,128]{2,1,0:T(8,128)} %get-tuple-element.21), channel_id=1, source_target_pairs={{0,16},{16,0},{1,17},{17,1},{2,18},{18,2},{3,19},{19,3},{4,20},{20... | collective-permute-start | bytes 1622024 | tf_op jit(solution)/shard_map/ppermute | solution.py:530
  5.2 1.4 %collective-permute-start.4 = (f32[4,264,128]{2,1,0:T(8,128)}, f32[4,264,128]{2,1,0:T(8,128)S(1)}, u32[]{:S(2)}, u32[]{:S(2)}) collective-permute-start(f32[4,264,128]{2,1,0:T(8,128)} %get-tuple-element.20.refs_0_), channel_id=1, source_target_pairs={{0,32},{32,64},{64,96},{96,0},{1,33},{33,65},{65,97},{97,1},{2,34}... | collective-permute-start | bytes 1622024 | tf_op jit(solution)/shard_map/ppermute | solution.py:531
  7.0 2.8 %collective-permute-start.3 = (f32[4,264,128]{2,1,0:T(8,128)S(1)}, f32[4,264,128]{2,1,0:T(8,128)S(1)}, u32[]{:S(2)}, u32[]{:S(2)}) collective-permute-start(f32[4,264,128]{2,1,0:T(8,128)S(1)} %collective-permute-done.1.refs_1_), channel_id=1, source_target_pairs={{0,96},{32,0},{64,32},{96,64},{1,97},{33,1},{65,33},{97,65},{2,98}... | collective-permute-start | bytes 1622024 | tf_op jit(solution)/shard_map/ppermute | solution.py:532
  11.9 2.2 %right_slots.1 = f32[16,296,128]{2,1,0:T(8,128)} custom-call(s32[3]{0:T(128)S(1)} %pad_add_fusion.ids, s32[8]{0:T(128)S(1)} %copy-done.3, s32[8]{0:T(128)S(1)} %collective-permute-done.rsector_other, s32[8,2]{1,0:T(8,128)S(1)} %copy.11.on, s32[8,2]{1,0:T(8,128)S(1)} %collective-permute-done.8.on_other, f32[8,16,256]{2,1,0:T(8,128)S(1)} %bitcast.8, ...), custom_call_target="tpu_custom_call" | custom-call | flops 4000000 | bytes 6000000 | tf_op jit(solution)/shard_map/right_slots/pallas_call | solution.py:187
  14.1 7.8 %all-to-all-start.1 = ((f32[16,296,128]{2,1,0:T(8,128)}), f32[16,296,128]{2,1,0:T(8,128)}, u32[]{:S(2)}, u32[]{:S(2)}) async-start(f32[16,296,128]{2,1,0:T(8,128)} %right_slots.1), calls=%async_computation.1 | async-start | bytes 4849664 | tf_op jit(solution)/shard_map/all_to_all | solution.py:539
  23.5 2.6 %collective-permute-start.6 = (f32[4,264,128]{2,1,0:T(8,128)S(1)}, f32[4,264,128]{2,1,0:T(8,128)S(1)}, u32[]{:S(2)}, u32[]{:S(2)}) collective-permute-start(f32[4,264,128]{2,1,0:T(8,128)S(1)} %collective-permute-done.3.refs_3_), channel_id=1, source_target_pairs={{0,96},{32,0},{64,32},{96,64},{1,97},{33,1},{65,33},{97,65},{2,98}... | collective-permute-start | bytes 1622024 | tf_op jit(solution)/shard_map/ppermute | solution.py:533
  26.1 9.2 %collective-permute-done.2.refs_2_ = f32[4,264,128]{2,1,0:T(8,128)S(1)} collective-permute-done((f32[4,264,128]{2,1,0:T(8,128)S(1)}, f32[4,264,128]{2,1,0:T(8,128)S(1)}, u32[]{:S(2)}, u32[]{:S(2)}) %collective-permute-start.2) | collective-permute-done | bytes 540704 | tf_op jit(solution)/shard_map/ppermute | solution.py:532
  35.3 1.4 %collective-permute-done.7.refs_7_ = f32[4,264,128]{2,1,0:T(8,128)S(1)} collective-permute-done((f32[4,264,128]{2,1,0:T(8,128)S(1)}, f32[4,264,128]{2,1,0:T(8,128)S(1)}, u32[]{:S(2)}, u32[]{:S(2)}) %collective-permute-start.7) | collective-permute-done | bytes 540704 | tf_op jit(solution)/shard_map/ppermute | solution.py:531
  36.6 11.6 %collective-permute-done.5.refs_4_ = f32[4,264,128]{2,1,0:T(8,128)S(1)} collective-permute-done((f32[4,264,128]{2,1,0:T(8,128)S(1)}, f32[4,264,128]{2,1,0:T(8,128)S(1)}, u32[]{:S(2)}, u32[]{:S(2)}) %collective-permute-start.5) | collective-permute-done | bytes 540704 | tf_op jit(solution)/shard_map/ppermute | solution.py:533
  48.2 2.0 %left_slots.1 = f32[16,264,128]{2,1,0:T(8,128)} custom-call(s32[3]{0:T(128)S(1)} %pad_add_fusion.ids, s32[64]{0:T(128)S(1)} %copy-done.4, f32[4,264,128]{2,1,0:T(8,128)S(1)} %copy-done.7, f32[4,264,128]{2,1,0:T(8,128)S(1)} %collective-permute-done.1.refs_1_, f32[4,264,128]{2,1,0:T(8,128)S(1)} %collective-permute-done.2.refs_2_, ...), custom_call_target="tpu_custom_call" | custom-call | flops 15000000512 | bytes 4000000 | tf_op jit(solution)/shard_map/left_slots/pallas_call | solution.py:235
  50.2 4.3 %all-to-all-done.1.slots = f32[16,296,128]{2,1,0:T(8,128)} async-done(((f32[16,296,128]{2,1,0:T(8,128)}), f32[16,296,128]{2,1,0:T(8,128)}, u32[]{:S(2)}, u32[]{:S(2)}) %all-to-all-start.1) | async-done | bytes 2424864 | tf_op jit(solution)/shard_map/all_to_all | solution.py:539
  54.5 5.9 %all-to-all-start = ((f32[16,264,128]{2,1,0:T(8,128)}), f32[16,264,128]{2,1,0:T(8,128)S(1)}, u32[]{:S(2)}, u32[]{:S(2)}) async-start(f32[16,264,128]{2,1,0:T(8,128)} %left_slots.1), calls=%async_computation | async-start | bytes 4325376 | tf_op jit(solution)/shard_map/all_to_all | solution.py:545
  60.5 5.3 %first_vector.1 = (bf16[4096,256]{1,0:T(8,128)(2,1)S(1)}, bf16[4096,256]{1,0:T(8,128)(2,1)S(1)}, bf16[256,4096]{1,0:T(8,128)(2,1)S(1)}, bf16[256,4096]{1,0:T(8,1...) custom-call(s32[3]{0:T(128)S(1)} %pad_add_fusion.ids, s32[8]{0:T(128)S(1)} %copy-done.3, ...), custom_call_target="tpu_custom_call" | custom-call | flops 1700000000 | bytes 12000000 | tf_op jit(solution)/shard_map/first_vector/pallas_call | solution.py:296
  65.8 1.3 copy-done
  67.2 1.4 %copy-done.1 = bf16[256,4096]{1,0:T(8,128)(2,1)} copy-done((bf16[256,4096]{1,0:T(8,128)(2,1)}, bf16[256,4096]{1,0:T(8,128)(2,1)S(1)}, u32[]{:S(2)}) %copy-start.1) | copy-done | bytes 2097176
  68.5 1.4 %copy-done.8 = bf16[4096,256]{1,0:T(8,128)(2,1)} copy-done((bf16[4096,256]{1,0:T(8,128)(2,1)}, bf16[4096,256]{1,0:T(8,128)(2,1)S(1)}, u32[]{:S(2)}) %copy-start.8) | copy-done | bytes 2097176
  69.9 1.3 copy-done.10
  71.3 15.4 %all-to-all-done.arrived = f32[16,264,128]{2,1,0:T(8,128)S(1)} async-done(((f32[16,264,128]{2,1,0:T(8,128)}), f32[16,264,128]{2,1,0:T(8,128)S(1)}, u32[]{:S(2)}, u32[]{:S(2)}) %all-to-all-start) | async-done | bytes 2162720 | tf_op jit(solution)/shard_map/all_to_all | solution.py:545
  86.7 4.2 %image_one.1 = (bf16[4096,256]{1,0:T(8,128)(2,1)S(1)}, bf16[4096,256]{1,0:T(8,128)(2,1)S(1)}, f32[256,256]{1,0:T(8,128)S(1)}) custom-call(f32[16,264,128]{2,1,0:T(8,128)S(1)} %all-to-all-done.arrived, bf16[256,4096]{1,0:T(8,128)(2,1)} %copy-done, bf16[256,4096]{1,0:T(8,128)(2,1)} %copy-done.1), custom_call_target="tpu_custom_call" | custom-call | flops 1700000000 | bytes 10000000 | tf_op jit(solution)/shard_map/image_one/pallas_call | solution.py:336
  90.9 5.5 %collective-permute-start.10 = (f32[256,256]{1,0:T(8,128)S(1)}, f32[256,256]{1,0:T(8,128)S(1)}, u32[]{:S(2)}, u32[]{:S(2)}) collective-permute-start(f32[256,256]{1,0:T(8,128)S(1)} %get-tuple-element.26.part_a), channel_id=1, source_target_pairs={{0,16},{16,0},{1,17},{17,1},{2,18},{18,2},{3,19},{19,3},{4,20},{20... | collective-permute-start | bytes 786440 | tf_op jit(solution)/shard_map/ppermute | solution.py:548
  96.5 1.2 collective-permute-done.10.part_b
  97.6 4.7 %image_two.1 = (f32[256,256]{1,0:T(8,128)S(1)}, f32[256,256]{1,0:T(8,128)S(1)}, f32[8,128]{1,0:T(8,128)S(1)}) custom-call(s32[3]{0:T(128)S(1)} %pad_add_fusion.ids, s32[8]{0:T(128)S(1)} %copy-done.3, s32[8]{0:T(128)S(1)} %collective-permute-done.rsector_other, s32[64]{0:T(128)S(1)} %copy-done.4, s32[32]{0:T(128)S(1)} %copy-done.5, s32[8]{0:T(128)S(1)} %copy-done.6, ...), custom_call_target="tpu_custom_call" | custom-call | flops 3300000000 | bytes 9000000 | tf_op jit(solution)/shard_map/image_two/pallas_call | solution.py:388
  102.8 1.2 collective-permute-done.11.part_b
  103.9 5.7 %image_three.1 = f32[16,24,256]{2,1,0:T(8,128)} custom-call(s32[3]{0:T(128)S(1)} %pad_add_fusion.ids, s32[8]{0:T(128)S(1)} %copy-done.3, s32[8]{0:T(128)S(1)} %collective-permute-done.rsector_other, s32[64]{0:T(128)S(1)} %copy-done.4, s32[32]{0:T(128)S(1)} %copy-done.5, s32[8]{0:T(128)S(1)} %copy-done.6, f32[256,256]{1,0:T(8,128)S(1)} %get-tuple-element.33.part_a, ...), custom_call_target="tpu_custom_call" | custom-call | flops 3300000000 | bytes 9000000 | tf_op jit(solution)/shard_map/image_three/pallas_call | solution.py:424
  109.6 3.6 %all-to-all-start.2 = ((f32[16,24,256]{2,1,0:T(8,128)}), f32[16,24,256]{2,1,0:T(8,128)S(1)}, u32[]{:S(2)}, u32[]{:S(2)}) async-start(f32[16,24,256]{2,1,0:T(8,128)} %image_three.1), calls=%async_computation.2 | async-start | bytes 786432 | tf_op jit(solution)/shard_map/all_to_all | solution.py:551
  113.2 9.2 %all-to-all-done.2.got = f32[16,24,256]{2,1,0:T(8,128)S(1)} async-done(((f32[16,24,256]{2,1,0:T(8,128)}), f32[16,24,256]{2,1,0:T(8,128)S(1)}, u32[]{:S(2)}, u32[]{:S(2)}) %all-to-all-start.2) | async-done | bytes 393248 | tf_op jit(solution)/shard_map/all_to_all | solution.py:551
  122.5 1.6 %collective-permute-start.16 = (f32[8,24,256]{2,1,0:T(8,128)S(1)}, f32[8,24,256]{2,1,0:T(8,128)S(1)}, u32[]{:S(2)}, u32[]{:S(2)}) collective-permute-start(f32[8,24,256]{2,1,0:T(8,128)S(1)} %constant_dynamic-slice_fusion), channel_id=1, source_target_pairs={{0,16},{16,0},{1,17},{17,1},{2,18},{18,2},{3,19},{19,3},{4,20},{20... | collective-permute-start | bytes 589832 | tf_op jit(solution)/shard_map/ppermute | solution.py:556
  125.6 1.0 collective-permute-done.14
  126.6 2.0 %collective-permute-done.13 = f32[16,128]{1,0:T(8,128)S(1)} collective-permute-done((f32[16,128]{1,0:T(8,128)S(1)}, f32[16,128]{1,0:T(8,128)S(1)}, u32[]{:S(2)}, u32[]{:S(2)}) %collective-permute-start.13) | collective-permute-done | bytes 8224 | tf_op jit(solution)/shard_map/ppermute | solution.py:554
  129.3 1.2 collective-permute-start.15
  131.4 2.2 %finish.1 = (f32[8,16,256]{2,1,0:T(8,128)}, f32[1,1]{1,0:T(1,128)}) custom-call(s32[3]{0:T(128)S(1)} %pad_add_fusion.ids, s32[64]{0:T(128)S(1)} %copy-done.4, s32[8]{0:T(128)S(1)} %copy-done.3, s32[32]{0:T(128)S(1)} %copy-done.5, s32[8]{0:T(128)S(1)} %copy-done.6, f32[64,128]{1,0:T(8,128)S(1)} %pad_maximum_fusion.own_stats, ...), custom_call_target="tpu_custom_call" | custom-call | tf_op jit(solution)/shard_map/finish/pallas_call | solution.py:504
  (47 shorter events, 7.7 us)
Async XLA Ops:
  0.7 9.1 %copy-start.2 = (f32[8,256,16]{1,2,0:T(8,128)S(1)}, f32[8,256,16]{1,2,0:T(8,128)}, u32[]{:S(2)}) copy-start(f32[8,256,16]{1,2,0:T(8,128)} %param.8) | copy-start | bytes 393220
  0.7 9.8 %copy-start.3 = (s32[8]{0:T(128)S(1)}, s32[8]{0:T(128)}, u32[]{:S(2)}) copy-start(s32[8]{0:T(128)} %rsector.9) | copy-start | bytes 100
  0.7 9.8 %copy-start.12 = (s32[8,2]{0,1:T(2,128)S(1)}, s32[8,2]{0,1:T(2,128)}, u32[]{:S(2)}) copy-start(s32[8,2]{0,1:T(2,128)} %param.13) | copy-start | bytes 196
  3.7 3.3 %collective-permute-start.1 = (f32[4,264,128]{2,1,0:T(8,128)}, f32[4,264,128]{2,1,0:T(8,128)S(1)}, u32[]{:S(2)}, u32[]{:S(2)}) collective-permute-start(f32[4,264,128]{2,1,0:T(8,128)} %get-tuple-element.21), channel_id=1, source_target_pairs={{0,16},{16,0},{1,17},{17,1},{2,18},{18,2},{3,19},{19,3},{4,20},{20... | collective-permute-start | bytes 1622024 | tf_op jit(solution)/shard_map/ppermute | solution.py:530
  5.2 18.2 %collective-permute-start.4 = (f32[4,264,128]{2,1,0:T(8,128)}, f32[4,264,128]{2,1,0:T(8,128)S(1)}, u32[]{:S(2)}, u32[]{:S(2)}) collective-permute-start(f32[4,264,128]{2,1,0:T(8,128)} %get-tuple-element.20.refs_0_), channel_id=1, source_target_pairs={{0,32},{32,64},{64,96},{96,0},{1,33},{33,65},{65,97},{97,1},{2,34}... | collective-permute-start | bytes 1622024 | tf_op jit(solution)/shard_map/ppermute | solution.py:531
  7.0 16.5 %collective-permute-start.3 = (f32[4,264,128]{2,1,0:T(8,128)S(1)}, f32[4,264,128]{2,1,0:T(8,128)S(1)}, u32[]{:S(2)}, u32[]{:S(2)}) collective-permute-start(f32[4,264,128]{2,1,0:T(8,128)S(1)} %collective-permute-done.1.refs_1_), channel_id=1, source_target_pairs={{0,96},{32,0},{64,32},{96,64},{1,97},{33,1},{65,33},{97,65},{2,98}... | collective-permute-start | bytes 1622024 | tf_op jit(solution)/shard_map/ppermute | solution.py:532
  9.8 2.1 %collective-permute-start.9 = (f32[8,16,256]{2,1,0:T(8,128)S(1)}, f32[8,16,256]{2,1,0:T(8,128)S(1)}, u32[]{:S(2)}, u32[]{:S(2)}) collective-permute-start(f32[8,16,256]{2,1,0:T(8,128)S(1)} %bitcast.7), channel_id=1, source_target_pairs={{0,16},{16,0},{1,17},{17,1},{2,18},{18,2},{3,19},{19,3},{4,20},{20... | collective-permute-start | bytes 393224 | tf_op jit(solution)/shard_map/ppermute | solution.py:527
  10.5 1.1 collective-permute-start
  10.6 1.2 collective-permute-start.8
  14.1 7.8 %copy-start.7 = (f32[4,264,128]{2,1,0:T(8,128)S(1)}, f32[4,264,128]{2,1,0:T(8,128)}, u32[]{:S(2)}) copy-start(f32[4,264,128]{2,1,0:T(8,128)} %get-tuple-element.20.refs_0_) | copy-start | bytes 1622020
  14.1 34.1 %copy-start.4 = (s32[64]{0:T(128)S(1)}, s32[64]{0:T(128)}, u32[]{:S(2)}) copy-start(s32[64]{0:T(128)} %sector.7) | copy-start | bytes 772
  14.1 40.4 %all-to-all-start.1 = ((f32[16,296,128]{2,1,0:T(8,128)}), f32[16,296,128]{2,1,0:T(8,128)}, u32[]{:S(2)}, u32[]{:S(2)}) async-start(f32[16,296,128]{2,1,0:T(8,128)} %right_slots.1), calls=%async_computation.1 | async-start | bytes 4849664 | tf_op jit(solution)/shard_map/all_to_all | solution.py:539
  21.9 13.4 %collective-permute-start.2 = (f32[4,264,128]{2,1,0:T(8,128)S(1)}, f32[4,264,128]{2,1,0:T(8,128)S(1)}, u32[]{:S(2)}, u32[]{:S(2)}) collective-permute-start(f32[4,264,128]{2,1,0:T(8,128)S(1)} %copy-done.7), channel_id=1, source_target_pairs={{0,96},{32,0},{64,32},{96,64},{1,97},{33,1},{65,33},{97,65},{2,98}... | collective-permute-start | bytes 1622024 | tf_op jit(solution)/shard_map/ppermute | solution.py:532
  22.4 14.2 %collective-permute-start.7 = (f32[4,264,128]{2,1,0:T(8,128)S(1)}, f32[4,264,128]{2,1,0:T(8,128)S(1)}, u32[]{:S(2)}, u32[]{:S(2)}) collective-permute-start(f32[4,264,128]{2,1,0:T(8,128)S(1)} %collective-permute-done.1.refs_1_), channel_id=1, source_target_pairs={{0,32},{32,64},{64,96},{96,0},{1,33},{33,65},{65,97},{97,1},{2,34}... | collective-permute-start | bytes 1622024 | tf_op jit(solution)/shard_map/ppermute | solution.py:531
  23.4 24.8 %collective-permute-start.5 = (f32[4,264,128]{2,1,0:T(8,128)S(1)}, f32[4,264,128]{2,1,0:T(8,128)S(1)}, u32[]{:S(2)}, u32[]{:S(2)}) collective-permute-start(f32[4,264,128]{2,1,0:T(8,128)S(1)} %collective-permute-done.4.refs_6_), channel_id=1, source_target_pairs={{0,32},{32,64},{64,96},{96,0},{1,33},{33,65},{65,97},{97,1},{2,34}... | collective-permute-start | bytes 1622024 | tf_op jit(solution)/shard_map/ppermute | solution.py:533
  23.5 24.7 %collective-permute-start.6 = (f32[4,264,128]{2,1,0:T(8,128)S(1)}, f32[4,264,128]{2,1,0:T(8,128)S(1)}, u32[]{:S(2)}, u32[]{:S(2)}) collective-permute-start(f32[4,264,128]{2,1,0:T(8,128)S(1)} %collective-permute-done.3.refs_3_), channel_id=1, source_target_pairs={{0,96},{32,0},{64,32},{96,64},{1,97},{33,1},{65,33},{97,65},{2,98}... | collective-permute-start | bytes 1622024 | tf_op jit(solution)/shard_map/ppermute | solution.py:533
  50.2 10.3 %copy-start.5 = (s32[32]{0:T(128)S(1)}, s32[32]{0:T(128)}, u32[]{:S(2)}) copy-start(s32[32]{0:T(128)} %lsize.7) | copy-start | bytes 388
  50.2 10.3 %copy-start.6 = (s32[8]{0:T(128)S(1)}, s32[8]{0:T(128)}, u32[]{:S(2)}) copy-start(s32[8]{0:T(128)} %rsize.7) | copy-start | bytes 100
  54.5 32.1 %all-to-all-start = ((f32[16,264,128]{2,1,0:T(8,128)}), f32[16,264,128]{2,1,0:T(8,128)S(1)}, u32[]{:S(2)}, u32[]{:S(2)}) async-start(f32[16,264,128]{2,1,0:T(8,128)} %left_slots.1), calls=%async_computation | async-start | bytes 4325376 | tf_op jit(solution)/shard_map/all_to_all | solution.py:545
  67.2 1.4 %copy-start.1 = (bf16[256,4096]{1,0:T(8,128)(2,1)}, bf16[256,4096]{1,0:T(8,128)(2,1)S(1)}, u32[]{:S(2)}) copy-start(bf16[256,4096]{1,0:T(8,128)(2,1)S(1)} %get-tuple-element.25.m_lo) | copy-start | bytes 6291460
  68.5 1.4 %copy-start.8 = (bf16[4096,256]{1,0:T(8,128)(2,1)}, bf16[4096,256]{1,0:T(8,128)(2,1)S(1)}, u32[]{:S(2)}) copy-start(bf16[4096,256]{1,0:T(8,128)(2,1)S(1)} %get-tuple-element.29.r_hi) | copy-start | bytes 6291460
  69.9 1.3 copy-start.10
  86.7 11.0 %copy-start.9 = (bf16[4096,256]{1,0:T(8,128)(2,1)S(1)}, bf16[4096,256]{1,0:T(8,128)(2,1)}, u32[]{:S(2)}) copy-start(bf16[4096,256]{1,0:T(8,128)(2,1)} %copy-done.8) | copy-start | bytes 6291460
  86.7 11.0 %copy-start.11 = (bf16[4096,256]{1,0:T(8,128)(2,1)S(1)}, bf16[4096,256]{1,0:T(8,128)(2,1)}, u32[]{:S(2)}) copy-start(bf16[4096,256]{1,0:T(8,128)(2,1)} %copy-done.10) | copy-start | bytes 6291460
  90.9 6.7 %collective-permute-start.10 = (f32[256,256]{1,0:T(8,128)S(1)}, f32[256,256]{1,0:T(8,128)S(1)}, u32[]{:S(2)}, u32[]{:S(2)}) collective-permute-start(f32[256,256]{1,0:T(8,128)S(1)} %get-tuple-element.26.part_a), channel_id=1, source_target_pairs={{0,16},{16,0},{1,17},{17,1},{2,18},{18,2},{3,19},{19,3},{4,20},{20... | collective-permute-start | bytes 786440 | tf_op jit(solution)/shard_map/ppermute | solution.py:548
  102.3 1.6 %collective-permute-start.11 = (f32[256,256]{1,0:T(8,128)S(1)}, f32[256,256]{1,0:T(8,128)S(1)}, u32[]{:S(2)}, u32[]{:S(2)}) collective-permute-start(f32[256,256]{1,0:T(8,128)S(1)} %get-tuple-element.33.part_a), channel_id=1, source_target_pairs={{0,16},{16,0},{1,17},{17,1},{2,18},{18,2},{3,19},{19,3},{4,20},{20... | collective-permute-start | bytes 786440 | tf_op jit(solution)/shard_map/ppermute | solution.py:549
  109.6 12.8 %all-to-all-start.2 = ((f32[16,24,256]{2,1,0:T(8,128)}), f32[16,24,256]{2,1,0:T(8,128)S(1)}, u32[]{:S(2)}, u32[]{:S(2)}) async-start(f32[16,24,256]{2,1,0:T(8,128)} %image_three.1), calls=%async_computation.2 | async-start | bytes 786432 | tf_op jit(solution)/shard_map/all_to_all | solution.py:551
  122.5 8.9 %collective-permute-start.16 = (f32[8,24,256]{2,1,0:T(8,128)S(1)}, f32[8,24,256]{2,1,0:T(8,128)S(1)}, u32[]{:S(2)}, u32[]{:S(2)}) collective-permute-start(f32[8,24,256]{2,1,0:T(8,128)S(1)} %constant_dynamic-slice_fusion), channel_id=1, source_target_pairs={{0,16},{16,0},{1,17},{17,1},{2,18},{18,2},{3,19},{19,3},{4,20},{20... | collective-permute-start | bytes 589832 | tf_op jit(solution)/shard_map/ppermute | solution.py:556
  124.1 2.5 %collective-permute-start.14 = (f32[16,128]{1,0:T(8,128)S(1)}, f32[16,128]{1,0:T(8,128)S(1)}, u32[]{:S(2)}, u32[]{:S(2)}) collective-permute-start(f32[16,128]{1,0:T(8,128)S(1)} %bitcast.10), channel_id=1, source_target_pairs={{0,96},{32,0},{64,32},{96,64},{1,97},{33,1},{65,33},{97,65},{2,98}... | collective-permute-start | bytes 24584 | tf_op jit(solution)/shard_map/ppermute | solution.py:554
  124.6 4.0 %collective-permute-start.13 = (f32[16,128]{1,0:T(8,128)S(1)}, f32[16,128]{1,0:T(8,128)S(1)}, u32[]{:S(2)}, u32[]{:S(2)}) collective-permute-start(f32[16,128]{1,0:T(8,128)S(1)} %bitcast.11), channel_id=1, source_target_pairs={{0,64},{32,96},{64,0},{96,32},{1,65},{33,97},{65,1},{97,33},{2,66}... | collective-permute-start | bytes 24584 | tf_op jit(solution)/shard_map/ppermute | solution.py:554
  124.6 4.7 %collective-permute-start.12 = (f32[16,128]{1,0:T(8,128)S(1)}, f32[16,128]{1,0:T(8,128)S(1)}, u32[]{:S(2)}, u32[]{:S(2)}) collective-permute-start(f32[16,128]{1,0:T(8,128)S(1)} %bitcast.12), channel_id=1, source_target_pairs={{0,32},{32,64},{64,96},{96,0},{1,33},{33,65},{65,97},{97,1},{2,34}... | collective-permute-start | bytes 24584 | tf_op jit(solution)/shard_map/ppermute | solution.py:554
  129.3 2.1 %collective-permute-start.15 = (f32[64,128]{1,0:T(8,128)S(1)}, f32[64,128]{1,0:T(8,128)S(1)}, u32[]{:S(2)}, u32[]{:S(2)}) collective-permute-start(f32[64,128]{1,0:T(8,128)S(1)} %pad_maximum_fusion.own_stats), channel_id=1, source_target_pairs={{0,16},{16,0},{1,17},{17,1},{2,18},{18,2},{3,19},{19,3},{4,20},{20... | collective-permute-start | bytes 98312 | tf_op jit(solution)/shard_map/ppermute | solution.py:558
  (1 other events, 1.3 us)

commit v11 on v10

--- a/solution.py
+++ b/solution.py
@@ -411,13 +411,13 @@
     alpha, norm, vec = lanczos(image, q2[...], q1[...], beta)
     pick = jnp.where(ids[1] == 0, q2[...], vec)
     for n in range(16):
-        slots[n, :16, :] = pick[16 * n : 16 * n + 16]
+        slots[n, :16, :] = pick[16 * n : 16 * n + 16, :HALF]
+        slots[n, 16:THIN, :] = pick[16 * n : 16 * n + 16, HALF:]
     stats = put(put(stats_in[...], 3, alpha), 4, norm)
     alpha = total(vec * half_image(vec, r_hi, r_lo, l_hi, l_lo))
     stats = put(stats, 5, alpha)
-    wide = jnp.concatenate([stats, jnp.zeros((8, HALF), f32)], axis=1)
     for n in range(16):
-        slots[n, 16:24, :] = wide
+        slots[n, THIN:, :] = stats
 
 
 def image_three(scalars, part, part_other, q1, q2, stats, stacks):
@@ -425,7 +425,7 @@
         image_three_body,
         in_specs=[smem()] * 6 + [vmem()] * 9,
         out_specs=vmem(),
-        out_shape=jax.ShapeDtypeStruct((16, 24, TILE), f32),
+        out_shape=jax.ShapeDtypeStruct((16, THIN + 8, HALF), f32),
         compiler_params=params(6),
         cost_estimate=cost(3_300_000_000, 9_000_000),
         name="image_three",
@@ -489,8 +489,9 @@
         live_left = lsize[sector[ids[0] * 16 + core * 8 + b]]
         live_right = rsize[rsector[b]]
         live = (jcol + ids[2] * 16 < live_right) & (irow < live_left)
-        keep = got[core * 8 + b, :16, :]
-        recv = back[b, :16, :]
+        at = core * 8 + b
+        keep = jnp.concatenate([got[at, :16, :], got[at, 16:THIN, :]], axis=1)
+        recv = jnp.concatenate([back[b, :16, :], back[b, 16:THIN, :]], axis=1)
         second = jnp.where(core == 0, keep, recv)
         third = jnp.where(core == 0, recv, keep)
         out[b] = (
@@ -528,6 +529,9 @@
 
     mine, folded, right_folded = fold(ids, left_env, right_env)
     theirs = lax.ppermute(folded, "c", SWAP)
+    theirs, rsector_other, on_other, thin_other = lax.optimization_barrier(
+        (theirs, rsector_other, on_other, thin_other)
+    )
     below = [lax.ppermute(x, "y", UP) for x in (mine, theirs)]
     above = [lax.ppermute(x, "y", DOWN) for x in (mine, theirs)]
     far = [lax.ppermute(below[0], "y", UP), lax.ppermute(above[1], "y", DOWN)]
@@ -549,11 +553,12 @@
     sent = image_three(scalars, part, lax.ppermute(part, "c", SWAP), q1, q2, stats, stacks)
 
     got = lax.all_to_all(sent, COL, 0, 0, tiled=True)
-    plane_stats = got[:, 16, :HALF]
+    plane_stats = got[:, THIN, :]
     turned = [
         lax.ppermute(plane_stats, "y", [(i, (i + k) % 4) for i in range(4)]) for k in (1, 2, 3)
     ]
-    back = lax.ppermute(lax.dynamic_slice_in_dim(got, (1 - core) * 8, 8), "c", SWAP)
+    give = lax.dynamic_slice(got, ((1 - core) * 8, 0, 0), (8, THIN, HALF))
+    back = lax.ppermute(give, "c", SWAP)
     own_stats = jnp.concatenate([plane_stats] + turned)
     other_stats = lax.ppermute(own_stats, "c", SWAP)
     out, energy = finish(

time: 134 us -> 129 us (0.963)
  waiting for transfers between devices: 59.2 us -> 52.6 us
  starting transfers between devices: 38.7 us -> 40.4 us
    ppermute x3, waiting for transfers between devices: 3.72 us -> 0.38 us  [local(): lax.ppermute(plane_stats, 'y', [(i, (i + k) % 4) for i in range(4)])]
    ppermute x1, starting transfers between devices: 1.21 us -> 3.61 us  [local(): other_stats = lax.ppermute(own_stats, 'c', SWAP)]
    all_to_all x1, starting transfers between devices: 5.95 us -> 3.72 us  [local(): left_arrived = lax.all_to_all(left_sent, COL, 0, 0, tiled=True)]
  transfers between devices with their start and end apart: 20 -> 20, of which waited for: 15 -> 10; matrix products, arithmetic and copies ran while one was open for 0% -> 0% of each run, Pallas kernels for 7% -> 7%
where the time goes in v11:
time: 129 us
  waiting for transfers between devices  52.6 us (41%)
  starting transfers between devices  40.4 us (31%)
  Pallas kernels  29.2 us (23%)
  local copies, waits for them, and re-layouts  5.57 us (4%)
    all_to_all x1, waiting for transfers between devices, local(): left_arrived = lax.all_to_all(left_sent, COL, 0, 0, tiled=True)  15.2 us
    ppermute x2, waiting for transfers between devices, local(): far = [lax.ppermute(below[0], 'y', UP), lax.ppermute(above[1], 'y', DOWN)]  11.6 us
    ppermute x2, waiting for transfers between devices, local(): above = [lax.ppermute(x, 'y', DOWN) for x in (mine, theirs)]  8.33 us
    all_to_all x1, waiting for transfers between devices, local(): got = lax.all_to_all(sent, COL, 0, 0, tiled=True)  7.92 us
    all_to_all x1, starting transfers between devices, local(): arrived = lax.all_to_all(slots, COL, 0, 0, tiled=True)  7.79 us
    ppermute x2, starting transfers between devices, local(): lax.ppermute(part, 'c', SWAP)  6.25 us
    pallas_call x1, Pallas kernels, image_three(): pl.pallas_call(image_three_body, in_specs=[smem()] * 6 + [vmem()] * 9, ou...  5.64 us
    unnamed x27, local copies, waits for them, and re-layouts  5.55 us
  transfers between devices with their start and end apart: 20, of which 10 were waited for; matrix products, arithmetic and copies ran while one was open for 0% of the time, Pallas kernels for 7%

profile of v11, /device:TPU:1, one launch (start us, length us, event | category | flops | bytes accessed | tf_op | source)
XLA Modules:
  0.0 128.9 jit_solution(12317881690722776149)
XLA Ops:
  0.7 3.0 %fold.1 = (f32[4,264,128]{2,1,0:T(8,128)}, f32[4,264,128]{2,1,0:T(8,128)}, f32[9,264,128]{2,1,0:T(8,128)S(1)}) custom-call(s32[3]{0:T(128)S(1)} %pad_add_fusion.ids, f32[4,2,256,256]{3,2,1,0:T(8,128)} %left_env.1, f32[8,2,256,256]{3,2,1,0:T(8,128)} %right_env.1), custom_call_target="tpu_custom_call" | custom-call | flops 1000000 | bytes 6000000 | tf_op jit(solution)/shard_map/fold/pallas_call | solution.py:144
  3.7 1.5 %collective-permute-start = (f32[4,264,128]{2,1,0:T(8,128)}, f32[4,264,128]{2,1,0:T(8,128)S(1)}, u32[]{:S(2)}, u32[]{:S(2)}) collective-permute-start(f32[4,264,128]{2,1,0:T(8,128)} %get-tuple-element.24), channel_id=1, source_target_pairs={{0,16},{16,0},{1,17},{17,1},{2,18},{18,2},{3,19},{19,3},{4,20},{20... | collective-permute-start | bytes 1622024 | tf_op jit(solution)/shard_map/ppermute | solution.py:531
  5.9 1.4 %collective-permute-start.6 = (f32[4,264,128]{2,1,0:T(8,128)}, f32[4,264,128]{2,1,0:T(8,128)S(1)}, u32[]{:S(2)}, u32[]{:S(2)}) collective-permute-start(f32[4,264,128]{2,1,0:T(8,128)} %get-tuple-element.26.refs_0_), channel_id=1, source_target_pairs={{0,32},{32,64},{64,96},{96,0},{1,33},{33,65},{65,97},{97,1},{2,34}... | collective-permute-start | bytes 1622024 | tf_op jit(solution)/shard_map/ppermute | solution.py:535
  7.3 2.5 %collective-permute-start.5 = (f32[4,264,128]{2,1,0:T(8,128)S(1)}, f32[4,264,128]{2,1,0:T(8,128)S(1)}, u32[]{:S(2)}, u32[]{:S(2)}) collective-permute-start(f32[4,264,128]{2,1,0:T(8,128)S(1)} %collective-permute-done.refs_1_), channel_id=1, source_target_pairs={{0,96},{32,0},{64,32},{96,64},{1,97},{33,1},{65,33},{97,65},{2,98}... | collective-permute-start | bytes 1622024 | tf_op jit(solution)/shard_map/ppermute | solution.py:536
  9.9 2.2 %right_slots.1 = f32[16,296,128]{2,1,0:T(8,128)} custom-call(s32[3]{0:T(128)S(1)} %pad_add_fusion.ids, s32[8]{0:T(128)S(1)} %copy-done.3, s32[8]{0:T(128)S(1)} %collective-permute-done.1.rsector_other, s32[8,2]{1,0:T(8,128)S(1)} %copy.10.on, s32[8,2]{1,0:T(8,128)S(1)} %collective-permute-done.2.on_other, f32[8,16,256]{2,1,0:T(8,128)S(1)} %bitcast.8, ...), custom_call_target="tpu_custom_call" | custom-call | flops 4000000 | bytes 6000000 | tf_op jit(solution)/shard_map/right_slots/pallas_call | solution.py:187
  12.1 7.8 %all-to-all-start.1 = ((f32[16,296,128]{2,1,0:T(8,128)}), f32[16,296,128]{2,1,0:T(8,128)}, u32[]{:S(2)}, u32[]{:S(2)}) async-start(f32[16,296,128]{2,1,0:T(8,128)} %right_slots.1), calls=%async_computation.1 | async-start | bytes 4849664 | tf_op jit(solution)/shard_map/all_to_all | solution.py:543
  20.4 1.0 collective-permute-start.9
  21.4 3.1 %collective-permute-start.8 = (f32[4,264,128]{2,1,0:T(8,128)S(1)}, f32[4,264,128]{2,1,0:T(8,128)S(1)}, u32[]{:S(2)}, u32[]{:S(2)}) collective-permute-start(f32[4,264,128]{2,1,0:T(8,128)S(1)} %collective-permute-done.5.refs_3_), channel_id=1, source_target_pairs={{0,96},{32,0},{64,32},{96,64},{1,97},{33,1},{65,33},{97,65},{2,98}... | collective-permute-start | bytes 1622024 | tf_op jit(solution)/shard_map/ppermute | solution.py:537
  24.6 8.3 %collective-permute-done.4.refs_2_ = f32[4,264,128]{2,1,0:T(8,128)S(1)} collective-permute-done((f32[4,264,128]{2,1,0:T(8,128)S(1)}, f32[4,264,128]{2,1,0:T(8,128)S(1)}, u32[]{:S(2)}, u32[]{:S(2)}) %collective-permute-start.4) | collective-permute-done | bytes 540704 | tf_op jit(solution)/shard_map/ppermute | solution.py:536
  32.9 1.1 collective-permute-done.9.refs_7_
  34.0 11.6 %collective-permute-done.7.refs_4_ = f32[4,264,128]{2,1,0:T(8,128)S(1)} collective-permute-done((f32[4,264,128]{2,1,0:T(8,128)S(1)}, f32[4,264,128]{2,1,0:T(8,128)S(1)}, u32[]{:S(2)}, u32[]{:S(2)}) %collective-permute-start.7) | collective-permute-done | bytes 540704 | tf_op jit(solution)/shard_map/ppermute | solution.py:537
  45.6 2.0 %left_slots.1 = f32[16,264,128]{2,1,0:T(8,128)} custom-call(s32[3]{0:T(128)S(1)} %pad_add_fusion.ids, s32[64]{0:T(128)S(1)} %copy-done.4, f32[4,264,128]{2,1,0:T(8,128)S(1)} %copy-done.7, f32[4,264,128]{2,1,0:T(8,128)S(1)} %collective-permute-done.refs_1_, f32[4,264,128]{2,1,0:T(8,128)S(1)} %collective-permute-done.4.refs_2_, ...), custom_call_target="tpu_custom_call" | custom-call | flops 15000000512 | bytes 4000000 | tf_op jit(solution)/shard_map/left_slots/pallas_call | solution.py:235
  47.6 4.9 %all-to-all-done.1.slots = f32[16,296,128]{2,1,0:T(8,128)} async-done(((f32[16,296,128]{2,1,0:T(8,128)}), f32[16,296,128]{2,1,0:T(8,128)}, u32[]{:S(2)}, u32[]{:S(2)}) %all-to-all-start.1) | async-done | bytes 2424864 | tf_op jit(solution)/shard_map/all_to_all | solution.py:543
  52.5 3.7 %all-to-all-start = ((f32[16,264,128]{2,1,0:T(8,128)}), f32[16,264,128]{2,1,0:T(8,128)S(1)}, u32[]{:S(2)}, u32[]{:S(2)}) async-start(f32[16,264,128]{2,1,0:T(8,128)} %left_slots.1), calls=%async_computation | async-start | bytes 4325376 | tf_op jit(solution)/shard_map/all_to_all | solution.py:549
  56.2 5.3 %first_vector.1 = (bf16[4096,256]{1,0:T(8,128)(2,1)S(1)}, bf16[4096,256]{1,0:T(8,128)(2,1)S(1)}, bf16[256,4096]{1,0:T(8,128)(2,1)S(1)}, bf16[256,4096]{1,0:T(8,1...) custom-call(s32[3]{0:T(128)S(1)} %pad_add_fusion.ids, s32[8]{0:T(128)S(1)} %copy-done.3, ...), custom_call_target="tpu_custom_call" | custom-call | flops 1700000000 | bytes 12000000 | tf_op jit(solution)/shard_map/first_vector/pallas_call | solution.py:296
  61.6 1.3 %copy-done = bf16[256,4096]{1,0:T(8,128)(2,1)} copy-done((bf16[256,4096]{1,0:T(8,128)(2,1)}, bf16[256,4096]{1,0:T(8,128)(2,1)S(1)}, u32[]{:S(2)}) %copy-start) | copy-done | bytes 2097176
  62.9 1.4 %copy-done.1 = bf16[256,4096]{1,0:T(8,128)(2,1)} copy-done((bf16[256,4096]{1,0:T(8,128)(2,1)}, bf16[256,4096]{1,0:T(8,128)(2,1)S(1)}, u32[]{:S(2)}) %copy-start.1) | copy-done | bytes 2097176
  64.2 1.4 %copy-done.8 = bf16[4096,256]{1,0:T(8,128)(2,1)} copy-done((bf16[4096,256]{1,0:T(8,128)(2,1)}, bf16[4096,256]{1,0:T(8,128)(2,1)S(1)}, u32[]{:S(2)}) %copy-start.8) | copy-done | bytes 2097176
  65.6 1.3 %copy-done.10 = bf16[4096,256]{1,0:T(8,128)(2,1)} copy-done((bf16[4096,256]{1,0:T(8,128)(2,1)}, bf16[4096,256]{1,0:T(8,128)(2,1)S(1)}, u32[]{:S(2)}) %copy-start.10) | copy-done | bytes 2097176
  67.0 15.2 %all-to-all-done.arrived = f32[16,264,128]{2,1,0:T(8,128)S(1)} async-done(((f32[16,264,128]{2,1,0:T(8,128)}), f32[16,264,128]{2,1,0:T(8,128)S(1)}, u32[]{:S(2)}, u32[]{:S(2)}) %all-to-all-start) | async-done | bytes 2162720 | tf_op jit(solution)/shard_map/all_to_all | solution.py:549
  82.2 4.2 %image_one.1 = (bf16[4096,256]{1,0:T(8,128)(2,1)S(1)}, bf16[4096,256]{1,0:T(8,128)(2,1)S(1)}, f32[256,256]{1,0:T(8,128)S(1)}) custom-call(f32[16,264,128]{2,1,0:T(8,128)S(1)} %all-to-all-done.arrived, bf16[256,4096]{1,0:T(8,128)(2,1)} %copy-done, bf16[256,4096]{1,0:T(8,128)(2,1)} %copy-done.1), custom_call_target="tpu_custom_call" | custom-call | flops 1700000000 | bytes 10000000 | tf_op jit(solution)/shard_map/image_one/pallas_call | solution.py:336
  86.5 5.8 %collective-permute-start.10 = (f32[256,256]{1,0:T(8,128)S(1)}, f32[256,256]{1,0:T(8,128)S(1)}, u32[]{:S(2)}, u32[]{:S(2)}) collective-permute-start(f32[256,256]{1,0:T(8,128)S(1)} %get-tuple-element.34.part_a), channel_id=1, source_target_pairs={{0,16},{16,0},{1,17},{17,1},{2,18},{18,2},{3,19},{19,3},{4,20},{20... | collective-permute-start | bytes 786440 | tf_op jit(solution)/shard_map/ppermute | solution.py:552
  92.3 1.2 collective-permute-done.10.part_b
  93.4 4.7 %image_two.1 = (f32[256,256]{1,0:T(8,128)S(1)}, f32[256,256]{1,0:T(8,128)S(1)}, f32[8,128]{1,0:T(8,128)S(1)}) custom-call(s32[3]{0:T(128)S(1)} %pad_add_fusion.ids, s32[8]{0:T(128)S(1)} %copy-done.3, s32[8]{0:T(128)S(1)} %collective-permute-done.1.rsector_other, s32[64]{0:T(128)S(1)} %copy-done.4, s32[32]{0:T(128)S(1)} %copy-done.5, s32[8]{0:T(128)S(1)} %copy-done.6, ...), custom_call_target="tpu_custom_call" | custom-call | flops 3300000000 | bytes 9000000 | tf_op jit(solution)/shard_map/image_two/pallas_call | solution.py:388
  98.6 1.2 collective-permute-done.11.part_b
  99.8 5.6 %image_three.1 = f32[16,40,128]{2,1,0:T(8,128)} custom-call(s32[3]{0:T(128)S(1)} %pad_add_fusion.ids, s32[8]{0:T(128)S(1)} %copy-done.3, s32[8]{0:T(128)S(1)} %collective-permute-done.1.rsector_other, s32[64]{0:T(128)S(1)} %copy-done.4, s32[32]{0:T(128)S(1)} %copy-done.5, s32[8]{0:T(128)S(1)} %copy-done.6, f32[256,256]{1,0:T(8,128)S(1)} %get-tuple-element.41.part_a, ...), custom_call_target="tpu_custom_call" | custom-call | flops 3300000000 | bytes 9000000 | tf_op jit(solution)/shard_map/image_three/pallas_call | solution.py:424
  105.4 3.6 %all-to-all-start.2 = ((f32[16,40,128]{2,1,0:T(8,128)}), f32[16,40,128]{2,1,0:T(8,128)S(1)}, u32[]{:S(2)}, u32[]{:S(2)}) async-start(f32[16,40,128]{2,1,0:T(8,128)} %image_three.1), calls=%async_computation.2 | async-start | bytes 655360 | tf_op jit(solution)/shard_map/all_to_all | solution.py:555
  109.0 7.9 %all-to-all-done.2.got = f32[16,40,128]{2,1,0:T(8,128)S(1)} async-done(((f32[16,40,128]{2,1,0:T(8,128)}), f32[16,40,128]{2,1,0:T(8,128)S(1)}, u32[]{:S(2)}, u32[]{:S(2)}) %all-to-all-start.2) | async-done | bytes 327712 | tf_op jit(solution)/shard_map/all_to_all | solution.py:555
  117.0 1.1 collective-permute-start.14
  118.7 3.0 %collective-permute-start.16 = (f32[8,32,128]{2,1,0:T(8,128)S(1)}, f32[8,32,128]{2,1,0:T(8,128)S(1)}, u32[]{:S(2)}, u32[]{:S(2)}) collective-permute-start(f32[8,32,128]{2,1,0:T(8,128)S(1)} %constant_dynamic-slice_fusion), channel_id=1, source_target_pairs={{0,16},{16,0},{1,17},{17,1},{2,18},{18,2},{3,19},{19,3},{4,20},{20... | collective-permute-start | bytes 393224 | tf_op jit(solution)/shard_map/ppermute | solution.py:561
  122.1 3.6 %collective-permute-start.15 = (f32[64,128]{1,0:T(8,128)S(1)}, f32[64,128]{1,0:T(8,128)S(1)}, u32[]{:S(2)}, u32[]{:S(2)}) collective-permute-start(f32[64,128]{1,0:T(8,128)S(1)} %pad_maximum_fusion.own_stats), channel_id=1, source_target_pairs={{0,16},{16,0},{1,17},{17,1},{2,18},{18,2},{3,19},{19,3},{4,20},{20... | collective-permute-start | bytes 98312 | tf_op jit(solution)/shard_map/ppermute | solution.py:563
  126.5 2.2 %finish.1 = (f32[8,16,256]{2,1,0:T(8,128)}, f32[1,1]{1,0:T(1,128)}) custom-call(s32[3]{0:T(128)S(1)} %pad_add_fusion.ids, s32[64]{0:T(128)S(1)} %copy-done.4, s32[8]{0:T(128)S(1)} %copy-done.3, s32[32]{0:T(128)S(1)} %copy-done.5, s32[8]{0:T(128)S(1)} %copy-done.6, f32[64,128]{1,0:T(8,128)S(1)} %pad_maximum_fusion.own_stats, ...), custom_call_target="tpu_custom_call" | custom-call | tf_op jit(solution)/shard_map/finish/pallas_call | solution.py:505
  (47 shorter events, 3.8 us)
Async XLA Ops:
  0.7 4.5 %copy-start.2 = (f32[8,256,16]{1,2,0:T(8,128)S(1)}, f32[8,256,16]{1,2,0:T(8,128)}, u32[]{:S(2)}) copy-start(f32[8,256,16]{1,2,0:T(8,128)} %param.8) | copy-start | bytes 393220
  0.7 4.6 %copy-start.3 = (s32[8]{0:T(128)S(1)}, s32[8]{0:T(128)}, u32[]{:S(2)}) copy-start(s32[8]{0:T(128)} %rsector.9) | copy-start | bytes 100
  0.7 5.0 %copy-start.12 = (s32[8,2]{0,1:T(2,128)S(1)}, s32[8,2]{0,1:T(2,128)}, u32[]{:S(2)}) copy-start(s32[8,2]{0,1:T(2,128)} %param.13) | copy-start | bytes 196
  3.7 3.6 %collective-permute-start = (f32[4,264,128]{2,1,0:T(8,128)}, f32[4,264,128]{2,1,0:T(8,128)S(1)}, u32[]{:S(2)}, u32[]{:S(2)}) collective-permute-start(f32[4,264,128]{2,1,0:T(8,128)} %get-tuple-element.24), channel_id=1, source_target_pairs={{0,16},{16,0},{1,17},{17,1},{2,18},{18,2},{3,19},{19,3},{4,20},{20... | collective-permute-start | bytes 1622024 | tf_op jit(solution)/shard_map/ppermute | solution.py:531
  5.2 2.1 %collective-permute-start.3 = (f32[8,16,256]{2,1,0:T(8,128)S(1)}, f32[8,16,256]{2,1,0:T(8,128)S(1)}, u32[]{:S(2)}, u32[]{:S(2)}) collective-permute-start(f32[8,16,256]{2,1,0:T(8,128)S(1)} %bitcast.7), channel_id=1, source_target_pairs={{0,16},{16,0},{1,17},{17,1},{2,18},{18,2},{3,19},{19,3},{4,20},{20... | collective-permute-start | bytes 393224 | tf_op jit(solution)/shard_map/ppermute | solution.py:528
  5.3 2.0 %collective-permute-start.1 = (s32[8]{0:T(128)S(1)}, s32[8]{0:T(128)S(1)}, u32[]{:S(2)}, u32[]{:S(2)}) collective-permute-start(s32[8]{0:T(128)S(1)} %copy-done.3), channel_id=1, source_target_pairs={{0,16},{16,0},{1,17},{17,1},{2,18},{18,2},{3,19},{19,3},{4,20},{20... | collective-permute-start | bytes 104 | tf_op jit(solution)/shard_map/ppermute | solution.py:526
  5.8 1.5 %collective-permute-start.2 = (s32[8,2]{1,0:T(8,128)S(1)}, s32[8,2]{1,0:T(8,128)S(1)}, u32[]{:S(2)}, u32[]{:S(2)}) collective-permute-start(s32[8,2]{1,0:T(8,128)S(1)} %copy.10.on), channel_id=1, source_target_pairs={{0,16},{16,0},{1,17},{17,1},{2,18},{18,2},{3,19},{19,3},{4,20},{20... | collective-permute-start | bytes 200 | tf_op jit(solution)/shard_map/ppermute | solution.py:527
  5.9 15.5 %collective-permute-start.6 = (f32[4,264,128]{2,1,0:T(8,128)}, f32[4,264,128]{2,1,0:T(8,128)S(1)}, u32[]{:S(2)}, u32[]{:S(2)}) collective-permute-start(f32[4,264,128]{2,1,0:T(8,128)} %get-tuple-element.26.refs_0_), channel_id=1, source_target_pairs={{0,32},{32,64},{64,96},{96,0},{1,33},{33,65},{65,97},{97,1},{2,34}... | collective-permute-start | bytes 1622024 | tf_op jit(solution)/shard_map/ppermute | solution.py:535
  7.3 14.1 %collective-permute-start.5 = (f32[4,264,128]{2,1,0:T(8,128)S(1)}, f32[4,264,128]{2,1,0:T(8,128)S(1)}, u32[]{:S(2)}, u32[]{:S(2)}) collective-permute-start(f32[4,264,128]{2,1,0:T(8,128)S(1)} %collective-permute-done.refs_1_), channel_id=1, source_target_pairs={{0,96},{32,0},{64,32},{96,64},{1,97},{33,1},{65,33},{97,65},{2,98}... | collective-permute-start | bytes 1622024 | tf_op jit(solution)/shard_map/ppermute | solution.py:536
  12.0 7.8 %copy-start.7 = (f32[4,264,128]{2,1,0:T(8,128)S(1)}, f32[4,264,128]{2,1,0:T(8,128)}, u32[]{:S(2)}) copy-start(f32[4,264,128]{2,1,0:T(8,128)} %get-tuple-element.26.refs_0_) | copy-start | bytes 1622020
  12.1 33.5 %copy-start.4 = (s32[64]{0:T(128)S(1)}, s32[64]{0:T(128)}, u32[]{:S(2)}) copy-start(s32[64]{0:T(128)} %sector.7) | copy-start | bytes 772
  12.1 40.4 %all-to-all-start.1 = ((f32[16,296,128]{2,1,0:T(8,128)}), f32[16,296,128]{2,1,0:T(8,128)}, u32[]{:S(2)}, u32[]{:S(2)}) async-start(f32[16,296,128]{2,1,0:T(8,128)} %right_slots.1), calls=%async_computation.1 | async-start | bytes 4849664 | tf_op jit(solution)/shard_map/all_to_all | solution.py:543
  19.9 13.0 %collective-permute-start.4 = (f32[4,264,128]{2,1,0:T(8,128)S(1)}, f32[4,264,128]{2,1,0:T(8,128)S(1)}, u32[]{:S(2)}, u32[]{:S(2)}) collective-permute-start(f32[4,264,128]{2,1,0:T(8,128)S(1)} %copy-done.7), channel_id=1, source_target_pairs={{0,96},{32,0},{64,32},{96,64},{1,97},{33,1},{65,33},{97,65},{2,98}... | collective-permute-start | bytes 1622024 | tf_op jit(solution)/shard_map/ppermute | solution.py:536
  20.4 13.6 %collective-permute-start.9 = (f32[4,264,128]{2,1,0:T(8,128)S(1)}, f32[4,264,128]{2,1,0:T(8,128)S(1)}, u32[]{:S(2)}, u32[]{:S(2)}) collective-permute-start(f32[4,264,128]{2,1,0:T(8,128)S(1)} %collective-permute-done.refs_1_), channel_id=1, source_target_pairs={{0,32},{32,64},{64,96},{96,0},{1,33},{33,65},{65,97},{97,1},{2,34}... | collective-permute-start | bytes 1622024 | tf_op jit(solution)/shard_map/ppermute | solution.py:535
  21.4 24.2 %collective-permute-start.7 = (f32[4,264,128]{2,1,0:T(8,128)S(1)}, f32[4,264,128]{2,1,0:T(8,128)S(1)}, u32[]{:S(2)}, u32[]{:S(2)}) collective-permute-start(f32[4,264,128]{2,1,0:T(8,128)S(1)} %collective-permute-done.6.refs_6_), channel_id=1, source_target_pairs={{0,32},{32,64},{64,96},{96,0},{1,33},{33,65},{65,97},{97,1},{2,34}... | collective-permute-start | bytes 1622024 | tf_op jit(solution)/shard_map/ppermute | solution.py:537
  21.4 24.1 %collective-permute-start.8 = (f32[4,264,128]{2,1,0:T(8,128)S(1)}, f32[4,264,128]{2,1,0:T(8,128)S(1)}, u32[]{:S(2)}, u32[]{:S(2)}) collective-permute-start(f32[4,264,128]{2,1,0:T(8,128)S(1)} %collective-permute-done.5.refs_3_), channel_id=1, source_target_pairs={{0,96},{32,0},{64,32},{96,64},{1,97},{33,1},{65,33},{97,65},{2,98}... | collective-permute-start | bytes 1622024 | tf_op jit(solution)/shard_map/ppermute | solution.py:537
  47.5 8.7 %copy-start.5 = (s32[32]{0:T(128)S(1)}, s32[32]{0:T(128)}, u32[]{:S(2)}) copy-start(s32[32]{0:T(128)} %lsize.7) | copy-start | bytes 388
  47.6 8.6 %copy-start.6 = (s32[8]{0:T(128)S(1)}, s32[8]{0:T(128)}, u32[]{:S(2)}) copy-start(s32[8]{0:T(128)} %rsize.7) | copy-start | bytes 100
  52.5 29.7 %all-to-all-start = ((f32[16,264,128]{2,1,0:T(8,128)}), f32[16,264,128]{2,1,0:T(8,128)S(1)}, u32[]{:S(2)}, u32[]{:S(2)}) async-start(f32[16,264,128]{2,1,0:T(8,128)} %left_slots.1), calls=%async_computation | async-start | bytes 4325376 | tf_op jit(solution)/shard_map/all_to_all | solution.py:549
  62.9 1.4 %copy-start.1 = (bf16[256,4096]{1,0:T(8,128)(2,1)}, bf16[256,4096]{1,0:T(8,128)(2,1)S(1)}, u32[]{:S(2)}) copy-start(bf16[256,4096]{1,0:T(8,128)(2,1)S(1)} %get-tuple-element.33.m_lo) | copy-start | bytes 6291460
  64.2 1.4 %copy-start.8 = (bf16[4096,256]{1,0:T(8,128)(2,1)}, bf16[4096,256]{1,0:T(8,128)(2,1)S(1)}, u32[]{:S(2)}) copy-start(bf16[4096,256]{1,0:T(8,128)(2,1)S(1)} %get-tuple-element.37.r_hi) | copy-start | bytes 6291460
  65.6 1.3 %copy-start.10 = (bf16[4096,256]{1,0:T(8,128)(2,1)}, bf16[4096,256]{1,0:T(8,128)(2,1)S(1)}, u32[]{:S(2)}) copy-start(bf16[4096,256]{1,0:T(8,128)(2,1)S(1)} %get-tuple-element.38.r_lo) | copy-start | bytes 6291460
  82.2 11.2 %copy-start.9 = (bf16[4096,256]{1,0:T(8,128)(2,1)S(1)}, bf16[4096,256]{1,0:T(8,128)(2,1)}, u32[]{:S(2)}) copy-start(bf16[4096,256]{1,0:T(8,128)(2,1)} %copy-done.8) | copy-start | bytes 6291460
  82.2 11.2 %copy-start.11 = (bf16[4096,256]{1,0:T(8,128)(2,1)S(1)}, bf16[4096,256]{1,0:T(8,128)(2,1)}, u32[]{:S(2)}) copy-start(bf16[4096,256]{1,0:T(8,128)(2,1)} %copy-done.10) | copy-start | bytes 6291460
  86.5 7.0 %collective-permute-start.10 = (f32[256,256]{1,0:T(8,128)S(1)}, f32[256,256]{1,0:T(8,128)S(1)}, u32[]{:S(2)}, u32[]{:S(2)}) collective-permute-start(f32[256,256]{1,0:T(8,128)S(1)} %get-tuple-element.34.part_a), channel_id=1, source_target_pairs={{0,16},{16,0},{1,17},{17,1},{2,18},{18,2},{3,19},{19,3},{4,20},{20... | collective-permute-start | bytes 786440 | tf_op jit(solution)/shard_map/ppermute | solution.py:552
  98.1 1.6 %collective-permute-start.11 = (f32[256,256]{1,0:T(8,128)S(1)}, f32[256,256]{1,0:T(8,128)S(1)}, u32[]{:S(2)}, u32[]{:S(2)}) collective-permute-start(f32[256,256]{1,0:T(8,128)S(1)} %get-tuple-element.41.part_a), channel_id=1, source_target_pairs={{0,16},{16,0},{1,17},{17,1},{2,18},{18,2},{3,19},{19,3},{4,20},{20... | collective-permute-start | bytes 786440 | tf_op jit(solution)/shard_map/ppermute | solution.py:553
  105.4 11.6 %all-to-all-start.2 = ((f32[16,40,128]{2,1,0:T(8,128)}), f32[16,40,128]{2,1,0:T(8,128)S(1)}, u32[]{:S(2)}, u32[]{:S(2)}) async-start(f32[16,40,128]{2,1,0:T(8,128)} %image_three.1), calls=%async_computation.2 | async-start | bytes 655360 | tf_op jit(solution)/shard_map/all_to_all | solution.py:555
  117.0 4.7 %collective-permute-start.14 = (f32[16,128]{1,0:T(8,128)S(1)}, f32[16,128]{1,0:T(8,128)S(1)}, u32[]{:S(2)}, u32[]{:S(2)}) collective-permute-start(f32[16,128]{1,0:T(8,128)S(1)} %bitcast.10), channel_id=1, source_target_pairs={{0,96},{32,0},{64,32},{96,64},{1,97},{33,1},{65,33},{97,65},{2,98}... | collective-permute-start | bytes 24584 | tf_op jit(solution)/shard_map/ppermute | solution.py:558
  118.1 4.0 %collective-permute-start.13 = (f32[16,128]{1,0:T(8,128)S(1)}, f32[16,128]{1,0:T(8,128)S(1)}, u32[]{:S(2)}, u32[]{:S(2)}) collective-permute-start(f32[16,128]{1,0:T(8,128)S(1)} %bitcast.11), channel_id=1, source_target_pairs={{0,64},{32,96},{64,0},{96,32},{1,65},{33,97},{65,1},{97,33},{2,66}... | collective-permute-start | bytes 24584 | tf_op jit(solution)/shard_map/ppermute | solution.py:558
  118.1 4.0 %collective-permute-start.12 = (f32[16,128]{1,0:T(8,128)S(1)}, f32[16,128]{1,0:T(8,128)S(1)}, u32[]{:S(2)}, u32[]{:S(2)}) collective-permute-start(f32[16,128]{1,0:T(8,128)S(1)} %bitcast.12), channel_id=1, source_target_pairs={{0,32},{32,64},{64,96},{96,0},{1,33},{33,65},{65,97},{97,1},{2,34}... | collective-permute-start | bytes 24584 | tf_op jit(solution)/shard_map/ppermute | solution.py:558
  118.7 7.8 %collective-permute-start.16 = (f32[8,32,128]{2,1,0:T(8,128)S(1)}, f32[8,32,128]{2,1,0:T(8,128)S(1)}, u32[]{:S(2)}, u32[]{:S(2)}) collective-permute-start(f32[8,32,128]{2,1,0:T(8,128)S(1)} %constant_dynamic-slice_fusion), channel_id=1, source_target_pairs={{0,16},{16,0},{1,17},{17,1},{2,18},{18,2},{3,19},{19,3},{4,20},{20... | collective-permute-start | bytes 393224 | tf_op jit(solution)/shard_map/ppermute | solution.py:561
  122.1 4.5 %collective-permute-start.15 = (f32[64,128]{1,0:T(8,128)S(1)}, f32[64,128]{1,0:T(8,128)S(1)}, u32[]{:S(2)}, u32[]{:S(2)}) collective-permute-start(f32[64,128]{1,0:T(8,128)S(1)} %pad_maximum_fusion.own_stats), channel_id=1, source_target_pairs={{0,16},{16,0},{1,17},{17,1},{2,18},{18,2},{3,19},{19,3},{4,20},{20... | collective-permute-start | bytes 98312 | tf_op jit(solution)/shard_map/ppermute | solution.py:563
  (1 other events, 1.3 us)

commit v12 on v11

--- a/solution.py
+++ b/solution.py
@@ -91,10 +91,11 @@
     return hi, (x - hi.astype(f32)).astype(bf16)
 
 
+def dot(a, b):
+    return jnp.dot(a, b, preferred_element_type=f32)
+
+
 def dot3(a_hi, a_lo, b_hi, b_lo):
-    def dot(a, b):
-        return jnp.dot(a, b, preferred_element_type=f32)
-
     return dot(a_hi, b_hi) + (dot(a_hi, b_lo) + dot(a_lo, b_hi))
 
 
@@ -316,19 +317,18 @@
 
 
 def image_one_body(arrived, m_hi, m_lo, l_hi, l_lo, part, here_hi, here_lo, sem):
-    fetches = [
-        pltpu.make_async_copy(m_hi, here_hi, sem.at[0]),
-        pltpu.make_async_copy(m_lo, here_lo, sem.at[1]),
-    ]
-    for fetch in fetches:
-        fetch.start()
+    high = pltpu.make_async_copy(m_hi, here_hi, sem.at[0])
+    low = pltpu.make_async_copy(m_lo, here_lo, sem.at[1])
+    high.start()
     for n in range(TERMS):
         hi, lo = split(get_folded(arrived, n, 0))
         l_hi[n * TILE : (n + 1) * TILE, :] = hi
         l_lo[n * TILE : (n + 1) * TILE, :] = lo
-    for fetch in fetches:
-        fetch.wait()
-    part[...] = dot3(here_hi[...], here_lo[...], l_hi[...], l_lo[...])
+    high.wait()
+    low.start()
+    acc = dot(here_hi[...], l_lo[...]) + dot(here_hi[...], l_hi[...])
+    low.wait()
+    part[...] = acc + dot(here_lo[...], l_hi[...])
 
 
 def image_one(arrived, m_hi, m_lo):
@@ -402,7 +402,7 @@
 
 def image_three_body(
     ids, rsector, rsector_other, sector, lsize, rsize,
-    part_a, part_b, q1, q2, stats_in, r_hi, r_lo, l_hi, l_lo, slots,
+    part_a, part_b, q1, q2, stats_in, r_hi, r_lo, l_hi, l_lo, out, cols, tail, sem,
 ):
     mask = mask_of(*live_sizes(ids, rsector, rsector_other, sector, lsize, rsize))
     image = jnp.where(mask, part_a[...] + part_b[...], 0.0)
@@ -411,21 +411,32 @@
     alpha, norm, vec = lanczos(image, q2[...], q1[...], beta)
     pick = jnp.where(ids[1] == 0, q2[...], vec)
     for n in range(16):
-        slots[n, :16, :] = pick[16 * n : 16 * n + 16, :HALF]
-        slots[n, 16:THIN, :] = pick[16 * n : 16 * n + 16, HALF:]
+        cols[n, :16, :] = pick[16 * n : 16 * n + 16, :HALF]
+        cols[n, 16:, :] = pick[16 * n : 16 * n + 16, HALF:]
+    columns = pltpu.make_async_copy(cols, out.at[:, pl.ds(0, THIN), :], sem.at[0])
+    columns.start()
     stats = put(put(stats_in[...], 3, alpha), 4, norm)
     alpha = total(vec * half_image(vec, r_hi, r_lo, l_hi, l_lo))
     stats = put(stats, 5, alpha)
     for n in range(16):
-        slots[n, THIN:, :] = stats
+        tail[n] = stats
+    numbers = pltpu.make_async_copy(tail, out.at[:, pl.ds(THIN, 8), :], sem.at[1])
+    numbers.start()
+    numbers.wait()
+    columns.wait()
 
 
 def image_three(scalars, part, part_other, q1, q2, stats, stacks):
     return pl.pallas_call(
         image_three_body,
         in_specs=[smem()] * 6 + [vmem()] * 9,
-        out_specs=vmem(),
-        out_shape=jax.ShapeDtypeStruct((16, THIN + 8, HALF), f32),
+        out_specs=hbm(),
+        out_shape=pltpu.HBM((16, THIN + 8, HALF), f32),
+        scratch_shapes=[
+            pltpu.VMEM((16, THIN, HALF), f32),
+            pltpu.VMEM((16, 8, HALF), f32),
+            pltpu.SemaphoreType.DMA((2,)),
+        ],
         compiler_params=params(6),
         cost_estimate=cost(3_300_000_000, 9_000_000),
         name="image_three",

time: 129 us -> 131 us (1.016)
  Pallas kernels: 29.2 us -> 31.1 us
    pallas_call x1, Pallas kernels: 4.25 us -> 6.17 us  [image_one(): pl.pallas_call(image_one_body, in_specs=[vmem(), hbm(), hbm()], out_specs...]
where the time goes in v12:
time: 131 us
  waiting for transfers between devices  52.6 us (40%)
  starting transfers between devices  40.4 us (31%)
  Pallas kernels  31.1 us (24%)
  local copies, waits for them, and re-layouts  5.57 us (4%)
    all_to_all x1, waiting for transfers between devices, local(): left_arrived = lax.all_to_all(left_sent, COL, 0, 0, tiled=True)  15.2 us
    ppermute x2, waiting for transfers between devices, local(): far = [lax.ppermute(below[0], 'y', UP), lax.ppermute(above[1], 'y', DOWN)]  11.6 us
    ppermute x2, waiting for transfers between devices, local(): above = [lax.ppermute(x, 'y', DOWN) for x in (mine, theirs)]  8.33 us
    all_to_all x1, waiting for transfers between devices, local(): got = lax.all_to_all(sent, COL, 0, 0, tiled=True)  7.93 us
    all_to_all x1, starting transfers between devices, local(): arrived = lax.all_to_all(slots, COL, 0, 0, tiled=True)  7.79 us
    ppermute x2, starting transfers between devices, local(): lax.ppermute(part, 'c', SWAP)  6.25 us
    pallas_call x1, Pallas kernels, image_one(): pl.pallas_call(image_one_body, in_specs=[vmem(), hbm(), hbm()], out_specs...  6.17 us
    unnamed x27, local copies, waits for them, and re-layouts  5.55 us
  transfers between devices with their start and end apart: 20, of which 10 were waited for; matrix products, arithmetic and copies ran while one was open for 0% of the time, Pallas kernels for 7%

profile of v12, /device:TPU:1, one launch (start us, length us, event | category | flops | bytes accessed | tf_op | source)
XLA Modules:
  0.0 130.8 jit_solution(170413310819974163)
XLA Ops:
  0.7 3.0 %fold.1 = (f32[4,264,128]{2,1,0:T(8,128)}, f32[4,264,128]{2,1,0:T(8,128)}, f32[9,264,128]{2,1,0:T(8,128)S(1)}) custom-call(s32[3]{0:T(128)S(1)} %pad_add_fusion.ids, f32[4,2,256,256]{3,2,1,0:T(8,128)} %left_env.1, f32[8,2,256,256]{3,2,1,0:T(8,128)} %right_env.1), custom_call_target="tpu_custom_call" | custom-call | flops 1000000 | bytes 6000000 | tf_op jit(solution)/shard_map/fold/pallas_call | solution.py:145
  3.7 1.5 %collective-permute-start = (f32[4,264,128]{2,1,0:T(8,128)}, f32[4,264,128]{2,1,0:T(8,128)S(1)}, u32[]{:S(2)}, u32[]{:S(2)}) collective-permute-start(f32[4,264,128]{2,1,0:T(8,128)} %get-tuple-element.24), channel_id=1, source_target_pairs={{0,16},{16,0},{1,17},{17,1},{2,18},{18,2},{3,19},{19,3},{4,20},{20... | collective-permute-start | bytes 1622024 | tf_op jit(solution)/shard_map/ppermute | solution.py:542
  5.9 1.4 %collective-permute-start.6 = (f32[4,264,128]{2,1,0:T(8,128)}, f32[4,264,128]{2,1,0:T(8,128)S(1)}, u32[]{:S(2)}, u32[]{:S(2)}) collective-permute-start(f32[4,264,128]{2,1,0:T(8,128)} %get-tuple-element.26.refs_0_), channel_id=1, source_target_pairs={{0,32},{32,64},{64,96},{96,0},{1,33},{33,65},{65,97},{97,1},{2,34}... | collective-permute-start | bytes 1622024 | tf_op jit(solution)/shard_map/ppermute | solution.py:546
  7.3 2.5 %collective-permute-start.5 = (f32[4,264,128]{2,1,0:T(8,128)S(1)}, f32[4,264,128]{2,1,0:T(8,128)S(1)}, u32[]{:S(2)}, u32[]{:S(2)}) collective-permute-start(f32[4,264,128]{2,1,0:T(8,128)S(1)} %collective-permute-done.refs_1_), channel_id=1, source_target_pairs={{0,96},{32,0},{64,32},{96,64},{1,97},{33,1},{65,33},{97,65},{2,98}... | collective-permute-start | bytes 1622024 | tf_op jit(solution)/shard_map/ppermute | solution.py:547
  9.9 2.2 %right_slots.1 = f32[16,296,128]{2,1,0:T(8,128)} custom-call(s32[3]{0:T(128)S(1)} %pad_add_fusion.ids, s32[8]{0:T(128)S(1)} %copy-done.3, s32[8]{0:T(128)S(1)} %collective-permute-done.1.rsector_other, s32[8,2]{1,0:T(8,128)S(1)} %copy.10.on, s32[8,2]{1,0:T(8,128)S(1)} %collective-permute-done.2.on_other, f32[8,16,256]{2,1,0:T(8,128)S(1)} %bitcast.8, ...), custom_call_target="tpu_custom_call" | custom-call | flops 4000000 | bytes 6000000 | tf_op jit(solution)/shard_map/right_slots/pallas_call | solution.py:188
  12.1 7.8 %all-to-all-start.1 = ((f32[16,296,128]{2,1,0:T(8,128)}), f32[16,296,128]{2,1,0:T(8,128)}, u32[]{:S(2)}, u32[]{:S(2)}) async-start(f32[16,296,128]{2,1,0:T(8,128)} %right_slots.1), calls=%async_computation.1 | async-start | bytes 4849664 | tf_op jit(solution)/shard_map/all_to_all | solution.py:554
  20.4 1.0 collective-permute-start.9
  21.4 3.1 %collective-permute-start.8 = (f32[4,264,128]{2,1,0:T(8,128)S(1)}, f32[4,264,128]{2,1,0:T(8,128)S(1)}, u32[]{:S(2)}, u32[]{:S(2)}) collective-permute-start(f32[4,264,128]{2,1,0:T(8,128)S(1)} %collective-permute-done.5.refs_3_), channel_id=1, source_target_pairs={{0,96},{32,0},{64,32},{96,64},{1,97},{33,1},{65,33},{97,65},{2,98}... | collective-permute-start | bytes 1622024 | tf_op jit(solution)/shard_map/ppermute | solution.py:548
  24.6 8.3 %collective-permute-done.4.refs_2_ = f32[4,264,128]{2,1,0:T(8,128)S(1)} collective-permute-done((f32[4,264,128]{2,1,0:T(8,128)S(1)}, f32[4,264,128]{2,1,0:T(8,128)S(1)}, u32[]{:S(2)}, u32[]{:S(2)}) %collective-permute-start.4) | collective-permute-done | bytes 540704 | tf_op jit(solution)/shard_map/ppermute | solution.py:547
  32.9 1.1 collective-permute-done.9.refs_7_
  34.0 11.6 %collective-permute-done.7.refs_4_ = f32[4,264,128]{2,1,0:T(8,128)S(1)} collective-permute-done((f32[4,264,128]{2,1,0:T(8,128)S(1)}, f32[4,264,128]{2,1,0:T(8,128)S(1)}, u32[]{:S(2)}, u32[]{:S(2)}) %collective-permute-start.7) | collective-permute-done | bytes 540704 | tf_op jit(solution)/shard_map/ppermute | solution.py:548
  45.6 2.0 %left_slots.1 = f32[16,264,128]{2,1,0:T(8,128)} custom-call(s32[3]{0:T(128)S(1)} %pad_add_fusion.ids, s32[64]{0:T(128)S(1)} %copy-done.4, f32[4,264,128]{2,1,0:T(8,128)S(1)} %copy-done.7, f32[4,264,128]{2,1,0:T(8,128)S(1)} %collective-permute-done.refs_1_, f32[4,264,128]{2,1,0:T(8,128)S(1)} %collective-permute-done.4.refs_2_, ...), custom_call_target="tpu_custom_call" | custom-call | flops 15000000512 | bytes 4000000 | tf_op jit(solution)/shard_map/left_slots/pallas_call | solution.py:236
  47.6 4.9 %all-to-all-done.1.slots = f32[16,296,128]{2,1,0:T(8,128)} async-done(((f32[16,296,128]{2,1,0:T(8,128)}), f32[16,296,128]{2,1,0:T(8,128)}, u32[]{:S(2)}, u32[]{:S(2)}) %all-to-all-start.1) | async-done | bytes 2424864 | tf_op jit(solution)/shard_map/all_to_all | solution.py:554
  52.5 3.7 %all-to-all-start = ((f32[16,264,128]{2,1,0:T(8,128)}), f32[16,264,128]{2,1,0:T(8,128)S(1)}, u32[]{:S(2)}, u32[]{:S(2)}) async-start(f32[16,264,128]{2,1,0:T(8,128)} %left_slots.1), calls=%async_computation | async-start | bytes 4325376 | tf_op jit(solution)/shard_map/all_to_all | solution.py:560
  56.2 5.3 %first_vector.1 = (bf16[4096,256]{1,0:T(8,128)(2,1)S(1)}, bf16[4096,256]{1,0:T(8,128)(2,1)S(1)}, bf16[256,4096]{1,0:T(8,128)(2,1)S(1)}, bf16[256,4096]{1,0:T(8,1...) custom-call(s32[3]{0:T(128)S(1)} %pad_add_fusion.ids, s32[8]{0:T(128)S(1)} %copy-done.3, ...), custom_call_target="tpu_custom_call" | custom-call | flops 1700000000 | bytes 12000000 | tf_op jit(solution)/shard_map/first_vector/pallas_call | solution.py:297
  61.6 1.3 %copy-done = bf16[256,4096]{1,0:T(8,128)(2,1)} copy-done((bf16[256,4096]{1,0:T(8,128)(2,1)}, bf16[256,4096]{1,0:T(8,128)(2,1)S(1)}, u32[]{:S(2)}) %copy-start) | copy-done | bytes 2097176
  62.9 1.4 %copy-done.1 = bf16[256,4096]{1,0:T(8,128)(2,1)} copy-done((bf16[256,4096]{1,0:T(8,128)(2,1)}, bf16[256,4096]{1,0:T(8,128)(2,1)S(1)}, u32[]{:S(2)}) %copy-start.1) | copy-done | bytes 2097176
  64.2 1.4 %copy-done.8 = bf16[4096,256]{1,0:T(8,128)(2,1)} copy-done((bf16[4096,256]{1,0:T(8,128)(2,1)}, bf16[4096,256]{1,0:T(8,128)(2,1)S(1)}, u32[]{:S(2)}) %copy-start.8) | copy-done | bytes 2097176
  65.6 1.3 %copy-done.10 = bf16[4096,256]{1,0:T(8,128)(2,1)} copy-done((bf16[4096,256]{1,0:T(8,128)(2,1)}, bf16[4096,256]{1,0:T(8,128)(2,1)S(1)}, u32[]{:S(2)}) %copy-start.10) | copy-done | bytes 2097176
  67.0 15.2 %all-to-all-done.arrived = f32[16,264,128]{2,1,0:T(8,128)S(1)} async-done(((f32[16,264,128]{2,1,0:T(8,128)}), f32[16,264,128]{2,1,0:T(8,128)S(1)}, u32[]{:S(2)}, u32[]{:S(2)}) %all-to-all-start) | async-done | bytes 2162720 | tf_op jit(solution)/shard_map/all_to_all | solution.py:560
  82.2 6.2 %image_one.1 = (bf16[4096,256]{1,0:T(8,128)(2,1)S(1)}, bf16[4096,256]{1,0:T(8,128)(2,1)S(1)}, f32[256,256]{1,0:T(8,128)S(1)}) custom-call(f32[16,264,128]{2,1,0:T(8,128)S(1)} %all-to-all-done.arrived, bf16[256,4096]{1,0:T(8,128)(2,1)} %copy-done, bf16[256,4096]{1,0:T(8,128)(2,1)} %copy-done.1), custom_call_target="tpu_custom_call" | custom-call | flops 1700000000 | bytes 10000000 | tf_op jit(solution)/shard_map/image_one/pallas_call | solution.py:336
  88.4 5.8 %collective-permute-start.10 = (f32[256,256]{1,0:T(8,128)S(1)}, f32[256,256]{1,0:T(8,128)S(1)}, u32[]{:S(2)}, u32[]{:S(2)}) collective-permute-start(f32[256,256]{1,0:T(8,128)S(1)} %get-tuple-element.34.part_a), channel_id=1, source_target_pairs={{0,16},{16,0},{1,17},{17,1},{2,18},{18,2},{3,19},{19,3},{4,20},{20... | collective-permute-start | bytes 786440 | tf_op jit(solution)/shard_map/ppermute | solution.py:563
  94.2 1.2 collective-permute-done.10.part_b
  95.4 4.7 %image_two.1 = (f32[256,256]{1,0:T(8,128)S(1)}, f32[256,256]{1,0:T(8,128)S(1)}, f32[8,128]{1,0:T(8,128)S(1)}) custom-call(s32[3]{0:T(128)S(1)} %pad_add_fusion.ids, s32[8]{0:T(128)S(1)} %copy-done.3, s32[8]{0:T(128)S(1)} %collective-permute-done.1.rsector_other, s32[64]{0:T(128)S(1)} %copy-done.4, s32[32]{0:T(128)S(1)} %copy-done.5, s32[8]{0:T(128)S(1)} %copy-done.6, ...), custom_call_target="tpu_custom_call" | custom-call | flops 3300000000 | bytes 9000000 | tf_op jit(solution)/shard_map/image_two/pallas_call | solution.py:388
  100.5 1.2 collective-permute-done.11.part_b
  101.7 5.5 %image_three.1 = f32[16,40,128]{2,1,0:T(8,128)} custom-call(s32[3]{0:T(128)S(1)} %pad_add_fusion.ids, s32[8]{0:T(128)S(1)} %copy-done.3, s32[8]{0:T(128)S(1)} %collective-permute-done.1.rsector_other, s32[64]{0:T(128)S(1)} %copy-done.4, s32[32]{0:T(128)S(1)} %copy-done.5, s32[8]{0:T(128)S(1)} %copy-done.6, f32[256,256]{1,0:T(8,128)S(1)} %get-tuple-element.41.part_a, ...), custom_call_target="tpu_custom_call" | custom-call | flops 3300000000 | bytes 9000000 | tf_op jit(solution)/shard_map/image_three/pallas_call | solution.py:430
  107.2 3.7 %all-to-all-start.2 = ((f32[16,40,128]{2,1,0:T(8,128)}), f32[16,40,128]{2,1,0:T(8,128)S(1)}, u32[]{:S(2)}, u32[]{:S(2)}) async-start(f32[16,40,128]{2,1,0:T(8,128)} %image_three.1), calls=%async_computation.2 | async-start | bytes 655360 | tf_op jit(solution)/shard_map/all_to_all | solution.py:566
  110.9 7.9 %all-to-all-done.2.got = f32[16,40,128]{2,1,0:T(8,128)S(1)} async-done(((f32[16,40,128]{2,1,0:T(8,128)}), f32[16,40,128]{2,1,0:T(8,128)S(1)}, u32[]{:S(2)}, u32[]{:S(2)}) %all-to-all-start.2) | async-done | bytes 327712 | tf_op jit(solution)/shard_map/all_to_all | solution.py:566
  118.8 1.1 collective-permute-start.14
  120.6 2.9 %collective-permute-start.16 = (f32[8,32,128]{2,1,0:T(8,128)S(1)}, f32[8,32,128]{2,1,0:T(8,128)S(1)}, u32[]{:S(2)}, u32[]{:S(2)}) collective-permute-start(f32[8,32,128]{2,1,0:T(8,128)S(1)} %constant_dynamic-slice_fusion), channel_id=1, source_target_pairs={{0,16},{16,0},{1,17},{17,1},{2,18},{18,2},{3,19},{19,3},{4,20},{20... | collective-permute-start | bytes 393224 | tf_op jit(solution)/shard_map/ppermute | solution.py:572
  123.9 3.6 %collective-permute-start.15 = (f32[64,128]{1,0:T(8,128)S(1)}, f32[64,128]{1,0:T(8,128)S(1)}, u32[]{:S(2)}, u32[]{:S(2)}) collective-permute-start(f32[64,128]{1,0:T(8,128)S(1)} %pad_maximum_fusion.own_stats), channel_id=1, source_target_pairs={{0,16},{16,0},{1,17},{17,1},{2,18},{18,2},{3,19},{19,3},{4,20},{20... | collective-permute-start | bytes 98312 | tf_op jit(solution)/shard_map/ppermute | solution.py:574
  128.4 2.2 %finish.1 = (f32[8,16,256]{2,1,0:T(8,128)}, f32[1,1]{1,0:T(1,128)}) custom-call(s32[3]{0:T(128)S(1)} %pad_add_fusion.ids, s32[64]{0:T(128)S(1)} %copy-done.4, s32[8]{0:T(128)S(1)} %copy-done.3, s32[32]{0:T(128)S(1)} %copy-done.5, s32[8]{0:T(128)S(1)} %copy-done.6, f32[64,128]{1,0:T(8,128)S(1)} %pad_maximum_fusion.own_stats, ...), custom_call_target="tpu_custom_call" | custom-call | tf_op jit(solution)/shard_map/finish/pallas_call | solution.py:516
  (47 shorter events, 3.8 us)
Async XLA Ops:
  0.7 4.5 %copy-start.2 = (f32[8,256,16]{1,2,0:T(8,128)S(1)}, f32[8,256,16]{1,2,0:T(8,128)}, u32[]{:S(2)}) copy-start(f32[8,256,16]{1,2,0:T(8,128)} %param.8) | copy-start | bytes 393220
  0.7 4.6 %copy-start.3 = (s32[8]{0:T(128)S(1)}, s32[8]{0:T(128)}, u32[]{:S(2)}) copy-start(s32[8]{0:T(128)} %rsector.9) | copy-start | bytes 100
  0.7 5.0 %copy-start.12 = (s32[8,2]{0,1:T(2,128)S(1)}, s32[8,2]{0,1:T(2,128)}, u32[]{:S(2)}) copy-start(s32[8,2]{0,1:T(2,128)} %param.13) | copy-start | bytes 196
  3.7 3.6 %collective-permute-start = (f32[4,264,128]{2,1,0:T(8,128)}, f32[4,264,128]{2,1,0:T(8,128)S(1)}, u32[]{:S(2)}, u32[]{:S(2)}) collective-permute-start(f32[4,264,128]{2,1,0:T(8,128)} %get-tuple-element.24), channel_id=1, source_target_pairs={{0,16},{16,0},{1,17},{17,1},{2,18},{18,2},{3,19},{19,3},{4,20},{20... | collective-permute-start | bytes 1622024 | tf_op jit(solution)/shard_map/ppermute | solution.py:542
  5.2 2.1 %collective-permute-start.3 = (f32[8,16,256]{2,1,0:T(8,128)S(1)}, f32[8,16,256]{2,1,0:T(8,128)S(1)}, u32[]{:S(2)}, u32[]{:S(2)}) collective-permute-start(f32[8,16,256]{2,1,0:T(8,128)S(1)} %bitcast.7), channel_id=1, source_target_pairs={{0,16},{16,0},{1,17},{17,1},{2,18},{18,2},{3,19},{19,3},{4,20},{20... | collective-permute-start | bytes 393224 | tf_op jit(solution)/shard_map/ppermute | solution.py:539
  5.3 2.0 %collective-permute-start.1 = (s32[8]{0:T(128)S(1)}, s32[8]{0:T(128)S(1)}, u32[]{:S(2)}, u32[]{:S(2)}) collective-permute-start(s32[8]{0:T(128)S(1)} %copy-done.3), channel_id=1, source_target_pairs={{0,16},{16,0},{1,17},{17,1},{2,18},{18,2},{3,19},{19,3},{4,20},{20... | collective-permute-start | bytes 104 | tf_op jit(solution)/shard_map/ppermute | solution.py:537
  5.8 1.5 %collective-permute-start.2 = (s32[8,2]{1,0:T(8,128)S(1)}, s32[8,2]{1,0:T(8,128)S(1)}, u32[]{:S(2)}, u32[]{:S(2)}) collective-permute-start(s32[8,2]{1,0:T(8,128)S(1)} %copy.10.on), channel_id=1, source_target_pairs={{0,16},{16,0},{1,17},{17,1},{2,18},{18,2},{3,19},{19,3},{4,20},{20... | collective-permute-start | bytes 200 | tf_op jit(solution)/shard_map/ppermute | solution.py:538
  5.9 15.5 %collective-permute-start.6 = (f32[4,264,128]{2,1,0:T(8,128)}, f32[4,264,128]{2,1,0:T(8,128)S(1)}, u32[]{:S(2)}, u32[]{:S(2)}) collective-permute-start(f32[4,264,128]{2,1,0:T(8,128)} %get-tuple-element.26.refs_0_), channel_id=1, source_target_pairs={{0,32},{32,64},{64,96},{96,0},{1,33},{33,65},{65,97},{97,1},{2,34}... | collective-permute-start | bytes 1622024 | tf_op jit(solution)/shard_map/ppermute | solution.py:546
  7.3 14.1 %collective-permute-start.5 = (f32[4,264,128]{2,1,0:T(8,128)S(1)}, f32[4,264,128]{2,1,0:T(8,128)S(1)}, u32[]{:S(2)}, u32[]{:S(2)}) collective-permute-start(f32[4,264,128]{2,1,0:T(8,128)S(1)} %collective-permute-done.refs_1_), channel_id=1, source_target_pairs={{0,96},{32,0},{64,32},{96,64},{1,97},{33,1},{65,33},{97,65},{2,98}... | collective-permute-start | bytes 1622024 | tf_op jit(solution)/shard_map/ppermute | solution.py:547
  12.0 7.8 %copy-start.7 = (f32[4,264,128]{2,1,0:T(8,128)S(1)}, f32[4,264,128]{2,1,0:T(8,128)}, u32[]{:S(2)}) copy-start(f32[4,264,128]{2,1,0:T(8,128)} %get-tuple-element.26.refs_0_) | copy-start | bytes 1622020
  12.1 33.5 %copy-start.4 = (s32[64]{0:T(128)S(1)}, s32[64]{0:T(128)}, u32[]{:S(2)}) copy-start(s32[64]{0:T(128)} %sector.7) | copy-start | bytes 772
  12.1 40.4 %all-to-all-start.1 = ((f32[16,296,128]{2,1,0:T(8,128)}), f32[16,296,128]{2,1,0:T(8,128)}, u32[]{:S(2)}, u32[]{:S(2)}) async-start(f32[16,296,128]{2,1,0:T(8,128)} %right_slots.1), calls=%async_computation.1 | async-start | bytes 4849664 | tf_op jit(solution)/shard_map/all_to_all | solution.py:554
  19.9 13.0 %collective-permute-start.4 = (f32[4,264,128]{2,1,0:T(8,128)S(1)}, f32[4,264,128]{2,1,0:T(8,128)S(1)}, u32[]{:S(2)}, u32[]{:S(2)}) collective-permute-start(f32[4,264,128]{2,1,0:T(8,128)S(1)} %copy-done.7), channel_id=1, source_target_pairs={{0,96},{32,0},{64,32},{96,64},{1,97},{33,1},{65,33},{97,65},{2,98}... | collective-permute-start | bytes 1622024 | tf_op jit(solution)/shard_map/ppermute | solution.py:547
  20.4 13.6 %collective-permute-start.9 = (f32[4,264,128]{2,1,0:T(8,128)S(1)}, f32[4,264,128]{2,1,0:T(8,128)S(1)}, u32[]{:S(2)}, u32[]{:S(2)}) collective-permute-start(f32[4,264,128]{2,1,0:T(8,128)S(1)} %collective-permute-done.refs_1_), channel_id=1, source_target_pairs={{0,32},{32,64},{64,96},{96,0},{1,33},{33,65},{65,97},{97,1},{2,34}... | collective-permute-start | bytes 1622024 | tf_op jit(solution)/shard_map/ppermute | solution.py:546
  21.4 24.2 %collective-permute-start.7 = (f32[4,264,128]{2,1,0:T(8,128)S(1)}, f32[4,264,128]{2,1,0:T(8,128)S(1)}, u32[]{:S(2)}, u32[]{:S(2)}) collective-permute-start(f32[4,264,128]{2,1,0:T(8,128)S(1)} %collective-permute-done.6.refs_6_), channel_id=1, source_target_pairs={{0,32},{32,64},{64,96},{96,0},{1,33},{33,65},{65,97},{97,1},{2,34}... | collective-permute-start | bytes 1622024 | tf_op jit(solution)/shard_map/ppermute | solution.py:548
  21.4 24.1 %collective-permute-start.8 = (f32[4,264,128]{2,1,0:T(8,128)S(1)}, f32[4,264,128]{2,1,0:T(8,128)S(1)}, u32[]{:S(2)}, u32[]{:S(2)}) collective-permute-start(f32[4,264,128]{2,1,0:T(8,128)S(1)} %collective-permute-done.5.refs_3_), channel_id=1, source_target_pairs={{0,96},{32,0},{64,32},{96,64},{1,97},{33,1},{65,33},{97,65},{2,98}... | collective-permute-start | bytes 1622024 | tf_op jit(solution)/shard_map/ppermute | solution.py:548
  47.5 8.7 %copy-start.5 = (s32[32]{0:T(128)S(1)}, s32[32]{0:T(128)}, u32[]{:S(2)}) copy-start(s32[32]{0:T(128)} %lsize.7) | copy-start | bytes 388
  47.6 8.6 %copy-start.6 = (s32[8]{0:T(128)S(1)}, s32[8]{0:T(128)}, u32[]{:S(2)}) copy-start(s32[8]{0:T(128)} %rsize.7) | copy-start | bytes 100
  52.5 29.7 %all-to-all-start = ((f32[16,264,128]{2,1,0:T(8,128)}), f32[16,264,128]{2,1,0:T(8,128)S(1)}, u32[]{:S(2)}, u32[]{:S(2)}) async-start(f32[16,264,128]{2,1,0:T(8,128)} %left_slots.1), calls=%async_computation | async-start | bytes 4325376 | tf_op jit(solution)/shard_map/all_to_all | solution.py:560
  62.9 1.4 %copy-start.1 = (bf16[256,4096]{1,0:T(8,128)(2,1)}, bf16[256,4096]{1,0:T(8,128)(2,1)S(1)}, u32[]{:S(2)}) copy-start(bf16[256,4096]{1,0:T(8,128)(2,1)S(1)} %get-tuple-element.33.m_lo) | copy-start | bytes 6291460
  64.2 1.4 %copy-start.8 = (bf16[4096,256]{1,0:T(8,128)(2,1)}, bf16[4096,256]{1,0:T(8,128)(2,1)S(1)}, u32[]{:S(2)}) copy-start(bf16[4096,256]{1,0:T(8,128)(2,1)S(1)} %get-tuple-element.37.r_hi) | copy-start | bytes 6291460
  65.6 1.3 %copy-start.10 = (bf16[4096,256]{1,0:T(8,128)(2,1)}, bf16[4096,256]{1,0:T(8,128)(2,1)S(1)}, u32[]{:S(2)}) copy-start(bf16[4096,256]{1,0:T(8,128)(2,1)S(1)} %get-tuple-element.38.r_lo) | copy-start | bytes 6291460
  82.2 13.1 %copy-start.9 = (bf16[4096,256]{1,0:T(8,128)(2,1)S(1)}, bf16[4096,256]{1,0:T(8,128)(2,1)}, u32[]{:S(2)}) copy-start(bf16[4096,256]{1,0:T(8,128)(2,1)} %copy-done.8) | copy-start | bytes 6291460
  82.2 13.1 %copy-start.11 = (bf16[4096,256]{1,0:T(8,128)(2,1)S(1)}, bf16[4096,256]{1,0:T(8,128)(2,1)}, u32[]{:S(2)}) copy-start(bf16[4096,256]{1,0:T(8,128)(2,1)} %copy-done.10) | copy-start | bytes 6291460
  88.4 7.0 %collective-permute-start.10 = (f32[256,256]{1,0:T(8,128)S(1)}, f32[256,256]{1,0:T(8,128)S(1)}, u32[]{:S(2)}, u32[]{:S(2)}) collective-permute-start(f32[256,256]{1,0:T(8,128)S(1)} %get-tuple-element.34.part_a), channel_id=1, source_target_pairs={{0,16},{16,0},{1,17},{17,1},{2,18},{18,2},{3,19},{19,3},{4,20},{20... | collective-permute-start | bytes 786440 | tf_op jit(solution)/shard_map/ppermute | solution.py:563
  100.1 1.6 %collective-permute-start.11 = (f32[256,256]{1,0:T(8,128)S(1)}, f32[256,256]{1,0:T(8,128)S(1)}, u32[]{:S(2)}, u32[]{:S(2)}) collective-permute-start(f32[256,256]{1,0:T(8,128)S(1)} %get-tuple-element.41.part_a), channel_id=1, source_target_pairs={{0,16},{16,0},{1,17},{17,1},{2,18},{18,2},{3,19},{19,3},{4,20},{20... | collective-permute-start | bytes 786440 | tf_op jit(solution)/shard_map/ppermute | solution.py:564
  107.2 11.6 %all-to-all-start.2 = ((f32[16,40,128]{2,1,0:T(8,128)}), f32[16,40,128]{2,1,0:T(8,128)S(1)}, u32[]{:S(2)}, u32[]{:S(2)}) async-start(f32[16,40,128]{2,1,0:T(8,128)} %image_three.1), calls=%async_computation.2 | async-start | bytes 655360 | tf_op jit(solution)/shard_map/all_to_all | solution.py:566
  118.8 4.7 %collective-permute-start.14 = (f32[16,128]{1,0:T(8,128)S(1)}, f32[16,128]{1,0:T(8,128)S(1)}, u32[]{:S(2)}, u32[]{:S(2)}) collective-permute-start(f32[16,128]{1,0:T(8,128)S(1)} %bitcast.10), channel_id=1, source_target_pairs={{0,96},{32,0},{64,32},{96,64},{1,97},{33,1},{65,33},{97,65},{2,98}... | collective-permute-start | bytes 24584 | tf_op jit(solution)/shard_map/ppermute | solution.py:569
  119.9 4.0 %collective-permute-start.13 = (f32[16,128]{1,0:T(8,128)S(1)}, f32[16,128]{1,0:T(8,128)S(1)}, u32[]{:S(2)}, u32[]{:S(2)}) collective-permute-start(f32[16,128]{1,0:T(8,128)S(1)} %bitcast.11), channel_id=1, source_target_pairs={{0,64},{32,96},{64,0},{96,32},{1,65},{33,97},{65,1},{97,33},{2,66}... | collective-permute-start | bytes 24584 | tf_op jit(solution)/shard_map/ppermute | solution.py:569
  119.9 4.0 %collective-permute-start.12 = (f32[16,128]{1,0:T(8,128)S(1)}, f32[16,128]{1,0:T(8,128)S(1)}, u32[]{:S(2)}, u32[]{:S(2)}) collective-permute-start(f32[16,128]{1,0:T(8,128)S(1)} %bitcast.12), channel_id=1, source_target_pairs={{0,32},{32,64},{64,96},{96,0},{1,33},{33,65},{65,97},{97,1},{2,34}... | collective-permute-start | bytes 24584 | tf_op jit(solution)/shard_map/ppermute | solution.py:569
  120.6 7.8 %collective-permute-start.16 = (f32[8,32,128]{2,1,0:T(8,128)S(1)}, f32[8,32,128]{2,1,0:T(8,128)S(1)}, u32[]{:S(2)}, u32[]{:S(2)}) collective-permute-start(f32[8,32,128]{2,1,0:T(8,128)S(1)} %constant_dynamic-slice_fusion), channel_id=1, source_target_pairs={{0,16},{16,0},{1,17},{17,1},{2,18},{18,2},{3,19},{19,3},{4,20},{20... | collective-permute-start | bytes 393224 | tf_op jit(solution)/shard_map/ppermute | solution.py:572
  123.9 4.5 %collective-permute-start.15 = (f32[64,128]{1,0:T(8,128)S(1)}, f32[64,128]{1,0:T(8,128)S(1)}, u32[]{:S(2)}, u32[]{:S(2)}) collective-permute-start(f32[64,128]{1,0:T(8,128)S(1)} %pad_maximum_fusion.own_stats), channel_id=1, source_target_pairs={{0,16},{16,0},{1,17},{17,1},{2,18},{18,2},{3,19},{19,3},{4,20},{20... | collective-permute-start | bytes 98312 | tf_op jit(solution)/shard_map/ppermute | solution.py:574
  (1 other events, 1.3 us)

commit v13 on v11

--- a/solution.py
+++ b/solution.py
@@ -11,7 +11,8 @@
 HALF = 128
 TERMS = 16
 FOLDED = 264
-THIN = 32
+THIN = 16
+COLS = 32
 SLOT = THIN + FOLDED
 COL = ("x", "z")
 ALL = ("y", "c", "x", "z")
@@ -177,8 +178,7 @@
     for slot in range(TERMS):
         here = slot // 8 == ids[1]
         block = jnp.where(here, thin[slot % 8], thin_other[slot % 8])
-        cols[slot, :16, :] = block[:, :HALF]
-        cols[slot, 16:, :] = block[:, HALF:]
+        cols[slot] = jnp.where(ids[1] == 0, block[:, :HALF], block[:, HALF:])
     pltpu.make_async_copy(cols, out.at[:, pl.ds(0, THIN), :], sem).start()
     pltpu.make_async_copy(out, out, sem).wait()
 
@@ -256,7 +256,7 @@
 
 
 def first_body(
-    ids, rsector, rsector_other, sector, lsize, rsize, slots,
+    ids, rsector, rsector_other, sector, lsize, rsize, halves, slots,
     r_hi, r_lo, m_hi, m_lo, q1, stats, arrived, sem,
 ):
     live_right, live_left = live_sizes(ids, rsector, rsector_other, sector, lsize, rsize)
@@ -272,12 +272,11 @@
         hi, lo = split(full)
         r_hi[n * TILE : (n + 1) * TILE, :] = hi
         r_lo[n * TILE : (n + 1) * TILE, :] = lo
+    mine = jnp.concatenate([arrived[n, :THIN, :] for n in range(TERMS)], axis=0)
+    theirs = jnp.concatenate([halves[n] for n in range(TERMS)], axis=0)
+    first = ids[1] == 0
     block = jnp.concatenate(
-        [
-            jnp.concatenate([arrived[n, :16, :], arrived[n, 16:THIN, :]], axis=1)
-            for n in range(TERMS)
-        ],
-        axis=0,
+        [jnp.where(first, mine, theirs), jnp.where(first, theirs, mine)], axis=1
     )
     start = jnp.where(mask_of(live_right, live_left), block, 0.0)
     norm = jnp.sqrt(total(start * start))
@@ -292,10 +291,10 @@
         m_lo[:, rows] = lo
 
 
-def first_vector(scalars, slots):
+def first_vector(scalars, halves, slots):
     return pl.pallas_call(
         first_body,
-        in_specs=[smem()] * 6 + [hbm()],
+        in_specs=[smem()] * 6 + [vmem(), hbm()],
         out_specs=[vmem()] * 6,
         out_shape=[
             jax.ShapeDtypeStruct((TERMS * TILE, TILE), bf16),
@@ -312,7 +311,7 @@
         compiler_params=params(10),
         cost_estimate=cost(1_700_000_000, 12_000_000),
         name="first_vector",
-    )(*scalars, in_hbm(slots))
+    )(*scalars, halves, in_hbm(slots))
 
 
 def image_one_body(arrived, m_hi, m_lo, l_hi, l_lo, part, here_hi, here_lo, sem):
@@ -412,12 +411,12 @@
     pick = jnp.where(ids[1] == 0, q2[...], vec)
     for n in range(16):
         slots[n, :16, :] = pick[16 * n : 16 * n + 16, :HALF]
-        slots[n, 16:THIN, :] = pick[16 * n : 16 * n + 16, HALF:]
+        slots[n, 16:COLS, :] = pick[16 * n : 16 * n + 16, HALF:]
     stats = put(put(stats_in[...], 3, alpha), 4, norm)
     alpha = total(vec * half_image(vec, r_hi, r_lo, l_hi, l_lo))
     stats = put(stats, 5, alpha)
     for n in range(16):
-        slots[n, THIN:, :] = stats
+        slots[n, COLS:, :] = stats
 
 
 def image_three(scalars, part, part_other, q1, q2, stats, stacks):
@@ -425,7 +424,7 @@
         image_three_body,
         in_specs=[smem()] * 6 + [vmem()] * 9,
         out_specs=vmem(),
-        out_shape=jax.ShapeDtypeStruct((16, THIN + 8, HALF), f32),
+        out_shape=jax.ShapeDtypeStruct((16, COLS + 8, HALF), f32),
         compiler_params=params(6),
         cost_estimate=cost(3_300_000_000, 9_000_000),
         name="image_three",
@@ -490,8 +489,8 @@
         live_right = rsize[rsector[b]]
         live = (jcol + ids[2] * 16 < live_right) & (irow < live_left)
         at = core * 8 + b
-        keep = jnp.concatenate([got[at, :16, :], got[at, 16:THIN, :]], axis=1)
-        recv = jnp.concatenate([back[b, :16, :], back[b, 16:THIN, :]], axis=1)
+        keep = jnp.concatenate([got[at, :16, :], got[at, 16:COLS, :]], axis=1)
+        recv = jnp.concatenate([back[b, :16, :], back[b, 16:COLS, :]], axis=1)
         second = jnp.where(core == 0, keep, recv)
         third = jnp.where(core == 0, recv, keep)
         out[b] = (
@@ -542,7 +541,8 @@
     slots, theirs_now = lax.optimization_barrier((slots, theirs))
     arrived = lax.all_to_all(slots, COL, 0, 0, tiled=True)
     scalars = (ids, right_sector, rsector_other, left_sector, left_size, right_size)
-    r_hi, r_lo, m_hi, m_lo, q1, stats = first_vector(scalars, arrived)
+    halves = lax.ppermute(arrived[:, :THIN, :], "c", SWAP)
+    r_hi, r_lo, m_hi, m_lo, q1, stats = first_vector(scalars, halves, arrived)
 
     pieces = [mine, theirs] + above + far + below
     left_sent = left_slots(ids, left_sector, pieces)
@@ -553,11 +553,11 @@
     sent = image_three(scalars, part, lax.ppermute(part, "c", SWAP), q1, q2, stats, stacks)
 
     got = lax.all_to_all(sent, COL, 0, 0, tiled=True)
-    plane_stats = got[:, THIN, :]
+    plane_stats = got[:, COLS, :]
     turned = [
         lax.ppermute(plane_stats, "y", [(i, (i + k) % 4) for i in range(4)]) for k in (1, 2, 3)
     ]
-    give = lax.dynamic_slice(got, ((1 - core) * 8, 0, 0), (8, THIN, HALF))
+    give = lax.dynamic_slice(got, ((1 - core) * 8, 0, 0), (8, COLS, HALF))
     back = lax.ppermute(give, "c", SWAP)
     own_stats = jnp.concatenate([plane_stats] + turned)
     other_stats = lax.ppermute(own_stats, "c", SWAP)

time: 129 us -> 129 us (level)
  waiting for transfers between devices: 52.6 us -> 47.2 us
  starting transfers between devices: 40.4 us -> 45.2 us
    all_to_all x1, waiting for transfers between devices: 15.2 us -> 10.3 us  [local(): left_arrived = lax.all_to_all(left_sent, COL, 0, 0, tiled=True)]
    ppermute x0 -> x1, starting transfers between devices: none -> 2.95 us  [local(): halves = lax.ppermute(arrived[:, :THIN, :], 'c', SWAP)]
    ppermute x3, starting transfers between devices: 1.75 us -> 3.8 us  [local(): lax.ppermute(plane_stats, 'y', [(i, (i + k) % 4) for i in range(4)])]
    all_to_all x1, waiting for transfers between devices: 4.89 us -> 3.29 us  [local(): arrived = lax.all_to_all(slots, COL, 0, 0, tiled=True)]
  transfers between devices with their start and end apart: 20 -> 21, of which waited for: 10 -> 11; matrix products, arithmetic and copies ran while one was open for 0% -> 1% of each run, Pallas kernels for 7% -> 7%
where the time goes in v13:
time: 129 us
  waiting for transfers between devices  47.2 us (37%)
  starting transfers between devices  45.2 us (35%)
  Pallas kernels  29.2 us (23%)
  local copies, waits for them, and re-layouts  6.49 us (5%)
    ppermute x2, waiting for transfers between devices, local(): far = [lax.ppermute(below[0], 'y', UP), lax.ppermute(above[1], 'y', DOWN)]  11.6 us
    all_to_all x1, waiting for transfers between devices, local(): left_arrived = lax.all_to_all(left_sent, COL, 0, 0, tiled=True)  10.3 us
    ppermute x2, waiting for transfers between devices, local(): above = [lax.ppermute(x, 'y', DOWN) for x in (mine, theirs)]  8.28 us
    all_to_all x1, waiting for transfers between devices, local(): got = lax.all_to_all(sent, COL, 0, 0, tiled=True)  7.9 us
    all_to_all x1, starting transfers between devices, local(): arrived = lax.all_to_all(slots, COL, 0, 0, tiled=True)  7.79 us
    ppermute x2, starting transfers between devices, local(): lax.ppermute(part, 'c', SWAP)  6.2 us
    pallas_call x1, Pallas kernels, image_three(): pl.pallas_call(image_three_body, in_specs=[smem()] * 6 + [vmem()] * 9, ou...  5.64 us
    unnamed x27, local copies, waits for them, and re-layouts  5.55 us
  transfers between devices with their start and end apart: 21, of which 11 were waited for; matrix products, arithmetic and copies ran while one was open for 1% of the time, Pallas kernels for 7%

profile of v13, /device:TPU:1, one launch (start us, length us, event | category | flops | bytes accessed | tf_op | source)
XLA Modules:
  0.0 129.1 jit_solution(15468024649604606134)
XLA Ops:
  0.7 3.0 %fold.1 = (f32[4,264,128]{2,1,0:T(8,128)}, f32[4,264,128]{2,1,0:T(8,128)}, f32[9,264,128]{2,1,0:T(8,128)S(1)}) custom-call(s32[3]{0:T(128)S(1)} %pad_add_fusion.ids, f32[4,2,256,256]{3,2,1,0:T(8,128)} %left_env.1, f32[8,2,256,256]{3,2,1,0:T(8,128)} %right_env.1), custom_call_target="tpu_custom_call" | custom-call | flops 1000000 | bytes 6000000 | tf_op jit(solution)/shard_map/fold/pallas_call | solution.py:145
  3.7 1.5 %collective-permute-start = (f32[4,264,128]{2,1,0:T(8,128)}, f32[4,264,128]{2,1,0:T(8,128)S(1)}, u32[]{:S(2)}, u32[]{:S(2)}) collective-permute-start(f32[4,264,128]{2,1,0:T(8,128)} %get-tuple-element.24), channel_id=1, source_target_pairs={{0,16},{16,0},{1,17},{17,1},{2,18},{18,2},{3,19},{19,3},{4,20},{20... | collective-permute-start | bytes 1622024 | tf_op jit(solution)/shard_map/ppermute | solution.py:530
  5.9 1.4 %collective-permute-start.6 = (f32[4,264,128]{2,1,0:T(8,128)}, f32[4,264,128]{2,1,0:T(8,128)S(1)}, u32[]{:S(2)}, u32[]{:S(2)}) collective-permute-start(f32[4,264,128]{2,1,0:T(8,128)} %get-tuple-element.26.refs_0_), channel_id=1, source_target_pairs={{0,32},{32,64},{64,96},{96,0},{1,33},{33,65},{65,97},{97,1},{2,34}... | collective-permute-start | bytes 1622024 | tf_op jit(solution)/shard_map/ppermute | solution.py:534
  7.3 2.5 %collective-permute-start.5 = (f32[4,264,128]{2,1,0:T(8,128)S(1)}, f32[4,264,128]{2,1,0:T(8,128)S(1)}, u32[]{:S(2)}, u32[]{:S(2)}) collective-permute-start(f32[4,264,128]{2,1,0:T(8,128)S(1)} %collective-permute-done.refs_1_), channel_id=1, source_target_pairs={{0,96},{32,0},{64,32},{96,64},{1,97},{33,1},{65,33},{97,65},{2,98}... | collective-permute-start | bytes 1622024 | tf_op jit(solution)/shard_map/ppermute | solution.py:535
  9.9 2.1 %right_slots.1 = f32[16,280,128]{2,1,0:T(8,128)} custom-call(s32[3]{0:T(128)S(1)} %pad_add_fusion.ids, s32[8]{0:T(128)S(1)} %copy-done.3, s32[8]{0:T(128)S(1)} %collective-permute-done.1.rsector_other, s32[8,2]{1,0:T(8,128)S(1)} %copy.10.on, s32[8,2]{1,0:T(8,128)S(1)} %collective-permute-done.2.on_other, f32[8,16,256]{2,1,0:T(8,128)S(1)} %bitcast.8, ...), custom_call_target="tpu_custom_call" | custom-call | flops 4000000 | bytes 6000000 | tf_op jit(solution)/shard_map/right_slots/pallas_call | solution.py:187
  12.0 7.8 %all-to-all-start.1 = ((f32[16,280,128]{2,1,0:T(8,128)}), f32[16,280,128]{2,1,0:T(8,128)}, u32[]{:S(2)}, u32[]{:S(2)}) async-start(f32[16,280,128]{2,1,0:T(8,128)} %right_slots.1), calls=%async_computation.1 | async-start | bytes 4587520 | tf_op jit(solution)/shard_map/all_to_all | solution.py:542
  21.4 3.2 %collective-permute-start.8 = (f32[4,264,128]{2,1,0:T(8,128)S(1)}, f32[4,264,128]{2,1,0:T(8,128)S(1)}, u32[]{:S(2)}, u32[]{:S(2)}) collective-permute-start(f32[4,264,128]{2,1,0:T(8,128)S(1)} %collective-permute-done.5.refs_3_), channel_id=1, source_target_pairs={{0,96},{32,0},{64,32},{96,64},{1,97},{33,1},{65,33},{97,65},{2,98}... | collective-permute-start | bytes 1622024 | tf_op jit(solution)/shard_map/ppermute | solution.py:536
  24.6 8.3 %collective-permute-done.4.refs_2_ = f32[4,264,128]{2,1,0:T(8,128)S(1)} collective-permute-done((f32[4,264,128]{2,1,0:T(8,128)S(1)}, f32[4,264,128]{2,1,0:T(8,128)S(1)}, u32[]{:S(2)}, u32[]{:S(2)}) %collective-permute-start.4) | collective-permute-done | bytes 540704 | tf_op jit(solution)/shard_map/ppermute | solution.py:535
  32.8 1.1 collective-permute-done.9.refs_7_
  33.9 11.6 %collective-permute-done.7.refs_4_ = f32[4,264,128]{2,1,0:T(8,128)S(1)} collective-permute-done((f32[4,264,128]{2,1,0:T(8,128)S(1)}, f32[4,264,128]{2,1,0:T(8,128)S(1)}, u32[]{:S(2)}, u32[]{:S(2)}) %collective-permute-start.7) | collective-permute-done | bytes 540704 | tf_op jit(solution)/shard_map/ppermute | solution.py:536
  45.5 2.0 %left_slots.1 = f32[16,264,128]{2,1,0:T(8,128)} custom-call(s32[3]{0:T(128)S(1)} %pad_add_fusion.ids, s32[64]{0:T(128)S(1)} %copy-done.4, f32[4,264,128]{2,1,0:T(8,128)S(1)} %copy-done.7, f32[4,264,128]{2,1,0:T(8,128)S(1)} %collective-permute-done.refs_1_, f32[4,264,128]{2,1,0:T(8,128)S(1)} %collective-permute-done.4.refs_2_, ...), custom_call_target="tpu_custom_call" | custom-call | flops 15000000512 | bytes 4000000 | tf_op jit(solution)/shard_map/left_slots/pallas_call | solution.py:235
  47.5 3.3 %all-to-all-done.1.slots = f32[16,280,128]{2,1,0:T(8,128)} async-done(((f32[16,280,128]{2,1,0:T(8,128)}), f32[16,280,128]{2,1,0:T(8,128)}, u32[]{:S(2)}, u32[]{:S(2)}) %all-to-all-start.1) | async-done | bytes 2293792 | tf_op jit(solution)/shard_map/all_to_all | solution.py:542
  50.8 3.7 %all-to-all-start = ((f32[16,264,128]{2,1,0:T(8,128)}), f32[16,264,128]{2,1,0:T(8,128)S(1)}, u32[]{:S(2)}, u32[]{:S(2)}) async-start(f32[16,264,128]{2,1,0:T(8,128)} %left_slots.1), calls=%async_computation | async-start | bytes 4325376 | tf_op jit(solution)/shard_map/all_to_all | solution.py:549
  55.5 2.9 %collective-permute-start.10 = (f32[16,16,128]{2,1,0:T(8,128)S(1)}, f32[16,16,128]{2,1,0:T(8,128)S(1)}, u32[]{:S(2)}, u32[]{:S(2)}) collective-permute-start(f32[16,16,128]{2,1,0:T(8,128)S(1)} %slice.8), channel_id=1, source_target_pairs={{0,16},{16,0},{1,17},{17,1},{2,18},{18,2},{3,19},{19,3},{4,20},{20... | collective-permute-start | bytes 393224 | tf_op jit(solution)/shard_map/ppermute | solution.py:544
  59.4 5.3 %first_vector.1 = (bf16[4096,256]{1,0:T(8,128)(2,1)S(1)}, bf16[4096,256]{1,0:T(8,128)(2,1)S(1)}, bf16[256,4096]{1,0:T(8,128)(2,1)S(1)}, bf16[256,4096]{1,0:T(8,1...) custom-call(s32[3]{0:T(128)S(1)} %pad_add_fusion.ids, s32[8]{0:T(128)S(1)} %copy-done.3, ...), custom_call_target="tpu_custom_call" | custom-call | flops 1700000000 | bytes 12000000 | tf_op jit(solution)/shard_map/first_vector/pallas_call | solution.py:295
  64.7 1.3 %copy-done = bf16[256,4096]{1,0:T(8,128)(2,1)} copy-done((bf16[256,4096]{1,0:T(8,128)(2,1)}, bf16[256,4096]{1,0:T(8,128)(2,1)S(1)}, u32[]{:S(2)}) %copy-start) | copy-done | bytes 2097176
  66.1 1.4 %copy-done.1 = bf16[256,4096]{1,0:T(8,128)(2,1)} copy-done((bf16[256,4096]{1,0:T(8,128)(2,1)}, bf16[256,4096]{1,0:T(8,128)(2,1)S(1)}, u32[]{:S(2)}) %copy-start.1) | copy-done | bytes 2097176
  67.4 1.4 %copy-done.8 = bf16[4096,256]{1,0:T(8,128)(2,1)} copy-done((bf16[4096,256]{1,0:T(8,128)(2,1)}, bf16[4096,256]{1,0:T(8,128)(2,1)S(1)}, u32[]{:S(2)}) %copy-start.8) | copy-done | bytes 2097176
  68.8 1.3 %copy-done.10 = bf16[4096,256]{1,0:T(8,128)(2,1)} copy-done((bf16[4096,256]{1,0:T(8,128)(2,1)}, bf16[4096,256]{1,0:T(8,128)(2,1)S(1)}, u32[]{:S(2)}) %copy-start.10) | copy-done | bytes 2097176
  70.2 10.3 %all-to-all-done.arrived = f32[16,264,128]{2,1,0:T(8,128)S(1)} async-done(((f32[16,264,128]{2,1,0:T(8,128)}), f32[16,264,128]{2,1,0:T(8,128)S(1)}, u32[]{:S(2)}, u32[]{:S(2)}) %all-to-all-start) | async-done | bytes 2162720 | tf_op jit(solution)/shard_map/all_to_all | solution.py:549
  80.5 4.2 %image_one.1 = (bf16[4096,256]{1,0:T(8,128)(2,1)S(1)}, bf16[4096,256]{1,0:T(8,128)(2,1)S(1)}, f32[256,256]{1,0:T(8,128)S(1)}) custom-call(f32[16,264,128]{2,1,0:T(8,128)S(1)} %all-to-all-done.arrived, bf16[256,4096]{1,0:T(8,128)(2,1)} %copy-done, bf16[256,4096]{1,0:T(8,128)(2,1)} %copy-done.1), custom_call_target="tpu_custom_call" | custom-call | flops 1700000000 | bytes 10000000 | tf_op jit(solution)/shard_map/image_one/pallas_call | solution.py:335
  84.8 5.7 %collective-permute-start.11 = (f32[256,256]{1,0:T(8,128)S(1)}, f32[256,256]{1,0:T(8,128)S(1)}, u32[]{:S(2)}, u32[]{:S(2)}) collective-permute-start(f32[256,256]{1,0:T(8,128)S(1)} %get-tuple-element.34.part_a), channel_id=1, source_target_pairs={{0,16},{16,0},{1,17},{17,1},{2,18},{18,2},{3,19},{19,3},{4,20},{20... | collective-permute-start | bytes 786440 | tf_op jit(solution)/shard_map/ppermute | solution.py:552
  90.5 1.2 collective-permute-done.11.part_b
  91.7 4.7 %image_two.1 = (f32[256,256]{1,0:T(8,128)S(1)}, f32[256,256]{1,0:T(8,128)S(1)}, f32[8,128]{1,0:T(8,128)S(1)}) custom-call(s32[3]{0:T(128)S(1)} %pad_add_fusion.ids, s32[8]{0:T(128)S(1)} %copy-done.3, s32[8]{0:T(128)S(1)} %collective-permute-done.1.rsector_other, s32[64]{0:T(128)S(1)} %copy-done.4, s32[32]{0:T(128)S(1)} %copy-done.5, s32[8]{0:T(128)S(1)} %copy-done.6, ...), custom_call_target="tpu_custom_call" | custom-call | flops 3300000000 | bytes 9000000 | tf_op jit(solution)/shard_map/image_two/pallas_call | solution.py:387
  96.8 1.2 collective-permute-done.12.part_b
  98.0 5.6 %image_three.1 = f32[16,40,128]{2,1,0:T(8,128)} custom-call(s32[3]{0:T(128)S(1)} %pad_add_fusion.ids, s32[8]{0:T(128)S(1)} %copy-done.3, s32[8]{0:T(128)S(1)} %collective-permute-done.1.rsector_other, s32[64]{0:T(128)S(1)} %copy-done.4, s32[32]{0:T(128)S(1)} %copy-done.5, s32[8]{0:T(128)S(1)} %copy-done.6, f32[256,256]{1,0:T(8,128)S(1)} %get-tuple-element.41.part_a, ...), custom_call_target="tpu_custom_call" | custom-call | flops 3300000000 | bytes 9000000 | tf_op jit(solution)/shard_map/image_three/pallas_call | solution.py:423
  103.6 3.5 %all-to-all-start.2 = ((f32[16,40,128]{2,1,0:T(8,128)}), f32[16,40,128]{2,1,0:T(8,128)S(1)}, u32[]{:S(2)}, u32[]{:S(2)}) async-start(f32[16,40,128]{2,1,0:T(8,128)} %image_three.1), calls=%async_computation.2 | async-start | bytes 655360 | tf_op jit(solution)/shard_map/all_to_all | solution.py:555
  107.2 7.9 %all-to-all-done.2.got = f32[16,40,128]{2,1,0:T(8,128)S(1)} async-done(((f32[16,40,128]{2,1,0:T(8,128)}), f32[16,40,128]{2,1,0:T(8,128)S(1)}, u32[]{:S(2)}, u32[]{:S(2)}) %all-to-all-start.2) | async-done | bytes 327712 | tf_op jit(solution)/shard_map/all_to_all | solution.py:555
  115.1 3.1 %collective-permute-start.15 = (f32[16,128]{1,0:T(8,128)S(1)}, f32[16,128]{1,0:T(8,128)S(1)}, u32[]{:S(2)}, u32[]{:S(2)}) collective-permute-start(f32[16,128]{1,0:T(8,128)S(1)} %bitcast.10), channel_id=1, source_target_pairs={{0,96},{32,0},{64,32},{96,64},{1,97},{33,1},{65,33},{97,65},{2,98}... | collective-permute-start | bytes 24584 | tf_op jit(solution)/shard_map/ppermute | solution.py:558
  118.9 2.8 %collective-permute-start.17 = (f32[8,32,128]{2,1,0:T(8,128)S(1)}, f32[8,32,128]{2,1,0:T(8,128)S(1)}, u32[]{:S(2)}, u32[]{:S(2)}) collective-permute-start(f32[8,32,128]{2,1,0:T(8,128)S(1)} %constant_dynamic-slice_fusion), channel_id=1, source_target_pairs={{0,16},{16,0},{1,17},{17,1},{2,18},{18,2},{3,19},{19,3},{4,20},{20... | collective-permute-start | bytes 393224 | tf_op jit(solution)/shard_map/ppermute | solution.py:561
  122.3 3.6 %collective-permute-start.16 = (f32[64,128]{1,0:T(8,128)S(1)}, f32[64,128]{1,0:T(8,128)S(1)}, u32[]{:S(2)}, u32[]{:S(2)}) collective-permute-start(f32[64,128]{1,0:T(8,128)S(1)} %pad_maximum_fusion.own_stats), channel_id=1, source_target_pairs={{0,16},{16,0},{1,17},{17,1},{2,18},{18,2},{3,19},{19,3},{4,20},{20... | collective-permute-start | bytes 98312 | tf_op jit(solution)/shard_map/ppermute | solution.py:563
  126.7 2.2 %finish.1 = (f32[8,16,256]{2,1,0:T(8,128)}, f32[1,1]{1,0:T(1,128)}) custom-call(s32[3]{0:T(128)S(1)} %pad_add_fusion.ids, s32[64]{0:T(128)S(1)} %copy-done.4, s32[8]{0:T(128)S(1)} %copy-done.3, s32[32]{0:T(128)S(1)} %copy-done.5, s32[8]{0:T(128)S(1)} %copy-done.6, f32[64,128]{1,0:T(8,128)S(1)} %pad_maximum_fusion.own_stats, ...), custom_call_target="tpu_custom_call" | custom-call | tf_op jit(solution)/shard_map/finish/pallas_call | solution.py:504
  (50 shorter events, 6.8 us)
Async XLA Ops:
  0.7 4.5 %copy-start.2 = (f32[8,256,16]{1,2,0:T(8,128)S(1)}, f32[8,256,16]{1,2,0:T(8,128)}, u32[]{:S(2)}) copy-start(f32[8,256,16]{1,2,0:T(8,128)} %param.8) | copy-start | bytes 393220
  0.7 4.6 %copy-start.3 = (s32[8]{0:T(128)S(1)}, s32[8]{0:T(128)}, u32[]{:S(2)}) copy-start(s32[8]{0:T(128)} %rsector.9) | copy-start | bytes 100
  0.7 5.0 %copy-start.12 = (s32[8,2]{0,1:T(2,128)S(1)}, s32[8,2]{0,1:T(2,128)}, u32[]{:S(2)}) copy-start(s32[8,2]{0,1:T(2,128)} %param.13) | copy-start | bytes 196
  3.7 3.6 %collective-permute-start = (f32[4,264,128]{2,1,0:T(8,128)}, f32[4,264,128]{2,1,0:T(8,128)S(1)}, u32[]{:S(2)}, u32[]{:S(2)}) collective-permute-start(f32[4,264,128]{2,1,0:T(8,128)} %get-tuple-element.24), channel_id=1, source_target_pairs={{0,16},{16,0},{1,17},{17,1},{2,18},{18,2},{3,19},{19,3},{4,20},{20... | collective-permute-start | bytes 1622024 | tf_op jit(solution)/shard_map/ppermute | solution.py:530
  5.2 2.1 %collective-permute-start.3 = (f32[8,16,256]{2,1,0:T(8,128)S(1)}, f32[8,16,256]{2,1,0:T(8,128)S(1)}, u32[]{:S(2)}, u32[]{:S(2)}) collective-permute-start(f32[8,16,256]{2,1,0:T(8,128)S(1)} %bitcast.7), channel_id=1, source_target_pairs={{0,16},{16,0},{1,17},{17,1},{2,18},{18,2},{3,19},{19,3},{4,20},{20... | collective-permute-start | bytes 393224 | tf_op jit(solution)/shard_map/ppermute | solution.py:527
  5.3 2.0 %collective-permute-start.1 = (s32[8]{0:T(128)S(1)}, s32[8]{0:T(128)S(1)}, u32[]{:S(2)}, u32[]{:S(2)}) collective-permute-start(s32[8]{0:T(128)S(1)} %copy-done.3), channel_id=1, source_target_pairs={{0,16},{16,0},{1,17},{17,1},{2,18},{18,2},{3,19},{19,3},{4,20},{20... | collective-permute-start | bytes 104 | tf_op jit(solution)/shard_map/ppermute | solution.py:525
  5.8 1.5 %collective-permute-start.2 = (s32[8,2]{1,0:T(8,128)S(1)}, s32[8,2]{1,0:T(8,128)S(1)}, u32[]{:S(2)}, u32[]{:S(2)}) collective-permute-start(s32[8,2]{1,0:T(8,128)S(1)} %copy.10.on), channel_id=1, source_target_pairs={{0,16},{16,0},{1,17},{17,1},{2,18},{18,2},{3,19},{19,3},{4,20},{20... | collective-permute-start | bytes 200 | tf_op jit(solution)/shard_map/ppermute | solution.py:526
  5.9 15.4 %collective-permute-start.6 = (f32[4,264,128]{2,1,0:T(8,128)}, f32[4,264,128]{2,1,0:T(8,128)S(1)}, u32[]{:S(2)}, u32[]{:S(2)}) collective-permute-start(f32[4,264,128]{2,1,0:T(8,128)} %get-tuple-element.26.refs_0_), channel_id=1, source_target_pairs={{0,32},{32,64},{64,96},{96,0},{1,33},{33,65},{65,97},{97,1},{2,34}... | collective-permute-start | bytes 1622024 | tf_op jit(solution)/shard_map/ppermute | solution.py:534
  7.3 14.1 %collective-permute-start.5 = (f32[4,264,128]{2,1,0:T(8,128)S(1)}, f32[4,264,128]{2,1,0:T(8,128)S(1)}, u32[]{:S(2)}, u32[]{:S(2)}) collective-permute-start(f32[4,264,128]{2,1,0:T(8,128)S(1)} %collective-permute-done.refs_1_), channel_id=1, source_target_pairs={{0,96},{32,0},{64,32},{96,64},{1,97},{33,1},{65,33},{97,65},{2,98}... | collective-permute-start | bytes 1622024 | tf_op jit(solution)/shard_map/ppermute | solution.py:535
  12.0 7.8 %copy-start.7 = (f32[4,264,128]{2,1,0:T(8,128)S(1)}, f32[4,264,128]{2,1,0:T(8,128)}, u32[]{:S(2)}) copy-start(f32[4,264,128]{2,1,0:T(8,128)} %get-tuple-element.26.refs_0_) | copy-start | bytes 1622020
  12.0 33.5 %copy-start.4 = (s32[64]{0:T(128)S(1)}, s32[64]{0:T(128)}, u32[]{:S(2)}) copy-start(s32[64]{0:T(128)} %sector.7) | copy-start | bytes 772
  12.0 38.8 %all-to-all-start.1 = ((f32[16,280,128]{2,1,0:T(8,128)}), f32[16,280,128]{2,1,0:T(8,128)}, u32[]{:S(2)}, u32[]{:S(2)}) async-start(f32[16,280,128]{2,1,0:T(8,128)} %right_slots.1), calls=%async_computation.1 | async-start | bytes 4587520 | tf_op jit(solution)/shard_map/all_to_all | solution.py:542
  19.8 13.0 %collective-permute-start.4 = (f32[4,264,128]{2,1,0:T(8,128)S(1)}, f32[4,264,128]{2,1,0:T(8,128)S(1)}, u32[]{:S(2)}, u32[]{:S(2)}) collective-permute-start(f32[4,264,128]{2,1,0:T(8,128)S(1)} %copy-done.7), channel_id=1, source_target_pairs={{0,96},{32,0},{64,32},{96,64},{1,97},{33,1},{65,33},{97,65},{2,98}... | collective-permute-start | bytes 1622024 | tf_op jit(solution)/shard_map/ppermute | solution.py:535
  20.3 13.6 %collective-permute-start.9 = (f32[4,264,128]{2,1,0:T(8,128)S(1)}, f32[4,264,128]{2,1,0:T(8,128)S(1)}, u32[]{:S(2)}, u32[]{:S(2)}) collective-permute-start(f32[4,264,128]{2,1,0:T(8,128)S(1)} %collective-permute-done.refs_1_), channel_id=1, source_target_pairs={{0,32},{32,64},{64,96},{96,0},{1,33},{33,65},{65,97},{97,1},{2,34}... | collective-permute-start | bytes 1622024 | tf_op jit(solution)/shard_map/ppermute | solution.py:534
  21.3 24.2 %collective-permute-start.7 = (f32[4,264,128]{2,1,0:T(8,128)S(1)}, f32[4,264,128]{2,1,0:T(8,128)S(1)}, u32[]{:S(2)}, u32[]{:S(2)}) collective-permute-start(f32[4,264,128]{2,1,0:T(8,128)S(1)} %collective-permute-done.6.refs_6_), channel_id=1, source_target_pairs={{0,32},{32,64},{64,96},{96,0},{1,33},{33,65},{65,97},{97,1},{2,34}... | collective-permute-start | bytes 1622024 | tf_op jit(solution)/shard_map/ppermute | solution.py:536
  21.4 24.1 %collective-permute-start.8 = (f32[4,264,128]{2,1,0:T(8,128)S(1)}, f32[4,264,128]{2,1,0:T(8,128)S(1)}, u32[]{:S(2)}, u32[]{:S(2)}) collective-permute-start(f32[4,264,128]{2,1,0:T(8,128)S(1)} %collective-permute-done.5.refs_3_), channel_id=1, source_target_pairs={{0,96},{32,0},{64,32},{96,64},{1,97},{33,1},{65,33},{97,65},{2,98}... | collective-permute-start | bytes 1622024 | tf_op jit(solution)/shard_map/ppermute | solution.py:536
  47.5 11.9 %copy-start.5 = (s32[32]{0:T(128)S(1)}, s32[32]{0:T(128)}, u32[]{:S(2)}) copy-start(s32[32]{0:T(128)} %lsize.7) | copy-start | bytes 388
  47.5 11.9 %copy-start.6 = (s32[8]{0:T(128)S(1)}, s32[8]{0:T(128)}, u32[]{:S(2)}) copy-start(s32[8]{0:T(128)} %rsize.7) | copy-start | bytes 100
  50.8 29.7 %all-to-all-start = ((f32[16,264,128]{2,1,0:T(8,128)}), f32[16,264,128]{2,1,0:T(8,128)S(1)}, u32[]{:S(2)}, u32[]{:S(2)}) async-start(f32[16,264,128]{2,1,0:T(8,128)} %left_slots.1), calls=%async_computation | async-start | bytes 4325376 | tf_op jit(solution)/shard_map/all_to_all | solution.py:549
  55.5 3.9 %collective-permute-start.10 = (f32[16,16,128]{2,1,0:T(8,128)S(1)}, f32[16,16,128]{2,1,0:T(8,128)S(1)}, u32[]{:S(2)}, u32[]{:S(2)}) collective-permute-start(f32[16,16,128]{2,1,0:T(8,128)S(1)} %slice.8), channel_id=1, source_target_pairs={{0,16},{16,0},{1,17},{17,1},{2,18},{18,2},{3,19},{19,3},{4,20},{20... | collective-permute-start | bytes 393224 | tf_op jit(solution)/shard_map/ppermute | solution.py:544
  66.1 1.4 %copy-start.1 = (bf16[256,4096]{1,0:T(8,128)(2,1)}, bf16[256,4096]{1,0:T(8,128)(2,1)S(1)}, u32[]{:S(2)}) copy-start(bf16[256,4096]{1,0:T(8,128)(2,1)S(1)} %get-tuple-element.33.m_lo) | copy-start | bytes 6291460
  67.4 1.4 %copy-start.8 = (bf16[4096,256]{1,0:T(8,128)(2,1)}, bf16[4096,256]{1,0:T(8,128)(2,1)S(1)}, u32[]{:S(2)}) copy-start(bf16[4096,256]{1,0:T(8,128)(2,1)S(1)} %get-tuple-element.37.r_hi) | copy-start | bytes 6291460
  80.5 11.2 %copy-start.9 = (bf16[4096,256]{1,0:T(8,128)(2,1)S(1)}, bf16[4096,256]{1,0:T(8,128)(2,1)}, u32[]{:S(2)}) copy-start(bf16[4096,256]{1,0:T(8,128)(2,1)} %copy-done.8) | copy-start | bytes 6291460
  80.5 11.2 %copy-start.11 = (bf16[4096,256]{1,0:T(8,128)(2,1)S(1)}, bf16[4096,256]{1,0:T(8,128)(2,1)}, u32[]{:S(2)}) copy-start(bf16[4096,256]{1,0:T(8,128)(2,1)} %copy-done.10) | copy-start | bytes 6291460
  84.8 6.9 %collective-permute-start.11 = (f32[256,256]{1,0:T(8,128)S(1)}, f32[256,256]{1,0:T(8,128)S(1)}, u32[]{:S(2)}, u32[]{:S(2)}) collective-permute-start(f32[256,256]{1,0:T(8,128)S(1)} %get-tuple-element.34.part_a), channel_id=1, source_target_pairs={{0,16},{16,0},{1,17},{17,1},{2,18},{18,2},{3,19},{19,3},{4,20},{20... | collective-permute-start | bytes 786440 | tf_op jit(solution)/shard_map/ppermute | solution.py:552
  96.4 1.6 %collective-permute-start.12 = (f32[256,256]{1,0:T(8,128)S(1)}, f32[256,256]{1,0:T(8,128)S(1)}, u32[]{:S(2)}, u32[]{:S(2)}) collective-permute-start(f32[256,256]{1,0:T(8,128)S(1)} %get-tuple-element.41.part_a), channel_id=1, source_target_pairs={{0,16},{16,0},{1,17},{17,1},{2,18},{18,2},{3,19},{19,3},{4,20},{20... | collective-permute-start | bytes 786440 | tf_op jit(solution)/shard_map/ppermute | solution.py:553
  103.6 11.5 %all-to-all-start.2 = ((f32[16,40,128]{2,1,0:T(8,128)}), f32[16,40,128]{2,1,0:T(8,128)S(1)}, u32[]{:S(2)}, u32[]{:S(2)}) async-start(f32[16,40,128]{2,1,0:T(8,128)} %image_three.1), calls=%async_computation.2 | async-start | bytes 655360 | tf_op jit(solution)/shard_map/all_to_all | solution.py:555
  115.1 6.6 %collective-permute-start.15 = (f32[16,128]{1,0:T(8,128)S(1)}, f32[16,128]{1,0:T(8,128)S(1)}, u32[]{:S(2)}, u32[]{:S(2)}) collective-permute-start(f32[16,128]{1,0:T(8,128)S(1)} %bitcast.10), channel_id=1, source_target_pairs={{0,96},{32,0},{64,32},{96,64},{1,97},{33,1},{65,33},{97,65},{2,98}... | collective-permute-start | bytes 24584 | tf_op jit(solution)/shard_map/ppermute | solution.py:558
  118.2 4.0 %collective-permute-start.14 = (f32[16,128]{1,0:T(8,128)S(1)}, f32[16,128]{1,0:T(8,128)S(1)}, u32[]{:S(2)}, u32[]{:S(2)}) collective-permute-start(f32[16,128]{1,0:T(8,128)S(1)} %bitcast.11), channel_id=1, source_target_pairs={{0,64},{32,96},{64,0},{96,32},{1,65},{33,97},{65,1},{97,33},{2,66}... | collective-permute-start | bytes 24584 | tf_op jit(solution)/shard_map/ppermute | solution.py:558
  118.2 4.0 %collective-permute-start.13 = (f32[16,128]{1,0:T(8,128)S(1)}, f32[16,128]{1,0:T(8,128)S(1)}, u32[]{:S(2)}, u32[]{:S(2)}) collective-permute-start(f32[16,128]{1,0:T(8,128)S(1)} %bitcast.12), channel_id=1, source_target_pairs={{0,32},{32,64},{64,96},{96,0},{1,33},{33,65},{65,97},{97,1},{2,34}... | collective-permute-start | bytes 24584 | tf_op jit(solution)/shard_map/ppermute | solution.py:558
  118.9 7.8 %collective-permute-start.17 = (f32[8,32,128]{2,1,0:T(8,128)S(1)}, f32[8,32,128]{2,1,0:T(8,128)S(1)}, u32[]{:S(2)}, u32[]{:S(2)}) collective-permute-start(f32[8,32,128]{2,1,0:T(8,128)S(1)} %constant_dynamic-slice_fusion), channel_id=1, source_target_pairs={{0,16},{16,0},{1,17},{17,1},{2,18},{18,2},{3,19},{19,3},{4,20},{20... | collective-permute-start | bytes 393224 | tf_op jit(solution)/shard_map/ppermute | solution.py:561
  122.3 4.5 %collective-permute-start.16 = (f32[64,128]{1,0:T(8,128)S(1)}, f32[64,128]{1,0:T(8,128)S(1)}, u32[]{:S(2)}, u32[]{:S(2)}) collective-permute-start(f32[64,128]{1,0:T(8,128)S(1)} %pad_maximum_fusion.own_stats), channel_id=1, source_target_pairs={{0,16},{16,0},{1,17},{17,1},{2,18},{18,2},{3,19},{19,3},{4,20},{20... | collective-permute-start | bytes 98312 | tf_op jit(solution)/shard_map/ppermute | solution.py:563
  (2 other events, 2.7 us)

commit v14 on v13

--- a/solution.py
+++ b/solution.py
@@ -7,6 +7,7 @@
 
 ITERS = 2
 LEFT_FLOPS = 15_000_000_000
+NEAR_FLOPS = 1_000_000_000
 TILE = 256
 HALF = 128
 TERMS = 16
@@ -199,49 +200,79 @@
     )(ids, rsector, rsector_other, on, on_other, thin, thin_other, folded)
 
 
-def left_slots_body(ids, left_sector, *refs):
-    mine, theirs = refs[:2]
-    above, far, below = refs[2:4], refs[4:6], refs[6:8]
-    out, sem = refs[8:]
-
-    def store(src, slot):
-        return pltpu.make_async_copy(src, out.at[slot], sem)
-
+def where_from(ids, left_sector, slot):
+    sector = left_sector[ids[0] * 16 + slot]
+    home = sector // 4
+    return sector % 4, (home // 2 - ids[0] + 4) % 4, home % 2 == ids[1]
+
+
+def send_tiles(out, sem, cases_of):
     def start(slot, carry):
-        sector = left_sector[ids[0] * 16 + slot]
-        home = sector // 4
-        tile = sector % 4
-        away = (home // 2 - ids[0] + 4) % 4
-        same = home % 2 == ids[1]
-        cases = [(same, mine, tile), (~same, theirs, tile)]
-        cases = [(case & (away == 0), src, at) for case, src, at in cases]
-        for n, half in ((0, same), (1, ~same)):
-            cases.append((half & (away == 1), above[n], tile))
-            cases.append((half & (away == 2), far[n], tile))
-            cases.append((half & (away == 3), below[n], tile))
-        for case, src, at in cases:
+        for case, src, tile in cases_of(slot):
 
             @pl.when(case)
             def _():
-                store(src.at[at], slot).start()
+                pltpu.make_async_copy(src.at[tile], out.at[slot], sem).start()
 
         return carry
 
+    def finish(slot, carry):
+        for case, src, tile in cases_of(slot):
+
+            @pl.when(case)
+            def _():
+                pltpu.make_async_copy(src.at[tile], out.at[slot], sem).wait()
+
+        return carry
+
     lax.fori_loop(0, TERMS, start, 0)
-    pltpu.make_async_copy(out, out, sem).wait()
-
-
-def left_slots(ids, left_sector, pieces):
-    return pl.pallas_call(
-        left_slots_body,
-        in_specs=[smem(), smem()] + [vmem()] * 8,
+    lax.fori_loop(0, TERMS, finish, 0)
+
+
+def near_slots_body(ids, left_sector, mine, theirs, above_a, above_b, below_a, below_b, out, sem):
+    def cases_of(slot):
+        tile, away, same = where_from(ids, left_sector, slot)
+        by_away = {0: (mine, theirs), 1: (above_a, above_b), 3: (below_a, below_b)}
+        cases = []
+        for planes, (first, second) in by_away.items():
+            cases.append((same & (away == planes), first, tile))
+            cases.append((~same & (away == planes), second, tile))
+        return cases
+
+    send_tiles(out, sem, cases_of)
+
+
+def far_slots_body(ids, left_sector, far_a, far_b, near, out, sem):
+    def cases_of(slot):
+        tile, away, same = where_from(ids, left_sector, slot)
+        return [(same & (away == 2), far_a, tile), (~same & (away == 2), far_b, tile)]
+
+    send_tiles(out, sem, cases_of)
+
+
+def left_slots(ids, left_sector, near, far):
+    slots = pltpu.HBM((TERMS, FOLDED, HALF), f32)
+    ready = pl.pallas_call(
+        near_slots_body,
+        in_specs=[smem(), smem()] + [vmem()] * 6,
         out_specs=hbm(),
-        out_shape=pltpu.HBM((TERMS, FOLDED, HALF), f32),
+        out_shape=slots,
         scratch_shapes=[pltpu.SemaphoreType.DMA(())],
         compiler_params=params(8),
+        cost_estimate=cost(NEAR_FLOPS, 4_000_000),
+        name="near_slots",
+    )(ids, left_sector, *near)
+    return pl.pallas_call(
+        far_slots_body,
+        in_specs=[smem(), smem()] + [vmem()] * 2 + [hbm()],
+        out_specs=hbm(),
+        out_shape=slots,
+        scratch_shapes=[pltpu.SemaphoreType.DMA(())],
+        input_output_aliases={4: 0},
+        compiler_params=params(4),
         cost_estimate=cost(LEFT_FLOPS, 4_000_000),
-        name="left_slots",
-    )(ids, left_sector, *pieces)
+        name="far_slots",
+    )(ids, left_sector, *far, in_hbm(ready))
 
 
 def live_sizes(ids, rsector, rsector_other, left_sector, left_size, right_size):
@@ -544,8 +575,7 @@
     halves = lax.ppermute(arrived[:, :THIN, :], "c", SWAP)
     r_hi, r_lo, m_hi, m_lo, q1, stats = first_vector(scalars, halves, arrived)
 
-    pieces = [mine, theirs] + above + far + below
-    left_sent = left_slots(ids, left_sector, pieces)
+    left_sent = left_slots(ids, left_sector, [mine, theirs] + above + below, far)
     left_arrived = lax.all_to_all(left_sent, COL, 0, 0, tiled=True)
     l_hi, l_lo, part = image_one(left_arrived, m_hi, m_lo)
     stacks = (r_hi, r_lo, l_hi, l_lo)

time: 129 us -> 129 us (level)
  waiting for transfers between devices: 47.2 us -> 45.8 us
  Pallas kernels: 29.2 us -> 30.6 us
    ppermute x2, waiting for transfers between devices: 11.6 us -> 9.75 us  [local(): far = [lax.ppermute(below[0], 'y', UP), lax.ppermute(above[1], 'y', DOWN)]]
    pallas_call x1 -> x2, Pallas kernels: 1.96 us -> 3.36 us  [the longest x1 1.83 us: left_slots(): pl.pallas_call(near_slots_body, in_specs=[smem(), smem()] + [vmem()] * 6,...]
  transfers between devices with their start and end apart: 21 -> 21, of which waited for: 11 -> 11; matrix products, arithmetic and copies ran while one was open for 1% -> 1% of each run, Pallas kernels for 7% -> 8%
where the time goes in v14:
time: 129 us
  waiting for transfers between devices  45.8 us (36%)
  starting transfers between devices  44.8 us (35%)
  Pallas kernels  30.6 us (24%)
  local copies, waits for them, and re-layouts  6.49 us (5%)
    all_to_all x1, waiting for transfers between devices, local(): left_arrived = lax.all_to_all(left_sent, COL, 0, 0, tiled=True)  10.3 us
    ppermute x2, waiting for transfers between devices, local(): far = [lax.ppermute(below[0], 'y', UP), lax.ppermute(above[1], 'y', DOWN)]  9.75 us
    ppermute x2, waiting for transfers between devices, local(): above = [lax.ppermute(x, 'y', DOWN) for x in (mine, theirs)]  8.28 us
    all_to_all x1, waiting for transfers between devices, local(): got = lax.all_to_all(sent, COL, 0, 0, tiled=True)  7.9 us
    all_to_all x1, starting transfers between devices, local(): arrived = lax.all_to_all(slots, COL, 0, 0, tiled=True)  7.79 us
    ppermute x2, starting transfers between devices, local(): lax.ppermute(part, 'c', SWAP)  6.2 us
    pallas_call x1, Pallas kernels, image_three(): pl.pallas_call(image_three_body, in_specs=[smem()] * 6 + [vmem()] * 9, ou...  5.64 us
    unnamed x27, local copies, waits for them, and re-layouts  5.55 us
  transfers between devices with their start and end apart: 21, of which 11 were waited for; matrix products, arithmetic and copies ran while one was open for 1% of the time, Pallas kernels for 8%

profile of v14, /device:TPU:1, one launch (start us, length us, event | category | flops | bytes accessed | tf_op | source)
XLA Modules:
  0.0 128.7 jit_solution(7218331440287049509)
XLA Ops:
  0.7 3.0 %fold.1 = (f32[4,264,128]{2,1,0:T(8,128)}, f32[4,264,128]{2,1,0:T(8,128)}, f32[9,264,128]{2,1,0:T(8,128)S(1)}) custom-call(s32[3]{0:T(128)S(1)} %pad_add_fusion.ids, f32[4,2,256,256]{3,2,1,0:T(8,128)} %left_env.1, f32[8,2,256,256]{3,2,1,0:T(8,128)} %right_env.1), custom_call_target="tpu_custom_call" | custom-call | flops 1000000 | bytes 6000000 | tf_op jit(solution)/shard_map/fold/pallas_call | solution.py:146
  3.7 1.5 %collective-permute-start = (f32[4,264,128]{2,1,0:T(8,128)}, f32[4,264,128]{2,1,0:T(8,128)S(1)}, u32[]{:S(2)}, u32[]{:S(2)}) collective-permute-start(f32[4,264,128]{2,1,0:T(8,128)} %get-tuple-element.24), channel_id=1, source_target_pairs={{0,16},{16,0},{1,17},{17,1},{2,18},{18,2},{3,19},{19,3},{4,20},{20... | collective-permute-start | bytes 1622024 | tf_op jit(solution)/shard_map/ppermute | solution.py:561
  5.9 1.4 %collective-permute-start.4 = (f32[4,264,128]{2,1,0:T(8,128)}, f32[4,264,128]{2,1,0:T(8,128)S(1)}, u32[]{:S(2)}, u32[]{:S(2)}) collective-permute-start(f32[4,264,128]{2,1,0:T(8,128)} %get-tuple-element.26.mine), channel_id=1, source_target_pairs={{0,32},{32,64},{64,96},{96,0},{1,33},{33,65},{65,97},{97,1},{2,34}... | collective-permute-start | bytes 1622024 | tf_op jit(solution)/shard_map/ppermute | solution.py:565
  7.3 2.5 %collective-permute-start.6 = (f32[4,264,128]{2,1,0:T(8,128)S(1)}, f32[4,264,128]{2,1,0:T(8,128)S(1)}, u32[]{:S(2)}, u32[]{:S(2)}) collective-permute-start(f32[4,264,128]{2,1,0:T(8,128)S(1)} %collective-permute-done.theirs), channel_id=1, source_target_pairs={{0,96},{32,0},{64,32},{96,64},{1,97},{33,1},{65,33},{97,65},{2,98}... | collective-permute-start | bytes 1622024 | tf_op jit(solution)/shard_map/ppermute | solution.py:566
  9.9 2.1 %right_slots.1 = f32[16,280,128]{2,1,0:T(8,128)} custom-call(s32[3]{0:T(128)S(1)} %pad_add_fusion.ids, s32[8]{0:T(128)S(1)} %copy-done.5, s32[8]{0:T(128)S(1)} %collective-permute-done.1.rsector_other, s32[8,2]{1,0:T(8,128)S(1)} %copy.11.on, s32[8,2]{1,0:T(8,128)S(1)} %collective-permute-done.2.on_other, f32[8,16,256]{2,1,0:T(8,128)S(1)} %bitcast.8, ...), custom_call_target="tpu_custom_call" | custom-call | flops 4000000 | bytes 6000000 | tf_op jit(solution)/shard_map/right_slots/pallas_call | solution.py:188
  12.0 7.8 %all-to-all-start.1 = ((f32[16,280,128]{2,1,0:T(8,128)}), f32[16,280,128]{2,1,0:T(8,128)}, u32[]{:S(2)}, u32[]{:S(2)}) async-start(f32[16,280,128]{2,1,0:T(8,128)} %right_slots.1), calls=%async_computation.1 | async-start | bytes 4587520 | tf_op jit(solution)/shard_map/all_to_all | solution.py:573
  21.4 3.2 %collective-permute-start.7 = (f32[4,264,128]{2,1,0:T(8,128)S(1)}, f32[4,264,128]{2,1,0:T(8,128)S(1)}, u32[]{:S(2)}, u32[]{:S(2)}) collective-permute-start(f32[4,264,128]{2,1,0:T(8,128)S(1)} %collective-permute-done.6.above_b), channel_id=1, source_target_pairs={{0,96},{32,0},{64,32},{96,64},{1,97},{33,1},{65,33},{97,65},{2,98}... | collective-permute-start | bytes 1622024 | tf_op jit(solution)/shard_map/ppermute | solution.py:567
  24.6 8.3 %collective-permute-done.8.above_a = f32[4,264,128]{2,1,0:T(8,128)S(1)} collective-permute-done((f32[4,264,128]{2,1,0:T(8,128)S(1)}, f32[4,264,128]{2,1,0:T(8,128)S(1)}, u32[]{:S(2)}, u32[]{:S(2)}) %collective-permute-start.8) | collective-permute-done | bytes 540704 | tf_op jit(solution)/shard_map/ppermute | solution.py:566
  33.9 1.8 %near_slots.1.near = f32[16,264,128]{2,1,0:T(8,128)} custom-call(s32[3]{0:T(128)S(1)} %pad_add_fusion.ids, s32[64]{0:T(128)S(1)} %copy-done.4, f32[4,264,128]{2,1,0:T(8,128)S(1)} %copy-done.2, f32[4,264,128]{2,1,0:T(8,128)S(1)} %collective-permute-done.theirs, f32[4,264,128]{2,1,0:T(8,128)S(1)} %collective-permute-done.8.above_a, ...), custom_call_target="tpu_custom_call" | custom-call | flops 1000000000 | bytes 4000000 | tf_op jit(solution)/shard_map/near_slots/pallas_call | solution.py:255
  35.8 9.7 %collective-permute-done.5.far_a = f32[4,264,128]{2,1,0:T(8,128)S(1)} collective-permute-done((f32[4,264,128]{2,1,0:T(8,128)S(1)}, f32[4,264,128]{2,1,0:T(8,128)S(1)}, u32[]{:S(2)}, u32[]{:S(2)}) %collective-permute-start.5) | collective-permute-done | bytes 540704 | tf_op jit(solution)/shard_map/ppermute | solution.py:567
  45.5 1.5 %far_slots.1 = f32[16,264,128]{2,1,0:T(8,128)} custom-call(s32[3]{0:T(128)S(1)} %pad_add_fusion.ids, s32[64]{0:T(128)S(1)} %copy-done.4, f32[4,264,128]{2,1,0:T(8,128)S(1)} %collective-permute-done.5.far_a, f32[4,264,128]{2,1,0:T(8,128)S(1)} %collective-permute-done.7.far_b, f32[16,264,128]{2,1,0:T(8,128)} %near_slots.1.near), custom_call_target="tpu_custom_call", output_to_operand_aliasing={{}: (4, {})} | custom-call | flops 15000000512 | bytes 4000000 | tf_op jit(solution)/shard_map/far_slots/pallas_call | solution.py:265
  47.1 3.7 %all-to-all-done.1.slots = f32[16,280,128]{2,1,0:T(8,128)} async-done(((f32[16,280,128]{2,1,0:T(8,128)}), f32[16,280,128]{2,1,0:T(8,128)}, u32[]{:S(2)}, u32[]{:S(2)}) %all-to-all-start.1) | async-done | bytes 2293792 | tf_op jit(solution)/shard_map/all_to_all | solution.py:573
  50.8 3.7 %all-to-all-start = ((f32[16,264,128]{2,1,0:T(8,128)}), f32[16,264,128]{2,1,0:T(8,128)S(1)}, u32[]{:S(2)}, u32[]{:S(2)}) async-start(f32[16,264,128]{2,1,0:T(8,128)} %far_slots.1), calls=%async_computation | async-start | bytes 4325376 | tf_op jit(solution)/shard_map/all_to_all | solution.py:579
  55.5 2.9 %collective-permute-start.10 = (f32[16,16,128]{2,1,0:T(8,128)S(1)}, f32[16,16,128]{2,1,0:T(8,128)S(1)}, u32[]{:S(2)}, u32[]{:S(2)}) collective-permute-start(f32[16,16,128]{2,1,0:T(8,128)S(1)} %slice.8), channel_id=1, source_target_pairs={{0,16},{16,0},{1,17},{17,1},{2,18},{18,2},{3,19},{19,3},{4,20},{20... | collective-permute-start | bytes 393224 | tf_op jit(solution)/shard_map/ppermute | solution.py:575
  59.4 5.3 %first_vector.1 = (bf16[4096,256]{1,0:T(8,128)(2,1)S(1)}, bf16[4096,256]{1,0:T(8,128)(2,1)S(1)}, bf16[256,4096]{1,0:T(8,128)(2,1)S(1)}, bf16[256,4096]{1,0:T(8,1...) custom-call(s32[3]{0:T(128)S(1)} %pad_add_fusion.ids, s32[8]{0:T(128)S(1)} %copy-done.5, ...), custom_call_target="tpu_custom_call" | custom-call | flops 1700000000 | bytes 12000000 | tf_op jit(solution)/shard_map/first_vector/pallas_call | solution.py:326
  64.7 1.3 %copy-done = bf16[256,4096]{1,0:T(8,128)(2,1)} copy-done((bf16[256,4096]{1,0:T(8,128)(2,1)}, bf16[256,4096]{1,0:T(8,128)(2,1)S(1)}, u32[]{:S(2)}) %copy-start) | copy-done | bytes 2097176
  66.1 1.4 %copy-done.1 = bf16[256,4096]{1,0:T(8,128)(2,1)} copy-done((bf16[256,4096]{1,0:T(8,128)(2,1)}, bf16[256,4096]{1,0:T(8,128)(2,1)S(1)}, u32[]{:S(2)}) %copy-start.1) | copy-done | bytes 2097176
  67.4 1.4 %copy-done.8 = bf16[4096,256]{1,0:T(8,128)(2,1)} copy-done((bf16[4096,256]{1,0:T(8,128)(2,1)}, bf16[4096,256]{1,0:T(8,128)(2,1)S(1)}, u32[]{:S(2)}) %copy-start.8) | copy-done | bytes 2097176
  68.8 1.3 %copy-done.10 = bf16[4096,256]{1,0:T(8,128)(2,1)} copy-done((bf16[4096,256]{1,0:T(8,128)(2,1)}, bf16[4096,256]{1,0:T(8,128)(2,1)S(1)}, u32[]{:S(2)}) %copy-start.10) | copy-done | bytes 2097176
  70.2 10.3 %all-to-all-done.arrived = f32[16,264,128]{2,1,0:T(8,128)S(1)} async-done(((f32[16,264,128]{2,1,0:T(8,128)}), f32[16,264,128]{2,1,0:T(8,128)S(1)}, u32[]{:S(2)}, u32[]{:S(2)}) %all-to-all-start) | async-done | bytes 2162720 | tf_op jit(solution)/shard_map/all_to_all | solution.py:579
  80.5 4.2 %image_one.1 = (bf16[4096,256]{1,0:T(8,128)(2,1)S(1)}, bf16[4096,256]{1,0:T(8,128)(2,1)S(1)}, f32[256,256]{1,0:T(8,128)S(1)}) custom-call(f32[16,264,128]{2,1,0:T(8,128)S(1)} %all-to-all-done.arrived, bf16[256,4096]{1,0:T(8,128)(2,1)} %copy-done, bf16[256,4096]{1,0:T(8,128)(2,1)} %copy-done.1), custom_call_target="tpu_custom_call" | custom-call | flops 1700000000 | bytes 10000000 | tf_op jit(solution)/shard_map/image_one/pallas_call | solution.py:366
  84.8 5.7 %collective-permute-start.11 = (f32[256,256]{1,0:T(8,128)S(1)}, f32[256,256]{1,0:T(8,128)S(1)}, u32[]{:S(2)}, u32[]{:S(2)}) collective-permute-start(f32[256,256]{1,0:T(8,128)S(1)} %get-tuple-element.34.part_a), channel_id=1, source_target_pairs={{0,16},{16,0},{1,17},{17,1},{2,18},{18,2},{3,19},{19,3},{4,20},{20... | collective-permute-start | bytes 786440 | tf_op jit(solution)/shard_map/ppermute | solution.py:582
  90.5 1.2 collective-permute-done.11.part_b
  91.7 4.7 %image_two.1 = (f32[256,256]{1,0:T(8,128)S(1)}, f32[256,256]{1,0:T(8,128)S(1)}, f32[8,128]{1,0:T(8,128)S(1)}) custom-call(s32[3]{0:T(128)S(1)} %pad_add_fusion.ids, s32[8]{0:T(128)S(1)} %copy-done.5, s32[8]{0:T(128)S(1)} %collective-permute-done.1.rsector_other, s32[64]{0:T(128)S(1)} %copy-done.4, s32[32]{0:T(128)S(1)} %copy-done.6, s32[8]{0:T(128)S(1)} %copy-done.7, ...), custom_call_target="tpu_custom_call" | custom-call | flops 3300000000 | bytes 9000000 | tf_op jit(solution)/shard_map/image_two/pallas_call | solution.py:418
  96.8 1.2 collective-permute-done.12.part_b
  98.0 5.6 %image_three.1 = f32[16,40,128]{2,1,0:T(8,128)} custom-call(s32[3]{0:T(128)S(1)} %pad_add_fusion.ids, s32[8]{0:T(128)S(1)} %copy-done.5, s32[8]{0:T(128)S(1)} %collective-permute-done.1.rsector_other, s32[64]{0:T(128)S(1)} %copy-done.4, s32[32]{0:T(128)S(1)} %copy-done.6, s32[8]{0:T(128)S(1)} %copy-done.7, f32[256,256]{1,0:T(8,128)S(1)} %get-tuple-element.41.part_a, ...), custom_call_target="tpu_custom_call" | custom-call | flops 3300000000 | bytes 9000000 | tf_op jit(solution)/shard_map/image_three/pallas_call | solution.py:454
  103.6 3.5 %all-to-all-start.2 = ((f32[16,40,128]{2,1,0:T(8,128)}), f32[16,40,128]{2,1,0:T(8,128)S(1)}, u32[]{:S(2)}, u32[]{:S(2)}) async-start(f32[16,40,128]{2,1,0:T(8,128)} %image_three.1), calls=%async_computation.2 | async-start | bytes 655360 | tf_op jit(solution)/shard_map/all_to_all | solution.py:585
  107.2 7.9 %all-to-all-done.2.got = f32[16,40,128]{2,1,0:T(8,128)S(1)} async-done(((f32[16,40,128]{2,1,0:T(8,128)}), f32[16,40,128]{2,1,0:T(8,128)S(1)}, u32[]{:S(2)}, u32[]{:S(2)}) %all-to-all-start.2) | async-done | bytes 327712 | tf_op jit(solution)/shard_map/all_to_all | solution.py:585
  115.1 2.7 %collective-permute-start.15 = (f32[16,128]{1,0:T(8,128)S(1)}, f32[16,128]{1,0:T(8,128)S(1)}, u32[]{:S(2)}, u32[]{:S(2)}) collective-permute-start(f32[16,128]{1,0:T(8,128)S(1)} %bitcast.10), channel_id=1, source_target_pairs={{0,96},{32,0},{64,32},{96,64},{1,97},{33,1},{65,33},{97,65},{2,98}... | collective-permute-start | bytes 24584 | tf_op jit(solution)/shard_map/ppermute | solution.py:588
  118.5 2.8 %collective-permute-start.17 = (f32[8,32,128]{2,1,0:T(8,128)S(1)}, f32[8,32,128]{2,1,0:T(8,128)S(1)}, u32[]{:S(2)}, u32[]{:S(2)}) collective-permute-start(f32[8,32,128]{2,1,0:T(8,128)S(1)} %constant_dynamic-slice_fusion), channel_id=1, source_target_pairs={{0,16},{16,0},{1,17},{17,1},{2,18},{18,2},{3,19},{19,3},{4,20},{20... | collective-permute-start | bytes 393224 | tf_op jit(solution)/shard_map/ppermute | solution.py:591
  121.8 3.6 %collective-permute-start.16 = (f32[64,128]{1,0:T(8,128)S(1)}, f32[64,128]{1,0:T(8,128)S(1)}, u32[]{:S(2)}, u32[]{:S(2)}) collective-permute-start(f32[64,128]{1,0:T(8,128)S(1)} %pad_maximum_fusion.own_stats), channel_id=1, source_target_pairs={{0,16},{16,0},{1,17},{17,1},{2,18},{18,2},{3,19},{19,3},{4,20},{20... | collective-permute-start | bytes 98312 | tf_op jit(solution)/shard_map/ppermute | solution.py:593
  126.3 2.2 %finish.1 = (f32[8,16,256]{2,1,0:T(8,128)}, f32[1,1]{1,0:T(1,128)}) custom-call(s32[3]{0:T(128)S(1)} %pad_add_fusion.ids, s32[64]{0:T(128)S(1)} %copy-done.4, s32[8]{0:T(128)S(1)} %copy-done.5, s32[32]{0:T(128)S(1)} %copy-done.6, s32[8]{0:T(128)S(1)} %copy-done.7, f32[64,128]{1,0:T(8,128)S(1)} %pad_maximum_fusion.own_stats, ...), custom_call_target="tpu_custom_call" | custom-call | tf_op jit(solution)/shard_map/finish/pallas_call | solution.py:535
  (51 shorter events, 7.9 us)
Async XLA Ops:
  0.7 4.5 %copy-start.3 = (f32[8,256,16]{1,2,0:T(8,128)S(1)}, f32[8,256,16]{1,2,0:T(8,128)}, u32[]{:S(2)}) copy-start(f32[8,256,16]{1,2,0:T(8,128)} %param.8) | copy-start | bytes 393220
  0.7 4.6 %copy-start.5 = (s32[8]{0:T(128)S(1)}, s32[8]{0:T(128)}, u32[]{:S(2)}) copy-start(s32[8]{0:T(128)} %rsector.9) | copy-start | bytes 100
  0.7 5.0 %copy-start.12 = (s32[8,2]{0,1:T(2,128)S(1)}, s32[8,2]{0,1:T(2,128)}, u32[]{:S(2)}) copy-start(s32[8,2]{0,1:T(2,128)} %param.13) | copy-start | bytes 196
  3.7 3.6 %collective-permute-start = (f32[4,264,128]{2,1,0:T(8,128)}, f32[4,264,128]{2,1,0:T(8,128)S(1)}, u32[]{:S(2)}, u32[]{:S(2)}) collective-permute-start(f32[4,264,128]{2,1,0:T(8,128)} %get-tuple-element.24), channel_id=1, source_target_pairs={{0,16},{16,0},{1,17},{17,1},{2,18},{18,2},{3,19},{19,3},{4,20},{20... | collective-permute-start | bytes 1622024 | tf_op jit(solution)/shard_map/ppermute | solution.py:561
  5.2 2.1 %collective-permute-start.3 = (f32[8,16,256]{2,1,0:T(8,128)S(1)}, f32[8,16,256]{2,1,0:T(8,128)S(1)}, u32[]{:S(2)}, u32[]{:S(2)}) collective-permute-start(f32[8,16,256]{2,1,0:T(8,128)S(1)} %bitcast.7), channel_id=1, source_target_pairs={{0,16},{16,0},{1,17},{17,1},{2,18},{18,2},{3,19},{19,3},{4,20},{20... | collective-permute-start | bytes 393224 | tf_op jit(solution)/shard_map/ppermute | solution.py:558
  5.3 2.0 %collective-permute-start.1 = (s32[8]{0:T(128)S(1)}, s32[8]{0:T(128)S(1)}, u32[]{:S(2)}, u32[]{:S(2)}) collective-permute-start(s32[8]{0:T(128)S(1)} %copy-done.5), channel_id=1, source_target_pairs={{0,16},{16,0},{1,17},{17,1},{2,18},{18,2},{3,19},{19,3},{4,20},{20... | collective-permute-start | bytes 104 | tf_op jit(solution)/shard_map/ppermute | solution.py:556
  5.8 1.5 %collective-permute-start.2 = (s32[8,2]{1,0:T(8,128)S(1)}, s32[8,2]{1,0:T(8,128)S(1)}, u32[]{:S(2)}, u32[]{:S(2)}) collective-permute-start(s32[8,2]{1,0:T(8,128)S(1)} %copy.11.on), channel_id=1, source_target_pairs={{0,16},{16,0},{1,17},{17,1},{2,18},{18,2},{3,19},{19,3},{4,20},{20... | collective-permute-start | bytes 200 | tf_op jit(solution)/shard_map/ppermute | solution.py:557
  5.9 15.4 %collective-permute-start.4 = (f32[4,264,128]{2,1,0:T(8,128)}, f32[4,264,128]{2,1,0:T(8,128)S(1)}, u32[]{:S(2)}, u32[]{:S(2)}) collective-permute-start(f32[4,264,128]{2,1,0:T(8,128)} %get-tuple-element.26.mine), channel_id=1, source_target_pairs={{0,32},{32,64},{64,96},{96,0},{1,33},{33,65},{65,97},{97,1},{2,34}... | collective-permute-start | bytes 1622024 | tf_op jit(solution)/shard_map/ppermute | solution.py:565
  7.3 14.1 %collective-permute-start.6 = (f32[4,264,128]{2,1,0:T(8,128)S(1)}, f32[4,264,128]{2,1,0:T(8,128)S(1)}, u32[]{:S(2)}, u32[]{:S(2)}) collective-permute-start(f32[4,264,128]{2,1,0:T(8,128)S(1)} %collective-permute-done.theirs), channel_id=1, source_target_pairs={{0,96},{32,0},{64,32},{96,64},{1,97},{33,1},{65,33},{97,65},{2,98}... | collective-permute-start | bytes 1622024 | tf_op jit(solution)/shard_map/ppermute | solution.py:566
  12.0 7.8 %copy-start.2 = (f32[4,264,128]{2,1,0:T(8,128)S(1)}, f32[4,264,128]{2,1,0:T(8,128)}, u32[]{:S(2)}) copy-start(f32[4,264,128]{2,1,0:T(8,128)} %get-tuple-element.26.mine) | copy-start | bytes 1622020
  12.0 21.9 %copy-start.4 = (s32[64]{0:T(128)S(1)}, s32[64]{0:T(128)}, u32[]{:S(2)}) copy-start(s32[64]{0:T(128)} %sector.7) | copy-start | bytes 772
  12.0 38.8 %all-to-all-start.1 = ((f32[16,280,128]{2,1,0:T(8,128)}), f32[16,280,128]{2,1,0:T(8,128)}, u32[]{:S(2)}, u32[]{:S(2)}) async-start(f32[16,280,128]{2,1,0:T(8,128)} %right_slots.1), calls=%async_computation.1 | async-start | bytes 4587520 | tf_op jit(solution)/shard_map/all_to_all | solution.py:573
  19.8 13.0 %collective-permute-start.8 = (f32[4,264,128]{2,1,0:T(8,128)S(1)}, f32[4,264,128]{2,1,0:T(8,128)S(1)}, u32[]{:S(2)}, u32[]{:S(2)}) collective-permute-start(f32[4,264,128]{2,1,0:T(8,128)S(1)} %copy-done.2), channel_id=1, source_target_pairs={{0,96},{32,0},{64,32},{96,64},{1,97},{33,1},{65,33},{97,65},{2,98}... | collective-permute-start | bytes 1622024 | tf_op jit(solution)/shard_map/ppermute | solution.py:566
  20.3 13.6 %collective-permute-start.9 = (f32[4,264,128]{2,1,0:T(8,128)S(1)}, f32[4,264,128]{2,1,0:T(8,128)S(1)}, u32[]{:S(2)}, u32[]{:S(2)}) collective-permute-start(f32[4,264,128]{2,1,0:T(8,128)S(1)} %collective-permute-done.theirs), channel_id=1, source_target_pairs={{0,32},{32,64},{64,96},{96,0},{1,33},{33,65},{65,97},{97,1},{2,34}... | collective-permute-start | bytes 1622024 | tf_op jit(solution)/shard_map/ppermute | solution.py:565
  21.3 24.2 %collective-permute-start.5 = (f32[4,264,128]{2,1,0:T(8,128)S(1)}, f32[4,264,128]{2,1,0:T(8,128)S(1)}, u32[]{:S(2)}, u32[]{:S(2)}) collective-permute-start(f32[4,264,128]{2,1,0:T(8,128)S(1)} %collective-permute-done.4.below_a), channel_id=1, source_target_pairs={{0,32},{32,64},{64,96},{96,0},{1,33},{33,65},{65,97},{97,1},{2,34}... | collective-permute-start | bytes 1622024 | tf_op jit(solution)/shard_map/ppermute | solution.py:567
  21.4 24.1 %collective-permute-start.7 = (f32[4,264,128]{2,1,0:T(8,128)S(1)}, f32[4,264,128]{2,1,0:T(8,128)S(1)}, u32[]{:S(2)}, u32[]{:S(2)}) collective-permute-start(f32[4,264,128]{2,1,0:T(8,128)S(1)} %collective-permute-done.6.above_b), channel_id=1, source_target_pairs={{0,96},{32,0},{64,32},{96,64},{1,97},{33,1},{65,33},{97,65},{2,98}... | collective-permute-start | bytes 1622024 | tf_op jit(solution)/shard_map/ppermute | solution.py:567
  47.1 12.3 %copy-start.6 = (s32[32]{0:T(128)S(1)}, s32[32]{0:T(128)}, u32[]{:S(2)}) copy-start(s32[32]{0:T(128)} %lsize.7) | copy-start | bytes 388
  47.1 12.3 %copy-start.7 = (s32[8]{0:T(128)S(1)}, s32[8]{0:T(128)}, u32[]{:S(2)}) copy-start(s32[8]{0:T(128)} %rsize.7) | copy-start | bytes 100
  50.8 29.7 %all-to-all-start = ((f32[16,264,128]{2,1,0:T(8,128)}), f32[16,264,128]{2,1,0:T(8,128)S(1)}, u32[]{:S(2)}, u32[]{:S(2)}) async-start(f32[16,264,128]{2,1,0:T(8,128)} %far_slots.1), calls=%async_computation | async-start | bytes 4325376 | tf_op jit(solution)/shard_map/all_to_all | solution.py:579
  55.5 3.9 %collective-permute-start.10 = (f32[16,16,128]{2,1,0:T(8,128)S(1)}, f32[16,16,128]{2,1,0:T(8,128)S(1)}, u32[]{:S(2)}, u32[]{:S(2)}) collective-permute-start(f32[16,16,128]{2,1,0:T(8,128)S(1)} %slice.8), channel_id=1, source_target_pairs={{0,16},{16,0},{1,17},{17,1},{2,18},{18,2},{3,19},{19,3},{4,20},{20... | collective-permute-start | bytes 393224 | tf_op jit(solution)/shard_map/ppermute | solution.py:575
  66.1 1.4 %copy-start.1 = (bf16[256,4096]{1,0:T(8,128)(2,1)}, bf16[256,4096]{1,0:T(8,128)(2,1)S(1)}, u32[]{:S(2)}) copy-start(bf16[256,4096]{1,0:T(8,128)(2,1)S(1)} %get-tuple-element.33.m_lo) | copy-start | bytes 6291460
  67.4 1.4 %copy-start.8 = (bf16[4096,256]{1,0:T(8,128)(2,1)}, bf16[4096,256]{1,0:T(8,128)(2,1)S(1)}, u32[]{:S(2)}) copy-start(bf16[4096,256]{1,0:T(8,128)(2,1)S(1)} %get-tuple-element.37.r_hi) | copy-start | bytes 6291460
  80.5 11.2 %copy-start.9 = (bf16[4096,256]{1,0:T(8,128)(2,1)S(1)}, bf16[4096,256]{1,0:T(8,128)(2,1)}, u32[]{:S(2)}) copy-start(bf16[4096,256]{1,0:T(8,128)(2,1)} %copy-done.8) | copy-start | bytes 6291460
  80.5 11.2 %copy-start.11 = (bf16[4096,256]{1,0:T(8,128)(2,1)S(1)}, bf16[4096,256]{1,0:T(8,128)(2,1)}, u32[]{:S(2)}) copy-start(bf16[4096,256]{1,0:T(8,128)(2,1)} %copy-done.10) | copy-start | bytes 6291460
  84.8 6.9 %collective-permute-start.11 = (f32[256,256]{1,0:T(8,128)S(1)}, f32[256,256]{1,0:T(8,128)S(1)}, u32[]{:S(2)}, u32[]{:S(2)}) collective-permute-start(f32[256,256]{1,0:T(8,128)S(1)} %get-tuple-element.34.part_a), channel_id=1, source_target_pairs={{0,16},{16,0},{1,17},{17,1},{2,18},{18,2},{3,19},{19,3},{4,20},{20... | collective-permute-start | bytes 786440 | tf_op jit(solution)/shard_map/ppermute | solution.py:582
  96.4 1.6 %collective-permute-start.12 = (f32[256,256]{1,0:T(8,128)S(1)}, f32[256,256]{1,0:T(8,128)S(1)}, u32[]{:S(2)}, u32[]{:S(2)}) collective-permute-start(f32[256,256]{1,0:T(8,128)S(1)} %get-tuple-element.41.part_a), channel_id=1, source_target_pairs={{0,16},{16,0},{1,17},{17,1},{2,18},{18,2},{3,19},{19,3},{4,20},{20... | collective-permute-start | bytes 786440 | tf_op jit(solution)/shard_map/ppermute | solution.py:583
  103.6 11.5 %all-to-all-start.2 = ((f32[16,40,128]{2,1,0:T(8,128)}), f32[16,40,128]{2,1,0:T(8,128)S(1)}, u32[]{:S(2)}, u32[]{:S(2)}) async-start(f32[16,40,128]{2,1,0:T(8,128)} %image_three.1), calls=%async_computation.2 | async-start | bytes 655360 | tf_op jit(solution)/shard_map/all_to_all | solution.py:585
  115.1 6.2 %collective-permute-start.15 = (f32[16,128]{1,0:T(8,128)S(1)}, f32[16,128]{1,0:T(8,128)S(1)}, u32[]{:S(2)}, u32[]{:S(2)}) collective-permute-start(f32[16,128]{1,0:T(8,128)S(1)} %bitcast.10), channel_id=1, source_target_pairs={{0,96},{32,0},{64,32},{96,64},{1,97},{33,1},{65,33},{97,65},{2,98}... | collective-permute-start | bytes 24584 | tf_op jit(solution)/shard_map/ppermute | solution.py:588
  117.8 4.0 %collective-permute-start.14 = (f32[16,128]{1,0:T(8,128)S(1)}, f32[16,128]{1,0:T(8,128)S(1)}, u32[]{:S(2)}, u32[]{:S(2)}) collective-permute-start(f32[16,128]{1,0:T(8,128)S(1)} %bitcast.11), channel_id=1, source_target_pairs={{0,64},{32,96},{64,0},{96,32},{1,65},{33,97},{65,1},{97,33},{2,66}... | collective-permute-start | bytes 24584 | tf_op jit(solution)/shard_map/ppermute | solution.py:588
  117.8 4.0 %collective-permute-start.13 = (f32[16,128]{1,0:T(8,128)S(1)}, f32[16,128]{1,0:T(8,128)S(1)}, u32[]{:S(2)}, u32[]{:S(2)}) collective-permute-start(f32[16,128]{1,0:T(8,128)S(1)} %bitcast.12), channel_id=1, source_target_pairs={{0,32},{32,64},{64,96},{96,0},{1,33},{33,65},{65,97},{97,1},{2,34}... | collective-permute-start | bytes 24584 | tf_op jit(solution)/shard_map/ppermute | solution.py:588
  118.5 7.8 %collective-permute-start.17 = (f32[8,32,128]{2,1,0:T(8,128)S(1)}, f32[8,32,128]{2,1,0:T(8,128)S(1)}, u32[]{:S(2)}, u32[]{:S(2)}) collective-permute-start(f32[8,32,128]{2,1,0:T(8,128)S(1)} %constant_dynamic-slice_fusion), channel_id=1, source_target_pairs={{0,16},{16,0},{1,17},{17,1},{2,18},{18,2},{3,19},{19,3},{4,20},{20... | collective-permute-start | bytes 393224 | tf_op jit(solution)/shard_map/ppermute | solution.py:591
  121.8 4.5 %collective-permute-start.16 = (f32[64,128]{1,0:T(8,128)S(1)}, f32[64,128]{1,0:T(8,128)S(1)}, u32[]{:S(2)}, u32[]{:S(2)}) collective-permute-start(f32[64,128]{1,0:T(8,128)S(1)} %pad_maximum_fusion.own_stats), channel_id=1, source_target_pairs={{0,16},{16,0},{1,17},{17,1},{2,18},{18,2},{3,19},{19,3},{4,20},{20... | collective-permute-start | bytes 98312 | tf_op jit(solution)/shard_map/ppermute | solution.py:593
  (2 other events, 2.7 us)

commit v15 on v14

--- a/solution.py
+++ b/solution.py
@@ -206,48 +206,40 @@
     return sector % 4, (home // 2 - ids[0] + 4) % 4, home % 2 == ids[1]
 
 
-def send_tiles(out, sem, cases_of):
-    def start(slot, carry):
-        for case, src, tile in cases_of(slot):
+def near_slots_body(ids, left_sector, mine, theirs, above_a, above_b, below_a, below_b, out, sem):
+    for slot in range(TERMS):
+        tile, away, same = where_from(ids, left_sector, slot)
+        sources = [
+            (same & (away % 2 == 0), mine),
+            (~same & (away % 2 == 0), theirs),
+            (same & (away == 1), above_a),
+            (~same & (away == 1), above_b),
+            (same & (away == 3), below_a),
+            (~same & (away == 3), below_b),
+        ]
+        for case, src in sources:
 
             @pl.when(case)
             def _():
                 pltpu.make_async_copy(src.at[tile], out.at[slot], sem).start()
 
-        return carry
-
-    def finish(slot, carry):
-        for case, src, tile in cases_of(slot):
-
-            @pl.when(case)
+    pltpu.make_async_copy(out, out, sem).wait()
+
+
+def far_slots_body(ids, left_sector, far_a, far_b, near, out, sem):
+    places = [where_from(ids, left_sector, slot) for slot in range(TERMS)]
+    for slot, (tile, away, same) in enumerate(places):
+        for case, src in ((same, far_a), (~same, far_b)):
+
+            @pl.when(case & (away == 2))
             def _():
-                pltpu.make_async_copy(src.at[tile], out.at[slot], sem).wait()
-
-        return carry
-
-    lax.fori_loop(0, TERMS, start, 0)
-    lax.fori_loop(0, TERMS, finish, 0)
-
-
-def near_slots_body(ids, left_sector, mine, theirs, above_a, above_b, below_a, below_b, out, sem):
-    def cases_of(slot):
-        tile, away, same = where_from(ids, left_sector, slot)
-        by_away = {0: (mine, theirs), 1: (above_a, above_b), 3: (below_a, below_b)}
-        cases = []
-        for planes, (first, second) in by_away.items():
-            cases.append((same & (away == planes), first, tile))
-            cases.append((~same & (away == planes), second, tile))
-        return cases
-
-    send_tiles(out, sem, cases_of)
-
-
-def far_slots_body(ids, left_sector, far_a, far_b, near, out, sem):
-    def cases_of(slot):
-        tile, away, same = where_from(ids, left_sector, slot)
-        return [(same & (away == 2), far_a, tile), (~same & (away == 2), far_b, tile)]
-
-    send_tiles(out, sem, cases_of)
+                pltpu.make_async_copy(src.at[tile], out.at[slot], sem).start()
+
+    for slot, (tile, away, same) in enumerate(places):
+
+        @pl.when(away == 2)
+        def _():
+            pltpu.make_async_copy(far_a.at[0], out.at[slot], sem).wait()
 
 
 def left_slots(ids, left_sector, near, far):

time: 129 us -> 128 us (level)
  transfers between devices with their start and end apart: 21 -> 21, of which waited for: 11 -> 11; matrix products, arithmetic and copies ran while one was open for 1% -> 1% of each run, Pallas kernels for 8% -> 9%
where the time goes in v15:
time: 128 us
  waiting for transfers between devices  45.7 us (36%)
  starting transfers between devices  44.1 us (34%)
  Pallas kernels  30.7 us (24%)
  local copies, waits for them, and re-layouts  6.49 us (5%)
    all_to_all x1, waiting for transfers between devices, local(): left_arrived = lax.all_to_all(left_sent, COL, 0, 0, tiled=True)  10.3 us
    ppermute x2, waiting for transfers between devices, local(): far = [lax.ppermute(below[0], 'y', UP), lax.ppermute(above[1], 'y', DOWN)]  9.62 us
    ppermute x2, waiting for transfers between devices, local(): above = [lax.ppermute(x, 'y', DOWN) for x in (mine, theirs)]  8.28 us
    all_to_all x1, waiting for transfers between devices, local(): got = lax.all_to_all(sent, COL, 0, 0, tiled=True)  7.9 us
    all_to_all x1, starting transfers between devices, local(): arrived = lax.all_to_all(slots, COL, 0, 0, tiled=True)  7.79 us
    ppermute x2, starting transfers between devices, local(): lax.ppermute(part, 'c', SWAP)  6.2 us
    pallas_call x1, Pallas kernels, image_three(): pl.pallas_call(image_three_body, in_specs=[smem()] * 6 + [vmem()] * 9, ou...  5.64 us
    unnamed x27, local copies, waits for them, and re-layouts  5.55 us
  transfers between devices with their start and end apart: 21, of which 11 were waited for; matrix products, arithmetic and copies ran while one was open for 1% of the time, Pallas kernels for 9%

profile of v15, /device:TPU:1, one launch (start us, length us, event | category | flops | bytes accessed | tf_op | source)
XLA Modules:
  0.0 128.0 jit_solution(8698059763754490229)
XLA Ops:
  0.7 3.0 %fold.1 = (f32[4,264,128]{2,1,0:T(8,128)}, f32[4,264,128]{2,1,0:T(8,128)}, f32[9,264,128]{2,1,0:T(8,128)S(1)}) custom-call(s32[3]{0:T(128)S(1)} %pad_add_fusion.ids, f32[4,2,256,256]{3,2,1,0:T(8,128)} %left_env.1, f32[8,2,256,256]{3,2,1,0:T(8,128)} %right_env.1), custom_call_target="tpu_custom_call" | custom-call | flops 1000000 | bytes 6000000 | tf_op jit(solution)/shard_map/fold/pallas_call | solution.py:146
  3.7 1.5 %collective-permute-start = (f32[4,264,128]{2,1,0:T(8,128)}, f32[4,264,128]{2,1,0:T(8,128)S(1)}, u32[]{:S(2)}, u32[]{:S(2)}) collective-permute-start(f32[4,264,128]{2,1,0:T(8,128)} %get-tuple-element.24), channel_id=1, source_target_pairs={{0,16},{16,0},{1,17},{17,1},{2,18},{18,2},{3,19},{19,3},{4,20},{20... | collective-permute-start | bytes 1622024 | tf_op jit(solution)/shard_map/ppermute | solution.py:553
  5.9 1.4 %collective-permute-start.4 = (f32[4,264,128]{2,1,0:T(8,128)}, f32[4,264,128]{2,1,0:T(8,128)S(1)}, u32[]{:S(2)}, u32[]{:S(2)}) collective-permute-start(f32[4,264,128]{2,1,0:T(8,128)} %get-tuple-element.26.mine), channel_id=1, source_target_pairs={{0,32},{32,64},{64,96},{96,0},{1,33},{33,65},{65,97},{97,1},{2,34}... | collective-permute-start | bytes 1622024 | tf_op jit(solution)/shard_map/ppermute | solution.py:557
  7.3 2.5 %collective-permute-start.6 = (f32[4,264,128]{2,1,0:T(8,128)S(1)}, f32[4,264,128]{2,1,0:T(8,128)S(1)}, u32[]{:S(2)}, u32[]{:S(2)}) collective-permute-start(f32[4,264,128]{2,1,0:T(8,128)S(1)} %collective-permute-done.theirs), channel_id=1, source_target_pairs={{0,96},{32,0},{64,32},{96,64},{1,97},{33,1},{65,33},{97,65},{2,98}... | collective-permute-start | bytes 1622024 | tf_op jit(solution)/shard_map/ppermute | solution.py:558
  9.9 2.1 %right_slots.1 = f32[16,280,128]{2,1,0:T(8,128)} custom-call(s32[3]{0:T(128)S(1)} %pad_add_fusion.ids, s32[8]{0:T(128)S(1)} %copy-done.5, s32[8]{0:T(128)S(1)} %collective-permute-done.1.rsector_other, s32[8,2]{1,0:T(8,128)S(1)} %copy.11.on, s32[8,2]{1,0:T(8,128)S(1)} %collective-permute-done.2.on_other, f32[8,16,256]{2,1,0:T(8,128)S(1)} %bitcast.8, ...), custom_call_target="tpu_custom_call" | custom-call | flops 4000000 | bytes 6000000 | tf_op jit(solution)/shard_map/right_slots/pallas_call | solution.py:188
  12.0 7.8 %all-to-all-start.1 = ((f32[16,280,128]{2,1,0:T(8,128)}), f32[16,280,128]{2,1,0:T(8,128)}, u32[]{:S(2)}, u32[]{:S(2)}) async-start(f32[16,280,128]{2,1,0:T(8,128)} %right_slots.1), calls=%async_computation.1 | async-start | bytes 4587520 | tf_op jit(solution)/shard_map/all_to_all | solution.py:565
  21.4 3.2 %collective-permute-start.7 = (f32[4,264,128]{2,1,0:T(8,128)S(1)}, f32[4,264,128]{2,1,0:T(8,128)S(1)}, u32[]{:S(2)}, u32[]{:S(2)}) collective-permute-start(f32[4,264,128]{2,1,0:T(8,128)S(1)} %collective-permute-done.6.above_b), channel_id=1, source_target_pairs={{0,96},{32,0},{64,32},{96,64},{1,97},{33,1},{65,33},{97,65},{2,98}... | collective-permute-start | bytes 1622024 | tf_op jit(solution)/shard_map/ppermute | solution.py:559
  24.6 8.3 %collective-permute-done.8.above_a = f32[4,264,128]{2,1,0:T(8,128)S(1)} collective-permute-done((f32[4,264,128]{2,1,0:T(8,128)S(1)}, f32[4,264,128]{2,1,0:T(8,128)S(1)}, u32[]{:S(2)}, u32[]{:S(2)}) %collective-permute-start.8) | collective-permute-done | bytes 540704 | tf_op jit(solution)/shard_map/ppermute | solution.py:558
  33.9 2.0 %near_slots.1.near = f32[16,264,128]{2,1,0:T(8,128)} custom-call(s32[3]{0:T(128)S(1)} %pad_add_fusion.ids, s32[64]{0:T(128)S(1)} %copy-done.4, f32[4,264,128]{2,1,0:T(8,128)S(1)} %copy-done.2, f32[4,264,128]{2,1,0:T(8,128)S(1)} %collective-permute-done.theirs, f32[4,264,128]{2,1,0:T(8,128)S(1)} %collective-permute-done.8.above_a, ...), custom_call_target="tpu_custom_call" | custom-call | flops 1000000000 | bytes 4000000 | tf_op jit(solution)/shard_map/near_slots/pallas_call | solution.py:247
  35.9 9.6 %collective-permute-done.5.far_a = f32[4,264,128]{2,1,0:T(8,128)S(1)} collective-permute-done((f32[4,264,128]{2,1,0:T(8,128)S(1)}, f32[4,264,128]{2,1,0:T(8,128)S(1)}, u32[]{:S(2)}, u32[]{:S(2)}) %collective-permute-start.5) | collective-permute-done | bytes 540704 | tf_op jit(solution)/shard_map/ppermute | solution.py:559
  45.5 1.5 %far_slots.1 = f32[16,264,128]{2,1,0:T(8,128)} custom-call(s32[3]{0:T(128)S(1)} %pad_add_fusion.ids, s32[64]{0:T(128)S(1)} %copy-done.4, f32[4,264,128]{2,1,0:T(8,128)S(1)} %collective-permute-done.5.far_a, f32[4,264,128]{2,1,0:T(8,128)S(1)} %collective-permute-done.7.far_b, f32[16,264,128]{2,1,0:T(8,128)} %near_slots.1.near), custom_call_target="tpu_custom_call", output_to_operand_aliasing={{}: (4, {})} | custom-call | flops 15000000512 | bytes 4000000 | tf_op jit(solution)/shard_map/far_slots/pallas_call | solution.py:257
  47.1 3.8 %all-to-all-done.1.slots = f32[16,280,128]{2,1,0:T(8,128)} async-done(((f32[16,280,128]{2,1,0:T(8,128)}), f32[16,280,128]{2,1,0:T(8,128)}, u32[]{:S(2)}, u32[]{:S(2)}) %all-to-all-start.1) | async-done | bytes 2293792 | tf_op jit(solution)/shard_map/all_to_all | solution.py:565
  50.8 3.7 %all-to-all-start = ((f32[16,264,128]{2,1,0:T(8,128)}), f32[16,264,128]{2,1,0:T(8,128)S(1)}, u32[]{:S(2)}, u32[]{:S(2)}) async-start(f32[16,264,128]{2,1,0:T(8,128)} %far_slots.1), calls=%async_computation | async-start | bytes 4325376 | tf_op jit(solution)/shard_map/all_to_all | solution.py:571
  55.5 2.9 %collective-permute-start.10 = (f32[16,16,128]{2,1,0:T(8,128)S(1)}, f32[16,16,128]{2,1,0:T(8,128)S(1)}, u32[]{:S(2)}, u32[]{:S(2)}) collective-permute-start(f32[16,16,128]{2,1,0:T(8,128)S(1)} %slice.8), channel_id=1, source_target_pairs={{0,16},{16,0},{1,17},{17,1},{2,18},{18,2},{3,19},{19,3},{4,20},{20... | collective-permute-start | bytes 393224 | tf_op jit(solution)/shard_map/ppermute | solution.py:567
  59.4 5.3 %first_vector.1 = (bf16[4096,256]{1,0:T(8,128)(2,1)S(1)}, bf16[4096,256]{1,0:T(8,128)(2,1)S(1)}, bf16[256,4096]{1,0:T(8,128)(2,1)S(1)}, bf16[256,4096]{1,0:T(8,1...) custom-call(s32[3]{0:T(128)S(1)} %pad_add_fusion.ids, s32[8]{0:T(128)S(1)} %copy-done.5, ...), custom_call_target="tpu_custom_call" | custom-call | flops 1700000000 | bytes 12000000 | tf_op jit(solution)/shard_map/first_vector/pallas_call | solution.py:318
  64.7 1.3 %copy-done = bf16[256,4096]{1,0:T(8,128)(2,1)} copy-done((bf16[256,4096]{1,0:T(8,128)(2,1)}, bf16[256,4096]{1,0:T(8,128)(2,1)S(1)}, u32[]{:S(2)}) %copy-start) | copy-done | bytes 2097176
  66.1 1.4 %copy-done.1 = bf16[256,4096]{1,0:T(8,128)(2,1)} copy-done((bf16[256,4096]{1,0:T(8,128)(2,1)}, bf16[256,4096]{1,0:T(8,128)(2,1)S(1)}, u32[]{:S(2)}) %copy-start.1) | copy-done | bytes 2097176
  67.4 1.4 %copy-done.8 = bf16[4096,256]{1,0:T(8,128)(2,1)} copy-done((bf16[4096,256]{1,0:T(8,128)(2,1)}, bf16[4096,256]{1,0:T(8,128)(2,1)S(1)}, u32[]{:S(2)}) %copy-start.8) | copy-done | bytes 2097176
  68.8 1.3 %copy-done.10 = bf16[4096,256]{1,0:T(8,128)(2,1)} copy-done((bf16[4096,256]{1,0:T(8,128)(2,1)}, bf16[4096,256]{1,0:T(8,128)(2,1)S(1)}, u32[]{:S(2)}) %copy-start.10) | copy-done | bytes 2097176
  70.2 10.3 %all-to-all-done.arrived = f32[16,264,128]{2,1,0:T(8,128)S(1)} async-done(((f32[16,264,128]{2,1,0:T(8,128)}), f32[16,264,128]{2,1,0:T(8,128)S(1)}, u32[]{:S(2)}, u32[]{:S(2)}) %all-to-all-start) | async-done | bytes 2162720 | tf_op jit(solution)/shard_map/all_to_all | solution.py:571
  80.5 4.2 %image_one.1 = (bf16[4096,256]{1,0:T(8,128)(2,1)S(1)}, bf16[4096,256]{1,0:T(8,128)(2,1)S(1)}, f32[256,256]{1,0:T(8,128)S(1)}) custom-call(f32[16,264,128]{2,1,0:T(8,128)S(1)} %all-to-all-done.arrived, bf16[256,4096]{1,0:T(8,128)(2,1)} %copy-done, bf16[256,4096]{1,0:T(8,128)(2,1)} %copy-done.1), custom_call_target="tpu_custom_call" | custom-call | flops 1700000000 | bytes 10000000 | tf_op jit(solution)/shard_map/image_one/pallas_call | solution.py:358
  84.8 5.7 %collective-permute-start.11 = (f32[256,256]{1,0:T(8,128)S(1)}, f32[256,256]{1,0:T(8,128)S(1)}, u32[]{:S(2)}, u32[]{:S(2)}) collective-permute-start(f32[256,256]{1,0:T(8,128)S(1)} %get-tuple-element.34.part_a), channel_id=1, source_target_pairs={{0,16},{16,0},{1,17},{17,1},{2,18},{18,2},{3,19},{19,3},{4,20},{20... | collective-permute-start | bytes 786440 | tf_op jit(solution)/shard_map/ppermute | solution.py:574
  90.5 1.2 collective-permute-done.11.part_b
  91.7 4.7 %image_two.1 = (f32[256,256]{1,0:T(8,128)S(1)}, f32[256,256]{1,0:T(8,128)S(1)}, f32[8,128]{1,0:T(8,128)S(1)}) custom-call(s32[3]{0:T(128)S(1)} %pad_add_fusion.ids, s32[8]{0:T(128)S(1)} %copy-done.5, s32[8]{0:T(128)S(1)} %collective-permute-done.1.rsector_other, s32[64]{0:T(128)S(1)} %copy-done.4, s32[32]{0:T(128)S(1)} %copy-done.6, s32[8]{0:T(128)S(1)} %copy-done.7, ...), custom_call_target="tpu_custom_call" | custom-call | flops 3300000000 | bytes 9000000 | tf_op jit(solution)/shard_map/image_two/pallas_call | solution.py:410
  96.8 1.2 collective-permute-done.12.part_b
  98.0 5.6 %image_three.1 = f32[16,40,128]{2,1,0:T(8,128)} custom-call(s32[3]{0:T(128)S(1)} %pad_add_fusion.ids, s32[8]{0:T(128)S(1)} %copy-done.5, s32[8]{0:T(128)S(1)} %collective-permute-done.1.rsector_other, s32[64]{0:T(128)S(1)} %copy-done.4, s32[32]{0:T(128)S(1)} %copy-done.6, s32[8]{0:T(128)S(1)} %copy-done.7, f32[256,256]{1,0:T(8,128)S(1)} %get-tuple-element.41.part_a, ...), custom_call_target="tpu_custom_call" | custom-call | flops 3300000000 | bytes 9000000 | tf_op jit(solution)/shard_map/image_three/pallas_call | solution.py:446
  103.6 3.5 %all-to-all-start.2 = ((f32[16,40,128]{2,1,0:T(8,128)}), f32[16,40,128]{2,1,0:T(8,128)S(1)}, u32[]{:S(2)}, u32[]{:S(2)}) async-start(f32[16,40,128]{2,1,0:T(8,128)} %image_three.1), calls=%async_computation.2 | async-start | bytes 655360 | tf_op jit(solution)/shard_map/all_to_all | solution.py:577
  107.2 7.9 %all-to-all-done.2.got = f32[16,40,128]{2,1,0:T(8,128)S(1)} async-done(((f32[16,40,128]{2,1,0:T(8,128)}), f32[16,40,128]{2,1,0:T(8,128)S(1)}, u32[]{:S(2)}, u32[]{:S(2)}) %all-to-all-start.2) | async-done | bytes 327712 | tf_op jit(solution)/shard_map/all_to_all | solution.py:577
  115.1 2.0 %collective-permute-start.15 = (f32[16,128]{1,0:T(8,128)S(1)}, f32[16,128]{1,0:T(8,128)S(1)}, u32[]{:S(2)}, u32[]{:S(2)}) collective-permute-start(f32[16,128]{1,0:T(8,128)S(1)} %bitcast.10), channel_id=1, source_target_pairs={{0,96},{32,0},{64,32},{96,64},{1,97},{33,1},{65,33},{97,65},{2,98}... | collective-permute-start | bytes 24584 | tf_op jit(solution)/shard_map/ppermute | solution.py:580
  117.8 2.8 %collective-permute-start.17 = (f32[8,32,128]{2,1,0:T(8,128)S(1)}, f32[8,32,128]{2,1,0:T(8,128)S(1)}, u32[]{:S(2)}, u32[]{:S(2)}) collective-permute-start(f32[8,32,128]{2,1,0:T(8,128)S(1)} %constant_dynamic-slice_fusion), channel_id=1, source_target_pairs={{0,16},{16,0},{1,17},{17,1},{2,18},{18,2},{3,19},{19,3},{4,20},{20... | collective-permute-start | bytes 393224 | tf_op jit(solution)/shard_map/ppermute | solution.py:583
  121.2 3.6 %collective-permute-start.16 = (f32[64,128]{1,0:T(8,128)S(1)}, f32[64,128]{1,0:T(8,128)S(1)}, u32[]{:S(2)}, u32[]{:S(2)}) collective-permute-start(f32[64,128]{1,0:T(8,128)S(1)} %pad_maximum_fusion.own_stats), channel_id=1, source_target_pairs={{0,16},{16,0},{1,17},{17,1},{2,18},{18,2},{3,19},{19,3},{4,20},{20... | collective-permute-start | bytes 98312 | tf_op jit(solution)/shard_map/ppermute | solution.py:585
  125.6 2.2 %finish.1 = (f32[8,16,256]{2,1,0:T(8,128)}, f32[1,1]{1,0:T(1,128)}) custom-call(s32[3]{0:T(128)S(1)} %pad_add_fusion.ids, s32[64]{0:T(128)S(1)} %copy-done.4, s32[8]{0:T(128)S(1)} %copy-done.5, s32[32]{0:T(128)S(1)} %copy-done.6, s32[8]{0:T(128)S(1)} %copy-done.7, f32[64,128]{1,0:T(8,128)S(1)} %pad_maximum_fusion.own_stats, ...), custom_call_target="tpu_custom_call" | custom-call | tf_op jit(solution)/shard_map/finish/pallas_call | solution.py:527
  (51 shorter events, 7.9 us)
Async XLA Ops:
  0.7 4.5 %copy-start.3 = (f32[8,256,16]{1,2,0:T(8,128)S(1)}, f32[8,256,16]{1,2,0:T(8,128)}, u32[]{:S(2)}) copy-start(f32[8,256,16]{1,2,0:T(8,128)} %param.8) | copy-start | bytes 393220
  0.7 4.6 %copy-start.5 = (s32[8]{0:T(128)S(1)}, s32[8]{0:T(128)}, u32[]{:S(2)}) copy-start(s32[8]{0:T(128)} %rsector.9) | copy-start | bytes 100
  0.7 5.0 %copy-start.12 = (s32[8,2]{0,1:T(2,128)S(1)}, s32[8,2]{0,1:T(2,128)}, u32[]{:S(2)}) copy-start(s32[8,2]{0,1:T(2,128)} %param.13) | copy-start | bytes 196
  3.7 3.6 %collective-permute-start = (f32[4,264,128]{2,1,0:T(8,128)}, f32[4,264,128]{2,1,0:T(8,128)S(1)}, u32[]{:S(2)}, u32[]{:S(2)}) collective-permute-start(f32[4,264,128]{2,1,0:T(8,128)} %get-tuple-element.24), channel_id=1, source_target_pairs={{0,16},{16,0},{1,17},{17,1},{2,18},{18,2},{3,19},{19,3},{4,20},{20... | collective-permute-start | bytes 1622024 | tf_op jit(solution)/shard_map/ppermute | solution.py:553
  5.2 2.1 %collective-permute-start.3 = (f32[8,16,256]{2,1,0:T(8,128)S(1)}, f32[8,16,256]{2,1,0:T(8,128)S(1)}, u32[]{:S(2)}, u32[]{:S(2)}) collective-permute-start(f32[8,16,256]{2,1,0:T(8,128)S(1)} %bitcast.7), channel_id=1, source_target_pairs={{0,16},{16,0},{1,17},{17,1},{2,18},{18,2},{3,19},{19,3},{4,20},{20... | collective-permute-start | bytes 393224 | tf_op jit(solution)/shard_map/ppermute | solution.py:550
  5.3 2.0 %collective-permute-start.1 = (s32[8]{0:T(128)S(1)}, s32[8]{0:T(128)S(1)}, u32[]{:S(2)}, u32[]{:S(2)}) collective-permute-start(s32[8]{0:T(128)S(1)} %copy-done.5), channel_id=1, source_target_pairs={{0,16},{16,0},{1,17},{17,1},{2,18},{18,2},{3,19},{19,3},{4,20},{20... | collective-permute-start | bytes 104 | tf_op jit(solution)/shard_map/ppermute | solution.py:548
  5.8 1.5 %collective-permute-start.2 = (s32[8,2]{1,0:T(8,128)S(1)}, s32[8,2]{1,0:T(8,128)S(1)}, u32[]{:S(2)}, u32[]{:S(2)}) collective-permute-start(s32[8,2]{1,0:T(8,128)S(1)} %copy.11.on), channel_id=1, source_target_pairs={{0,16},{16,0},{1,17},{17,1},{2,18},{18,2},{3,19},{19,3},{4,20},{20... | collective-permute-start | bytes 200 | tf_op jit(solution)/shard_map/ppermute | solution.py:549
  5.9 15.4 %collective-permute-start.4 = (f32[4,264,128]{2,1,0:T(8,128)}, f32[4,264,128]{2,1,0:T(8,128)S(1)}, u32[]{:S(2)}, u32[]{:S(2)}) collective-permute-start(f32[4,264,128]{2,1,0:T(8,128)} %get-tuple-element.26.mine), channel_id=1, source_target_pairs={{0,32},{32,64},{64,96},{96,0},{1,33},{33,65},{65,97},{97,1},{2,34}... | collective-permute-start | bytes 1622024 | tf_op jit(solution)/shard_map/ppermute | solution.py:557
  7.3 14.1 %collective-permute-start.6 = (f32[4,264,128]{2,1,0:T(8,128)S(1)}, f32[4,264,128]{2,1,0:T(8,128)S(1)}, u32[]{:S(2)}, u32[]{:S(2)}) collective-permute-start(f32[4,264,128]{2,1,0:T(8,128)S(1)} %collective-permute-done.theirs), channel_id=1, source_target_pairs={{0,96},{32,0},{64,32},{96,64},{1,97},{33,1},{65,33},{97,65},{2,98}... | collective-permute-start | bytes 1622024 | tf_op jit(solution)/shard_map/ppermute | solution.py:558
  12.0 7.8 %copy-start.2 = (f32[4,264,128]{2,1,0:T(8,128)S(1)}, f32[4,264,128]{2,1,0:T(8,128)}, u32[]{:S(2)}) copy-start(f32[4,264,128]{2,1,0:T(8,128)} %get-tuple-element.26.mine) | copy-start | bytes 1622020
  12.0 21.9 %copy-start.4 = (s32[64]{0:T(128)S(1)}, s32[64]{0:T(128)}, u32[]{:S(2)}) copy-start(s32[64]{0:T(128)} %sector.7) | copy-start | bytes 772
  12.0 38.8 %all-to-all-start.1 = ((f32[16,280,128]{2,1,0:T(8,128)}), f32[16,280,128]{2,1,0:T(8,128)}, u32[]{:S(2)}, u32[]{:S(2)}) async-start(f32[16,280,128]{2,1,0:T(8,128)} %right_slots.1), calls=%async_computation.1 | async-start | bytes 4587520 | tf_op jit(solution)/shard_map/all_to_all | solution.py:565
  19.8 13.0 %collective-permute-start.8 = (f32[4,264,128]{2,1,0:T(8,128)S(1)}, f32[4,264,128]{2,1,0:T(8,128)S(1)}, u32[]{:S(2)}, u32[]{:S(2)}) collective-permute-start(f32[4,264,128]{2,1,0:T(8,128)S(1)} %copy-done.2), channel_id=1, source_target_pairs={{0,96},{32,0},{64,32},{96,64},{1,97},{33,1},{65,33},{97,65},{2,98}... | collective-permute-start | bytes 1622024 | tf_op jit(solution)/shard_map/ppermute | solution.py:558
  20.3 13.6 %collective-permute-start.9 = (f32[4,264,128]{2,1,0:T(8,128)S(1)}, f32[4,264,128]{2,1,0:T(8,128)S(1)}, u32[]{:S(2)}, u32[]{:S(2)}) collective-permute-start(f32[4,264,128]{2,1,0:T(8,128)S(1)} %collective-permute-done.theirs), channel_id=1, source_target_pairs={{0,32},{32,64},{64,96},{96,0},{1,33},{33,65},{65,97},{97,1},{2,34}... | collective-permute-start | bytes 1622024 | tf_op jit(solution)/shard_map/ppermute | solution.py:557
  21.3 24.2 %collective-permute-start.5 = (f32[4,264,128]{2,1,0:T(8,128)S(1)}, f32[4,264,128]{2,1,0:T(8,128)S(1)}, u32[]{:S(2)}, u32[]{:S(2)}) collective-permute-start(f32[4,264,128]{2,1,0:T(8,128)S(1)} %collective-permute-done.4.below_a), channel_id=1, source_target_pairs={{0,32},{32,64},{64,96},{96,0},{1,33},{33,65},{65,97},{97,1},{2,34}... | collective-permute-start | bytes 1622024 | tf_op jit(solution)/shard_map/ppermute | solution.py:559
  21.4 24.1 %collective-permute-start.7 = (f32[4,264,128]{2,1,0:T(8,128)S(1)}, f32[4,264,128]{2,1,0:T(8,128)S(1)}, u32[]{:S(2)}, u32[]{:S(2)}) collective-permute-start(f32[4,264,128]{2,1,0:T(8,128)S(1)} %collective-permute-done.6.above_b), channel_id=1, source_target_pairs={{0,96},{32,0},{64,32},{96,64},{1,97},{33,1},{65,33},{97,65},{2,98}... | collective-permute-start | bytes 1622024 | tf_op jit(solution)/shard_map/ppermute | solution.py:559
  47.0 12.4 %copy-start.6 = (s32[32]{0:T(128)S(1)}, s32[32]{0:T(128)}, u32[]{:S(2)}) copy-start(s32[32]{0:T(128)} %lsize.7) | copy-start | bytes 388
  47.0 12.4 %copy-start.7 = (s32[8]{0:T(128)S(1)}, s32[8]{0:T(128)}, u32[]{:S(2)}) copy-start(s32[8]{0:T(128)} %rsize.7) | copy-start | bytes 100
  50.8 29.7 %all-to-all-start = ((f32[16,264,128]{2,1,0:T(8,128)}), f32[16,264,128]{2,1,0:T(8,128)S(1)}, u32[]{:S(2)}, u32[]{:S(2)}) async-start(f32[16,264,128]{2,1,0:T(8,128)} %far_slots.1), calls=%async_computation | async-start | bytes 4325376 | tf_op jit(solution)/shard_map/all_to_all | solution.py:571
  55.5 3.9 %collective-permute-start.10 = (f32[16,16,128]{2,1,0:T(8,128)S(1)}, f32[16,16,128]{2,1,0:T(8,128)S(1)}, u32[]{:S(2)}, u32[]{:S(2)}) collective-permute-start(f32[16,16,128]{2,1,0:T(8,128)S(1)} %slice.8), channel_id=1, source_target_pairs={{0,16},{16,0},{1,17},{17,1},{2,18},{18,2},{3,19},{19,3},{4,20},{20... | collective-permute-start | bytes 393224 | tf_op jit(solution)/shard_map/ppermute | solution.py:567
  66.1 1.4 %copy-start.1 = (bf16[256,4096]{1,0:T(8,128)(2,1)}, bf16[256,4096]{1,0:T(8,128)(2,1)S(1)}, u32[]{:S(2)}) copy-start(bf16[256,4096]{1,0:T(8,128)(2,1)S(1)} %get-tuple-element.33.m_lo) | copy-start | bytes 6291460
  67.4 1.4 %copy-start.8 = (bf16[4096,256]{1,0:T(8,128)(2,1)}, bf16[4096,256]{1,0:T(8,128)(2,1)S(1)}, u32[]{:S(2)}) copy-start(bf16[4096,256]{1,0:T(8,128)(2,1)S(1)} %get-tuple-element.37.r_hi) | copy-start | bytes 6291460
  80.5 11.2 %copy-start.9 = (bf16[4096,256]{1,0:T(8,128)(2,1)S(1)}, bf16[4096,256]{1,0:T(8,128)(2,1)}, u32[]{:S(2)}) copy-start(bf16[4096,256]{1,0:T(8,128)(2,1)} %copy-done.8) | copy-start | bytes 6291460
  80.5 11.2 %copy-start.11 = (bf16[4096,256]{1,0:T(8,128)(2,1)S(1)}, bf16[4096,256]{1,0:T(8,128)(2,1)}, u32[]{:S(2)}) copy-start(bf16[4096,256]{1,0:T(8,128)(2,1)} %copy-done.10) | copy-start | bytes 6291460
  84.8 6.9 %collective-permute-start.11 = (f32[256,256]{1,0:T(8,128)S(1)}, f32[256,256]{1,0:T(8,128)S(1)}, u32[]{:S(2)}, u32[]{:S(2)}) collective-permute-start(f32[256,256]{1,0:T(8,128)S(1)} %get-tuple-element.34.part_a), channel_id=1, source_target_pairs={{0,16},{16,0},{1,17},{17,1},{2,18},{18,2},{3,19},{19,3},{4,20},{20... | collective-permute-start | bytes 786440 | tf_op jit(solution)/shard_map/ppermute | solution.py:574
  96.4 1.6 %collective-permute-start.12 = (f32[256,256]{1,0:T(8,128)S(1)}, f32[256,256]{1,0:T(8,128)S(1)}, u32[]{:S(2)}, u32[]{:S(2)}) collective-permute-start(f32[256,256]{1,0:T(8,128)S(1)} %get-tuple-element.41.part_a), channel_id=1, source_target_pairs={{0,16},{16,0},{1,17},{17,1},{2,18},{18,2},{3,19},{19,3},{4,20},{20... | collective-permute-start | bytes 786440 | tf_op jit(solution)/shard_map/ppermute | solution.py:575
  103.6 11.5 %all-to-all-start.2 = ((f32[16,40,128]{2,1,0:T(8,128)}), f32[16,40,128]{2,1,0:T(8,128)S(1)}, u32[]{:S(2)}, u32[]{:S(2)}) async-start(f32[16,40,128]{2,1,0:T(8,128)} %image_three.1), calls=%async_computation.2 | async-start | bytes 655360 | tf_op jit(solution)/shard_map/all_to_all | solution.py:577
  115.1 5.5 %collective-permute-start.15 = (f32[16,128]{1,0:T(8,128)S(1)}, f32[16,128]{1,0:T(8,128)S(1)}, u32[]{:S(2)}, u32[]{:S(2)}) collective-permute-start(f32[16,128]{1,0:T(8,128)S(1)} %bitcast.10), channel_id=1, source_target_pairs={{0,96},{32,0},{64,32},{96,64},{1,97},{33,1},{65,33},{97,65},{2,98}... | collective-permute-start | bytes 24584 | tf_op jit(solution)/shard_map/ppermute | solution.py:580
  117.2 4.0 %collective-permute-start.14 = (f32[16,128]{1,0:T(8,128)S(1)}, f32[16,128]{1,0:T(8,128)S(1)}, u32[]{:S(2)}, u32[]{:S(2)}) collective-permute-start(f32[16,128]{1,0:T(8,128)S(1)} %bitcast.11), channel_id=1, source_target_pairs={{0,64},{32,96},{64,0},{96,32},{1,65},{33,97},{65,1},{97,33},{2,66}... | collective-permute-start | bytes 24584 | tf_op jit(solution)/shard_map/ppermute | solution.py:580
  117.2 4.0 %collective-permute-start.13 = (f32[16,128]{1,0:T(8,128)S(1)}, f32[16,128]{1,0:T(8,128)S(1)}, u32[]{:S(2)}, u32[]{:S(2)}) collective-permute-start(f32[16,128]{1,0:T(8,128)S(1)} %bitcast.12), channel_id=1, source_target_pairs={{0,32},{32,64},{64,96},{96,0},{1,33},{33,65},{65,97},{97,1},{2,34}... | collective-permute-start | bytes 24584 | tf_op jit(solution)/shard_map/ppermute | solution.py:580
  117.8 7.8 %collective-permute-start.17 = (f32[8,32,128]{2,1,0:T(8,128)S(1)}, f32[8,32,128]{2,1,0:T(8,128)S(1)}, u32[]{:S(2)}, u32[]{:S(2)}) collective-permute-start(f32[8,32,128]{2,1,0:T(8,128)S(1)} %constant_dynamic-slice_fusion), channel_id=1, source_target_pairs={{0,16},{16,0},{1,17},{17,1},{2,18},{18,2},{3,19},{19,3},{4,20},{20... | collective-permute-start | bytes 393224 | tf_op jit(solution)/shard_map/ppermute | solution.py:583
  121.2 4.5 %collective-permute-start.16 = (f32[64,128]{1,0:T(8,128)S(1)}, f32[64,128]{1,0:T(8,128)S(1)}, u32[]{:S(2)}, u32[]{:S(2)}) collective-permute-start(f32[64,128]{1,0:T(8,128)S(1)} %pad_maximum_fusion.own_stats), channel_id=1, source_target_pairs={{0,16},{16,0},{1,17},{17,1},{2,18},{18,2},{3,19},{19,3},{4,20},{20... | collective-permute-start | bytes 98312 | tf_op jit(solution)/shard_map/ppermute | solution.py:585
  (2 other events, 2.7 us)

commit v16 on v14

--- a/solution.py
+++ b/solution.py
@@ -562,14 +562,16 @@
     theirs, rsector_other, on_other, thin_other = lax.optimization_barrier(
         (theirs, rsector_other, on_other, thin_other)
     )
-    below = [lax.ppermute(x, "y", UP) for x in (mine, theirs)]
-    above = [lax.ppermute(x, "y", DOWN) for x in (mine, theirs)]
-    far = [lax.ppermute(below[0], "y", UP), lax.ppermute(above[1], "y", DOWN)]
+    below = [lax.ppermute(mine, "y", UP)]
+    above = [lax.ppermute(mine, "y", DOWN)]
 
     slots = right_slots(
         ids, right_sector, rsector_other, term_on, on_other, thin, thin_other, right_folded
     )
-    slots, theirs_now = lax.optimization_barrier((slots, theirs))
+    slots, theirs = lax.optimization_barrier((slots, theirs))
+    below.append(lax.ppermute(theirs, "y", UP))
+    above.append(lax.ppermute(theirs, "y", DOWN))
+    far = [lax.ppermute(below[0], "y", UP), lax.ppermute(above[1], "y", DOWN)]
     arrived = lax.all_to_all(slots, COL, 0, 0, tiled=True)
     scalars = (ids, right_sector, rsector_other, left_sector, left_size, right_size)
     halves = lax.ppermute(arrived[:, :THIN, :], "c", SWAP)

time: 129 us -> 131 us (1.016)
    all_to_all x1, waiting for transfers between devices: 10.3 us -> 11.9 us  [local(): left_arrived = lax.all_to_all(left_sent, COL, 0, 0, tiled=True)]
    all_to_all x1, starting transfers between devices: 3.72 us -> 5.09 us  [local(): left_arrived = lax.all_to_all(left_sent, COL, 0, 0, tiled=True)]
    ppermute x1, starting transfers between devices: 2.95 us -> 1.58 us  [local(): halves = lax.ppermute(arrived[:, :THIN, :], 'c', SWAP)]
  transfers between devices with their start and end apart: 21 -> 21, of which waited for: 11 -> 12; matrix products, arithmetic and copies ran while one was open for 1% -> 1% of each run, Pallas kernels for 8% -> 8%
where the time goes in v16:
time: 131 us
  waiting for transfers between devices  47 us (36%)
  starting transfers between devices  45.6 us (35%)
  Pallas kernels  30.7 us (23%)
  local copies, waits for them, and re-layouts  6.49 us (5%)
    all_to_all x1, waiting for transfers between devices, local(): left_arrived = lax.all_to_all(left_sent, COL, 0, 0, tiled=True)  11.9 us
    ppermute x2, waiting for transfers between devices, local(): far = [lax.ppermute(below[0], 'y', UP), lax.ppermute(above[1], 'y', DOWN)]  9.78 us
    ppermute x1, waiting for transfers between devices, local(): above = [lax.ppermute(mine, 'y', DOWN)]  8.07 us
    all_to_all x1, waiting for transfers between devices, local(): got = lax.all_to_all(sent, COL, 0, 0, tiled=True)  7.92 us
    all_to_all x1, starting transfers between devices, local(): arrived = lax.all_to_all(slots, COL, 0, 0, tiled=True)  7.64 us
    ppermute x2, starting transfers between devices, local(): lax.ppermute(part, 'c', SWAP)  6.12 us
    pallas_call x1, Pallas kernels, image_three(): pl.pallas_call(image_three_body, in_specs=[smem()] * 6 + [vmem()] * 9, ou...  5.63 us
    unnamed x27, local copies, waits for them, and re-layouts  5.55 us
  transfers between devices with their start and end apart: 21, of which 12 were waited for; matrix products, arithmetic and copies ran while one was open for 1% of the time, Pallas kernels for 8%

profile of v16, /device:TPU:1, one launch (start us, length us, event | category | flops | bytes accessed | tf_op | source)
XLA Modules:
  0.0 130.9 jit_solution(17852281778575758513)
XLA Ops:
  0.7 3.0 %fold.1 = (f32[4,264,128]{2,1,0:T(8,128)}, f32[4,264,128]{2,1,0:T(8,128)}, f32[9,264,128]{2,1,0:T(8,128)S(1)}) custom-call(s32[3]{0:T(128)S(1)} %pad_add_fusion.ids, f32[4,2,256,256]{3,2,1,0:T(8,128)} %left_env.1, f32[8,2,256,256]{3,2,1,0:T(8,128)} %right_env.1), custom_call_target="tpu_custom_call" | custom-call | flops 1000000 | bytes 6000000 | tf_op jit(solution)/shard_map/fold/pallas_call | solution.py:146
  3.7 1.5 %collective-permute-start = (f32[4,264,128]{2,1,0:T(8,128)}, f32[4,264,128]{2,1,0:T(8,128)S(1)}, u32[]{:S(2)}, u32[]{:S(2)}) collective-permute-start(f32[4,264,128]{2,1,0:T(8,128)} %get-tuple-element.25), channel_id=1, source_target_pairs={{0,16},{16,0},{1,17},{17,1},{2,18},{18,2},{3,19},{19,3},{4,20},{20... | collective-permute-start | bytes 1622024 | tf_op jit(solution)/shard_map/ppermute | solution.py:561
  5.9 1.4 %collective-permute-start.4 = (f32[4,264,128]{2,1,0:T(8,128)}, f32[4,264,128]{2,1,0:T(8,128)S(1)}, u32[]{:S(2)}, u32[]{:S(2)}) collective-permute-start(f32[4,264,128]{2,1,0:T(8,128)} %get-tuple-element.27.mine), channel_id=1, source_target_pairs={{0,32},{32,64},{64,96},{96,0},{1,33},{33,65},{65,97},{97,1},{2,34}... | collective-permute-start | bytes 1622024 | tf_op jit(solution)/shard_map/ppermute | solution.py:565
  7.3 2.1 %right_slots.1 = f32[16,280,128]{2,1,0:T(8,128)} custom-call(s32[3]{0:T(128)S(1)} %pad_add_fusion.ids, s32[8]{0:T(128)S(1)} %copy-done.5, s32[8]{0:T(128)S(1)} %collective-permute-done.1.rsector_other, s32[8,2]{1,0:T(8,128)S(1)} %copy.11.on, s32[8,2]{1,0:T(8,128)S(1)} %collective-permute-done.2.on_other, f32[8,16,256]{2,1,0:T(8,128)S(1)} %bitcast.8, ...), custom_call_target="tpu_custom_call" | custom-call | flops 4000000 | bytes 6000000 | tf_op jit(solution)/shard_map/right_slots/pallas_call | solution.py:188
  9.5 2.6 %collective-permute-start.6 = (f32[4,264,128]{2,1,0:T(8,128)S(1)}, f32[4,264,128]{2,1,0:T(8,128)S(1)}, u32[]{:S(2)}, u32[]{:S(2)}) collective-permute-start(f32[4,264,128]{2,1,0:T(8,128)S(1)} %collective-permute-done.theirs), channel_id=1, source_target_pairs={{0,96},{32,0},{64,32},{96,64},{1,97},{33,1},{65,33},{97,65},{2,98}... | collective-permute-start | bytes 1622024 | tf_op jit(solution)/shard_map/ppermute | solution.py:573
  12.0 7.6 %all-to-all-start.1 = ((f32[16,280,128]{2,1,0:T(8,128)}), f32[16,280,128]{2,1,0:T(8,128)}, u32[]{:S(2)}, u32[]{:S(2)}) async-start(f32[16,280,128]{2,1,0:T(8,128)} %right_slots.1), calls=%async_computation.1 | async-start | bytes 4587520 | tf_op jit(solution)/shard_map/all_to_all | solution.py:575
  21.2 2.1 %collective-permute-done.6.above_b = f32[4,264,128]{2,1,0:T(8,128)S(1)} collective-permute-done((f32[4,264,128]{2,1,0:T(8,128)S(1)}, f32[4,264,128]{2,1,0:T(8,128)S(1)}, u32[]{:S(2)}, u32[]{:S(2)}) %collective-permute-start.6) | collective-permute-done | bytes 540704 | tf_op jit(solution)/shard_map/ppermute | solution.py:573
  23.3 3.5 %collective-permute-start.7 = (f32[4,264,128]{2,1,0:T(8,128)S(1)}, f32[4,264,128]{2,1,0:T(8,128)S(1)}, u32[]{:S(2)}, u32[]{:S(2)}) collective-permute-start(f32[4,264,128]{2,1,0:T(8,128)S(1)} %collective-permute-done.6.above_b), channel_id=1, source_target_pairs={{0,96},{32,0},{64,32},{96,64},{1,97},{33,1},{65,33},{97,65},{2,98}... | collective-permute-start | bytes 1622024 | tf_op jit(solution)/shard_map/ppermute | solution.py:574
  26.8 8.1 %collective-permute-done.8.above_a = f32[4,264,128]{2,1,0:T(8,128)S(1)} collective-permute-done((f32[4,264,128]{2,1,0:T(8,128)S(1)}, f32[4,264,128]{2,1,0:T(8,128)S(1)}, u32[]{:S(2)}, u32[]{:S(2)}) %collective-permute-start.8) | collective-permute-done | bytes 540704 | tf_op jit(solution)/shard_map/ppermute | solution.py:566
  34.9 1.8 %near_slots.1.near = f32[16,264,128]{2,1,0:T(8,128)} custom-call(s32[3]{0:T(128)S(1)} %pad_add_fusion.ids, s32[64]{0:T(128)S(1)} %copy-done.4, f32[4,264,128]{2,1,0:T(8,128)S(1)} %copy-done.2, f32[4,264,128]{2,1,0:T(8,128)S(1)} %collective-permute-done.theirs, f32[4,264,128]{2,1,0:T(8,128)S(1)} %collective-permute-done.8.above_a, ...), custom_call_target="tpu_custom_call" | custom-call | flops 1000000000 | bytes 4000000 | tf_op jit(solution)/shard_map/near_slots/pallas_call | solution.py:255
  36.7 8.7 %collective-permute-done.5.far_a = f32[4,264,128]{2,1,0:T(8,128)S(1)} collective-permute-done((f32[4,264,128]{2,1,0:T(8,128)S(1)}, f32[4,264,128]{2,1,0:T(8,128)S(1)}, u32[]{:S(2)}, u32[]{:S(2)}) %collective-permute-start.5) | collective-permute-done | bytes 540704 | tf_op jit(solution)/shard_map/ppermute | solution.py:574
  46.5 1.6 %far_slots.1 = f32[16,264,128]{2,1,0:T(8,128)} custom-call(s32[3]{0:T(128)S(1)} %pad_add_fusion.ids, s32[64]{0:T(128)S(1)} %copy-done.4, f32[4,264,128]{2,1,0:T(8,128)S(1)} %collective-permute-done.5.far_a, f32[4,264,128]{2,1,0:T(8,128)S(1)} %collective-permute-done.7.far_b, f32[16,264,128]{2,1,0:T(8,128)} %near_slots.1.near), custom_call_target="tpu_custom_call", output_to_operand_aliasing={{}: (4, {})} | custom-call | flops 15000000512 | bytes 4000000 | tf_op jit(solution)/shard_map/far_slots/pallas_call | solution.py:265
  48.1 2.5 %all-to-all-done.1.slots = f32[16,280,128]{2,1,0:T(8,128)} async-done(((f32[16,280,128]{2,1,0:T(8,128)}), f32[16,280,128]{2,1,0:T(8,128)}, u32[]{:S(2)}, u32[]{:S(2)}) %all-to-all-start.1) | async-done | bytes 2293792 | tf_op jit(solution)/shard_map/all_to_all | solution.py:575
  50.7 5.1 %all-to-all-start = ((f32[16,264,128]{2,1,0:T(8,128)}), f32[16,264,128]{2,1,0:T(8,128)S(1)}, u32[]{:S(2)}, u32[]{:S(2)}) async-start(f32[16,264,128]{2,1,0:T(8,128)} %far_slots.1), calls=%async_computation | async-start | bytes 4325376 | tf_op jit(solution)/shard_map/all_to_all | solution.py:581
  56.7 1.6 %collective-permute-start.10 = (f32[16,16,128]{2,1,0:T(8,128)S(1)}, f32[16,16,128]{2,1,0:T(8,128)S(1)}, u32[]{:S(2)}, u32[]{:S(2)}) collective-permute-start(f32[16,16,128]{2,1,0:T(8,128)S(1)} %slice.8), channel_id=1, source_target_pairs={{0,16},{16,0},{1,17},{17,1},{2,18},{18,2},{3,19},{19,3},{4,20},{20... | collective-permute-start | bytes 393224 | tf_op jit(solution)/shard_map/ppermute | solution.py:577
  59.3 5.3 %first_vector.1 = (bf16[4096,256]{1,0:T(8,128)(2,1)S(1)}, bf16[4096,256]{1,0:T(8,128)(2,1)S(1)}, bf16[256,4096]{1,0:T(8,128)(2,1)S(1)}, bf16[256,4096]{1,0:T(8,1...) custom-call(s32[3]{0:T(128)S(1)} %pad_add_fusion.ids, s32[8]{0:T(128)S(1)} %copy-done.5, ...), custom_call_target="tpu_custom_call" | custom-call | flops 1700000000 | bytes 12000000 | tf_op jit(solution)/shard_map/first_vector/pallas_call | solution.py:326
  64.6 1.3 %copy-done = bf16[256,4096]{1,0:T(8,128)(2,1)} copy-done((bf16[256,4096]{1,0:T(8,128)(2,1)}, bf16[256,4096]{1,0:T(8,128)(2,1)S(1)}, u32[]{:S(2)}) %copy-start) | copy-done | bytes 2097176
  65.9 1.4 %copy-done.1 = bf16[256,4096]{1,0:T(8,128)(2,1)} copy-done((bf16[256,4096]{1,0:T(8,128)(2,1)}, bf16[256,4096]{1,0:T(8,128)(2,1)S(1)}, u32[]{:S(2)}) %copy-start.1) | copy-done | bytes 2097176
  67.3 1.4 %copy-done.8 = bf16[4096,256]{1,0:T(8,128)(2,1)} copy-done((bf16[4096,256]{1,0:T(8,128)(2,1)}, bf16[4096,256]{1,0:T(8,128)(2,1)S(1)}, u32[]{:S(2)}) %copy-start.8) | copy-done | bytes 2097176
  68.7 1.3 %copy-done.10 = bf16[4096,256]{1,0:T(8,128)(2,1)} copy-done((bf16[4096,256]{1,0:T(8,128)(2,1)}, bf16[4096,256]{1,0:T(8,128)(2,1)S(1)}, u32[]{:S(2)}) %copy-start.10) | copy-done | bytes 2097176
  70.1 11.9 %all-to-all-done.arrived = f32[16,264,128]{2,1,0:T(8,128)S(1)} async-done(((f32[16,264,128]{2,1,0:T(8,128)}), f32[16,264,128]{2,1,0:T(8,128)S(1)}, u32[]{:S(2)}, u32[]{:S(2)}) %all-to-all-start) | async-done | bytes 2162720 | tf_op jit(solution)/shard_map/all_to_all | solution.py:581
  82.0 4.2 %image_one.1 = (bf16[4096,256]{1,0:T(8,128)(2,1)S(1)}, bf16[4096,256]{1,0:T(8,128)(2,1)S(1)}, f32[256,256]{1,0:T(8,128)S(1)}) custom-call(f32[16,264,128]{2,1,0:T(8,128)S(1)} %all-to-all-done.arrived, bf16[256,4096]{1,0:T(8,128)(2,1)} %copy-done, bf16[256,4096]{1,0:T(8,128)(2,1)} %copy-done.1), custom_call_target="tpu_custom_call" | custom-call | flops 1700000000 | bytes 10000000 | tf_op jit(solution)/shard_map/image_one/pallas_call | solution.py:366
  86.3 5.7 %collective-permute-start.11 = (f32[256,256]{1,0:T(8,128)S(1)}, f32[256,256]{1,0:T(8,128)S(1)}, u32[]{:S(2)}, u32[]{:S(2)}) collective-permute-start(f32[256,256]{1,0:T(8,128)S(1)} %get-tuple-element.36.part_a), channel_id=1, source_target_pairs={{0,16},{16,0},{1,17},{17,1},{2,18},{18,2},{3,19},{19,3},{4,20},{20... | collective-permute-start | bytes 786440 | tf_op jit(solution)/shard_map/ppermute | solution.py:584
  93.1 4.7 %image_two.1 = (f32[256,256]{1,0:T(8,128)S(1)}, f32[256,256]{1,0:T(8,128)S(1)}, f32[8,128]{1,0:T(8,128)S(1)}) custom-call(s32[3]{0:T(128)S(1)} %pad_add_fusion.ids, s32[8]{0:T(128)S(1)} %copy-done.5, s32[8]{0:T(128)S(1)} %collective-permute-done.1.rsector_other, s32[64]{0:T(128)S(1)} %copy-done.4, s32[32]{0:T(128)S(1)} %copy-done.6, s32[8]{0:T(128)S(1)} %copy-done.7, ...), custom_call_target="tpu_custom_call" | custom-call | flops 3300000000 | bytes 9000000 | tf_op jit(solution)/shard_map/image_two/pallas_call | solution.py:418
  98.2 1.2 collective-permute-done.12.part_b
  99.4 5.6 %image_three.1 = f32[16,40,128]{2,1,0:T(8,128)} custom-call(s32[3]{0:T(128)S(1)} %pad_add_fusion.ids, s32[8]{0:T(128)S(1)} %copy-done.5, s32[8]{0:T(128)S(1)} %collective-permute-done.1.rsector_other, s32[64]{0:T(128)S(1)} %copy-done.4, s32[32]{0:T(128)S(1)} %copy-done.6, s32[8]{0:T(128)S(1)} %copy-done.7, f32[256,256]{1,0:T(8,128)S(1)} %get-tuple-element.43.part_a, ...), custom_call_target="tpu_custom_call" | custom-call | flops 3300000000 | bytes 9000000 | tf_op jit(solution)/shard_map/image_three/pallas_call | solution.py:454
  105.0 3.7 %all-to-all-start.2 = ((f32[16,40,128]{2,1,0:T(8,128)}), f32[16,40,128]{2,1,0:T(8,128)S(1)}, u32[]{:S(2)}, u32[]{:S(2)}) async-start(f32[16,40,128]{2,1,0:T(8,128)} %image_three.1), calls=%async_computation.2 | async-start | bytes 655360 | tf_op jit(solution)/shard_map/all_to_all | solution.py:587
  108.7 7.9 %all-to-all-done.2.got = f32[16,40,128]{2,1,0:T(8,128)S(1)} async-done(((f32[16,40,128]{2,1,0:T(8,128)}), f32[16,40,128]{2,1,0:T(8,128)S(1)}, u32[]{:S(2)}, u32[]{:S(2)}) %all-to-all-start.2) | async-done | bytes 327712 | tf_op jit(solution)/shard_map/all_to_all | solution.py:587
  116.7 3.3 %collective-permute-start.15 = (f32[16,128]{1,0:T(8,128)S(1)}, f32[16,128]{1,0:T(8,128)S(1)}, u32[]{:S(2)}, u32[]{:S(2)}) collective-permute-start(f32[16,128]{1,0:T(8,128)S(1)} %bitcast.10), channel_id=1, source_target_pairs={{0,96},{32,0},{64,32},{96,64},{1,97},{33,1},{65,33},{97,65},{2,98}... | collective-permute-start | bytes 24584 | tf_op jit(solution)/shard_map/ppermute | solution.py:590
  120.7 2.8 %collective-permute-start.17 = (f32[8,32,128]{2,1,0:T(8,128)S(1)}, f32[8,32,128]{2,1,0:T(8,128)S(1)}, u32[]{:S(2)}, u32[]{:S(2)}) collective-permute-start(f32[8,32,128]{2,1,0:T(8,128)S(1)} %constant_dynamic-slice_fusion), channel_id=1, source_target_pairs={{0,16},{16,0},{1,17},{17,1},{2,18},{18,2},{3,19},{19,3},{4,20},{20... | collective-permute-start | bytes 393224 | tf_op jit(solution)/shard_map/ppermute | solution.py:593
  124.0 3.6 %collective-permute-start.16 = (f32[64,128]{1,0:T(8,128)S(1)}, f32[64,128]{1,0:T(8,128)S(1)}, u32[]{:S(2)}, u32[]{:S(2)}) collective-permute-start(f32[64,128]{1,0:T(8,128)S(1)} %pad_maximum_fusion.own_stats), channel_id=1, source_target_pairs={{0,16},{16,0},{1,17},{17,1},{2,18},{18,2},{3,19},{19,3},{4,20},{20... | collective-permute-start | bytes 98312 | tf_op jit(solution)/shard_map/ppermute | solution.py:595
  128.5 2.2 %finish.1 = (f32[8,16,256]{2,1,0:T(8,128)}, f32[1,1]{1,0:T(1,128)}) custom-call(s32[3]{0:T(128)S(1)} %pad_add_fusion.ids, s32[64]{0:T(128)S(1)} %copy-done.4, s32[8]{0:T(128)S(1)} %copy-done.5, s32[32]{0:T(128)S(1)} %copy-done.6, s32[8]{0:T(128)S(1)} %copy-done.7, f32[64,128]{1,0:T(8,128)S(1)} %pad_maximum_fusion.own_stats, ...), custom_call_target="tpu_custom_call" | custom-call | tf_op jit(solution)/shard_map/finish/pallas_call | solution.py:535
  (51 shorter events, 9.1 us)
Async XLA Ops:
  0.7 4.5 %copy-start.3 = (f32[8,256,16]{1,2,0:T(8,128)S(1)}, f32[8,256,16]{1,2,0:T(8,128)}, u32[]{:S(2)}) copy-start(f32[8,256,16]{1,2,0:T(8,128)} %param.8) | copy-start | bytes 393220
  0.7 4.6 %copy-start.5 = (s32[8]{0:T(128)S(1)}, s32[8]{0:T(128)}, u32[]{:S(2)}) copy-start(s32[8]{0:T(128)} %rsector.9) | copy-start | bytes 100
  0.7 5.0 %copy-start.12 = (s32[8,2]{0,1:T(2,128)S(1)}, s32[8,2]{0,1:T(2,128)}, u32[]{:S(2)}) copy-start(s32[8,2]{0,1:T(2,128)} %param.13) | copy-start | bytes 196
  3.7 3.6 %collective-permute-start = (f32[4,264,128]{2,1,0:T(8,128)}, f32[4,264,128]{2,1,0:T(8,128)S(1)}, u32[]{:S(2)}, u32[]{:S(2)}) collective-permute-start(f32[4,264,128]{2,1,0:T(8,128)} %get-tuple-element.25), channel_id=1, source_target_pairs={{0,16},{16,0},{1,17},{17,1},{2,18},{18,2},{3,19},{19,3},{4,20},{20... | collective-permute-start | bytes 1622024 | tf_op jit(solution)/shard_map/ppermute | solution.py:561
  5.2 2.1 %collective-permute-start.3 = (f32[8,16,256]{2,1,0:T(8,128)S(1)}, f32[8,16,256]{2,1,0:T(8,128)S(1)}, u32[]{:S(2)}, u32[]{:S(2)}) collective-permute-start(f32[8,16,256]{2,1,0:T(8,128)S(1)} %bitcast.7), channel_id=1, source_target_pairs={{0,16},{16,0},{1,17},{17,1},{2,18},{18,2},{3,19},{19,3},{4,20},{20... | collective-permute-start | bytes 393224 | tf_op jit(solution)/shard_map/ppermute | solution.py:558
  5.3 2.0 %collective-permute-start.1 = (s32[8]{0:T(128)S(1)}, s32[8]{0:T(128)S(1)}, u32[]{:S(2)}, u32[]{:S(2)}) collective-permute-start(s32[8]{0:T(128)S(1)} %copy-done.5), channel_id=1, source_target_pairs={{0,16},{16,0},{1,17},{17,1},{2,18},{18,2},{3,19},{19,3},{4,20},{20... | collective-permute-start | bytes 104 | tf_op jit(solution)/shard_map/ppermute | solution.py:556
  5.8 1.5 %collective-permute-start.2 = (s32[8,2]{1,0:T(8,128)S(1)}, s32[8,2]{1,0:T(8,128)S(1)}, u32[]{:S(2)}, u32[]{:S(2)}) collective-permute-start(s32[8,2]{1,0:T(8,128)S(1)} %copy.11.on), channel_id=1, source_target_pairs={{0,16},{16,0},{1,17},{17,1},{2,18},{18,2},{3,19},{19,3},{4,20},{20... | collective-permute-start | bytes 200 | tf_op jit(solution)/shard_map/ppermute | solution.py:557
  5.9 15.3 %collective-permute-start.4 = (f32[4,264,128]{2,1,0:T(8,128)}, f32[4,264,128]{2,1,0:T(8,128)S(1)}, u32[]{:S(2)}, u32[]{:S(2)}) collective-permute-start(f32[4,264,128]{2,1,0:T(8,128)} %get-tuple-element.27.mine), channel_id=1, source_target_pairs={{0,32},{32,64},{64,96},{96,0},{1,33},{33,65},{65,97},{97,1},{2,34}... | collective-permute-start | bytes 1622024 | tf_op jit(solution)/shard_map/ppermute | solution.py:565
  9.4 10.2 %copy-start.2 = (f32[4,264,128]{2,1,0:T(8,128)S(1)}, f32[4,264,128]{2,1,0:T(8,128)}, u32[]{:S(2)}) copy-start(f32[4,264,128]{2,1,0:T(8,128)} %get-tuple-element.27.mine) | copy-start | bytes 1622020
  9.5 25.4 %copy-start.4 = (s32[64]{0:T(128)S(1)}, s32[64]{0:T(128)}, u32[]{:S(2)}) copy-start(s32[64]{0:T(128)} %sector.7) | copy-start | bytes 772
  9.5 13.8 %collective-permute-start.6 = (f32[4,264,128]{2,1,0:T(8,128)S(1)}, f32[4,264,128]{2,1,0:T(8,128)S(1)}, u32[]{:S(2)}, u32[]{:S(2)}) collective-permute-start(f32[4,264,128]{2,1,0:T(8,128)S(1)} %collective-permute-done.theirs), channel_id=1, source_target_pairs={{0,96},{32,0},{64,32},{96,64},{1,97},{33,1},{65,33},{97,65},{2,98}... | collective-permute-start | bytes 1622024 | tf_op jit(solution)/shard_map/ppermute | solution.py:573
  12.0 38.7 %all-to-all-start.1 = ((f32[16,280,128]{2,1,0:T(8,128)}), f32[16,280,128]{2,1,0:T(8,128)}, u32[]{:S(2)}, u32[]{:S(2)}) async-start(f32[16,280,128]{2,1,0:T(8,128)} %right_slots.1), calls=%async_computation.1 | async-start | bytes 4587520 | tf_op jit(solution)/shard_map/all_to_all | solution.py:575
  19.7 15.2 %collective-permute-start.8 = (f32[4,264,128]{2,1,0:T(8,128)S(1)}, f32[4,264,128]{2,1,0:T(8,128)S(1)}, u32[]{:S(2)}, u32[]{:S(2)}) collective-permute-start(f32[4,264,128]{2,1,0:T(8,128)S(1)} %copy-done.2), channel_id=1, source_target_pairs={{0,96},{32,0},{64,32},{96,64},{1,97},{33,1},{65,33},{97,65},{2,98}... | collective-permute-start | bytes 1622024 | tf_op jit(solution)/shard_map/ppermute | solution.py:566
  20.2 14.7 %collective-permute-start.9 = (f32[4,264,128]{2,1,0:T(8,128)S(1)}, f32[4,264,128]{2,1,0:T(8,128)S(1)}, u32[]{:S(2)}, u32[]{:S(2)}) collective-permute-start(f32[4,264,128]{2,1,0:T(8,128)S(1)} %collective-permute-done.theirs), channel_id=1, source_target_pairs={{0,32},{32,64},{64,96},{96,0},{1,33},{33,65},{65,97},{97,1},{2,34}... | collective-permute-start | bytes 1622024 | tf_op jit(solution)/shard_map/ppermute | solution.py:572
  21.2 24.2 %collective-permute-start.5 = (f32[4,264,128]{2,1,0:T(8,128)S(1)}, f32[4,264,128]{2,1,0:T(8,128)S(1)}, u32[]{:S(2)}, u32[]{:S(2)}) collective-permute-start(f32[4,264,128]{2,1,0:T(8,128)S(1)} %collective-permute-done.4.below_a), channel_id=1, source_target_pairs={{0,32},{32,64},{64,96},{96,0},{1,33},{33,65},{65,97},{97,1},{2,34}... | collective-permute-start | bytes 1622024 | tf_op jit(solution)/shard_map/ppermute | solution.py:574
  23.3 23.2 %collective-permute-start.7 = (f32[4,264,128]{2,1,0:T(8,128)S(1)}, f32[4,264,128]{2,1,0:T(8,128)S(1)}, u32[]{:S(2)}, u32[]{:S(2)}) collective-permute-start(f32[4,264,128]{2,1,0:T(8,128)S(1)} %collective-permute-done.6.above_b), channel_id=1, source_target_pairs={{0,96},{32,0},{64,32},{96,64},{1,97},{33,1},{65,33},{97,65},{2,98}... | collective-permute-start | bytes 1622024 | tf_op jit(solution)/shard_map/ppermute | solution.py:574
  48.1 11.1 %copy-start.6 = (s32[32]{0:T(128)S(1)}, s32[32]{0:T(128)}, u32[]{:S(2)}) copy-start(s32[32]{0:T(128)} %lsize.7) | copy-start | bytes 388
  48.1 11.1 %copy-start.7 = (s32[8]{0:T(128)S(1)}, s32[8]{0:T(128)}, u32[]{:S(2)}) copy-start(s32[8]{0:T(128)} %rsize.7) | copy-start | bytes 100
  50.7 31.3 %all-to-all-start = ((f32[16,264,128]{2,1,0:T(8,128)}), f32[16,264,128]{2,1,0:T(8,128)S(1)}, u32[]{:S(2)}, u32[]{:S(2)}) async-start(f32[16,264,128]{2,1,0:T(8,128)} %far_slots.1), calls=%async_computation | async-start | bytes 4325376 | tf_op jit(solution)/shard_map/all_to_all | solution.py:581
  56.7 2.6 %collective-permute-start.10 = (f32[16,16,128]{2,1,0:T(8,128)S(1)}, f32[16,16,128]{2,1,0:T(8,128)S(1)}, u32[]{:S(2)}, u32[]{:S(2)}) collective-permute-start(f32[16,16,128]{2,1,0:T(8,128)S(1)} %slice.8), channel_id=1, source_target_pairs={{0,16},{16,0},{1,17},{17,1},{2,18},{18,2},{3,19},{19,3},{4,20},{20... | collective-permute-start | bytes 393224 | tf_op jit(solution)/shard_map/ppermute | solution.py:577
  65.9 1.4 %copy-start.1 = (bf16[256,4096]{1,0:T(8,128)(2,1)}, bf16[256,4096]{1,0:T(8,128)(2,1)S(1)}, u32[]{:S(2)}) copy-start(bf16[256,4096]{1,0:T(8,128)(2,1)S(1)} %get-tuple-element.35.m_lo) | copy-start | bytes 6291460
  67.3 1.4 %copy-start.8 = (bf16[4096,256]{1,0:T(8,128)(2,1)}, bf16[4096,256]{1,0:T(8,128)(2,1)S(1)}, u32[]{:S(2)}) copy-start(bf16[4096,256]{1,0:T(8,128)(2,1)S(1)} %get-tuple-element.39.r_hi) | copy-start | bytes 6291460
  82.0 11.1 %copy-start.9 = (bf16[4096,256]{1,0:T(8,128)(2,1)S(1)}, bf16[4096,256]{1,0:T(8,128)(2,1)}, u32[]{:S(2)}) copy-start(bf16[4096,256]{1,0:T(8,128)(2,1)} %copy-done.8) | copy-start | bytes 6291460
  82.0 11.1 %copy-start.11 = (bf16[4096,256]{1,0:T(8,128)(2,1)S(1)}, bf16[4096,256]{1,0:T(8,128)(2,1)}, u32[]{:S(2)}) copy-start(bf16[4096,256]{1,0:T(8,128)(2,1)} %copy-done.10) | copy-start | bytes 6291460
  86.3 6.8 %collective-permute-start.11 = (f32[256,256]{1,0:T(8,128)S(1)}, f32[256,256]{1,0:T(8,128)S(1)}, u32[]{:S(2)}, u32[]{:S(2)}) collective-permute-start(f32[256,256]{1,0:T(8,128)S(1)} %get-tuple-element.36.part_a), channel_id=1, source_target_pairs={{0,16},{16,0},{1,17},{17,1},{2,18},{18,2},{3,19},{19,3},{4,20},{20... | collective-permute-start | bytes 786440 | tf_op jit(solution)/shard_map/ppermute | solution.py:584
  97.8 1.6 %collective-permute-start.12 = (f32[256,256]{1,0:T(8,128)S(1)}, f32[256,256]{1,0:T(8,128)S(1)}, u32[]{:S(2)}, u32[]{:S(2)}) collective-permute-start(f32[256,256]{1,0:T(8,128)S(1)} %get-tuple-element.43.part_a), channel_id=1, source_target_pairs={{0,16},{16,0},{1,17},{17,1},{2,18},{18,2},{3,19},{19,3},{4,20},{20... | collective-permute-start | bytes 786440 | tf_op jit(solution)/shard_map/ppermute | solution.py:585
  105.0 11.6 %all-to-all-start.2 = ((f32[16,40,128]{2,1,0:T(8,128)}), f32[16,40,128]{2,1,0:T(8,128)S(1)}, u32[]{:S(2)}, u32[]{:S(2)}) async-start(f32[16,40,128]{2,1,0:T(8,128)} %image_three.1), calls=%async_computation.2 | async-start | bytes 655360 | tf_op jit(solution)/shard_map/all_to_all | solution.py:587
  116.7 6.8 %collective-permute-start.15 = (f32[16,128]{1,0:T(8,128)S(1)}, f32[16,128]{1,0:T(8,128)S(1)}, u32[]{:S(2)}, u32[]{:S(2)}) collective-permute-start(f32[16,128]{1,0:T(8,128)S(1)} %bitcast.10), channel_id=1, source_target_pairs={{0,96},{32,0},{64,32},{96,64},{1,97},{33,1},{65,33},{97,65},{2,98}... | collective-permute-start | bytes 24584 | tf_op jit(solution)/shard_map/ppermute | solution.py:590
  120.0 4.0 %collective-permute-start.14 = (f32[16,128]{1,0:T(8,128)S(1)}, f32[16,128]{1,0:T(8,128)S(1)}, u32[]{:S(2)}, u32[]{:S(2)}) collective-permute-start(f32[16,128]{1,0:T(8,128)S(1)} %bitcast.11), channel_id=1, source_target_pairs={{0,64},{32,96},{64,0},{96,32},{1,65},{33,97},{65,1},{97,33},{2,66}... | collective-permute-start | bytes 24584 | tf_op jit(solution)/shard_map/ppermute | solution.py:590
  120.0 4.0 %collective-permute-start.13 = (f32[16,128]{1,0:T(8,128)S(1)}, f32[16,128]{1,0:T(8,128)S(1)}, u32[]{:S(2)}, u32[]{:S(2)}) collective-permute-start(f32[16,128]{1,0:T(8,128)S(1)} %bitcast.12), channel_id=1, source_target_pairs={{0,32},{32,64},{64,96},{96,0},{1,33},{33,65},{65,97},{97,1},{2,34}... | collective-permute-start | bytes 24584 | tf_op jit(solution)/shard_map/ppermute | solution.py:590
  120.7 7.8 %collective-permute-start.17 = (f32[8,32,128]{2,1,0:T(8,128)S(1)}, f32[8,32,128]{2,1,0:T(8,128)S(1)}, u32[]{:S(2)}, u32[]{:S(2)}) collective-permute-start(f32[8,32,128]{2,1,0:T(8,128)S(1)} %constant_dynamic-slice_fusion), channel_id=1, source_target_pairs={{0,16},{16,0},{1,17},{17,1},{2,18},{18,2},{3,19},{19,3},{4,20},{20... | collective-permute-start | bytes 393224 | tf_op jit(solution)/shard_map/ppermute | solution.py:593
  124.0 4.5 %collective-permute-start.16 = (f32[64,128]{1,0:T(8,128)S(1)}, f32[64,128]{1,0:T(8,128)S(1)}, u32[]{:S(2)}, u32[]{:S(2)}) collective-permute-start(f32[64,128]{1,0:T(8,128)S(1)} %pad_maximum_fusion.own_stats), channel_id=1, source_target_pairs={{0,16},{16,0},{1,17},{17,1},{2,18},{18,2},{3,19},{19,3},{4,20},{20... | collective-permute-start | bytes 98312 | tf_op jit(solution)/shard_map/ppermute | solution.py:595
  (2 other events, 2.7 us)

commit v17 on v14

--- a/solution.py
+++ b/solution.py
@@ -7,7 +7,7 @@
 
 ITERS = 2
 LEFT_FLOPS = 15_000_000_000
-NEAR_FLOPS = 1_000_000_000
+NEAR_FLOPS = 3_000_000_000
 TILE = 256
 HALF = 128
 TERMS = 16

time: 129 us -> 130 us (level)
  waiting for transfers between devices: 45.8 us -> 42.5 us
  starting transfers between devices: 44.8 us -> 48 us
    all_to_all x1, starting transfers between devices: 3.72 us -> 5.87 us  [local(): left_arrived = lax.all_to_all(left_sent, COL, 0, 0, tiled=True)]
    ppermute x3, starting transfers between devices: 3.36 us -> 1.8 us  [local(): lax.ppermute(plane_stats, 'y', [(i, (i + k) % 4) for i in range(4)])]
  transfers between devices with their start and end apart: 21 -> 21, of which waited for: 11 -> 12; matrix products, arithmetic and copies ran while one was open for 1% -> 1% of each run, Pallas kernels for 8% -> 9%
where the time goes in v17:
time: 130 us; the launch traced here: 129 us
  starting transfers between devices  48 us (37%)
  waiting for transfers between devices  42.5 us (33%)
  Pallas kernels  31.4 us (24%)
  local copies, waits for them, and re-layouts  6.49 us (5%)
    all_to_all x1, waiting for transfers between devices, local(): left_arrived = lax.all_to_all(left_sent, COL, 0, 0, tiled=True)  9.24 us
    ppermute x2, waiting for transfers between devices, local(): far = [lax.ppermute(below[0], 'y', UP), lax.ppermute(above[1], 'y', DOWN)]  8.95 us
    ppermute x2, waiting for transfers between devices, local(): above = [lax.ppermute(x, 'y', DOWN) for x in (mine, theirs)]  8.28 us
    all_to_all x1, waiting for transfers between devices, local(): got = lax.all_to_all(sent, COL, 0, 0, tiled=True)  7.94 us
    all_to_all x1, starting transfers between devices, local(): arrived = lax.all_to_all(slots, COL, 0, 0, tiled=True)  7.79 us
    ppermute x2, starting transfers between devices, local(): lax.ppermute(part, 'c', SWAP)  6.95 us
    all_to_all x1, starting transfers between devices, local(): left_arrived = lax.all_to_all(left_sent, COL, 0, 0, tiled=True)  5.87 us
    pallas_call x1, Pallas kernels, image_three(): pl.pallas_call(image_three_body, in_specs=[smem()] * 6 + [vmem()] * 9, ou...  5.63 us
  transfers between devices with their start and end apart: 21, of which 12 were waited for; matrix products, arithmetic and copies ran while one was open for 1% of the time, Pallas kernels for 9%

profile of v17, /device:TPU:1, one launch (start us, length us, event | category | flops | bytes accessed | tf_op | source)
XLA Modules:
  0.0 129.4 jit_solution(17306032051316446309)
XLA Ops:
  0.7 3.0 %fold.1 = (f32[4,264,128]{2,1,0:T(8,128)}, f32[4,264,128]{2,1,0:T(8,128)}, f32[9,264,128]{2,1,0:T(8,128)S(1)}) custom-call(s32[3]{0:T(128)S(1)} %pad_add_fusion.ids, f32[4,2,256,256]{3,2,1,0:T(8,128)} %left_env.1, f32[8,2,256,256]{3,2,1,0:T(8,128)} %right_env.1), custom_call_target="tpu_custom_call" | custom-call | flops 1000000 | bytes 6000000 | tf_op jit(solution)/shard_map/fold/pallas_call | solution.py:146
  3.7 1.5 %collective-permute-start = (f32[4,264,128]{2,1,0:T(8,128)}, f32[4,264,128]{2,1,0:T(8,128)S(1)}, u32[]{:S(2)}, u32[]{:S(2)}) collective-permute-start(f32[4,264,128]{2,1,0:T(8,128)} %get-tuple-element.24), channel_id=1, source_target_pairs={{0,16},{16,0},{1,17},{17,1},{2,18},{18,2},{3,19},{19,3},{4,20},{20... | collective-permute-start | bytes 1622024 | tf_op jit(solution)/shard_map/ppermute | solution.py:561
  5.9 1.4 %collective-permute-start.4 = (f32[4,264,128]{2,1,0:T(8,128)}, f32[4,264,128]{2,1,0:T(8,128)S(1)}, u32[]{:S(2)}, u32[]{:S(2)}) collective-permute-start(f32[4,264,128]{2,1,0:T(8,128)} %get-tuple-element.26.mine), channel_id=1, source_target_pairs={{0,32},{32,64},{64,96},{96,0},{1,33},{33,65},{65,97},{97,1},{2,34}... | collective-permute-start | bytes 1622024 | tf_op jit(solution)/shard_map/ppermute | solution.py:565
  7.3 2.5 %collective-permute-start.6 = (f32[4,264,128]{2,1,0:T(8,128)S(1)}, f32[4,264,128]{2,1,0:T(8,128)S(1)}, u32[]{:S(2)}, u32[]{:S(2)}) collective-permute-start(f32[4,264,128]{2,1,0:T(8,128)S(1)} %collective-permute-done.theirs), channel_id=1, source_target_pairs={{0,96},{32,0},{64,32},{96,64},{1,97},{33,1},{65,33},{97,65},{2,98}... | collective-permute-start | bytes 1622024 | tf_op jit(solution)/shard_map/ppermute | solution.py:566
  11.3 2.1 %right_slots.1 = f32[16,280,128]{2,1,0:T(8,128)} custom-call(s32[3]{0:T(128)S(1)} %pad_add_fusion.ids, s32[8]{0:T(128)S(1)} %copy-done.3, s32[8]{0:T(128)S(1)} %collective-permute-done.1.rsector_other, s32[8,2]{1,0:T(8,128)S(1)} %copy.11.on, s32[8,2]{1,0:T(8,128)S(1)} %collective-permute-done.2.on_other, f32[8,16,256]{2,1,0:T(8,128)S(1)} %bitcast.8, ...), custom_call_target="tpu_custom_call" | custom-call | flops 4000000 | bytes 6000000 | tf_op jit(solution)/shard_map/right_slots/pallas_call | solution.py:188
  13.5 7.8 %all-to-all-start.1 = ((f32[16,280,128]{2,1,0:T(8,128)}), f32[16,280,128]{2,1,0:T(8,128)}, u32[]{:S(2)}, u32[]{:S(2)}) async-start(f32[16,280,128]{2,1,0:T(8,128)} %right_slots.1), calls=%async_computation.1 | async-start | bytes 4587520 | tf_op jit(solution)/shard_map/all_to_all | solution.py:573
  21.4 3.2 %collective-permute-start.7 = (f32[4,264,128]{2,1,0:T(8,128)S(1)}, f32[4,264,128]{2,1,0:T(8,128)S(1)}, u32[]{:S(2)}, u32[]{:S(2)}) collective-permute-start(f32[4,264,128]{2,1,0:T(8,128)S(1)} %collective-permute-done.6.above_b), channel_id=1, source_target_pairs={{0,96},{32,0},{64,32},{96,64},{1,97},{33,1},{65,33},{97,65},{2,98}... | collective-permute-start | bytes 1622024 | tf_op jit(solution)/shard_map/ppermute | solution.py:567
  24.6 8.3 %collective-permute-done.8.above_a = f32[4,264,128]{2,1,0:T(8,128)} collective-permute-done((f32[4,264,128]{2,1,0:T(8,128)}, f32[4,264,128]{2,1,0:T(8,128)}, u32[]{:S(2)}, u32[]{:S(2)}) %collective-permute-start.8) | collective-permute-done | bytes 540704 | tf_op jit(solution)/shard_map/ppermute | solution.py:566
  32.8 2.5 %near_slots.1.near = f32[16,264,128]{2,1,0:T(8,128)} custom-call(s32[3]{0:T(128)S(1)} %pad_add_fusion.ids, s32[64]{0:T(128)S(1)} %copy-done.4, f32[4,264,128]{2,1,0:T(8,128)S(1)} %copy-done.7, f32[4,264,128]{2,1,0:T(8,128)S(1)} %collective-permute-done.theirs, f32[4,264,128]{2,1,0:T(8,128)} %collective-permute-done.8.above_a, ...), custom_call_target="tpu_custom_call" | custom-call | flops 3000000000 | bytes 4000000 | tf_op jit(solution)/shard_map/near_slots/pallas_call | solution.py:255
  35.4 8.9 %collective-permute-done.5.far_a = f32[4,264,128]{2,1,0:T(8,128)S(1)} collective-permute-done((f32[4,264,128]{2,1,0:T(8,128)S(1)}, f32[4,264,128]{2,1,0:T(8,128)S(1)}, u32[]{:S(2)}, u32[]{:S(2)}) %collective-permute-start.5) | collective-permute-done | bytes 540704 | tf_op jit(solution)/shard_map/ppermute | solution.py:567
  44.3 1.6 %far_slots.1 = f32[16,264,128]{2,1,0:T(8,128)} custom-call(s32[3]{0:T(128)S(1)} %pad_add_fusion.ids, s32[64]{0:T(128)S(1)} %copy-done.4, f32[4,264,128]{2,1,0:T(8,128)S(1)} %collective-permute-done.5.far_a, f32[4,264,128]{2,1,0:T(8,128)S(1)} %collective-permute-done.7.far_b, f32[16,264,128]{2,1,0:T(8,128)} %near_slots.1.near), custom_call_target="tpu_custom_call", output_to_operand_aliasing={{}: (4, {})} | custom-call | flops 15000000512 | bytes 4000000 | tf_op jit(solution)/shard_map/far_slots/pallas_call | solution.py:265
  46.0 3.0 %all-to-all-done.1.slots = f32[16,280,128]{2,1,0:T(8,128)} async-done(((f32[16,280,128]{2,1,0:T(8,128)}), f32[16,280,128]{2,1,0:T(8,128)}, u32[]{:S(2)}, u32[]{:S(2)}) %all-to-all-start.1) | async-done | bytes 2293792 | tf_op jit(solution)/shard_map/all_to_all | solution.py:573
  49.0 5.9 %all-to-all-start = ((f32[16,264,128]{2,1,0:T(8,128)}), f32[16,264,128]{2,1,0:T(8,128)S(1)}, u32[]{:S(2)}, u32[]{:S(2)}) async-start(f32[16,264,128]{2,1,0:T(8,128)} %far_slots.1), calls=%async_computation | async-start | bytes 4325376 | tf_op jit(solution)/shard_map/all_to_all | solution.py:579
  55.8 3.8 %collective-permute-start.10 = (f32[16,16,128]{2,1,0:T(8,128)S(1)}, f32[16,16,128]{2,1,0:T(8,128)S(1)}, u32[]{:S(2)}, u32[]{:S(2)}) collective-permute-start(f32[16,16,128]{2,1,0:T(8,128)S(1)} %slice.8), channel_id=1, source_target_pairs={{0,16},{16,0},{1,17},{17,1},{2,18},{18,2},{3,19},{19,3},{4,20},{20... | collective-permute-start | bytes 393224 | tf_op jit(solution)/shard_map/ppermute | solution.py:575
  60.6 5.3 %first_vector.1 = (bf16[4096,256]{1,0:T(8,128)(2,1)S(1)}, bf16[4096,256]{1,0:T(8,128)(2,1)S(1)}, bf16[256,4096]{1,0:T(8,128)(2,1)S(1)}, bf16[256,4096]{1,0:T(8,1...) custom-call(s32[3]{0:T(128)S(1)} %pad_add_fusion.ids, s32[8]{0:T(128)S(1)} %copy-done.3, ...), custom_call_target="tpu_custom_call" | custom-call | flops 1700000000 | bytes 12000000 | tf_op jit(solution)/shard_map/first_vector/pallas_call | solution.py:326
  65.9 1.3 %copy-done = bf16[256,4096]{1,0:T(8,128)(2,1)} copy-done((bf16[256,4096]{1,0:T(8,128)(2,1)}, bf16[256,4096]{1,0:T(8,128)(2,1)S(1)}, u32[]{:S(2)}) %copy-start) | copy-done | bytes 2097176
  67.2 1.4 %copy-done.1 = bf16[256,4096]{1,0:T(8,128)(2,1)} copy-done((bf16[256,4096]{1,0:T(8,128)(2,1)}, bf16[256,4096]{1,0:T(8,128)(2,1)S(1)}, u32[]{:S(2)}) %copy-start.1) | copy-done | bytes 2097176
  68.6 1.4 %copy-done.8 = bf16[4096,256]{1,0:T(8,128)(2,1)} copy-done((bf16[4096,256]{1,0:T(8,128)(2,1)}, bf16[4096,256]{1,0:T(8,128)(2,1)S(1)}, u32[]{:S(2)}) %copy-start.8) | copy-done | bytes 2097176
  70.0 1.3 %copy-done.10 = bf16[4096,256]{1,0:T(8,128)(2,1)} copy-done((bf16[4096,256]{1,0:T(8,128)(2,1)}, bf16[4096,256]{1,0:T(8,128)(2,1)S(1)}, u32[]{:S(2)}) %copy-start.10) | copy-done | bytes 2097176
  71.3 9.2 %all-to-all-done.arrived = f32[16,264,128]{2,1,0:T(8,128)S(1)} async-done(((f32[16,264,128]{2,1,0:T(8,128)}), f32[16,264,128]{2,1,0:T(8,128)S(1)}, u32[]{:S(2)}, u32[]{:S(2)}) %all-to-all-start) | async-done | bytes 2162720 | tf_op jit(solution)/shard_map/all_to_all | solution.py:579
  80.6 4.2 %image_one.1 = (bf16[4096,256]{1,0:T(8,128)(2,1)S(1)}, bf16[4096,256]{1,0:T(8,128)(2,1)S(1)}, f32[256,256]{1,0:T(8,128)S(1)}) custom-call(f32[16,264,128]{2,1,0:T(8,128)S(1)} %all-to-all-done.arrived, bf16[256,4096]{1,0:T(8,128)(2,1)} %copy-done, bf16[256,4096]{1,0:T(8,128)(2,1)} %copy-done.1), custom_call_target="tpu_custom_call" | custom-call | flops 1700000000 | bytes 10000000 | tf_op jit(solution)/shard_map/image_one/pallas_call | solution.py:366
  84.8 6.5 %collective-permute-start.11 = (f32[256,256]{1,0:T(8,128)S(1)}, f32[256,256]{1,0:T(8,128)S(1)}, u32[]{:S(2)}, u32[]{:S(2)}) collective-permute-start(f32[256,256]{1,0:T(8,128)S(1)} %get-tuple-element.34.part_a), channel_id=1, source_target_pairs={{0,16},{16,0},{1,17},{17,1},{2,18},{18,2},{3,19},{19,3},{4,20},{20... | collective-permute-start | bytes 786440 | tf_op jit(solution)/shard_map/ppermute | solution.py:582
  91.3 1.2 collective-permute-done.11.part_b
  92.5 4.7 %image_two.1 = (f32[256,256]{1,0:T(8,128)S(1)}, f32[256,256]{1,0:T(8,128)S(1)}, f32[8,128]{1,0:T(8,128)S(1)}) custom-call(s32[3]{0:T(128)S(1)} %pad_add_fusion.ids, s32[8]{0:T(128)S(1)} %copy-done.3, s32[8]{0:T(128)S(1)} %collective-permute-done.1.rsector_other, s32[64]{0:T(128)S(1)} %copy-done.4, s32[32]{0:T(128)S(1)} %copy-done.5, s32[8]{0:T(128)S(1)} %copy-done.6, ...), custom_call_target="tpu_custom_call" | custom-call | flops 3300000000 | bytes 9000000 | tf_op jit(solution)/shard_map/image_two/pallas_call | solution.py:418
  97.7 1.2 collective-permute-done.12.part_b
  98.8 5.6 %image_three.1 = f32[16,40,128]{2,1,0:T(8,128)} custom-call(s32[3]{0:T(128)S(1)} %pad_add_fusion.ids, s32[8]{0:T(128)S(1)} %copy-done.3, s32[8]{0:T(128)S(1)} %collective-permute-done.1.rsector_other, s32[64]{0:T(128)S(1)} %copy-done.4, s32[32]{0:T(128)S(1)} %copy-done.5, s32[8]{0:T(128)S(1)} %copy-done.6, f32[256,256]{1,0:T(8,128)S(1)} %get-tuple-element.41.part_a, ...), custom_call_target="tpu_custom_call" | custom-call | flops 3300000000 | bytes 9000000 | tf_op jit(solution)/shard_map/image_three/pallas_call | solution.py:454
  104.5 4.4 %all-to-all-start.2 = ((f32[16,40,128]{2,1,0:T(8,128)}), f32[16,40,128]{2,1,0:T(8,128)S(1)}, u32[]{:S(2)}, u32[]{:S(2)}) async-start(f32[16,40,128]{2,1,0:T(8,128)} %image_three.1), calls=%async_computation.2 | async-start | bytes 655360 | tf_op jit(solution)/shard_map/all_to_all | solution.py:585
  108.8 7.9 %all-to-all-done.2.got = f32[16,40,128]{2,1,0:T(8,128)S(1)} async-done(((f32[16,40,128]{2,1,0:T(8,128)}), f32[16,40,128]{2,1,0:T(8,128)S(1)}, u32[]{:S(2)}, u32[]{:S(2)}) %all-to-all-start.2) | async-done | bytes 327712 | tf_op jit(solution)/shard_map/all_to_all | solution.py:585
  116.8 1.1 collective-permute-start.15
  118.6 2.8 %collective-permute-start.17 = (f32[8,32,128]{2,1,0:T(8,128)S(1)}, f32[8,32,128]{2,1,0:T(8,128)S(1)}, u32[]{:S(2)}, u32[]{:S(2)}) collective-permute-start(f32[8,32,128]{2,1,0:T(8,128)S(1)} %constant_dynamic-slice_fusion), channel_id=1, source_target_pairs={{0,16},{16,0},{1,17},{17,1},{2,18},{18,2},{3,19},{19,3},{4,20},{20... | collective-permute-start | bytes 393224 | tf_op jit(solution)/shard_map/ppermute | solution.py:591
  122.3 3.9 %collective-permute-start.16 = (f32[64,128]{1,0:T(8,128)S(1)}, f32[64,128]{1,0:T(8,128)S(1)}, u32[]{:S(2)}, u32[]{:S(2)}) collective-permute-start(f32[64,128]{1,0:T(8,128)S(1)} %pad_maximum_fusion.own_stats), channel_id=1, source_target_pairs={{0,16},{16,0},{1,17},{17,1},{2,18},{18,2},{3,19},{19,3},{4,20},{20... | collective-permute-start | bytes 98312 | tf_op jit(solution)/shard_map/ppermute | solution.py:593
  127.1 2.2 %finish.1 = (f32[8,16,256]{2,1,0:T(8,128)}, f32[1,1]{1,0:T(1,128)}) custom-call(s32[3]{0:T(128)S(1)} %pad_add_fusion.ids, s32[64]{0:T(128)S(1)} %copy-done.4, s32[8]{0:T(128)S(1)} %copy-done.3, s32[32]{0:T(128)S(1)} %copy-done.5, s32[8]{0:T(128)S(1)} %copy-done.6, f32[64,128]{1,0:T(8,128)S(1)} %pad_maximum_fusion.own_stats, ...), custom_call_target="tpu_custom_call" | custom-call | tf_op jit(solution)/shard_map/finish/pallas_call | solution.py:535
  (51 shorter events, 7.3 us)
Async XLA Ops:
  0.7 4.5 %copy-start.2 = (f32[8,256,16]{1,2,0:T(8,128)S(1)}, f32[8,256,16]{1,2,0:T(8,128)}, u32[]{:S(2)}) copy-start(f32[8,256,16]{1,2,0:T(8,128)} %param.8) | copy-start | bytes 393220
  0.7 4.6 %copy-start.3 = (s32[8]{0:T(128)S(1)}, s32[8]{0:T(128)}, u32[]{:S(2)}) copy-start(s32[8]{0:T(128)} %rsector.9) | copy-start | bytes 100
  0.7 5.0 %copy-start.12 = (s32[8,2]{0,1:T(2,128)S(1)}, s32[8,2]{0,1:T(2,128)}, u32[]{:S(2)}) copy-start(s32[8,2]{0,1:T(2,128)} %param.13) | copy-start | bytes 196
  3.7 3.6 %collective-permute-start = (f32[4,264,128]{2,1,0:T(8,128)}, f32[4,264,128]{2,1,0:T(8,128)S(1)}, u32[]{:S(2)}, u32[]{:S(2)}) collective-permute-start(f32[4,264,128]{2,1,0:T(8,128)} %get-tuple-element.24), channel_id=1, source_target_pairs={{0,16},{16,0},{1,17},{17,1},{2,18},{18,2},{3,19},{19,3},{4,20},{20... | collective-permute-start | bytes 1622024 | tf_op jit(solution)/shard_map/ppermute | solution.py:561
  5.2 2.1 %collective-permute-start.3 = (f32[8,16,256]{2,1,0:T(8,128)S(1)}, f32[8,16,256]{2,1,0:T(8,128)S(1)}, u32[]{:S(2)}, u32[]{:S(2)}) collective-permute-start(f32[8,16,256]{2,1,0:T(8,128)S(1)} %bitcast.7), channel_id=1, source_target_pairs={{0,16},{16,0},{1,17},{17,1},{2,18},{18,2},{3,19},{19,3},{4,20},{20... | collective-permute-start | bytes 393224 | tf_op jit(solution)/shard_map/ppermute | solution.py:558
  5.3 2.0 %collective-permute-start.1 = (s32[8]{0:T(128)S(1)}, s32[8]{0:T(128)S(1)}, u32[]{:S(2)}, u32[]{:S(2)}) collective-permute-start(s32[8]{0:T(128)S(1)} %copy-done.3), channel_id=1, source_target_pairs={{0,16},{16,0},{1,17},{17,1},{2,18},{18,2},{3,19},{19,3},{4,20},{20... | collective-permute-start | bytes 104 | tf_op jit(solution)/shard_map/ppermute | solution.py:556
  5.8 1.5 %collective-permute-start.2 = (s32[8,2]{1,0:T(8,128)S(1)}, s32[8,2]{1,0:T(8,128)S(1)}, u32[]{:S(2)}, u32[]{:S(2)}) collective-permute-start(s32[8,2]{1,0:T(8,128)S(1)} %copy.11.on), channel_id=1, source_target_pairs={{0,16},{16,0},{1,17},{17,1},{2,18},{18,2},{3,19},{19,3},{4,20},{20... | collective-permute-start | bytes 200 | tf_op jit(solution)/shard_map/ppermute | solution.py:557
  5.9 15.4 %collective-permute-start.4 = (f32[4,264,128]{2,1,0:T(8,128)}, f32[4,264,128]{2,1,0:T(8,128)S(1)}, u32[]{:S(2)}, u32[]{:S(2)}) collective-permute-start(f32[4,264,128]{2,1,0:T(8,128)} %get-tuple-element.26.mine), channel_id=1, source_target_pairs={{0,32},{32,64},{64,96},{96,0},{1,33},{33,65},{65,97},{97,1},{2,34}... | collective-permute-start | bytes 1622024 | tf_op jit(solution)/shard_map/ppermute | solution.py:565
  7.3 14.1 %collective-permute-start.6 = (f32[4,264,128]{2,1,0:T(8,128)S(1)}, f32[4,264,128]{2,1,0:T(8,128)S(1)}, u32[]{:S(2)}, u32[]{:S(2)}) collective-permute-start(f32[4,264,128]{2,1,0:T(8,128)S(1)} %collective-permute-done.theirs), channel_id=1, source_target_pairs={{0,96},{32,0},{64,32},{96,64},{1,97},{33,1},{65,33},{97,65},{2,98}... | collective-permute-start | bytes 1622024 | tf_op jit(solution)/shard_map/ppermute | solution.py:566
  9.9 23.0 %collective-permute-start.8 = (f32[4,264,128]{2,1,0:T(8,128)}, f32[4,264,128]{2,1,0:T(8,128)}, u32[]{:S(2)}, u32[]{:S(2)}) collective-permute-start(f32[4,264,128]{2,1,0:T(8,128)} %get-tuple-element.26.mine), channel_id=1, source_target_pairs={{0,96},{32,0},{64,32},{96,64},{1,97},{33,1},{65,33},{97,65},{2,98}... | collective-permute-start | bytes 1622024 | tf_op jit(solution)/shard_map/ppermute | solution.py:566
  10.3 22.5 %collective-permute-start.9 = (f32[4,264,128]{2,1,0:T(8,128)S(1)}, f32[4,264,128]{2,1,0:T(8,128)}, u32[]{:S(2)}, u32[]{:S(2)}) collective-permute-start(f32[4,264,128]{2,1,0:T(8,128)S(1)} %collective-permute-done.theirs), channel_id=1, source_target_pairs={{0,32},{32,64},{64,96},{96,0},{1,33},{33,65},{65,97},{97,1},{2,34}... | collective-permute-start | bytes 1622024 | tf_op jit(solution)/shard_map/ppermute | solution.py:565
  13.5 19.4 %copy-start.4 = (s32[64]{0:T(128)S(1)}, s32[64]{0:T(128)}, u32[]{:S(2)}) copy-start(s32[64]{0:T(128)} %sector.7) | copy-start | bytes 772
  13.5 19.4 %copy-start.7 = (f32[4,264,128]{2,1,0:T(8,128)S(1)}, f32[4,264,128]{2,1,0:T(8,128)}, u32[]{:S(2)}) copy-start(f32[4,264,128]{2,1,0:T(8,128)} %get-tuple-element.26.mine) | copy-start | bytes 1622020
  13.5 35.5 %all-to-all-start.1 = ((f32[16,280,128]{2,1,0:T(8,128)}), f32[16,280,128]{2,1,0:T(8,128)}, u32[]{:S(2)}, u32[]{:S(2)}) async-start(f32[16,280,128]{2,1,0:T(8,128)} %right_slots.1), calls=%async_computation.1 | async-start | bytes 4587520 | tf_op jit(solution)/shard_map/all_to_all | solution.py:573
  21.3 23.0 %collective-permute-start.5 = (f32[4,264,128]{2,1,0:T(8,128)S(1)}, f32[4,264,128]{2,1,0:T(8,128)S(1)}, u32[]{:S(2)}, u32[]{:S(2)}) collective-permute-start(f32[4,264,128]{2,1,0:T(8,128)S(1)} %collective-permute-done.4.below_a), channel_id=1, source_target_pairs={{0,32},{32,64},{64,96},{96,0},{1,33},{33,65},{65,97},{97,1},{2,34}... | collective-permute-start | bytes 1622024 | tf_op jit(solution)/shard_map/ppermute | solution.py:567
  21.4 22.9 %collective-permute-start.7 = (f32[4,264,128]{2,1,0:T(8,128)S(1)}, f32[4,264,128]{2,1,0:T(8,128)S(1)}, u32[]{:S(2)}, u32[]{:S(2)}) collective-permute-start(f32[4,264,128]{2,1,0:T(8,128)S(1)} %collective-permute-done.6.above_b), channel_id=1, source_target_pairs={{0,96},{32,0},{64,32},{96,64},{1,97},{33,1},{65,33},{97,65},{2,98}... | collective-permute-start | bytes 1622024 | tf_op jit(solution)/shard_map/ppermute | solution.py:567
  45.9 14.6 %copy-start.5 = (s32[32]{0:T(128)S(1)}, s32[32]{0:T(128)}, u32[]{:S(2)}) copy-start(s32[32]{0:T(128)} %lsize.7) | copy-start | bytes 388
  46.0 14.6 %copy-start.6 = (s32[8]{0:T(128)S(1)}, s32[8]{0:T(128)}, u32[]{:S(2)}) copy-start(s32[8]{0:T(128)} %rsize.7) | copy-start | bytes 100
  49.0 31.6 %all-to-all-start = ((f32[16,264,128]{2,1,0:T(8,128)}), f32[16,264,128]{2,1,0:T(8,128)S(1)}, u32[]{:S(2)}, u32[]{:S(2)}) async-start(f32[16,264,128]{2,1,0:T(8,128)} %far_slots.1), calls=%async_computation | async-start | bytes 4325376 | tf_op jit(solution)/shard_map/all_to_all | solution.py:579
  55.8 4.8 %collective-permute-start.10 = (f32[16,16,128]{2,1,0:T(8,128)S(1)}, f32[16,16,128]{2,1,0:T(8,128)S(1)}, u32[]{:S(2)}, u32[]{:S(2)}) collective-permute-start(f32[16,16,128]{2,1,0:T(8,128)S(1)} %slice.8), channel_id=1, source_target_pairs={{0,16},{16,0},{1,17},{17,1},{2,18},{18,2},{3,19},{19,3},{4,20},{20... | collective-permute-start | bytes 393224 | tf_op jit(solution)/shard_map/ppermute | solution.py:575
  67.2 1.4 %copy-start.1 = (bf16[256,4096]{1,0:T(8,128)(2,1)}, bf16[256,4096]{1,0:T(8,128)(2,1)S(1)}, u32[]{:S(2)}) copy-start(bf16[256,4096]{1,0:T(8,128)(2,1)S(1)} %get-tuple-element.33.m_lo) | copy-start | bytes 6291460
  68.6 1.4 %copy-start.8 = (bf16[4096,256]{1,0:T(8,128)(2,1)}, bf16[4096,256]{1,0:T(8,128)(2,1)S(1)}, u32[]{:S(2)}) copy-start(bf16[4096,256]{1,0:T(8,128)(2,1)S(1)} %get-tuple-element.37.r_hi) | copy-start | bytes 6291460
  80.6 11.9 %copy-start.9 = (bf16[4096,256]{1,0:T(8,128)(2,1)S(1)}, bf16[4096,256]{1,0:T(8,128)(2,1)}, u32[]{:S(2)}) copy-start(bf16[4096,256]{1,0:T(8,128)(2,1)} %copy-done.8) | copy-start | bytes 6291460
  80.6 11.9 %copy-start.11 = (bf16[4096,256]{1,0:T(8,128)(2,1)S(1)}, bf16[4096,256]{1,0:T(8,128)(2,1)}, u32[]{:S(2)}) copy-start(bf16[4096,256]{1,0:T(8,128)(2,1)} %copy-done.10) | copy-start | bytes 6291460
  84.8 7.7 %collective-permute-start.11 = (f32[256,256]{1,0:T(8,128)S(1)}, f32[256,256]{1,0:T(8,128)S(1)}, u32[]{:S(2)}, u32[]{:S(2)}) collective-permute-start(f32[256,256]{1,0:T(8,128)S(1)} %get-tuple-element.34.part_a), channel_id=1, source_target_pairs={{0,16},{16,0},{1,17},{17,1},{2,18},{18,2},{3,19},{19,3},{4,20},{20... | collective-permute-start | bytes 786440 | tf_op jit(solution)/shard_map/ppermute | solution.py:582
  97.2 1.6 %collective-permute-start.12 = (f32[256,256]{1,0:T(8,128)S(1)}, f32[256,256]{1,0:T(8,128)S(1)}, u32[]{:S(2)}, u32[]{:S(2)}) collective-permute-start(f32[256,256]{1,0:T(8,128)S(1)} %get-tuple-element.41.part_a), channel_id=1, source_target_pairs={{0,16},{16,0},{1,17},{17,1},{2,18},{18,2},{3,19},{19,3},{4,20},{20... | collective-permute-start | bytes 786440 | tf_op jit(solution)/shard_map/ppermute | solution.py:583
  104.5 12.3 %all-to-all-start.2 = ((f32[16,40,128]{2,1,0:T(8,128)}), f32[16,40,128]{2,1,0:T(8,128)S(1)}, u32[]{:S(2)}, u32[]{:S(2)}) async-start(f32[16,40,128]{2,1,0:T(8,128)} %image_three.1), calls=%async_computation.2 | async-start | bytes 655360 | tf_op jit(solution)/shard_map/all_to_all | solution.py:585
  116.8 4.6 %collective-permute-start.15 = (f32[16,128]{1,0:T(8,128)S(1)}, f32[16,128]{1,0:T(8,128)S(1)}, u32[]{:S(2)}, u32[]{:S(2)}) collective-permute-start(f32[16,128]{1,0:T(8,128)S(1)} %bitcast.10), channel_id=1, source_target_pairs={{0,96},{32,0},{64,32},{96,64},{1,97},{33,1},{65,33},{97,65},{2,98}... | collective-permute-start | bytes 24584 | tf_op jit(solution)/shard_map/ppermute | solution.py:588
  117.9 4.0 %collective-permute-start.14 = (f32[16,128]{1,0:T(8,128)S(1)}, f32[16,128]{1,0:T(8,128)S(1)}, u32[]{:S(2)}, u32[]{:S(2)}) collective-permute-start(f32[16,128]{1,0:T(8,128)S(1)} %bitcast.11), channel_id=1, source_target_pairs={{0,64},{32,96},{64,0},{96,32},{1,65},{33,97},{65,1},{97,33},{2,66}... | collective-permute-start | bytes 24584 | tf_op jit(solution)/shard_map/ppermute | solution.py:588
  118.6 3.7 %collective-permute-start.13 = (f32[16,128]{1,0:T(8,128)S(1)}, f32[16,128]{1,0:T(8,128)S(1)}, u32[]{:S(2)}, u32[]{:S(2)}) collective-permute-start(f32[16,128]{1,0:T(8,128)S(1)} %bitcast.12), channel_id=1, source_target_pairs={{0,32},{32,64},{64,96},{96,0},{1,33},{33,65},{65,97},{97,1},{2,34}... | collective-permute-start | bytes 24584 | tf_op jit(solution)/shard_map/ppermute | solution.py:588
  118.6 8.5 %collective-permute-start.17 = (f32[8,32,128]{2,1,0:T(8,128)S(1)}, f32[8,32,128]{2,1,0:T(8,128)S(1)}, u32[]{:S(2)}, u32[]{:S(2)}) collective-permute-start(f32[8,32,128]{2,1,0:T(8,128)S(1)} %constant_dynamic-slice_fusion), channel_id=1, source_target_pairs={{0,16},{16,0},{1,17},{17,1},{2,18},{18,2},{3,19},{19,3},{4,20},{20... | collective-permute-start | bytes 393224 | tf_op jit(solution)/shard_map/ppermute | solution.py:591
  122.3 4.7 %collective-permute-start.16 = (f32[64,128]{1,0:T(8,128)S(1)}, f32[64,128]{1,0:T(8,128)S(1)}, u32[]{:S(2)}, u32[]{:S(2)}) collective-permute-start(f32[64,128]{1,0:T(8,128)S(1)} %pad_maximum_fusion.own_stats), channel_id=1, source_target_pairs={{0,16},{16,0},{1,17},{17,1},{2,18},{18,2},{3,19},{19,3},{4,20},{20... | collective-permute-start | bytes 98312 | tf_op jit(solution)/shard_map/ppermute | solution.py:593
  (2 other events, 2.7 us)

commit v18 on v14

--- a/solution.py
+++ b/solution.py
@@ -436,8 +436,7 @@
 ):
     mask = mask_of(*live_sizes(ids, rsector, rsector_other, sector, lsize, rsize))
     image = jnp.where(mask, part_a[...] + part_b[...], 0.0)
-    i, j = grids(8, HALF)
-    beta = total(jnp.where((j == 2) & (i == 0), stats_in[...], 0.0))
+    beta = stats_in[0:1, 2:3]
     alpha, norm, vec = lanczos(image, q2[...], q1[...], beta)
     pick = jnp.where(ids[1] == 0, q2[...], vec)
     for n in range(16):

time: 129 us -> 129 us (level)
  transfers between devices with their start and end apart: 21 -> 21, of which waited for: 11 -> 11; matrix products, arithmetic and copies ran while one was open for 1% -> 1% of each run, Pallas kernels for 8% -> 9%
where the time goes in v18:
time: 129 us
  waiting for transfers between devices  45.7 us (35%)
  starting transfers between devices  44.8 us (35%)
  Pallas kernels  30.7 us (24%)
  local copies, waits for them, and re-layouts  6.49 us (5%)
    all_to_all x1, waiting for transfers between devices, local(): left_arrived = lax.all_to_all(left_sent, COL, 0, 0, tiled=True)  10.3 us
    ppermute x2, waiting for transfers between devices, local(): far = [lax.ppermute(below[0], 'y', UP), lax.ppermute(above[1], 'y', DOWN)]  9.75 us
    ppermute x2, waiting for transfers between devices, local(): above = [lax.ppermute(x, 'y', DOWN) for x in (mine, theirs)]  8.28 us
    all_to_all x1, waiting for transfers between devices, local(): got = lax.all_to_all(sent, COL, 0, 0, tiled=True)  7.92 us
    all_to_all x1, starting transfers between devices, local(): arrived = lax.all_to_all(slots, COL, 0, 0, tiled=True)  7.79 us
    ppermute x2, starting transfers between devices, local(): lax.ppermute(part, 'c', SWAP)  6.2 us
    pallas_call x1, Pallas kernels, image_three(): pl.pallas_call(image_three_body, in_specs=[smem()] * 6 + [vmem()] * 9, ou...  5.64 us
    unnamed x27, local copies, waits for them, and re-layouts  5.55 us
  transfers between devices with their start and end apart: 21, of which 11 were waited for; matrix products, arithmetic and copies ran while one was open for 1% of the time, Pallas kernels for 9%

profile of v18, /device:TPU:1, one launch (start us, length us, event | category | flops | bytes accessed | tf_op | source)
XLA Modules:
  0.0 128.8 jit_solution(17753162710175114528)
XLA Ops:
  0.7 3.0 %fold.1 = (f32[4,264,128]{2,1,0:T(8,128)}, f32[4,264,128]{2,1,0:T(8,128)}, f32[9,264,128]{2,1,0:T(8,128)S(1)}) custom-call(s32[3]{0:T(128)S(1)} %pad_add_fusion.ids, f32[4,2,256,256]{3,2,1,0:T(8,128)} %left_env.1, f32[8,2,256,256]{3,2,1,0:T(8,128)} %right_env.1), custom_call_target="tpu_custom_call" | custom-call | flops 1000000 | bytes 6000000 | tf_op jit(solution)/shard_map/fold/pallas_call | solution.py:146
  3.7 1.5 %collective-permute-start = (f32[4,264,128]{2,1,0:T(8,128)}, f32[4,264,128]{2,1,0:T(8,128)S(1)}, u32[]{:S(2)}, u32[]{:S(2)}) collective-permute-start(f32[4,264,128]{2,1,0:T(8,128)} %get-tuple-element.24), channel_id=1, source_target_pairs={{0,16},{16,0},{1,17},{17,1},{2,18},{18,2},{3,19},{19,3},{4,20},{20... | collective-permute-start | bytes 1622024 | tf_op jit(solution)/shard_map/ppermute | solution.py:560
  5.9 1.4 %collective-permute-start.4 = (f32[4,264,128]{2,1,0:T(8,128)}, f32[4,264,128]{2,1,0:T(8,128)S(1)}, u32[]{:S(2)}, u32[]{:S(2)}) collective-permute-start(f32[4,264,128]{2,1,0:T(8,128)} %get-tuple-element.26.mine), channel_id=1, source_target_pairs={{0,32},{32,64},{64,96},{96,0},{1,33},{33,65},{65,97},{97,1},{2,34}... | collective-permute-start | bytes 1622024 | tf_op jit(solution)/shard_map/ppermute | solution.py:564
  7.3 2.5 %collective-permute-start.6 = (f32[4,264,128]{2,1,0:T(8,128)S(1)}, f32[4,264,128]{2,1,0:T(8,128)S(1)}, u32[]{:S(2)}, u32[]{:S(2)}) collective-permute-start(f32[4,264,128]{2,1,0:T(8,128)S(1)} %collective-permute-done.theirs), channel_id=1, source_target_pairs={{0,96},{32,0},{64,32},{96,64},{1,97},{33,1},{65,33},{97,65},{2,98}... | collective-permute-start | bytes 1622024 | tf_op jit(solution)/shard_map/ppermute | solution.py:565
  9.9 2.1 %right_slots.1 = f32[16,280,128]{2,1,0:T(8,128)} custom-call(s32[3]{0:T(128)S(1)} %pad_add_fusion.ids, s32[8]{0:T(128)S(1)} %copy-done.5, s32[8]{0:T(128)S(1)} %collective-permute-done.1.rsector_other, s32[8,2]{1,0:T(8,128)S(1)} %copy.11.on, s32[8,2]{1,0:T(8,128)S(1)} %collective-permute-done.2.on_other, f32[8,16,256]{2,1,0:T(8,128)S(1)} %bitcast.8, ...), custom_call_target="tpu_custom_call" | custom-call | flops 4000000 | bytes 6000000 | tf_op jit(solution)/shard_map/right_slots/pallas_call | solution.py:188
  12.0 7.8 %all-to-all-start.1 = ((f32[16,280,128]{2,1,0:T(8,128)}), f32[16,280,128]{2,1,0:T(8,128)}, u32[]{:S(2)}, u32[]{:S(2)}) async-start(f32[16,280,128]{2,1,0:T(8,128)} %right_slots.1), calls=%async_computation.1 | async-start | bytes 4587520 | tf_op jit(solution)/shard_map/all_to_all | solution.py:572
  21.4 3.2 %collective-permute-start.7 = (f32[4,264,128]{2,1,0:T(8,128)S(1)}, f32[4,264,128]{2,1,0:T(8,128)S(1)}, u32[]{:S(2)}, u32[]{:S(2)}) collective-permute-start(f32[4,264,128]{2,1,0:T(8,128)S(1)} %collective-permute-done.6.above_b), channel_id=1, source_target_pairs={{0,96},{32,0},{64,32},{96,64},{1,97},{33,1},{65,33},{97,65},{2,98}... | collective-permute-start | bytes 1622024 | tf_op jit(solution)/shard_map/ppermute | solution.py:566
  24.6 8.3 %collective-permute-done.8.above_a = f32[4,264,128]{2,1,0:T(8,128)S(1)} collective-permute-done((f32[4,264,128]{2,1,0:T(8,128)S(1)}, f32[4,264,128]{2,1,0:T(8,128)S(1)}, u32[]{:S(2)}, u32[]{:S(2)}) %collective-permute-start.8) | collective-permute-done | bytes 540704 | tf_op jit(solution)/shard_map/ppermute | solution.py:565
  33.9 1.8 %near_slots.1.near = f32[16,264,128]{2,1,0:T(8,128)} custom-call(s32[3]{0:T(128)S(1)} %pad_add_fusion.ids, s32[64]{0:T(128)S(1)} %copy-done.4, f32[4,264,128]{2,1,0:T(8,128)S(1)} %copy-done.2, f32[4,264,128]{2,1,0:T(8,128)S(1)} %collective-permute-done.theirs, f32[4,264,128]{2,1,0:T(8,128)S(1)} %collective-permute-done.8.above_a, ...), custom_call_target="tpu_custom_call" | custom-call | flops 1000000000 | bytes 4000000 | tf_op jit(solution)/shard_map/near_slots/pallas_call | solution.py:255
  35.8 9.8 %collective-permute-done.5.far_a = f32[4,264,128]{2,1,0:T(8,128)S(1)} collective-permute-done((f32[4,264,128]{2,1,0:T(8,128)S(1)}, f32[4,264,128]{2,1,0:T(8,128)S(1)}, u32[]{:S(2)}, u32[]{:S(2)}) %collective-permute-start.5) | collective-permute-done | bytes 540704 | tf_op jit(solution)/shard_map/ppermute | solution.py:566
  45.5 1.7 %far_slots.1 = f32[16,264,128]{2,1,0:T(8,128)} custom-call(s32[3]{0:T(128)S(1)} %pad_add_fusion.ids, s32[64]{0:T(128)S(1)} %copy-done.4, f32[4,264,128]{2,1,0:T(8,128)S(1)} %collective-permute-done.5.far_a, f32[4,264,128]{2,1,0:T(8,128)S(1)} %collective-permute-done.7.far_b, f32[16,264,128]{2,1,0:T(8,128)} %near_slots.1.near), custom_call_target="tpu_custom_call", output_to_operand_aliasing={{}: (4, {})} | custom-call | flops 15000000512 | bytes 4000000 | tf_op jit(solution)/shard_map/far_slots/pallas_call | solution.py:265
  47.2 3.6 %all-to-all-done.1.slots = f32[16,280,128]{2,1,0:T(8,128)} async-done(((f32[16,280,128]{2,1,0:T(8,128)}), f32[16,280,128]{2,1,0:T(8,128)}, u32[]{:S(2)}, u32[]{:S(2)}) %all-to-all-start.1) | async-done | bytes 2293792 | tf_op jit(solution)/shard_map/all_to_all | solution.py:572
  50.8 3.7 %all-to-all-start = ((f32[16,264,128]{2,1,0:T(8,128)}), f32[16,264,128]{2,1,0:T(8,128)S(1)}, u32[]{:S(2)}, u32[]{:S(2)}) async-start(f32[16,264,128]{2,1,0:T(8,128)} %far_slots.1), calls=%async_computation | async-start | bytes 4325376 | tf_op jit(solution)/shard_map/all_to_all | solution.py:578
  55.5 2.9 %collective-permute-start.10 = (f32[16,16,128]{2,1,0:T(8,128)S(1)}, f32[16,16,128]{2,1,0:T(8,128)S(1)}, u32[]{:S(2)}, u32[]{:S(2)}) collective-permute-start(f32[16,16,128]{2,1,0:T(8,128)S(1)} %slice.8), channel_id=1, source_target_pairs={{0,16},{16,0},{1,17},{17,1},{2,18},{18,2},{3,19},{19,3},{4,20},{20... | collective-permute-start | bytes 393224 | tf_op jit(solution)/shard_map/ppermute | solution.py:574
  59.4 5.3 %first_vector.1 = (bf16[4096,256]{1,0:T(8,128)(2,1)S(1)}, bf16[4096,256]{1,0:T(8,128)(2,1)S(1)}, bf16[256,4096]{1,0:T(8,128)(2,1)S(1)}, bf16[256,4096]{1,0:T(8,1...) custom-call(s32[3]{0:T(128)S(1)} %pad_add_fusion.ids, s32[8]{0:T(128)S(1)} %copy-done.5, ...), custom_call_target="tpu_custom_call" | custom-call | flops 1700000000 | bytes 12000000 | tf_op jit(solution)/shard_map/first_vector/pallas_call | solution.py:326
  64.7 1.3 %copy-done = bf16[256,4096]{1,0:T(8,128)(2,1)} copy-done((bf16[256,4096]{1,0:T(8,128)(2,1)}, bf16[256,4096]{1,0:T(8,128)(2,1)S(1)}, u32[]{:S(2)}) %copy-start) | copy-done | bytes 2097176
  66.1 1.4 %copy-done.1 = bf16[256,4096]{1,0:T(8,128)(2,1)} copy-done((bf16[256,4096]{1,0:T(8,128)(2,1)}, bf16[256,4096]{1,0:T(8,128)(2,1)S(1)}, u32[]{:S(2)}) %copy-start.1) | copy-done | bytes 2097176
  67.4 1.4 %copy-done.8 = bf16[4096,256]{1,0:T(8,128)(2,1)} copy-done((bf16[4096,256]{1,0:T(8,128)(2,1)}, bf16[4096,256]{1,0:T(8,128)(2,1)S(1)}, u32[]{:S(2)}) %copy-start.8) | copy-done | bytes 2097176
  68.8 1.3 %copy-done.10 = bf16[4096,256]{1,0:T(8,128)(2,1)} copy-done((bf16[4096,256]{1,0:T(8,128)(2,1)}, bf16[4096,256]{1,0:T(8,128)(2,1)S(1)}, u32[]{:S(2)}) %copy-start.10) | copy-done | bytes 2097176
  70.2 10.3 %all-to-all-done.arrived = f32[16,264,128]{2,1,0:T(8,128)S(1)} async-done(((f32[16,264,128]{2,1,0:T(8,128)}), f32[16,264,128]{2,1,0:T(8,128)S(1)}, u32[]{:S(2)}, u32[]{:S(2)}) %all-to-all-start) | async-done | bytes 2162720 | tf_op jit(solution)/shard_map/all_to_all | solution.py:578
  80.5 4.2 %image_one.1 = (bf16[4096,256]{1,0:T(8,128)(2,1)S(1)}, bf16[4096,256]{1,0:T(8,128)(2,1)S(1)}, f32[256,256]{1,0:T(8,128)S(1)}) custom-call(f32[16,264,128]{2,1,0:T(8,128)S(1)} %all-to-all-done.arrived, bf16[256,4096]{1,0:T(8,128)(2,1)} %copy-done, bf16[256,4096]{1,0:T(8,128)(2,1)} %copy-done.1), custom_call_target="tpu_custom_call" | custom-call | flops 1700000000 | bytes 10000000 | tf_op jit(solution)/shard_map/image_one/pallas_call | solution.py:366
  84.8 5.7 %collective-permute-start.11 = (f32[256,256]{1,0:T(8,128)S(1)}, f32[256,256]{1,0:T(8,128)S(1)}, u32[]{:S(2)}, u32[]{:S(2)}) collective-permute-start(f32[256,256]{1,0:T(8,128)S(1)} %get-tuple-element.34.part_a), channel_id=1, source_target_pairs={{0,16},{16,0},{1,17},{17,1},{2,18},{18,2},{3,19},{19,3},{4,20},{20... | collective-permute-start | bytes 786440 | tf_op jit(solution)/shard_map/ppermute | solution.py:581
  90.5 1.2 collective-permute-done.11.part_b
  91.7 4.7 %image_two.1 = (f32[256,256]{1,0:T(8,128)S(1)}, f32[256,256]{1,0:T(8,128)S(1)}, f32[8,128]{1,0:T(8,128)S(1)}) custom-call(s32[3]{0:T(128)S(1)} %pad_add_fusion.ids, s32[8]{0:T(128)S(1)} %copy-done.5, s32[8]{0:T(128)S(1)} %collective-permute-done.1.rsector_other, s32[64]{0:T(128)S(1)} %copy-done.4, s32[32]{0:T(128)S(1)} %copy-done.6, s32[8]{0:T(128)S(1)} %copy-done.7, ...), custom_call_target="tpu_custom_call" | custom-call | flops 3300000000 | bytes 9000000 | tf_op jit(solution)/shard_map/image_two/pallas_call | solution.py:418
  96.8 1.2 collective-permute-done.12.part_b
  98.0 5.6 %image_three.1 = f32[16,40,128]{2,1,0:T(8,128)} custom-call(s32[3]{0:T(128)S(1)} %pad_add_fusion.ids, s32[8]{0:T(128)S(1)} %copy-done.5, s32[8]{0:T(128)S(1)} %collective-permute-done.1.rsector_other, s32[64]{0:T(128)S(1)} %copy-done.4, s32[32]{0:T(128)S(1)} %copy-done.6, s32[8]{0:T(128)S(1)} %copy-done.7, f32[256,256]{1,0:T(8,128)S(1)} %get-tuple-element.41.part_a, ...), custom_call_target="tpu_custom_call" | custom-call | flops 3300000000 | bytes 9000000 | tf_op jit(solution)/shard_map/image_three/pallas_call | solution.py:453
  103.6 3.5 %all-to-all-start.2 = ((f32[16,40,128]{2,1,0:T(8,128)}), f32[16,40,128]{2,1,0:T(8,128)S(1)}, u32[]{:S(2)}, u32[]{:S(2)}) async-start(f32[16,40,128]{2,1,0:T(8,128)} %image_three.1), calls=%async_computation.2 | async-start | bytes 655360 | tf_op jit(solution)/shard_map/all_to_all | solution.py:584
  107.2 7.9 %all-to-all-done.2.got = f32[16,40,128]{2,1,0:T(8,128)S(1)} async-done(((f32[16,40,128]{2,1,0:T(8,128)}), f32[16,40,128]{2,1,0:T(8,128)S(1)}, u32[]{:S(2)}, u32[]{:S(2)}) %all-to-all-start.2) | async-done | bytes 327712 | tf_op jit(solution)/shard_map/all_to_all | solution.py:584
  115.1 2.8 %collective-permute-start.15 = (f32[16,128]{1,0:T(8,128)S(1)}, f32[16,128]{1,0:T(8,128)S(1)}, u32[]{:S(2)}, u32[]{:S(2)}) collective-permute-start(f32[16,128]{1,0:T(8,128)S(1)} %bitcast.10), channel_id=1, source_target_pairs={{0,96},{32,0},{64,32},{96,64},{1,97},{33,1},{65,33},{97,65},{2,98}... | collective-permute-start | bytes 24584 | tf_op jit(solution)/shard_map/ppermute | solution.py:587
  118.6 2.8 %collective-permute-start.17 = (f32[8,32,128]{2,1,0:T(8,128)S(1)}, f32[8,32,128]{2,1,0:T(8,128)S(1)}, u32[]{:S(2)}, u32[]{:S(2)}) collective-permute-start(f32[8,32,128]{2,1,0:T(8,128)S(1)} %constant_dynamic-slice_fusion), channel_id=1, source_target_pairs={{0,16},{16,0},{1,17},{17,1},{2,18},{18,2},{3,19},{19,3},{4,20},{20... | collective-permute-start | bytes 393224 | tf_op jit(solution)/shard_map/ppermute | solution.py:590
  121.9 3.6 %collective-permute-start.16 = (f32[64,128]{1,0:T(8,128)S(1)}, f32[64,128]{1,0:T(8,128)S(1)}, u32[]{:S(2)}, u32[]{:S(2)}) collective-permute-start(f32[64,128]{1,0:T(8,128)S(1)} %pad_maximum_fusion.own_stats), channel_id=1, source_target_pairs={{0,16},{16,0},{1,17},{17,1},{2,18},{18,2},{3,19},{19,3},{4,20},{20... | collective-permute-start | bytes 98312 | tf_op jit(solution)/shard_map/ppermute | solution.py:592
  126.4 2.2 %finish.1 = (f32[8,16,256]{2,1,0:T(8,128)}, f32[1,1]{1,0:T(1,128)}) custom-call(s32[3]{0:T(128)S(1)} %pad_add_fusion.ids, s32[64]{0:T(128)S(1)} %copy-done.4, s32[8]{0:T(128)S(1)} %copy-done.5, s32[32]{0:T(128)S(1)} %copy-done.6, s32[8]{0:T(128)S(1)} %copy-done.7, f32[64,128]{1,0:T(8,128)S(1)} %pad_maximum_fusion.own_stats, ...), custom_call_target="tpu_custom_call" | custom-call | tf_op jit(solution)/shard_map/finish/pallas_call | solution.py:534
  (51 shorter events, 7.9 us)
Async XLA Ops:
  0.7 4.5 %copy-start.3 = (f32[8,256,16]{1,2,0:T(8,128)S(1)}, f32[8,256,16]{1,2,0:T(8,128)}, u32[]{:S(2)}) copy-start(f32[8,256,16]{1,2,0:T(8,128)} %param.8) | copy-start | bytes 393220
  0.7 4.6 %copy-start.5 = (s32[8]{0:T(128)S(1)}, s32[8]{0:T(128)}, u32[]{:S(2)}) copy-start(s32[8]{0:T(128)} %rsector.9) | copy-start | bytes 100
  0.7 5.0 %copy-start.12 = (s32[8,2]{0,1:T(2,128)S(1)}, s32[8,2]{0,1:T(2,128)}, u32[]{:S(2)}) copy-start(s32[8,2]{0,1:T(2,128)} %param.13) | copy-start | bytes 196
  3.7 3.6 %collective-permute-start = (f32[4,264,128]{2,1,0:T(8,128)}, f32[4,264,128]{2,1,0:T(8,128)S(1)}, u32[]{:S(2)}, u32[]{:S(2)}) collective-permute-start(f32[4,264,128]{2,1,0:T(8,128)} %get-tuple-element.24), channel_id=1, source_target_pairs={{0,16},{16,0},{1,17},{17,1},{2,18},{18,2},{3,19},{19,3},{4,20},{20... | collective-permute-start | bytes 1622024 | tf_op jit(solution)/shard_map/ppermute | solution.py:560
  5.2 2.1 %collective-permute-start.3 = (f32[8,16,256]{2,1,0:T(8,128)S(1)}, f32[8,16,256]{2,1,0:T(8,128)S(1)}, u32[]{:S(2)}, u32[]{:S(2)}) collective-permute-start(f32[8,16,256]{2,1,0:T(8,128)S(1)} %bitcast.7), channel_id=1, source_target_pairs={{0,16},{16,0},{1,17},{17,1},{2,18},{18,2},{3,19},{19,3},{4,20},{20... | collective-permute-start | bytes 393224 | tf_op jit(solution)/shard_map/ppermute | solution.py:557
  5.3 2.0 %collective-permute-start.1 = (s32[8]{0:T(128)S(1)}, s32[8]{0:T(128)S(1)}, u32[]{:S(2)}, u32[]{:S(2)}) collective-permute-start(s32[8]{0:T(128)S(1)} %copy-done.5), channel_id=1, source_target_pairs={{0,16},{16,0},{1,17},{17,1},{2,18},{18,2},{3,19},{19,3},{4,20},{20... | collective-permute-start | bytes 104 | tf_op jit(solution)/shard_map/ppermute | solution.py:555
  5.8 1.5 %collective-permute-start.2 = (s32[8,2]{1,0:T(8,128)S(1)}, s32[8,2]{1,0:T(8,128)S(1)}, u32[]{:S(2)}, u32[]{:S(2)}) collective-permute-start(s32[8,2]{1,0:T(8,128)S(1)} %copy.11.on), channel_id=1, source_target_pairs={{0,16},{16,0},{1,17},{17,1},{2,18},{18,2},{3,19},{19,3},{4,20},{20... | collective-permute-start | bytes 200 | tf_op jit(solution)/shard_map/ppermute | solution.py:556
  5.9 15.4 %collective-permute-start.4 = (f32[4,264,128]{2,1,0:T(8,128)}, f32[4,264,128]{2,1,0:T(8,128)S(1)}, u32[]{:S(2)}, u32[]{:S(2)}) collective-permute-start(f32[4,264,128]{2,1,0:T(8,128)} %get-tuple-element.26.mine), channel_id=1, source_target_pairs={{0,32},{32,64},{64,96},{96,0},{1,33},{33,65},{65,97},{97,1},{2,34}... | collective-permute-start | bytes 1622024 | tf_op jit(solution)/shard_map/ppermute | solution.py:564
  7.3 14.1 %collective-permute-start.6 = (f32[4,264,128]{2,1,0:T(8,128)S(1)}, f32[4,264,128]{2,1,0:T(8,128)S(1)}, u32[]{:S(2)}, u32[]{:S(2)}) collective-permute-start(f32[4,264,128]{2,1,0:T(8,128)S(1)} %collective-permute-done.theirs), channel_id=1, source_target_pairs={{0,96},{32,0},{64,32},{96,64},{1,97},{33,1},{65,33},{97,65},{2,98}... | collective-permute-start | bytes 1622024 | tf_op jit(solution)/shard_map/ppermute | solution.py:565
  12.0 7.8 %copy-start.2 = (f32[4,264,128]{2,1,0:T(8,128)S(1)}, f32[4,264,128]{2,1,0:T(8,128)}, u32[]{:S(2)}) copy-start(f32[4,264,128]{2,1,0:T(8,128)} %get-tuple-element.26.mine) | copy-start | bytes 1622020
  12.0 21.9 %copy-start.4 = (s32[64]{0:T(128)S(1)}, s32[64]{0:T(128)}, u32[]{:S(2)}) copy-start(s32[64]{0:T(128)} %sector.7) | copy-start | bytes 772
  12.0 38.8 %all-to-all-start.1 = ((f32[16,280,128]{2,1,0:T(8,128)}), f32[16,280,128]{2,1,0:T(8,128)}, u32[]{:S(2)}, u32[]{:S(2)}) async-start(f32[16,280,128]{2,1,0:T(8,128)} %right_slots.1), calls=%async_computation.1 | async-start | bytes 4587520 | tf_op jit(solution)/shard_map/all_to_all | solution.py:572
  19.8 13.0 %collective-permute-start.8 = (f32[4,264,128]{2,1,0:T(8,128)S(1)}, f32[4,264,128]{2,1,0:T(8,128)S(1)}, u32[]{:S(2)}, u32[]{:S(2)}) collective-permute-start(f32[4,264,128]{2,1,0:T(8,128)S(1)} %copy-done.2), channel_id=1, source_target_pairs={{0,96},{32,0},{64,32},{96,64},{1,97},{33,1},{65,33},{97,65},{2,98}... | collective-permute-start | bytes 1622024 | tf_op jit(solution)/shard_map/ppermute | solution.py:565
  20.3 13.6 %collective-permute-start.9 = (f32[4,264,128]{2,1,0:T(8,128)S(1)}, f32[4,264,128]{2,1,0:T(8,128)S(1)}, u32[]{:S(2)}, u32[]{:S(2)}) collective-permute-start(f32[4,264,128]{2,1,0:T(8,128)S(1)} %collective-permute-done.theirs), channel_id=1, source_target_pairs={{0,32},{32,64},{64,96},{96,0},{1,33},{33,65},{65,97},{97,1},{2,34}... | collective-permute-start | bytes 1622024 | tf_op jit(solution)/shard_map/ppermute | solution.py:564
  21.3 24.2 %collective-permute-start.5 = (f32[4,264,128]{2,1,0:T(8,128)S(1)}, f32[4,264,128]{2,1,0:T(8,128)S(1)}, u32[]{:S(2)}, u32[]{:S(2)}) collective-permute-start(f32[4,264,128]{2,1,0:T(8,128)S(1)} %collective-permute-done.4.below_a), channel_id=1, source_target_pairs={{0,32},{32,64},{64,96},{96,0},{1,33},{33,65},{65,97},{97,1},{2,34}... | collective-permute-start | bytes 1622024 | tf_op jit(solution)/shard_map/ppermute | solution.py:566
  21.4 24.1 %collective-permute-start.7 = (f32[4,264,128]{2,1,0:T(8,128)S(1)}, f32[4,264,128]{2,1,0:T(8,128)S(1)}, u32[]{:S(2)}, u32[]{:S(2)}) collective-permute-start(f32[4,264,128]{2,1,0:T(8,128)S(1)} %collective-permute-done.6.above_b), channel_id=1, source_target_pairs={{0,96},{32,0},{64,32},{96,64},{1,97},{33,1},{65,33},{97,65},{2,98}... | collective-permute-start | bytes 1622024 | tf_op jit(solution)/shard_map/ppermute | solution.py:566
  47.2 12.2 %copy-start.6 = (s32[32]{0:T(128)S(1)}, s32[32]{0:T(128)}, u32[]{:S(2)}) copy-start(s32[32]{0:T(128)} %lsize.7) | copy-start | bytes 388
  47.2 12.2 %copy-start.7 = (s32[8]{0:T(128)S(1)}, s32[8]{0:T(128)}, u32[]{:S(2)}) copy-start(s32[8]{0:T(128)} %rsize.7) | copy-start | bytes 100
  50.8 29.7 %all-to-all-start = ((f32[16,264,128]{2,1,0:T(8,128)}), f32[16,264,128]{2,1,0:T(8,128)S(1)}, u32[]{:S(2)}, u32[]{:S(2)}) async-start(f32[16,264,128]{2,1,0:T(8,128)} %far_slots.1), calls=%async_computation | async-start | bytes 4325376 | tf_op jit(solution)/shard_map/all_to_all | solution.py:578
  55.5 3.9 %collective-permute-start.10 = (f32[16,16,128]{2,1,0:T(8,128)S(1)}, f32[16,16,128]{2,1,0:T(8,128)S(1)}, u32[]{:S(2)}, u32[]{:S(2)}) collective-permute-start(f32[16,16,128]{2,1,0:T(8,128)S(1)} %slice.8), channel_id=1, source_target_pairs={{0,16},{16,0},{1,17},{17,1},{2,18},{18,2},{3,19},{19,3},{4,20},{20... | collective-permute-start | bytes 393224 | tf_op jit(solution)/shard_map/ppermute | solution.py:574
  66.1 1.4 %copy-start.1 = (bf16[256,4096]{1,0:T(8,128)(2,1)}, bf16[256,4096]{1,0:T(8,128)(2,1)S(1)}, u32[]{:S(2)}) copy-start(bf16[256,4096]{1,0:T(8,128)(2,1)S(1)} %get-tuple-element.33.m_lo) | copy-start | bytes 6291460
  67.4 1.4 %copy-start.8 = (bf16[4096,256]{1,0:T(8,128)(2,1)}, bf16[4096,256]{1,0:T(8,128)(2,1)S(1)}, u32[]{:S(2)}) copy-start(bf16[4096,256]{1,0:T(8,128)(2,1)S(1)} %get-tuple-element.37.r_hi) | copy-start | bytes 6291460
  80.5 11.2 %copy-start.9 = (bf16[4096,256]{1,0:T(8,128)(2,1)S(1)}, bf16[4096,256]{1,0:T(8,128)(2,1)}, u32[]{:S(2)}) copy-start(bf16[4096,256]{1,0:T(8,128)(2,1)} %copy-done.8) | copy-start | bytes 6291460
  80.5 11.2 %copy-start.11 = (bf16[4096,256]{1,0:T(8,128)(2,1)S(1)}, bf16[4096,256]{1,0:T(8,128)(2,1)}, u32[]{:S(2)}) copy-start(bf16[4096,256]{1,0:T(8,128)(2,1)} %copy-done.10) | copy-start | bytes 6291460
  84.8 6.9 %collective-permute-start.11 = (f32[256,256]{1,0:T(8,128)S(1)}, f32[256,256]{1,0:T(8,128)S(1)}, u32[]{:S(2)}, u32[]{:S(2)}) collective-permute-start(f32[256,256]{1,0:T(8,128)S(1)} %get-tuple-element.34.part_a), channel_id=1, source_target_pairs={{0,16},{16,0},{1,17},{17,1},{2,18},{18,2},{3,19},{19,3},{4,20},{20... | collective-permute-start | bytes 786440 | tf_op jit(solution)/shard_map/ppermute | solution.py:581
  96.4 1.6 %collective-permute-start.12 = (f32[256,256]{1,0:T(8,128)S(1)}, f32[256,256]{1,0:T(8,128)S(1)}, u32[]{:S(2)}, u32[]{:S(2)}) collective-permute-start(f32[256,256]{1,0:T(8,128)S(1)} %get-tuple-element.41.part_a), channel_id=1, source_target_pairs={{0,16},{16,0},{1,17},{17,1},{2,18},{18,2},{3,19},{19,3},{4,20},{20... | collective-permute-start | bytes 786440 | tf_op jit(solution)/shard_map/ppermute | solution.py:582
  103.6 11.5 %all-to-all-start.2 = ((f32[16,40,128]{2,1,0:T(8,128)}), f32[16,40,128]{2,1,0:T(8,128)S(1)}, u32[]{:S(2)}, u32[]{:S(2)}) async-start(f32[16,40,128]{2,1,0:T(8,128)} %image_three.1), calls=%async_computation.2 | async-start | bytes 655360 | tf_op jit(solution)/shard_map/all_to_all | solution.py:584
  115.1 6.3 %collective-permute-start.15 = (f32[16,128]{1,0:T(8,128)S(1)}, f32[16,128]{1,0:T(8,128)S(1)}, u32[]{:S(2)}, u32[]{:S(2)}) collective-permute-start(f32[16,128]{1,0:T(8,128)S(1)} %bitcast.10), channel_id=1, source_target_pairs={{0,96},{32,0},{64,32},{96,64},{1,97},{33,1},{65,33},{97,65},{2,98}... | collective-permute-start | bytes 24584 | tf_op jit(solution)/shard_map/ppermute | solution.py:587
  117.9 4.0 %collective-permute-start.14 = (f32[16,128]{1,0:T(8,128)S(1)}, f32[16,128]{1,0:T(8,128)S(1)}, u32[]{:S(2)}, u32[]{:S(2)}) collective-permute-start(f32[16,128]{1,0:T(8,128)S(1)} %bitcast.11), channel_id=1, source_target_pairs={{0,64},{32,96},{64,0},{96,32},{1,65},{33,97},{65,1},{97,33},{2,66}... | collective-permute-start | bytes 24584 | tf_op jit(solution)/shard_map/ppermute | solution.py:587
  117.9 4.0 %collective-permute-start.13 = (f32[16,128]{1,0:T(8,128)S(1)}, f32[16,128]{1,0:T(8,128)S(1)}, u32[]{:S(2)}, u32[]{:S(2)}) collective-permute-start(f32[16,128]{1,0:T(8,128)S(1)} %bitcast.12), channel_id=1, source_target_pairs={{0,32},{32,64},{64,96},{96,0},{1,33},{33,65},{65,97},{97,1},{2,34}... | collective-permute-start | bytes 24584 | tf_op jit(solution)/shard_map/ppermute | solution.py:587
  118.6 7.8 %collective-permute-start.17 = (f32[8,32,128]{2,1,0:T(8,128)S(1)}, f32[8,32,128]{2,1,0:T(8,128)S(1)}, u32[]{:S(2)}, u32[]{:S(2)}) collective-permute-start(f32[8,32,128]{2,1,0:T(8,128)S(1)} %constant_dynamic-slice_fusion), channel_id=1, source_target_pairs={{0,16},{16,0},{1,17},{17,1},{2,18},{18,2},{3,19},{19,3},{4,20},{20... | collective-permute-start | bytes 393224 | tf_op jit(solution)/shard_map/ppermute | solution.py:590
  121.9 4.5 %collective-permute-start.16 = (f32[64,128]{1,0:T(8,128)S(1)}, f32[64,128]{1,0:T(8,128)S(1)}, u32[]{:S(2)}, u32[]{:S(2)}) collective-permute-start(f32[64,128]{1,0:T(8,128)S(1)} %pad_maximum_fusion.own_stats), channel_id=1, source_target_pairs={{0,16},{16,0},{1,17},{17,1},{2,18},{18,2},{3,19},{19,3},{4,20},{20... | collective-permute-start | bytes 98312 | tf_op jit(solution)/shard_map/ppermute | solution.py:592
  (2 other events, 2.7 us)
